TPU v7x, 256 devices: a whole 4x4x8 slice. The times are simulated.
256 devices in a mesh: ka: 32 (over y, z_hi, x), occ: 8 (over z_lo, core).
Axes of the slice: x: 4, y: 4, z: 8 (z_hi: 2, z_lo: 4; z = z_hi * 4 + z_lo), core: 2. Of those that a mesh axis runs over, the one named last changes fastest.
Arguments:
- factors: bfloat16 [64, 8, 192, 2, 768], P('ka'), may hold values from -0.23925781 to 0.23925781
- occupied_energy: float32 [8], replicated, may hold values from -2 to -0.5
- virtual_energy: bfloat16 [64, 192], P('ka'), may hold values from 0.5 to 3
- conserve: int32 [64, 2], P('ka'), may hold values from 0 to 63, as said below
- pair_lists: int32 [2, 16, 2], P(None, 'occ'), may hold values from 0 to 7, as said below
Outputs:
- density: float32 [64, 192, 2, 192], P('ka', 'occ')
Inputs may be any that keep to these rules, and one draw needn't show every extreme that they name: For a momentum ka among the 2 momenta of block d (momenta d * 2 to d * 2 + 1), (64 - conserve[ka, r]) mod 64 lies in block (d - r - 1) mod 32; the 2 momenta of one block name different momenta in each round. `pair_lists`: each entry is an ordered pair (i, j) of occupied orbitals; every round begins with the pairs (0, 0) and (7, 7); within a round no ordered pair repeats (16 of the 64 ordered pairs appear).
All inputs are finite; a program needn't handle non-finite values.
Results may differ from a plain program's by a relative error of at most 0.00082.
Values may be sent and summed in bfloat16 or wider, within the bound.
No kernel may reach another device: no remote copies, remote signals or barrier semaphores. Data moves between devices by JAX's collectives and lax.ppermute only.
A program may use at most 128 MiB of HBM per device.

v0:
```python
import jax
import jax.numpy as jnp
from jax import lax
from jax.sharding import PartitionSpec as P


def from_behind(array, axis, by):
    size = lax.axis_size(axis)
    return lax.ppermute(array, axis, [(i, (i + by) % size) for i in range(size)])


def cut_along(array, dim, size):
    before, after = (array.shape[:dim], array.shape[dim + 1 :])
    return jnp.moveaxis(array.reshape(*before, size, -1, *after), dim, 0)


def sent_and_summed(array, axis, dim):
    size = lax.axis_size(axis)
    parts = lax.all_to_all(cut_along(array, dim, size), axis, 0, 0, tiled=True)
    return jnp.sum(parts, axis=0)


def build_mates(received, auxiliary):
    real_part = received[..., :auxiliary]
    imaginary = received[..., auxiliary:]
    turned = jnp.concatenate([-imaginary, real_part], axis=-1)
    return jnp.concatenate([received, turned], axis=-2)


def amplitude(left_rows, mate_rows, energy_left, energy_right, occupied_sum):
    values = lax.dot_general(
        left_rows, mate_rows, (((1,), (1,)), ((), ())), preferred_element_type=jnp.float32
    )
    denominator = energy_left[:, None] + energy_right[None, :] - occupied_sum
    return values / jnp.concatenate([denominator, denominator], axis=1)


def density_term(amplitudes, swapped):
    virtuals = amplitudes.shape[0]
    combined = (2.0 * amplitudes - swapped).astype(jnp.bfloat16)
    rounded = amplitudes.astype(jnp.bfloat16)
    turned = jnp.concatenate([-rounded[:, virtuals:], rounded[:, :virtuals]], axis=1)
    stacked = jnp.concatenate([rounded, turned], axis=0)
    return lax.dot_general(
        combined, stacked, (((1,), (1,)), ((), ())), preferred_element_type=jnp.float32
    )


def pair_term(own_block, mate_block, energy_left, energy_right, occupied_energy, pair_row):
    leading = pair_row[0]
    trailing = pair_row[1]
    occupied_sum = occupied_energy[leading] + occupied_energy[trailing]
    amplitudes = amplitude(
        own_block[leading], mate_block[trailing], energy_left, energy_right, occupied_sum
    )
    swapped = amplitude(
        own_block[trailing], mate_block[leading], energy_left, energy_right, occupied_sum
    )
    return density_term(amplitudes, swapped)


def local(factors, occupied_energy, virtual_energy, conserve, pair_lists):
    momenta = factors.shape[0]
    orbitals = factors.shape[1]
    virtuals = factors.shape[2]
    auxiliary = factors.shape[4]
    own = factors.reshape(momenta, orbitals, virtuals, 2 * auxiliary)
    energy_own = virtual_energy.astype(jnp.float32)
    density = jnp.zeros((momenta, virtuals, 2 * virtuals), jnp.float32)
    for round_index in range(conserve.shape[1]):
        portion = orbitals // lax.axis_size("occ")
        portion_block = lax.dynamic_slice_in_dim(
            factors, lax.axis_index("occ") * portion, portion, 1
        )
        shifted, energy_mate = from_behind((portion_block, virtual_energy), "ka", round_index + 1)
        received = lax.all_gather(shifted, "occ", axis=1, tiled=True)
        mates = build_mates(received.reshape(momenta, orbitals, virtuals, 2 * auxiliary), auxiliary)
        energy_mate = energy_mate.astype(jnp.float32)
        for local_index in range(momenta):
            chosen = (momenta - conserve[local_index, round_index] % momenta) % momenta
            mate_block = lax.dynamic_index_in_dim(mates, chosen, 0, keepdims=False)
            energy_right = lax.dynamic_index_in_dim(energy_mate, chosen, 0, keepdims=False)
            own_block = own[local_index]
            energy_left = energy_own[local_index]

            def add_pair(partial_sum, pair_row):
                term = pair_term(
                    own_block, mate_block, energy_left, energy_right, occupied_energy, pair_row
                )
                return (partial_sum + term, None)

            running, ignored = lax.scan(add_pair, density[local_index], pair_lists[round_index])
            density = density.at[local_index].set(running)
    shaped = density.reshape(momenta, virtuals, 2, virtuals)
    return sent_and_summed(shaped, "occ", 1)


def solution(mesh):
    in_specs = (
        P("ka", None, None, None, None),
        P(),
        P("ka", None),
        P("ka", None),
        P(None, "occ", None),
    )
    out_specs = P("ka", "occ", None, None)
    return jax.shard_map(local, mesh=mesh, in_specs=in_specs, out_specs=out_specs, check_vma=False)
```

profile of v0, /device:TPU:10, one launch (start us, length us, event | category | flops | bytes accessed | tf_op | source)
XLA Modules:
  0.0 440.0 jit_solution(3128078142213431730)
XLA Ops:
  6.5 2.1 constant_dynamic-slice_fusion.8
  8.6 1.6 collective-permute-start
  10.2 26.2 %collective-permute-done = bf16[2,1,192,2,768]{4,3,2,1,0:T(2,128)(2,1)S(1)} collective-permute-done((bf16[2,1,192,2,768]{4,3,2,1,0:T(2,128)(2,1)S(1)}, bf16[2,1,192,2,768]{4,3,2,1,0:T(2,128)(2,1)S(1)}, u32[]{:S(2)}, u32[]{:S(2)}) %collective-permute-start) | collective-permute-done | bytes 1179680 | tf_op jit(solution)/shard_map/ppermute | solution.py:9
  36.4 1.0 copy-done.3
  37.5 15.0 %collective-permute-start.2 = (bf16[2,1,192,2,768]{4,3,2,1,0:T(2,128)(2,1)S(1)}, bf16[2,1,192,2,768]{4,3,2,1,0:T(2,128)(2,1)S(1)}, u32[]{:S(2)}, u32[]{:S(2)}) collective-permute-start(bf16[2,1,192,2,768]{4,3,2,1,0:T(2,128)(2,1)S(1)} %constant_dynamic-slice_fusion.8), channel_id=1, source_target_pairs={{0,16},{8,24},{16,32},{24,40},{32,48},{40,56},{48,64},{56,72},{64,... | collective-permute-start | bytes 3538952 | tf_op jit(solution)/shard_map/ppermute | solution.py:9
  52.5 47.4 %collective-permute-done.2 = bf16[2,1,192,2,768]{4,3,2,1,0:T(2,128)(2,1)S(1)} collective-permute-done((bf16[2,1,192,2,768]{4,3,2,1,0:T(2,128)(2,1)S(1)}, bf16[2,1,192,2,768]{4,3,2,1,0:T(2,128)(2,1)S(1)}, u32[]{:S(2)}, u32[]{:S(2)}) %collective-permute-start.2) | collective-permute-done | bytes 1179680 | tf_op jit(solution)/shard_map/ppermute | solution.py:9
  99.8 1.0 copy-done.2
  101.0 11.0 %collective-permute-start.3 = (bf16[2,192]{1,0:T(2,128)(2,1)}, bf16[2,192]{1,0:T(2,128)(2,1)S(1)}, u32[]{:S(2)}, u32[]{:S(2)}) collective-permute-start(bf16[2,192]{1,0:T(2,128)(2,1)} %param.23), channel_id=1, source_target_pairs={{0,16},{8,24},{16,32},{24,40},{32,48},{40,56},{48,64},{56,72},{64,... | collective-permute-start | bytes 2312 | tf_op jit(solution)/shard_map/ppermute | solution.py:9
  112.0 1.5 fusion.169
  121.4 0.8 fusion.170
  122.2 0.7 slice_bitcast_fusion.1
  122.9 9.8 %fusion.168 = (bf16[1,8,192,2,768]{4,3,2,1,0:T(2,128)(2,1)}, bf16[1,8,192,2,768]{4,3,2,1,0:T(2,128)(2,1)}) fusion(bf16[2,8,192,2,768]{4,3,2,1,0:T(2,128)(2,1)} %param.21), kind=kLoop, calls=%fused_computation.155 | loop fusion | bytes 18874368 | tf_op jit(solution)/shard_map/slice | solution.py:83
  132.7 11.3 %squeeze.153 = bf16[8,192,1536]{2,1,0:T(8,128)(2,1)} reshape(bf16[1,8,192,2,768]{4,3,2,1,0:T(2,128)(2,1)} %get-tuple-element.382) | data formatting | bytes 9437184 | tf_op jit(solution)/shard_map/squeeze | solution.py:83
  144.0 11.3 %squeeze.149 = bf16[8,192,1536]{2,1,0:T(8,128)(2,1)} reshape(bf16[1,8,192,2,768]{4,3,2,1,0:T(2,128)(2,1)} %get-tuple-element.381) | data formatting | bytes 9437184 | tf_op jit(solution)/shard_map/squeeze | solution.py:83
  155.4 41.6 %all-gather.3.cloned.1.call-done = bf16[2,8,192,2,768]{4,3,2,1,0:T(2,128)(2,1)} async-done(((bf16[2,1,192,2,768]{4,3,2,1,0:T(2,128)(2,1)}), bf16[2,8,192,2,768]{4,3,2,1,0:T(2,128)(2,1)}) %all-gather.3.cloned.1.call-update) | async-done | bytes 9437200 | tf_op jit(solution)/shard_map/all_gather | solution.py:76
  196.9 20.9 %reshape.159 = bf16[2,8,192,1536]{3,2,1,0:T(8,128)(2,1)} reshape(bf16[2,8,192,2,768]{4,3,2,1,0:T(2,128)(2,1)} %all-gather.3.cloned.1.call-done) | data formatting | bytes 18874368 | tf_op jit(solution)/shard_map/reshape | solution.py:77
  217.8 8.6 %slice_negate_fusion.5 = (bf16[2,8,192,768]{3,2,1,0:T(8,128)(2,1)}, bf16[2,8,192,768]{3,2,1,0:T(8,128)(2,1)}) fusion(bf16[2,8,192,1536]{3,2,1,0:T(8,128)(2,1)} %reshape.159), kind=kLoop, calls=%fused_computation.131 | loop fusion | flops 2359296 | bytes 18874368 | tf_op jit(solution)/shard_map/neg | solution.py:26
  226.5 6.4 %maximum_maximum_fusion = bf16[2,8,384,1536]{3,2,1,0:T(8,128)(2,1)S(1)} fusion(bf16[2,8,192,768]{3,2,1,0:T(8,128)(2,1)} %get-tuple-element.384, bf16[2,8,192,768]{3,2,1,0:T(8,128)(2,1)} %get-tuple-element.383, bf16[2,8,192,1536]{3,2,1,0:T(8,128)(2,1)S(1)} %copy-done), kind=kLoop, calls=%fused_computation.124 | loop fusion | flops 56623104 | bytes 37748736 | tf_op jit(solution)/shard_map/concatenate | solution.py:27
  232.9 6.9 %dynamic-slice_bitcast_fusion.3 = (bf16[8,384,1536]{2,1,0:T(8,128)(2,1)}, bf16[8,384,1536]{2,1,0:T(8,128)(2,1)}) fusion(bf16[2,8,384,1536]{3,2,1,0:T(8,128)(2,1)S(1)} %maximum_maximum_fusion, s32[]{:T(128)S(6)} %select_n.100, s32[]{:T(128)S(6)} %select_n.103), kind=kLoop, calls=%fused_computation.129 | loop fusion | bytes 37748744 | tf_op jit(solution)/shard_map/jit(dynamic_index_in_dim)/squeeze | solution.py:81
  239.8 21.5 %while.48 = (s32[]{:T(128)}, f32[192,384]{1,0:T(8,128)S(1)}, s32[2,2]{1,0:T(2,128)S(1)}, bf16[8,192,1536]{2,1,0:T(8,128)(2,1)}, bf16[8,384,1536]{2,1,0:T(8,128)(...) while((s32[]{:T(128)}, f32[192,384]{1,0:T(8,128)S(1)}, ...), condition=%wide.region_1.2_spmd.clone, body=%wide.region_0.1_spmd.clone.sunk | while | flops 511340544 | bytes 5900063 | solution.py:92
  246.1 2.0 fusion.212
  248.2 2.4 convolution_add_fusion.10
  256.9 2.0 fusion.212
  259.0 2.3 convolution_add_fusion.10
  261.3 0.7 copy-done.4
  262.0 1.0 copy.20
  263.0 21.5 %while.49 = (s32[]{:T(128)}, f32[192,384]{1,0:T(8,128)S(1)}, s32[2,2]{1,0:T(2,128)S(1)}, bf16[8,192,1536]{2,1,0:T(8,128)(2,1)}, bf16[8,384,1536]{2,1,0:T(8,128)(...) while((s32[]{:T(128)}, f32[192,384]{1,0:T(8,128)S(1)}, ...), condition=%wide.region_3.4_spmd.clone, body=%wide.region_2.3_spmd.clone.sunk | while | flops 511340544 | bytes 5900063 | solution.py:92
  269.3 2.0 fusion.218
  271.4 2.3 convolution_add_fusion.11
  280.1 2.0 fusion.218
  282.2 2.3 convolution_add_fusion.11
  284.6 36.5 %all-gather.5.cloned.1.call-done = bf16[2,8,192,2,768]{4,3,2,1,0:T(2,128)(2,1)} async-done(((bf16[2,1,192,2,768]{4,3,2,1,0:T(2,128)(2,1)}), bf16[2,8,192,2,768]{4,3,2,1,0:T(2,128)(2,1)}) %all-gather.5.cloned.1.call-update) | async-done | bytes 9437200 | tf_op jit(solution)/shard_map/all_gather | solution.py:76
  321.0 20.9 %reshape.161 = bf16[2,8,192,1536]{3,2,1,0:T(8,128)(2,1)} reshape(bf16[2,8,192,2,768]{4,3,2,1,0:T(2,128)(2,1)} %all-gather.5.cloned.1.call-done) | data formatting | bytes 18874368 | tf_op jit(solution)/shard_map/reshape | solution.py:77
  341.9 8.6 %slice_negate_fusion.4 = (bf16[2,8,192,768]{3,2,1,0:T(8,128)(2,1)}, bf16[2,8,192,768]{3,2,1,0:T(8,128)(2,1)}) fusion(bf16[2,8,192,1536]{3,2,1,0:T(8,128)(2,1)} %reshape.161), kind=kLoop, calls=%fused_computation.130 | loop fusion | flops 2359296 | bytes 18874368 | tf_op jit(solution)/shard_map/neg | solution.py:26
  350.6 6.3 %maximum_maximum_fusion.1 = bf16[2,8,384,1536]{3,2,1,0:T(8,128)(2,1)S(1)} fusion(bf16[2,8,192,768]{3,2,1,0:T(8,128)(2,1)} %get-tuple-element.380, bf16[2,8,192,768]{3,2,1,0:T(8,128)(2,1)} %get-tuple-element.379, bf16[2,8,192,1536]{3,2,1,0:T(8,128)(2,1)S(1)} %copy-done.1), kind=kLoop, calls=%fused_computation.125 | loop fusion | flops 56623104 | bytes 37748736 | tf_op jit(solution)/shard_map/concatenate | solution.py:27
  356.9 6.9 %dynamic-slice_bitcast_fusion = (bf16[8,384,1536]{2,1,0:T(8,128)(2,1)}, bf16[8,384,1536]{2,1,0:T(8,128)(2,1)}) fusion(bf16[2,8,384,1536]{3,2,1,0:T(8,128)(2,1)S(1)} %maximum_maximum_fusion.1, s32[]{:T(128)S(6)} %select_n.109, s32[]{:T(128)S(6)} %select_n.106), kind=kLoop, calls=%fused_computation.126 | loop fusion | bytes 37748744 | tf_op jit(solution)/shard_map/jit(dynamic_index_in_dim)/squeeze | solution.py:81
  363.8 21.7 %while.46 = (s32[]{:T(128)}, f32[192,384]{1,0:T(8,128)S(1)}, s32[2,2]{1,0:T(2,128)S(1)}, bf16[8,192,1536]{2,1,0:T(8,128)(2,1)}, bf16[8,384,1536]{2,1,0:T(8,128)(...) while((s32[]{:T(128)}, f32[192,384]{1,0:T(8,128)S(1)}, ...), condition=%wide.region_5.6_spmd, body=%wide.region_4.5_spmd.sunk | while | flops 511266816 | bytes 5900053 | solution.py:92
  370.3 2.0 fusion.200
  372.4 2.3 convolution_add_fusion.8
  381.1 2.0 fusion.200
  383.3 2.3 convolution_add_fusion.8
  385.7 22.2 %while.47 = (s32[]{:T(128)}, f32[192,384]{1,0:T(8,128)S(1)}, s32[2,2]{1,0:T(2,128)S(1)}, bf16[8,192,1536]{2,1,0:T(8,128)(2,1)}, bf16[8,384,1536]{2,1,0:T(8,128)(...) while((s32[]{:T(128)}, f32[192,384]{1,0:T(8,128)S(1)}, ...), condition=%wide.region_7.8_spmd, body=%wide.region_6.7_spmd.sunk | while | flops 511266816 | bytes 5900053 | solution.py:92
  392.4 2.0 fusion.206
  394.5 2.3 convolution_add_fusion.9
  403.4 2.0 fusion.206
  405.6 2.3 convolution_add_fusion.9
  408.7 23.4 %all_to_all.5 = f32[8,2,24,2,192]{4,3,2,1,0:T(2,128)S(1)} all-to-all(f32[8,2,24,2,192]{4,3,2,1,0:T(2,128)S(1)} %copy.6), channel_id=1, replica_groups=mesh['ka'=32,'occ'=8] {'occ'}, dimensions={0} | all-to-all | bytes 1179648 | tf_op jit(solution)/shard_map/all_to_all | solution.py:19
  432.1 1.0 reduce_sum.9
  (76 shorter events, 12.9 us)
Async XLA Ops:
  6.5 190.4 %all-gather.3.cloned.1.call-start = ((), (), s32[]{:S(2)}) async-start(), calls=%async_computation.1 | async-start | bytes 10616832 | tf_op jit(solution)/shard_map/all_gather | solution.py:76
  8.6 27.8 %collective-permute-start = (bf16[2,1,192,2,768]{4,3,2,1,0:T(2,128)(2,1)S(1)}, bf16[2,1,192,2,768]{4,3,2,1,0:T(2,128)(2,1)S(1)}, u32[]{:S(2)}, u32[]{:S(2)}) collective-permute-start(bf16[2,1,192,2,768]{4,3,2,1,0:T(2,128)(2,1)S(1)} %constant_dynamic-slice_fusion.8), channel_id=1, source_target_pairs={{0,8},{8,16},{16,24},{24,32},{32,40},{40,48},{48,56},{56,64},{64,7... | collective-permute-start | bytes 3538952 | tf_op jit(solution)/shard_map/ppermute | solution.py:9
  36.4 1.0 copy-start.3
  37.5 283.6 %all-gather.5.cloned.1.call-start = ((), (), s32[]{:S(2)}) async-start(), calls=%async_computation.2 | async-start | bytes 10616832 | tf_op jit(solution)/shard_map/all_gather | solution.py:76
  37.5 62.3 %collective-permute-start.2 = (bf16[2,1,192,2,768]{4,3,2,1,0:T(2,128)(2,1)S(1)}, bf16[2,1,192,2,768]{4,3,2,1,0:T(2,128)(2,1)S(1)}, u32[]{:S(2)}, u32[]{:S(2)}) collective-permute-start(bf16[2,1,192,2,768]{4,3,2,1,0:T(2,128)(2,1)S(1)} %constant_dynamic-slice_fusion.8), channel_id=1, source_target_pairs={{0,16},{8,24},{16,32},{24,40},{32,48},{40,56},{48,64},{56,72},{64,... | collective-permute-start | bytes 3538952 | tf_op jit(solution)/shard_map/ppermute | solution.py:9
  99.8 1.0 copy-start.2
  100.9 54.4 %collective-permute-start.1 = (bf16[2,192]{1,0:T(2,128)(2,1)}, bf16[2,192]{1,0:T(2,128)(2,1)S(1)}, u32[]{:S(2)}, u32[]{:S(2)}) collective-permute-start(bf16[2,192]{1,0:T(2,128)(2,1)} %param.23), channel_id=1, source_target_pairs={{0,8},{8,16},{16,24},{24,32},{32,40},{40,48},{48,56},{56,64},{64,7... | collective-permute-start | bytes 2312 | tf_op jit(solution)/shard_map/ppermute | solution.py:9
  101.0 54.3 %collective-permute-start.3 = (bf16[2,192]{1,0:T(2,128)(2,1)}, bf16[2,192]{1,0:T(2,128)(2,1)S(1)}, u32[]{:S(2)}, u32[]{:S(2)}) collective-permute-start(bf16[2,192]{1,0:T(2,128)(2,1)} %param.23), channel_id=1, source_target_pairs={{0,16},{8,24},{16,32},{24,40},{32,48},{40,56},{48,64},{56,72},{64,... | collective-permute-start | bytes 2312 | tf_op jit(solution)/shard_map/ppermute | solution.py:9
  217.8 8.7 %copy-start = (bf16[2,8,192,1536]{3,2,1,0:T(8,128)(2,1)S(1)}, bf16[2,8,192,1536]{3,2,1,0:T(8,128)(2,1)}, u32[]{:S(2)}) copy-start(bf16[2,8,192,1536]{3,2,1,0:T(8,128)(2,1)} %reshape.159) | copy-start | bytes 28311556
  232.9 6.9 %copy-start.6 = (f32[8]{0:T(128)S(1)}, f32[8]{0:T(128)}, u32[]{:S(2)}) copy-start(f32[8]{0:T(128)} %param.22) | copy-start | bytes 100
  239.8 23.2 %copy-start.7 = (f32[192,384]{1,0:T(8,128)S(1)}, f32[192,384]{1,0:T(8,128)}, u32[]{:S(2)}) copy-start(f32[192,384]{1,0:T(8,128)} %custom-call.1) | copy-start | bytes 884740
  261.3 0.7 copy-start.4
  284.6 36.5 %copy-start.8 = (f32[192,384]{1,0:T(8,128)}, f32[192,384]{1,0:T(8,128)S(1)}, u32[]{:S(2)}) copy-start(f32[192,384]{1,0:T(8,128)S(1)} %get-tuple-element.222) | copy-start | bytes 884740
  341.9 8.7 %copy-start.1 = (bf16[2,8,192,1536]{3,2,1,0:T(8,128)(2,1)S(1)}, bf16[2,8,192,1536]{3,2,1,0:T(8,128)(2,1)}, u32[]{:S(2)}) copy-start(bf16[2,8,192,1536]{3,2,1,0:T(8,128)(2,1)} %reshape.161) | copy-start | bytes 28311556
  363.8 21.7 %copy-start.5 = (f32[192,384]{1,0:T(8,128)S(1)}, f32[192,384]{1,0:T(8,128)}, u32[]{:S(2)}) copy-start(f32[192,384]{1,0:T(8,128)} %copy-done.4) | copy-start | bytes 884740
  363.8 21.7 %copy-start.9 = (f32[192,384]{1,0:T(8,128)S(1)}, f32[192,384]{1,0:T(8,128)}, u32[]{:S(2)}) copy-start(f32[192,384]{1,0:T(8,128)} %copy-done.8) | copy-start | bytes 884740
Sparse Core Ops, SparseCore 0:
  37.6 159.2 all-gather.2
  198.7 122.2 all-gather.4
where the time goes:
time: 444 us; the launch traced here: 440 us
  waiting for transfers between devices  152 us (34%)
  local copies, waits for them, and re-layouts  108 us (24%)
  loops' own time  40.8 us (9%)
  matrix products  34.6 us (8%)
  other arithmetic  32.6 us (7%)
  starting transfers between devices  27.6 us (6%)
  blocking collectives  23.4 us (5%)
  between operations  21.6 us (5%)
    all_gather x2, waiting for transfers between devices, local(): received = lax.all_gather(shifted, 'occ', axis=1, tiled=True)  78 us
    ppermute x4, waiting for transfers between devices, from_behind(): lax.ppermute(array, axis, [(i, (i + by) % size) for i in range(size)])  73.6 us
    reshape x2, local copies, waits for them, and re-layouts, local(): received.reshape(momenta, orbitals, virtuals, 2 * auxiliary)  41.7 us
    another operation x4, loops' own time, local(): lax.scan(add_pair, density[local_index], pair_lists[round_index])  40.8 us
    ppermute x4, starting transfers between devices, from_behind(): lax.ppermute(array, axis, [(i, (i + by) % size) for i in range(size)])  27.6 us
    all_to_all x1, blocking collectives, sent_and_summed(): parts = lax.all_to_all(cut_along(array, dim, size), axis, 0, 0, tiled=True)  23.4 us
    squeeze x2, local copies, waits for them, and re-layouts, local(): own_block = own[local_index]  22.6 us
    dot_general x8, matrix products, density_term(): lax.dot_general(combined, stacked, (((1,), (1,)), ((), ())), preferred_el...  18.4 us
  transfers between devices with their start and end apart: 6, of which 4 were waited for; matrix products, arithmetic and copies ran while one was open for 23% of the time, Pallas kernels for 0%

commit v1 on v0

v1 whole, which is shorter than its diff:
```python
import functools

import jax
import jax.numpy as jnp
from jax import lax
from jax.experimental import pallas as pl
from jax.experimental.pallas import tpu as pltpu
from jax.sharding import PartitionSpec as P

ROWS, COLUMNS, LINE, CORES = 8, 4, 4, 2


def device_index(row, column, place, core):
    return ((row % ROWS) * COLUMNS + column % COLUMNS) * LINE * CORES + place * CORES + core


def route(target):
    pairs = []
    for row in range(ROWS):
        for column in range(COLUMNS):
            for place in range(LINE):
                for core in range(CORES):
                    goal = target(row, column, place, core)
                    if goal is not None:
                        pairs.append((device_index(row, column, place, core), device_index(*goal)))
    return pairs


def shifted(by):
    def target(row, column, place, core):
        if column + by < COLUMNS:
            return row, column + by, place, core
        return row + 1, column + by - COLUMNS, LINE - 1 - place, core

    return route(target)


def round_kernel(first, chosen, pairs, place_ref, occupied, left_re, left_im, mate, own_energy, *refs):
    if first:
        keep, send, products, combined, rounded, turned, total = refs
    else:
        keep_in, send_in, keep, send, products, combined, rounded, turned, total = refs
    half = pl.program_id(0)
    step = pl.program_id(1)
    steps = pl.num_programs(1)
    per_step = left_re.shape[1]
    orbitals = steps_orbitals = products.shape[0]
    rows = products.shape[2]
    share = rows // (2 * orbitals)
    count = pairs.shape[0]
    virtuals = products.shape[3]
    piece = mate[0, :rows]
    contract = (((1,), (1,)), ((), ()))
    for inner in range(per_step):
        orbital = step * per_step + inner
        products[orbital, 0] = lax.dot_general(
            piece, left_re[0, inner], contract, preferred_element_type=jnp.float32
        )
        products[orbital, 1] = lax.dot_general(
            piece, left_im[0, inner], contract, preferred_element_type=jnp.float32
        )

    @pl.when(step == steps - 1)
    def _():
        energy_row = mate[0, rows : rows + 1, :128].astype(jnp.float32)
        spread = jnp.broadcast_to(energy_row, (share, 128))
        on_diagonal = lax.broadcasted_iota(jnp.int32, (share, 128), 0) == lax.broadcasted_iota(
            jnp.int32, (share, 128), 1
        )
        energy_mate = jnp.sum(jnp.where(on_diagonal, spread, 0.0), axis=1, keepdims=True)
        energy_sum = own_energy[0] + energy_mate

        def exchange(lead, trail):
            top = pl.multiple_of(trail * share, 8)
            bottom = pl.multiple_of((orbitals + trail) * share, 8)
            real = products[lead, 0, pl.ds(top, share)] + products[lead, 1, pl.ds(bottom, share)]
            imaginary = products[lead, 1, pl.ds(top, share)] - products[lead, 0, pl.ds(bottom, share)]
            return real, imaginary

        def one_pair(index):
            lead = pairs[index, 0]
            trail = pairs[index, 1]
            inverse = 1.0 / (energy_sum - (occupied[lead] + occupied[trail]))
            real, imaginary = exchange(lead, trail)
            swapped_real, swapped_imaginary = exchange(trail, lead)
            real, imaginary = real * inverse, imaginary * inverse
            return (
                2.0 * real - swapped_real * inverse,
                2.0 * imaginary - swapped_imaginary * inverse,
                real,
                imaginary,
            )

        def two_pairs(index, carry):
            low = one_pair(2 * index)
            high = one_pair(2 * index + 1)
            c_re, c_im, a_re, a_im = (
                jnp.concatenate([x, y], axis=0).astype(jnp.bfloat16) for x, y in zip(low, high)
            )
            top = pl.ds(pl.multiple_of(index * 2 * share, 16), 2 * share)
            bottom = pl.ds(pl.multiple_of((count + index * 2) * share, 16), 2 * share)
            combined[top] = c_re
            combined[bottom] = c_im
            rounded[top] = a_re
            rounded[bottom] = a_im
            turned[top] = -a_im
            turned[bottom] = a_re
            return carry

        lax.fori_loop(0, count // 2, two_pairs, 0)
        contract_rows = (((0,), (0,)), ((), ()))
        total[0] = lax.dot_general(
            combined[...], rounded[...], contract_rows, preferred_element_type=jnp.float32
        )
        total[1] = lax.dot_general(
            combined[...], turned[...], contract_rows, preferred_element_type=jnp.float32
        )
        mine = chosen[half]
        core = place_ref[0]
        for place in range(keep.shape[0]):
            for target, offset in ((keep, core), (send, 1 - core)):
                cut = pl.ds(pl.multiple_of((place * CORES + offset) * share, 8), share)
                value = total[:, cut]
                if not first:
                    value = value + (keep_in if target is keep else send_in)[place, mine]
                target[place, mine] = value


def round_density(chosen, pairs, core, occupied, left_re, left_im, mate, own_energy, before):
    momenta, orbitals, virtuals, auxiliary = left_re.shape
    share = virtuals // (LINE * CORES)
    per_step = 2
    count = pairs.shape[0]
    rows = 2 * orbitals * share
    block = jax.ShapeDtypeStruct((LINE, momenta, 2, share, virtuals), jnp.float32)
    whole = pl.BlockSpec((LINE, momenta, 2, share, virtuals), lambda m, s, *_: (0, 0, 0, 0, 0))
    left = pl.BlockSpec((1, per_step, virtuals, auxiliary), lambda m, s, chosen, *_: (chosen[m], s, 0, 0))
    in_specs = [
        pl.BlockSpec(memory_space=pltpu.SMEM),
        left,
        left,
        pl.BlockSpec((1, mate.shape[1], auxiliary), lambda m, s, *_: (m, 0, 0)),
        pl.BlockSpec((1, 1, virtuals), lambda m, s, chosen, *_: (chosen[m], 0, 0)),
    ]
    if before:
        in_specs += [whole, whole]
    return pl.pallas_call(
        functools.partial(round_kernel, not before),
        out_shape=(block, block),
        grid_spec=pltpu.PrefetchScalarGridSpec(
            num_scalar_prefetch=3,
            grid=(momenta, orbitals // per_step),
            in_specs=in_specs,
            out_specs=(whole, whole),
            scratch_shapes=[
                pltpu.VMEM((orbitals, 2, rows, virtuals), jnp.float32),
                pltpu.VMEM((2 * count * share, virtuals), jnp.bfloat16),
                pltpu.VMEM((2 * count * share, virtuals), jnp.bfloat16),
                pltpu.VMEM((2 * count * share, virtuals), jnp.bfloat16),
                pltpu.VMEM((2, virtuals, virtuals), jnp.float32),
            ],
        ),
        compiler_params=pltpu.CompilerParams(
            dimension_semantics=("arbitrary", "arbitrary"), vmem_limit_bytes=40 << 20
        ),
        cost_estimate=pl.CostEstimate(
            flops=momenta * (4 * rows * virtuals * auxiliary * orbitals + 8 * count * share * virtuals * virtuals),
            bytes_accessed=momenta * orbitals * virtuals * auxiliary * 4 + 2 * momenta * rows * auxiliary,
            transcendentals=0,
        ),
    )(chosen, pairs, core, occupied, left_re, left_im, mate, own_energy, *before)


def summed(keep, send):
    place = lax.axis_index("occ") // CORES
    devices = LINE * CORES
    held = keep + lax.ppermute(send, "occ", [(i, i ^ 1) for i in range(devices)])
    total = lax.dynamic_index_in_dim(held, place, 0, keepdims=False)
    for hop in range(1, LINE):
        part = lax.dynamic_index_in_dim(held, (place + hop) % LINE, 0, keepdims=False)
        ring = [(i, (i + CORES * hop) % devices) for i in range(devices)]
        total = total + lax.ppermute(part, "occ", ring)
    return jnp.transpose(total, (0, 2, 1, 3))


def local(factors, occupied_energy, virtual_energy, conserve, pair_lists):
    momenta, orbitals, virtuals, _, auxiliary = factors.shape
    devices = lax.axis_size("occ")
    share = virtuals // devices
    start = lax.axis_index("occ") * share
    cut = lax.dynamic_slice_in_dim(factors, start, share, 2)
    cut = jnp.transpose(cut, (0, 3, 1, 2, 4)).reshape(momenta, 2 * orbitals * share, auxiliary)
    energy_cut = lax.dynamic_slice_in_dim(virtual_energy, start, share, 1)
    energy_rows = jnp.pad(energy_cut[:, None, :], ((0, 0), (0, 7), (0, auxiliary - share)))
    outgoing = jnp.concatenate([cut, energy_rows], axis=1)
    left_re = factors[:, :, :, 0, :]
    left_im = factors[:, :, :, 1, :]
    own_energy = virtual_energy.astype(jnp.float32)[:, None, :]
    all_pairs = lax.all_gather(pair_lists, "occ", axis=1, tiled=True)
    core = (lax.axis_index("occ") % CORES).astype(jnp.int32).reshape(1)
    density = ()
    for round_index in range(conserve.shape[1]):
        mate = lax.ppermute(outgoing, ("ka", "occ"), shifted(round_index + 1))
        chosen = (conserve[0, round_index] + jnp.arange(momenta, dtype=jnp.int32)) % momenta
        density = round_density(
            chosen, all_pairs[round_index], core, occupied_energy, left_re, left_im, mate, own_energy, density
        )
    return summed(*density)


def solution(mesh):
    in_specs = (
        P("ka", None, None, None, None),
        P(),
        P("ka", None),
        P("ka", None),
        P(None, "occ", None),
    )
    out_specs = P("ka", "occ", None, None)
    return jax.shard_map(local, mesh=mesh, in_specs=in_specs, out_specs=out_specs, check_vma=False)
```

time: 444 us -> 153 us (0.34)
  the two profiles are of different devices: /device:TPU:10 before, /device:TPU:1 now
where the time goes in v1:
time: 153 us
  waiting for transfers between devices  71.7 us (47%)
  local copies, waits for them, and re-layouts  37.6 us (25%)
  Pallas kernels  18.9 us (12%)
  blocking collectives  14.6 us (10%)
  starting transfers between devices  7.33 us (5%)
  other arithmetic  2.41 us (2%)
    ppermute x2, waiting for transfers between devices, local(): mate = lax.ppermute(outgoing, ('ka', 'occ'), shifted(round_index + 1))  61.4 us
    slice x1, local copies, waits for them, and re-layouts, local(): left_im = factors[:, :, :, 1, :]  22.6 us
    pallas_call x2, Pallas kernels, round_density(): pl.pallas_call(functools.partial(round_kernel, not before), out_shape=(bl...  18.9 us
    all_gather x1, blocking collectives, local(): all_pairs = lax.all_gather(pair_lists, 'occ', axis=1, tiled=True)  14.6 us
    squeeze x1, local copies, waits for them, and re-layouts, local(): left_im = factors[:, :, :, 1, :]  10.8 us
    ppermute x3, waiting for transfers between devices, summed(): total = total + lax.ppermute(part, 'occ', ring)  8.96 us
    ppermute x2, starting transfers between devices, local(): mate = lax.ppermute(outgoing, ('ka', 'occ'), shifted(round_index + 1))  3.89 us
  transfers between devices with their start and end apart: 6, of which 4 were waited for; matrix products, arithmetic and copies ran while one was open for 23% of the time, Pallas kernels for 6%

profile of v1, /device:TPU:1, one launch (start us, length us, event | category | flops | bytes accessed | tf_op | source)
XLA Modules:
  0.0 152.8 jit_solution(9360203055287884210)
XLA Ops:
  0.0 0.8 fusion.5
  0.8 2.1 %dynamic-slice_bitcast_fusion = bf16[2,2,8,24,768]{4,1,3,2,0:T(2,128)(2,1)S(1)} fusion(bf16[2,8,192,2,768]{4,3,2,1,0:T(2,128)(2,1)} %param.5, s32[]{:T(128)S(6)} %select_n.52), kind=kLoop, calls=%fused_computation.5 | loop fusion | bytes 2359300 | tf_op jit(solution)/shard_map/transpose | solution.py:192
  2.8 0.1 copy.27
  3.0 1.1 fusion.1
  4.1 0.0 copy-start.3
  4.1 0.0 copy-start.1
  4.1 0.0 copy-start.2
  4.1 3.6 %collective-permute-start = (bf16[2,392,768]{2,1,0:T(8,128)(2,1)}, bf16[2,392,768]{2,1,0:T(8,128)(2,1)S(1)}, u32[]{:S(2)}, u32[]{:S(2)}) collective-permute-start(bf16[2,392,768]{2,1,0:T(8,128)(2,1)} %fusion.1), channel_id=1, source_target_pairs={{0,16},{1,17},{2,18},{3,19},{4,20},{5,21},{6,22},{7,23},{8,24},{9,... | collective-permute-start | bytes 3612680 | tf_op jit(solution)/shard_map/ppermute | solution.py:203
  7.7 0.3 collective-permute-start.1
  8.0 22.6 %fusion.8 = (bf16[2,8,192,1,768]{4,3,2,1,0:T(2,128)(2,1)}, bf16[2,8,192,1,768]{4,3,2,1,0:T(2,128)(2,1)}) fusion(bf16[2,8,192,2,768]{4,3,2,1,0:T(2,128)(2,1)} %param.5), kind=kLoop, calls=%fused_computation.23 | loop fusion | bytes 18874368 | tf_op jit(solution)/shard_map/slice | solution.py:197
  30.6 0.0 copy-done.3
  30.6 0.6 fusion.10
  31.1 0.0 copy-done.1
  31.1 14.6 %all_gather.3 = s32[2,16,2]{2,0,1:T(2,128)S(1)} all-gather(s32[2,2,2]{2,0,1:T(2,128)S(1)} %copy.23), channel_id=1, replica_groups=mesh['ka'=32,'occ'=8] {'occ'}, dimensions={1}, use_global_device_ids=true | all-gather | bytes 288 | tf_op jit(solution)/shard_map/all_gather | solution.py:199
  45.8 0.6 and_select_fusion.1.chosen
  46.3 0.0 copy-done.2
  46.4 0.7 and_select_fusion.chosen
  47.0 0.0 copy-start
  47.1 10.8 %copy_bitcast_fusion = (bf16[2,8,192,768]{3,2,1,0:T(8,128)(2,1)S(1)}, bf16[2,8,192,768]{3,2,1,0:T(8,128)(2,1)S(1)}) fusion(bf16[2,8,192,1,768]{4,3,2,1,0:T(2,128)(2,1)} %get-tuple-element.13, bf16[2,8,192,1,768]{4,3,2,1,0:T(2,128)(2,1)} %get-tuple-element.14), kind=kLoop, calls=%fused_computation | loop fusion | bytes 18874368 | tf_op jit(solution)/shard_map/squeeze | solution.py:197
  57.9 61.4 %collective-permute-done.1.mate = bf16[2,392,768]{2,1,0:T(8,128)(2,1)S(1)} collective-permute-done((bf16[2,392,768]{2,1,0:T(8,128)(2,1)}, bf16[2,392,768]{2,1,0:T(8,128)(2,1)S(1)}, u32[]{:S(2)}, u32[]{:S(2)}) %collective-permute-start.1) | collective-permute-done | bytes 1204256 | tf_op jit(solution)/shard_map/ppermute | solution.py:203
  119.3 0.0 copy-done
  119.3 9.4 %shard_map.55 = (f32[4,2,2,24,192]{4,3,2,1,0:T(8,128)S(1)}, f32[4,2,2,24,192]{4,3,2,1,0:T(8,128)S(1)}) custom-call(s32[2]{0:T(128)S(1)} %and_select_fusion.chosen, s32[16,2]{1,0:T(8,128)S(1)} %bitcast.31, s32[1]{0:T(128)} %bitcast.2.place_ref, f32[8]{0:T(128)S(1)} %copy-done, bf16[2,8,192,768]{3,2,1,0:T(8,128)(2,1)S(1)} %get-tuple-element.23.left_re, ...), custom_call_target="tpu_custom_call" | custom-call | flops 3850371072 | bytes 10616832 | tf_op jit(solution)/shard_map/pallas_call | solution.py:147
  128.7 0.0 collective-permute-done.mate
  128.7 9.5 %shard_map.56 = (f32[4,2,2,24,192]{4,3,2,1,0:T(8,128)S(1)}, f32[4,2,2,24,192]{4,3,2,1,0:T(8,128)S(1)}) custom-call(s32[2]{0:T(128)S(1)} %and_select_fusion.1.chosen, s32[16,2]{1,0:T(8,128)S(1)} %bitcast.30, s32[1]{0:T(128)} %bitcast.2.place_ref, f32[8]{0:T(128)S(1)} %copy-done, bf16[2,8,192,768]{3,2,1,0:T(8,128)(2,1)S(1)} %get-tuple-element.23.left_re, ...), custom_call_target="tpu_custom_call" | custom-call | flops 3850371072 | bytes 10616832 | tf_op jit(solution)/shard_map/pallas_call | solution.py:147
  138.2 1.0 collective-permute-start.2
  139.2 1.3 collective-permute-done.2
  140.6 0.1 add.84
  140.7 2.0 %collective-permute-start.5 = (f32[2,2,24,192]{3,2,1,0:T(8,128)S(1)}, f32[2,2,24,192]{3,2,1,0:T(8,128)S(1)}, u32[]{:S(2)}, u32[]{:S(2)}) collective-permute-start(f32[2,2,24,192]{3,2,1,0:T(8,128)S(1)} %get-tuple-element.16), channel_id=1, source_target_pairs={{0,6},{1,7},{2,0},{3,1},{4,2},{5,3},{6,4},{7,5},{8,14},{9,15},{10,... | collective-permute-start | bytes 221192 | tf_op jit(solution)/shard_map/ppermute | solution.py:182
  142.7 0.0 collective-permute-start.4
  142.7 0.4 collective-permute-start.3
  143.1 1.7 %collective-permute-done.5 = f32[2,2,24,192]{3,2,1,0:T(8,128)S(1)} collective-permute-done((f32[2,2,24,192]{3,2,1,0:T(8,128)S(1)}, f32[2,2,24,192]{3,2,1,0:T(8,128)S(1)}, u32[]{:S(2)}, u32[]{:S(2)}) %collective-permute-start.5) | collective-permute-done | bytes 73760 | tf_op jit(solution)/shard_map/ppermute | solution.py:182
  144.8 7.3 %collective-permute-done.4 = f32[2,2,24,192]{3,2,1,0:T(8,128)S(1)} collective-permute-done((f32[2,2,24,192]{3,2,1,0:T(8,128)S(1)}, f32[2,2,24,192]{3,2,1,0:T(8,128)S(1)}, u32[]{:S(2)}, u32[]{:S(2)}) %collective-permute-start.4) | collective-permute-done | bytes 73760 | tf_op jit(solution)/shard_map/ppermute | solution.py:182
  152.1 0.0 collective-permute-done.3
  152.1 0.7 copy.32
  (6 shorter events, 0.1 us)
Async XLA Ops:
  4.1 26.5 %copy-start.3 = (s32[2,2]{1,0:T(2,128)S(1)}, s32[2,2]{1,0:T(2,128)}, u32[]{:S(2)}) copy-start(s32[2,2]{1,0:T(2,128)} %param.8) | copy-start | bytes 52
  4.1 27.0 %copy-start.1 = (s32[2,2,2]{2,1,0:T(2,128)S(1)}, s32[2,2,2]{2,1,0:T(2,128)}, u32[]{:S(2)}) copy-start(s32[2,2,2]{2,1,0:T(2,128)} %param.9) | copy-start | bytes 100
  4.1 42.3 %copy-start.2 = (bf16[2,192]{1,0:T(2,128)(2,1)S(1)}, bf16[2,192]{1,0:T(2,128)(2,1)}, u32[]{:S(2)}) copy-start(bf16[2,192]{1,0:T(2,128)(2,1)} %param.7) | copy-start | bytes 2308
  4.1 124.6 %collective-permute-start = (bf16[2,392,768]{2,1,0:T(8,128)(2,1)}, bf16[2,392,768]{2,1,0:T(8,128)(2,1)S(1)}, u32[]{:S(2)}, u32[]{:S(2)}) collective-permute-start(bf16[2,392,768]{2,1,0:T(8,128)(2,1)} %fusion.1), channel_id=1, source_target_pairs={{0,16},{1,17},{2,18},{3,19},{4,20},{5,21},{6,22},{7,23},{8,24},{9,... | collective-permute-start | bytes 3612680 | tf_op jit(solution)/shard_map/ppermute | solution.py:203
  7.7 111.6 %collective-permute-start.1 = (bf16[2,392,768]{2,1,0:T(8,128)(2,1)}, bf16[2,392,768]{2,1,0:T(8,128)(2,1)S(1)}, u32[]{:S(2)}, u32[]{:S(2)}) collective-permute-start(bf16[2,392,768]{2,1,0:T(8,128)(2,1)} %fusion.1), channel_id=1, source_target_pairs={{0,8},{1,9},{2,10},{3,11},{4,12},{5,13},{6,14},{7,15},{8,16},{9,17... | collective-permute-start | bytes 3612680 | tf_op jit(solution)/shard_map/ppermute | solution.py:203
  47.0 72.2 %copy-start = (f32[8]{0:T(128)S(1)}, f32[8]{0:T(128)}, u32[]{:S(2)}) copy-start(f32[8]{0:T(128)} %occupied.3) | copy-start | bytes 100
  138.2 2.4 %collective-permute-start.2 = (f32[4,2,2,24,192]{4,3,2,1,0:T(8,128)S(1)}, f32[4,2,2,24,192]{4,3,2,1,0:T(8,128)S(1)}, u32[]{:S(2)}, u32[]{:S(2)}) collective-permute-start(f32[4,2,2,24,192]{4,3,2,1,0:T(8,128)S(1)} %get-tuple-element.12), channel_id=1, source_target_pairs={{0,1},{1,0},{2,3},{3,2},{4,5},{5,4},{6,7},{7,6},{8,9},{9,8},{10,11... | collective-permute-start | bytes 884744 | tf_op jit(solution)/shard_map/ppermute | solution.py:177
  140.7 4.1 %collective-permute-start.5 = (f32[2,2,24,192]{3,2,1,0:T(8,128)S(1)}, f32[2,2,24,192]{3,2,1,0:T(8,128)S(1)}, u32[]{:S(2)}, u32[]{:S(2)}) collective-permute-start(f32[2,2,24,192]{3,2,1,0:T(8,128)S(1)} %get-tuple-element.16), channel_id=1, source_target_pairs={{0,6},{1,7},{2,0},{3,1},{4,2},{5,3},{6,4},{7,5},{8,14},{9,15},{10,... | collective-permute-start | bytes 221192 | tf_op jit(solution)/shard_map/ppermute | solution.py:182
  142.7 9.3 %collective-permute-start.4 = (f32[2,2,24,192]{3,2,1,0:T(8,128)S(1)}, f32[2,2,24,192]{3,2,1,0:T(8,128)S(1)}, u32[]{:S(2)}, u32[]{:S(2)}) collective-permute-start(f32[2,2,24,192]{3,2,1,0:T(8,128)S(1)} %get-tuple-element.17), channel_id=1, source_target_pairs={{0,4},{1,5},{2,6},{3,7},{4,0},{5,1},{6,2},{7,3},{8,12},{9,13},{10,... | collective-permute-start | bytes 221192 | tf_op jit(solution)/shard_map/ppermute | solution.py:182
  142.7 9.3 %collective-permute-start.3 = (f32[2,2,24,192]{3,2,1,0:T(8,128)S(1)}, f32[2,2,24,192]{3,2,1,0:T(8,128)S(1)}, u32[]{:S(2)}, u32[]{:S(2)}) collective-permute-start(f32[2,2,24,192]{3,2,1,0:T(8,128)S(1)} %get-tuple-element.15), channel_id=1, source_target_pairs={{0,2},{1,3},{2,4},{3,5},{4,6},{5,7},{6,0},{7,1},{8,10},{9,11},{10,... | collective-permute-start | bytes 221192 | tf_op jit(solution)/shard_map/ppermute | solution.py:182

commit v2 on v0

v2 whole, which is shorter than its diff:
```python
import functools

import jax
import jax.numpy as jnp
from jax import lax
from jax.experimental import pallas as pl
from jax.experimental.pallas import tpu as pltpu
from jax.sharding import PartitionSpec as P

ROWS, COLUMNS, LINE, CORES = 8, 4, 4, 2
LANES, HEAD = 128, 8


def device_index(row, column, place, core):
    return ((row % ROWS) * COLUMNS + column) * LINE * CORES + place * CORES + core


def route(columns, by):
    pairs = []
    for row in range(ROWS):
        for column in columns:
            for place in range(LINE):
                for core in range(CORES):
                    goal = column + by
                    crosses = (column, by) in CROSSING
                    pairs.append(
                        (
                            device_index(row, column, place, core),
                            device_index(
                                row + crosses, goal % COLUMNS, LINE - 1 - place if crosses else place, core
                            ),
                        )
                    )
    return pairs


CROSSING = {(3, 1), (2, 2), (3, 2), (0, 0), (1, -1), (2, -1)}


def moved(array, columns, by):
    return lax.ppermute(array, ("ka", "occ"), route(columns, by))


def piece_kernel(later, chosen, pairs, flags, occupied, left, own_energy, *refs):
    mates = refs[:2]
    refs = refs[2:]
    if later:
        before, refs = refs[:4], refs[4:]
    keep, send, piece, products, combined, rounded, turned, total = refs
    orbitals = products.shape[0]
    virtuals = products.shape[3]
    rows = products.shape[2]
    share = rows // (2 * orbitals)
    count = pairs.shape[0]
    mine = chosen[0]
    first = flags[0] == 0

    @pl.when(first)
    def _():
        piece[...] = mates[0][...]

    @pl.when(jnp.logical_not(first))
    def _():
        piece[...] = mates[1][...]

    contract = (((1,), (1,)), ((), ()))
    for orbital in range(orbitals):
        for part in range(2):
            products[orbital, part] = lax.dot_general(
                piece[:rows],
                left[mine, orbital, part * virtuals : (part + 1) * virtuals],
                contract,
                preferred_element_type=jnp.float32,
            )

    energy_row = piece[rows : rows + 1, :LANES].astype(jnp.float32)
    spread = jnp.broadcast_to(energy_row, (share, LANES))
    on_diagonal = lax.broadcasted_iota(jnp.int32, (share, LANES), 0) == lax.broadcasted_iota(
        jnp.int32, (share, LANES), 1
    )
    energy_mate = jnp.sum(jnp.where(on_diagonal, spread, 0.0), axis=1, keepdims=True)
    energy_sum = own_energy[mine] + energy_mate

    def exchange(lead, trail):
        top = pl.ds(pl.multiple_of(trail * share, 8), share)
        bottom = pl.ds(pl.multiple_of((orbitals + trail) * share, 8), share)
        real = products[lead, 0, top] + products[lead, 1, bottom]
        imaginary = products[lead, 1, top] - products[lead, 0, bottom]
        return real, imaginary

    def one_pair(index):
        lead = pairs[index, 0]
        trail = pairs[index, 1]
        inverse = 1.0 / (energy_sum - (occupied[lead] + occupied[trail]))
        real, imaginary = exchange(lead, trail)
        swapped_real, swapped_imaginary = exchange(trail, lead)
        real, imaginary = real * inverse, imaginary * inverse
        return (
            2.0 * real - swapped_real * inverse,
            2.0 * imaginary - swapped_imaginary * inverse,
            real,
            imaginary,
        )

    def two_pairs(index, carry):
        low = one_pair(2 * index)
        high = one_pair(2 * index + 1)
        c_re, c_im, a_re, a_im = (
            jnp.concatenate([x, y], axis=0).astype(jnp.bfloat16) for x, y in zip(low, high)
        )
        top = pl.ds(pl.multiple_of(index * 2 * share, 16), 2 * share)
        bottom = pl.ds(pl.multiple_of((count + index * 2) * share, 16), 2 * share)
        combined[top] = c_re
        combined[bottom] = c_im
        rounded[top] = a_re
        rounded[bottom] = a_im
        turned[top] = -a_im
        turned[bottom] = a_re
        return carry

    lax.fori_loop(0, count // 2, two_pairs, 0)
    contract_rows = (((0,), (0,)), ((), ()))
    for part, right in enumerate((rounded, turned)):
        total[part] = lax.dot_general(
            combined[...], right[...], contract_rows, preferred_element_type=jnp.float32
        )
    core = flags[1]
    if later:
        same = flags[2] == 0
    for place in range(LINE):
        for out, target, offset in ((0, keep, core), (1, send, 1 - core)):
            cut = pl.ds(pl.multiple_of((place * CORES + offset) * share, 8), share)
            value = total[:, cut]
            if later:
                value = value + jnp.where(same, before[out][place], before[2 + out][place])
            target[place] = value


def piece_density(chosen, pairs, flags, occupied, left, own_energy, mates, before):
    orbitals, both, auxiliary = left.shape[1:]
    virtuals = both // 2
    share = virtuals // (LINE * CORES)
    count = pairs.shape[0]
    rows = 2 * orbitals * share
    block = jax.ShapeDtypeStruct((LINE, 2, share, virtuals), jnp.float32)
    scalars = pl.BlockSpec(memory_space=pltpu.SMEM)
    whole = pl.BlockSpec(memory_space=pltpu.VMEM)
    return pl.pallas_call(
        functools.partial(piece_kernel, bool(before)),
        out_shape=(block, block),
        in_specs=[scalars] * 4 + [whole] * (4 + len(before)),
        out_specs=(whole, whole),
        scratch_shapes=[
            pltpu.VMEM((rows + HEAD, auxiliary), jnp.bfloat16),
            pltpu.VMEM((orbitals, 2, rows, virtuals), jnp.float32),
            pltpu.VMEM((2 * count * share, virtuals), jnp.bfloat16),
            pltpu.VMEM((2 * count * share, virtuals), jnp.bfloat16),
            pltpu.VMEM((2 * count * share, virtuals), jnp.bfloat16),
            pltpu.VMEM((2, virtuals, virtuals), jnp.float32),
        ],
        compiler_params=pltpu.CompilerParams(vmem_limit_bytes=40 << 20),
        cost_estimate=pl.CostEstimate(
            flops=4 * rows * virtuals * auxiliary * orbitals + 8 * count * share * virtuals * virtuals,
            bytes_accessed=orbitals * both * auxiliary * 2 + 2 * rows * auxiliary,
            transcendentals=0,
        ),
    )(chosen, pairs, flags, occupied, left, own_energy, *mates, *before)


def summed(keep, send):
    place = lax.axis_index("occ") // CORES
    devices = LINE * CORES
    held = keep + lax.ppermute(send, "occ", [(i, i ^ 1) for i in range(devices)])
    total = lax.dynamic_index_in_dim(held, place, 0, keepdims=False)
    for hop in range(1, LINE):
        part = lax.dynamic_index_in_dim(held, (place + hop) % LINE, 0, keepdims=False)
        ring = [(i, (i + CORES * hop) % devices) for i in range(devices)]
        total = total + lax.ppermute(part, "occ", ring)
    return total


def all_pairs_of(pair_lists):
    gathered = pair_lists
    reach = 1
    while reach < LINE * CORES:
        other = lax.ppermute(gathered, "occ", [(i, i ^ reach) for i in range(LINE * CORES)])
        gathered = jnp.concatenate([gathered, other], axis=1)
        reach *= 2
    return gathered


def local(factors, occupied_energy, virtual_energy, conserve, pair_lists):
    momenta, orbitals, virtuals, _, auxiliary = factors.shape
    share = virtuals // (LINE * CORES)
    start = lax.axis_index("occ") * share

    def outgoing(momentum):
        cut = lax.dynamic_slice_in_dim(factors[momentum], start, share, 1)
        cut = jnp.transpose(cut, (2, 0, 1, 3)).reshape(2 * orbitals * share, auxiliary)
        energy = lax.dynamic_slice_in_dim(virtual_energy[momentum], start, share, 0)
        head = jnp.pad(energy[None, :], ((0, HEAD - 1), (0, auxiliary - share)))
        return jnp.concatenate([cut, head], axis=0)

    straight = outgoing(0)
    relayed = outgoing(1)
    cross_one = moved(straight, (3,), 1)
    cross_two = moved(straight, (2, 3), 2)
    hop_plus = lax.ppermute(relayed, ("ka", "occ"), ring_route(1))
    hop_minus = lax.ppermute(relayed, ("ka", "occ"), ring_route(-1))
    straight, hop_plus, hop_minus = lax.optimization_barrier((straight, hop_plus, hop_minus))
    up = moved(hop_plus, (0,), 0)
    back = moved(hop_minus, range(COLUMNS), -1)
    near_one = moved(straight, (0, 1, 2), 1)
    near_two = moved(straight, (0, 1), 2)

    left = jnp.transpose(factors, (0, 1, 3, 2, 4)).reshape(momenta, orbitals, 2 * virtuals, auxiliary)
    own_energy = virtual_energy.astype(jnp.float32)[:, None, :]
    pairs = all_pairs_of(pair_lists)
    core = lax.axis_index("occ") % CORES
    column = lax.axis_index("ka") % COLUMNS
    chosen = (conserve[0][:, None] + jnp.arange(momenta, dtype=jnp.int32)[None, :]) % momenta

    def density(round_index, momentum, mates, from_second, before, swapped):
        flags = jnp.stack([from_second.astype(jnp.int32), core.astype(jnp.int32), swapped])
        return piece_density(
            chosen[round_index, momentum].reshape(1), pairs[round_index], flags,
            occupied_energy, left, own_energy, mates, before,
        )

    zero = jnp.int32(0)
    early_b = density(0, 1, (up, hop_plus), column != 0, (), zero)
    early_a = density(0, 0, (cross_one, near_one), column != 0, (), zero)
    before = (*early_a, *early_b)
    late_b = density(1, 1, (back, back), column != column, before, (chosen[0, 0] != chosen[1, 1]).astype(jnp.int32))
    late_a = density(1, 0, (cross_two, near_two), column > 1, before, (chosen[0, 0] != chosen[1, 0]).astype(jnp.int32))
    of_b = summed(*late_b)
    of_a = summed(*late_a)
    stacked = jnp.stack([of_a, of_b])
    result = jnp.where(chosen[1, 0] == 0, stacked, stacked[::-1])
    return jnp.transpose(result, (0, 2, 1, 3))


def ring_route(by):
    pairs = []
    for row in range(ROWS):
        for column in range(COLUMNS):
            for place in range(LINE):
                for core in range(CORES):
                    pairs.append(
                        (
                            device_index(row, column, place, core),
                            device_index(row, (column + by) % COLUMNS, place, core),
                        )
                    )
    return pairs


def solution(mesh):
    in_specs = (
        P("ka", None, None, None, None),
        P(),
        P("ka", None),
        P("ka", None),
        P(None, "occ", None),
    )
    out_specs = P("ka", "occ", None, None)
    return jax.shard_map(local, mesh=mesh, in_specs=in_specs, out_specs=out_specs, check_vma=False)
```

time: 444 us -> 138 us (0.31)
  the two profiles are of different devices: /device:TPU:10 before, /device:TPU:1 now
where the time goes in v2:
time: 138 us; the launch traced here: 137 us
  starting transfers between devices  61.9 us (45%)
  local copies, waits for them, and re-layouts  27.4 us (20%)
  waiting for transfers between devices  22.7 us (16%)
  Pallas kernels  20.2 us (15%)
  between operations  3.39 us (2%)
  other arithmetic  1.55 us (1%)
    ppermute x3, starting transfers between devices, all_pairs_of(): lax.ppermute(gathered, 'occ', [(i, i ^ reach) for i in range(LINE * CORES)])  27.7 us
    pallas_call x4, Pallas kernels, piece_density(): pl.pallas_call(functools.partial(piece_kernel, bool(before)), out_shape=(...  20.2 us
    ppermute x6, starting transfers between devices, moved(): return lax.ppermute(array, ('ka', 'occ'), route(columns, by))  17.7 us
    slice x1, local copies, waits for them, and re-layouts, outgoing(): cut = lax.dynamic_slice_in_dim(factors[momentum], start, share, 1)  9.54 us
    transpose x1, local copies, waits for them, and re-layouts, local(): jnp.transpose(factors, (0, 1, 3, 2, 4))  9.3 us
    ppermute x6, waiting for transfers between devices, moved(): return lax.ppermute(array, ('ka', 'occ'), route(columns, by))  8.33 us
    ppermute x6, starting transfers between devices, summed(): total = total + lax.ppermute(part, 'occ', ring)  7.26 us
    ppermute x3, waiting for transfers between devices, all_pairs_of(): lax.ppermute(gathered, 'occ', [(i, i ^ reach) for i in range(LINE * CORES)])  7.21 us
  transfers between devices with their start and end apart: 19, of which 6 were waited for; matrix products, arithmetic and copies ran while one was open for 10% of the time, Pallas kernels for 15%

profile of v2, /device:TPU:1, one launch (start us, length us, event | category | flops | bytes accessed | tf_op | source)
XLA Modules:
  0.0 137.1 jit_solution(6239686110630091134)
XLA Ops:
  0.0 9.5 %fusion.12 = (bf16[1,8,192,2,768]{4,3,2,1,0:T(2,128)(2,1)}, bf16[1,8,192,2,768]{4,3,2,1,0:T(2,128)(2,1)}) fusion(bf16[2,8,192,2,768]{4,3,2,1,0:T(2,128)(2,1)} %param.5), kind=kLoop, calls=%fused_computation.39 | loop fusion | bytes 18874368 | tf_op jit(solution)/shard_map/slice | solution.py:198
  9.6 1.5 %constant_dynamic-slice_fusion.1 = bf16[1,8,24,2,768]{4,3,2,1,0:T(2,128)(2,1)S(1)} fusion(bf16[1,8,192,2,768]{4,3,2,1,0:T(2,128)(2,1)} %get-tuple-element.27, s32[]{:T(128)S(6)} %select_n.75), kind=kLoop, calls=%fused_computation.23 | loop fusion | bytes 1179652 | tf_op jit(solution)/shard_map/dynamic_slice | solution.py:198
  11.0 0.1 copy.44
  11.1 0.1 constant_dynamic-slice_fusion
  11.2 2.1 %collective-permute-start.4 = (bf16[392,768]{1,0:T(8,128)(2,1)S(1)}, bf16[392,768]{1,0:T(8,128)(2,1)S(1)}, u32[]{:S(2)}, u32[]{:S(2)}) collective-permute-start(bf16[392,768]{1,0:T(8,128)(2,1)S(1)} %fusion.3), channel_id=1, source_target_pairs={{0,8},{1,9},{2,10},{3,11},{4,12},{5,13},{6,14},{7,15},{8,16},{9,17... | collective-permute-start | bytes 1806344 | tf_op jit(solution)/shard_map/ppermute | solution.py:208
  13.4 1.4 collective-permute-start.5
  14.7 1.5 %constant_dynamic-slice_fusion.3 = bf16[1,8,24,2,768]{4,3,2,1,0:T(2,128)(2,1)S(1)} fusion(bf16[1,8,192,2,768]{4,3,2,1,0:T(2,128)(2,1)} %get-tuple-element.28, s32[]{:T(128)S(6)} %select_n.75), kind=kLoop, calls=%fused_computation.25 | loop fusion | bytes 1179652 | tf_op jit(solution)/shard_map/dynamic_slice | solution.py:198
  16.3 0.1 constant_dynamic-slice_fusion.2
  16.4 0.9 fusion.2
  17.2 1.3 collective-permute-start.7
  18.5 1.3 collective-permute-start.3
  19.8 0.1 copy.28
  19.9 3.1 %collective-permute-start = (s32[2,2,2]{1,2,0:T(2,128)S(1)}, s32[2,2,2]{1,2,0:T(2,128)S(1)}, u32[]{:S(2)}, u32[]{:S(2)}) collective-permute-start(s32[2,2,2]{1,2,0:T(2,128)S(1)} %copy.28), channel_id=1, source_target_pairs={{0,1},{1,0},{2,3},{3,2},{4,5},{5,4},{6,7},{7,6},{8,9},{9,8},{10,11... | collective-permute-start | bytes 104 | tf_op jit(solution)/shard_map/ppermute | solution.py:186
  23.0 0.1 and_select_fusion
  23.1 0.6 fusion.13
  23.7 2.0 %collective-permute-done.4.refs_1_ = bf16[392,768]{1,0:T(8,128)(2,1)S(1)} collective-permute-done((bf16[392,768]{1,0:T(8,128)(2,1)S(1)}, bf16[392,768]{1,0:T(8,128)(2,1)S(1)}, u32[]{:S(2)}, u32[]{:S(2)}) %collective-permute-start.4) | collective-permute-done | bytes 602144 | tf_op jit(solution)/shard_map/ppermute | solution.py:208
  25.7 1.6 %collective-permute-done.5 = bf16[392,768]{1,0:T(8,128)(2,1)} collective-permute-done((bf16[392,768]{1,0:T(8,128)(2,1)S(1)}, bf16[392,768]{1,0:T(8,128)(2,1)}, u32[]{:S(2)}, u32[]{:S(2)}) %collective-permute-start.5) | collective-permute-done | bytes 602144 | tf_op jit(solution)/shard_map/ppermute | solution.py:209
  27.3 10.9 %collective-permute-start.9 = (bf16[392,768]{1,0:T(8,128)(2,1)S(1)}, bf16[392,768]{1,0:T(8,128)(2,1)S(1)}, u32[]{:S(2)}, u32[]{:S(2)}) collective-permute-start(bf16[392,768]{1,0:T(8,128)(2,1)S(1)} %collective-permute-done.4.refs_1_), channel_id=1, source_target_pairs={{0,38},{1,39},{2,36},{3,37},{4,34},{5,35},{6,32},{7,33},{32,70},{3... | collective-permute-start | bytes 1806344 | tf_op jit(solution)/shard_map/ppermute | solution.py:41
  38.2 0.1 pad_add_fusion.4.flags
  40.7 0.1 pad_add_fusion.5.flags
  40.8 0.1 pad_add_fusion.3.flags
  40.9 0.1 pad_add_fusion
  41.0 24.6 %collective-permute-start.1 = (s32[2,4,2]{1,2,0:T(2,128)S(1)}, s32[2,4,2]{1,2,0:T(2,128)S(1)}, u32[]{:S(2)}, u32[]{:S(2)}) collective-permute-start(s32[2,4,2]{1,2,0:T(2,128)S(1)} %pad_add_fusion), channel_id=1, source_target_pairs={{0,2},{1,3},{2,0},{3,1},{4,6},{5,7},{6,4},{7,5},{8,10},{9,11},{10,... | collective-permute-start | bytes 200 | tf_op jit(solution)/shard_map/ppermute | solution.py:186
  65.5 2.1 %collective-permute-start.8 = (bf16[392,768]{1,0:T(8,128)(2,1)}, bf16[392,768]{1,0:T(8,128)(2,1)}, u32[]{:S(2)}, u32[]{:S(2)}) collective-permute-start(bf16[392,768]{1,0:T(8,128)(2,1)} %fusion.2), channel_id=1, source_target_pairs={{0,8},{1,9},{2,10},{3,11},{4,12},{5,13},{6,14},{7,15},{8,16},{9,17... | collective-permute-start | bytes 1806344 | tf_op jit(solution)/shard_map/ppermute | solution.py:41
  67.6 7.2 %collective-permute-done.1 = s32[2,4,2]{1,2,0:T(2,128)S(1)} collective-permute-done((s32[2,4,2]{1,2,0:T(2,128)S(1)}, s32[2,4,2]{1,2,0:T(2,128)S(1)}, u32[]{:S(2)}, u32[]{:S(2)}) %collective-permute-start.1) | collective-permute-done | bytes 96 | tf_op jit(solution)/shard_map/ppermute | solution.py:186
  74.8 0.1 pad_add_fusion.1
  75.0 9.3 %copy.29 = bf16[2,8,2,192,768]{4,3,2,1,0:T(8,128)(2,1)} copy(bf16[2,8,2,192,768]{4,2,3,1,0:T(2,128)(2,1)} %bitcast.68) | data formatting | bytes 18874368 | tf_op jit(solution)/shard_map/transpose | solution.py:216
  84.3 2.1 %collective-permute-start.6 = (bf16[392,768]{1,0:T(8,128)(2,1)}, bf16[392,768]{1,0:T(8,128)(2,1)}, u32[]{:S(2)}, u32[]{:S(2)}) collective-permute-start(bf16[392,768]{1,0:T(8,128)(2,1)} %fusion.2), channel_id=1, source_target_pairs={{0,16},{1,17},{2,18},{3,19},{4,20},{5,21},{6,22},{7,23},{8,24},{9,... | collective-permute-start | bytes 1806344 | tf_op jit(solution)/shard_map/ppermute | solution.py:41
  86.4 0.1 pad_add_fusion.2
  86.5 0.1 copy.34.pairs
  86.6 0.1 copy.36.pairs
  86.7 3.7 %copy-done = bf16[2,8,2,192,768]{4,3,2,1,0:T(8,128)(2,1)S(1)} copy-done((bf16[2,8,2,192,768]{4,3,2,1,0:T(8,128)(2,1)S(1)}, bf16[2,8,2,192,768]{4,3,2,1,0:T(8,128)(2,1)}, u32[]{:S(2)}) %copy-start) | copy-done | bytes 9437208
  90.4 4.8 %shard_map.56 = (f32[4,2,24,192]{3,2,1,0:T(8,128)S(1)}, f32[4,2,24,192]{3,2,1,0:T(8,128)S(1)}) custom-call(s32[1]{0:T(128)} %bitcast.18.chosen, s32[16,2]{1,0:T(8,128)S(1)} %copy.34.pairs, s32[3]{0:T(128)S(1)} %pad_add_fusion.4.flags, f32[8]{0:T(128)S(1)} %copy-done.2, bf16[2,8,384,768]{3,2,1,0:T(8,128)(2,1)S(1)} %bitcast.64, ...), custom_call_target="tpu_custom_call" | custom-call | flops 1925185536 | bytes 5308416 | tf_op jit(solution)/shard_map/pallas_call | solution.py:148
  95.3 5.4 %shard_map.55 = (f32[4,2,24,192]{3,2,1,0:T(8,128)S(1)}, f32[4,2,24,192]{3,2,1,0:T(8,128)S(1)}) custom-call(s32[1]{0:T(128)} %bitcast.15.chosen, s32[16,2]{1,0:T(8,128)S(1)} %copy.34.pairs, s32[3]{0:T(128)S(1)} %pad_add_fusion.4.flags, f32[8]{0:T(128)S(1)} %copy-done.2, bf16[2,8,384,768]{3,2,1,0:T(8,128)(2,1)S(1)} %bitcast.65, ...), custom_call_target="tpu_custom_call" | custom-call | flops 1925185536 | bytes 5308416 | tf_op jit(solution)/shard_map/pallas_call | solution.py:148
  100.6 5.3 %shard_map.57 = (f32[4,2,24,192]{3,2,1,0:T(8,128)S(1)}, f32[4,2,24,192]{3,2,1,0:T(8,128)S(1)}) custom-call(s32[1]{0:T(128)} %bitcast.2.chosen, s32[16,2]{1,0:T(8,128)S(1)} %copy.36.pairs, s32[3]{0:T(128)S(1)} %pad_add_fusion.3.flags, f32[8]{0:T(128)S(1)} %copy-done.2, bf16[2,8,384,768]{3,2,1,0:T(8,128)(2,1)S(1)} %bitcast.66, ...), custom_call_target="tpu_custom_call" | custom-call | flops 1925185536 | bytes 5308416 | tf_op jit(solution)/shard_map/pallas_call | solution.py:148
  105.9 2.6 %collective-permute-start.10 = (f32[4,2,24,192]{3,2,1,0:T(8,128)S(1)}, f32[4,2,24,192]{3,2,1,0:T(8,128)S(1)}, u32[]{:S(2)}, u32[]{:S(2)}) collective-permute-start(f32[4,2,24,192]{3,2,1,0:T(8,128)S(1)} %get-tuple-element.23), channel_id=1, source_target_pairs={{0,1},{1,0},{2,3},{3,2},{4,5},{5,4},{6,7},{7,6},{8,9},{9,8},{10,11... | collective-permute-start | bytes 442376 | tf_op jit(solution)/shard_map/ppermute | solution.py:173
  108.4 8.3 %collective-permute-done.14.refs_0_.refs_1_ = bf16[392,768]{1,0:T(8,128)(2,1)S(1)} collective-permute-done((bf16[392,768]{1,0:T(8,128)(2,1)}, bf16[392,768]{1,0:T(8,128)(2,1)S(1)}, u32[]{:S(2)}, u32[]{:S(2)}) %collective-permute-start.14) | collective-permute-done | bytes 602144 | tf_op jit(solution)/shard_map/ppermute | solution.py:41
  116.8 4.8 %shard_map.58 = (f32[4,2,24,192]{3,2,1,0:T(8,128)S(1)}, f32[4,2,24,192]{3,2,1,0:T(8,128)S(1)}) custom-call(s32[1]{0:T(128)} %bitcast.24.chosen, s32[16,2]{1,0:T(8,128)S(1)} %copy.36.pairs, s32[3]{0:T(128)S(1)} %pad_add_fusion.5.flags, f32[8]{0:T(128)S(1)} %copy-done.2, bf16[2,8,384,768]{3,2,1,0:T(8,128)(2,1)S(1)} %bitcast.67, ...), custom_call_target="tpu_custom_call" | custom-call | flops 1925185536 | bytes 5308416 | tf_op jit(solution)/shard_map/pallas_call | solution.py:148
  121.5 3.2 %collective-permute-start.15 = (f32[4,2,24,192]{3,2,1,0:T(8,128)S(1)}, f32[4,2,24,192]{3,2,1,0:T(8,128)S(1)}, u32[]{:S(2)}, u32[]{:S(2)}) collective-permute-start(f32[4,2,24,192]{3,2,1,0:T(8,128)S(1)} %get-tuple-element.26), channel_id=1, source_target_pairs={{0,1},{1,0},{2,3},{3,2},{4,5},{5,4},{6,7},{7,6},{8,9},{9,8},{10,11... | collective-permute-start | bytes 442376 | tf_op jit(solution)/shard_map/ppermute | solution.py:173
  125.4 0.1 collective-permute-start.11
  125.5 1.9 %collective-permute-start.12 = (f32[2,24,192]{2,1,0:T(8,128)S(1)}, f32[2,24,192]{2,1,0:T(8,128)S(1)}, u32[]{:S(2)}, u32[]{:S(2)}) collective-permute-start(f32[2,24,192]{2,1,0:T(8,128)S(1)} %get-tuple-element.31), channel_id=1, source_target_pairs={{0,4},{1,5},{2,6},{3,7},{4,0},{5,1},{6,2},{7,3},{8,12},{9,13},{10,... | collective-permute-start | bytes 110600 | tf_op jit(solution)/shard_map/ppermute | solution.py:178
  127.4 1.4 collective-permute-start.13
  128.8 0.4 collective-permute-start.16
  129.2 1.3 collective-permute-start.17
  130.5 2.3 %collective-permute-start.18 = (f32[2,24,192]{2,1,0:T(8,128)S(1)}, f32[2,24,192]{2,1,0:T(8,128)S(1)}, u32[]{:S(2)}, u32[]{:S(2)}) collective-permute-start(f32[2,24,192]{2,1,0:T(8,128)S(1)} %get-tuple-element.33), channel_id=1, source_target_pairs={{0,6},{1,7},{2,0},{3,1},{4,2},{5,3},{6,4},{7,5},{8,14},{9,15},{10,... | collective-permute-start | bytes 110600 | tf_op jit(solution)/shard_map/ppermute | solution.py:178
  132.8 1.0 collective-permute-done.16
  133.8 2.6 %collective-permute-done.17 = f32[2,24,192]{2,1,0:T(8,128)S(1)} collective-permute-done((f32[2,24,192]{2,1,0:T(8,128)S(1)}, f32[2,24,192]{2,1,0:T(8,128)S(1)}, u32[]{:S(2)}, u32[]{:S(2)}) %collective-permute-start.17) | collective-permute-done | bytes 36896 | tf_op jit(solution)/shard_map/ppermute | solution.py:178
  136.4 0.7 copy.38
  (40 shorter events, 0.4 us)
Async XLA Ops:
  0.0 9.5 %copy-start.3 = (bf16[2,192]{1,0:T(2,128)(2,1)S(1)}, bf16[2,192]{1,0:T(2,128)(2,1)}, u32[]{:S(2)}) copy-start(bf16[2,192]{1,0:T(2,128)(2,1)} %param.7) | copy-start | bytes 2308
  11.2 14.4 %collective-permute-start.4 = (bf16[392,768]{1,0:T(8,128)(2,1)S(1)}, bf16[392,768]{1,0:T(8,128)(2,1)S(1)}, u32[]{:S(2)}, u32[]{:S(2)}) collective-permute-start(bf16[392,768]{1,0:T(8,128)(2,1)S(1)} %fusion.3), channel_id=1, source_target_pairs={{0,8},{1,9},{2,10},{3,11},{4,12},{5,13},{6,14},{7,15},{8,16},{9,17... | collective-permute-start | bytes 1806344 | tf_op jit(solution)/shard_map/ppermute | solution.py:208
  13.4 13.9 %collective-permute-start.5 = (bf16[392,768]{1,0:T(8,128)(2,1)S(1)}, bf16[392,768]{1,0:T(8,128)(2,1)}, u32[]{:S(2)}, u32[]{:S(2)}) collective-permute-start(bf16[392,768]{1,0:T(8,128)(2,1)S(1)} %fusion.3), channel_id=1, source_target_pairs={{0,24},{1,25},{2,26},{3,27},{4,28},{5,29},{6,30},{7,31},{8,0},{9,1... | collective-permute-start | bytes 1806344 | tf_op jit(solution)/shard_map/ppermute | solution.py:209
  16.2 3.6 %copy-start.4 = (s32[2,2,2]{2,1,0:T(2,128)S(1)}, s32[2,2,2]{2,1,0:T(2,128)}, u32[]{:S(2)}) copy-start(s32[2,2,2]{2,1,0:T(2,128)} %param.9) | copy-start | bytes 100
  16.2 6.8 %copy-start.5 = (s32[2,2]{1,0:T(2,128)S(1)}, s32[2,2]{1,0:T(2,128)}, u32[]{:S(2)}) copy-start(s32[2,2]{1,0:T(2,128)} %param.8) | copy-start | bytes 52
  17.2 78.0 %collective-permute-start.7 = (bf16[392,768]{1,0:T(8,128)(2,1)}, bf16[392,768]{1,0:T(8,128)(2,1)S(1)}, u32[]{:S(2)}, u32[]{:S(2)}) collective-permute-start(bf16[392,768]{1,0:T(8,128)(2,1)} %fusion.2), channel_id=1, source_target_pairs={{24,38},{25,39},{26,36},{27,37},{28,34},{29,35},{30,32},{31,33},{5... | collective-permute-start | bytes 1806344 | tf_op jit(solution)/shard_map/ppermute | solution.py:41
  18.5 82.1 %collective-permute-start.3 = (bf16[392,768]{1,0:T(8,128)(2,1)}, bf16[392,768]{1,0:T(8,128)(2,1)S(1)}, u32[]{:S(2)}, u32[]{:S(2)}) collective-permute-start(bf16[392,768]{1,0:T(8,128)(2,1)} %fusion.2), channel_id=1, source_target_pairs={{16,38},{17,39},{18,36},{19,37},{20,34},{21,35},{22,32},{23,33},{2... | collective-permute-start | bytes 1806344 | tf_op jit(solution)/shard_map/ppermute | solution.py:41
  19.9 20.9 %collective-permute-start = (s32[2,2,2]{1,2,0:T(2,128)S(1)}, s32[2,2,2]{1,2,0:T(2,128)S(1)}, u32[]{:S(2)}, u32[]{:S(2)}) collective-permute-start(s32[2,2,2]{1,2,0:T(2,128)S(1)} %copy.28), channel_id=1, source_target_pairs={{0,1},{1,0},{2,3},{3,2},{4,5},{5,4},{6,7},{7,6},{8,9},{9,8},{10,11... | collective-permute-start | bytes 104 | tf_op jit(solution)/shard_map/ppermute | solution.py:186
  27.3 59.2 %collective-permute-start.9 = (bf16[392,768]{1,0:T(8,128)(2,1)S(1)}, bf16[392,768]{1,0:T(8,128)(2,1)S(1)}, u32[]{:S(2)}, u32[]{:S(2)}) collective-permute-start(bf16[392,768]{1,0:T(8,128)(2,1)S(1)} %collective-permute-done.4.refs_1_), channel_id=1, source_target_pairs={{0,38},{1,39},{2,36},{3,37},{4,34},{5,35},{6,32},{7,33},{32,70},{3... | collective-permute-start | bytes 1806344 | tf_op jit(solution)/shard_map/ppermute | solution.py:41
  41.0 33.9 %collective-permute-start.1 = (s32[2,4,2]{1,2,0:T(2,128)S(1)}, s32[2,4,2]{1,2,0:T(2,128)S(1)}, u32[]{:S(2)}, u32[]{:S(2)}) collective-permute-start(s32[2,4,2]{1,2,0:T(2,128)S(1)} %pad_add_fusion), channel_id=1, source_target_pairs={{0,2},{1,3},{2,0},{3,1},{4,6},{5,7},{6,4},{7,5},{8,10},{9,11},{10,... | collective-permute-start | bytes 200 | tf_op jit(solution)/shard_map/ppermute | solution.py:186
  65.5 29.7 %collective-permute-start.8 = (bf16[392,768]{1,0:T(8,128)(2,1)}, bf16[392,768]{1,0:T(8,128)(2,1)}, u32[]{:S(2)}, u32[]{:S(2)}) collective-permute-start(bf16[392,768]{1,0:T(8,128)(2,1)} %fusion.2), channel_id=1, source_target_pairs={{0,8},{1,9},{2,10},{3,11},{4,12},{5,13},{6,14},{7,15},{8,16},{9,17... | collective-permute-start | bytes 1806344 | tf_op jit(solution)/shard_map/ppermute | solution.py:41
  74.9 9.4 %collective-permute-start.2 = (s32[2,8,2]{1,2,0:T(2,128)S(1)}, s32[2,8,2]{1,2,0:T(2,128)S(1)}, u32[]{:S(2)}, u32[]{:S(2)}) collective-permute-start(s32[2,8,2]{1,2,0:T(2,128)S(1)} %pad_add_fusion.1), channel_id=1, source_target_pairs={{0,4},{1,5},{2,6},{3,7},{4,0},{5,1},{6,2},{7,3},{8,12},{9,13},{10,... | collective-permute-start | bytes 392 | tf_op jit(solution)/shard_map/ppermute | solution.py:186
  75.0 11.7 %copy-start.2 = (f32[8]{0:T(128)S(1)}, f32[8]{0:T(128)}, u32[]{:S(2)}) copy-start(f32[8]{0:T(128)} %occupied.7) | copy-start | bytes 100
  84.3 16.4 %collective-permute-start.6 = (bf16[392,768]{1,0:T(8,128)(2,1)}, bf16[392,768]{1,0:T(8,128)(2,1)}, u32[]{:S(2)}, u32[]{:S(2)}) collective-permute-start(bf16[392,768]{1,0:T(8,128)(2,1)} %fusion.2), channel_id=1, source_target_pairs={{0,16},{1,17},{2,18},{3,19},{4,20},{5,21},{6,22},{7,23},{8,24},{9,... | collective-permute-start | bytes 1806344 | tf_op jit(solution)/shard_map/ppermute | solution.py:41
  86.5 30.3 %collective-permute-start.14 = (bf16[392,768]{1,0:T(8,128)(2,1)}, bf16[392,768]{1,0:T(8,128)(2,1)S(1)}, u32[]{:S(2)}, u32[]{:S(2)}) collective-permute-start(bf16[392,768]{1,0:T(8,128)(2,1)} %collective-permute-done.5), channel_id=1, source_target_pairs={{0,24},{1,25},{2,26},{3,27},{4,28},{5,29},{6,30},{7,31},{8,38},{9,... | collective-permute-start | bytes 1806344 | tf_op jit(solution)/shard_map/ppermute | solution.py:41
  86.7 3.7 %copy-start = (bf16[2,8,2,192,768]{4,3,2,1,0:T(8,128)(2,1)S(1)}, bf16[2,8,2,192,768]{4,3,2,1,0:T(8,128)(2,1)}, u32[]{:S(2)}) copy-start(bf16[2,8,2,192,768]{4,3,2,1,0:T(8,128)(2,1)} %copy.29) | copy-start | bytes 28311556
  90.4 4.9 %copy-start.1 = (bf16[2,8,2,192,768]{4,3,2,1,0:T(8,128)(2,1)S(1)}, bf16[2,8,2,192,768]{4,3,2,1,0:T(8,128)(2,1)}, u32[]{:S(2)}) copy-start(bf16[2,8,2,192,768]{4,3,2,1,0:T(8,128)(2,1)} %copy.29) | copy-start | bytes 28311556
  105.9 19.5 %collective-permute-start.10 = (f32[4,2,24,192]{3,2,1,0:T(8,128)S(1)}, f32[4,2,24,192]{3,2,1,0:T(8,128)S(1)}, u32[]{:S(2)}, u32[]{:S(2)}) collective-permute-start(f32[4,2,24,192]{3,2,1,0:T(8,128)S(1)} %get-tuple-element.23), channel_id=1, source_target_pairs={{0,1},{1,0},{2,3},{3,2},{4,5},{5,4},{6,7},{7,6},{8,9},{9,8},{10,11... | collective-permute-start | bytes 442376 | tf_op jit(solution)/shard_map/ppermute | solution.py:173
  121.5 7.3 %collective-permute-start.15 = (f32[4,2,24,192]{3,2,1,0:T(8,128)S(1)}, f32[4,2,24,192]{3,2,1,0:T(8,128)S(1)}, u32[]{:S(2)}, u32[]{:S(2)}) collective-permute-start(f32[4,2,24,192]{3,2,1,0:T(8,128)S(1)} %get-tuple-element.26), channel_id=1, source_target_pairs={{0,1},{1,0},{2,3},{3,2},{4,5},{5,4},{6,7},{7,6},{8,9},{9,8},{10,11... | collective-permute-start | bytes 442376 | tf_op jit(solution)/shard_map/ppermute | solution.py:173
  125.4 5.1 %collective-permute-start.11 = (f32[2,24,192]{2,1,0:T(8,128)S(1)}, f32[2,24,192]{2,1,0:T(8,128)S(1)}, u32[]{:S(2)}, u32[]{:S(2)}) collective-permute-start(f32[2,24,192]{2,1,0:T(8,128)S(1)} %get-tuple-element.29), channel_id=1, source_target_pairs={{0,2},{1,3},{2,4},{3,5},{4,6},{5,7},{6,0},{7,1},{8,10},{9,11},{10,... | collective-permute-start | bytes 110600 | tf_op jit(solution)/shard_map/ppermute | solution.py:178
  125.5 7.2 %collective-permute-start.12 = (f32[2,24,192]{2,1,0:T(8,128)S(1)}, f32[2,24,192]{2,1,0:T(8,128)S(1)}, u32[]{:S(2)}, u32[]{:S(2)}) collective-permute-start(f32[2,24,192]{2,1,0:T(8,128)S(1)} %get-tuple-element.31), channel_id=1, source_target_pairs={{0,4},{1,5},{2,6},{3,7},{4,0},{5,1},{6,2},{7,3},{8,12},{9,13},{10,... | collective-permute-start | bytes 110600 | tf_op jit(solution)/shard_map/ppermute | solution.py:178
  127.4 5.3 %collective-permute-start.13 = (f32[2,24,192]{2,1,0:T(8,128)S(1)}, f32[2,24,192]{2,1,0:T(8,128)S(1)}, u32[]{:S(2)}, u32[]{:S(2)}) collective-permute-start(f32[2,24,192]{2,1,0:T(8,128)S(1)} %get-tuple-element.30), channel_id=1, source_target_pairs={{0,6},{1,7},{2,0},{3,1},{4,2},{5,3},{6,4},{7,5},{8,14},{9,15},{10,... | collective-permute-start | bytes 110600 | tf_op jit(solution)/shard_map/ppermute | solution.py:178
  128.8 5.0 %collective-permute-start.16 = (f32[2,24,192]{2,1,0:T(8,128)S(1)}, f32[2,24,192]{2,1,0:T(8,128)S(1)}, u32[]{:S(2)}, u32[]{:S(2)}) collective-permute-start(f32[2,24,192]{2,1,0:T(8,128)S(1)} %get-tuple-element.32), channel_id=1, source_target_pairs={{0,2},{1,3},{2,4},{3,5},{4,6},{5,7},{6,0},{7,1},{8,10},{9,11},{10,... | collective-permute-start | bytes 110600 | tf_op jit(solution)/shard_map/ppermute | solution.py:178
  129.2 7.2 %collective-permute-start.17 = (f32[2,24,192]{2,1,0:T(8,128)S(1)}, f32[2,24,192]{2,1,0:T(8,128)S(1)}, u32[]{:S(2)}, u32[]{:S(2)}) collective-permute-start(f32[2,24,192]{2,1,0:T(8,128)S(1)} %get-tuple-element.34), channel_id=1, source_target_pairs={{0,4},{1,5},{2,6},{3,7},{4,0},{5,1},{6,2},{7,3},{8,12},{9,13},{10,... | collective-permute-start | bytes 110600 | tf_op jit(solution)/shard_map/ppermute | solution.py:178
  130.5 5.9 %collective-permute-start.18 = (f32[2,24,192]{2,1,0:T(8,128)S(1)}, f32[2,24,192]{2,1,0:T(8,128)S(1)}, u32[]{:S(2)}, u32[]{:S(2)}) collective-permute-start(f32[2,24,192]{2,1,0:T(8,128)S(1)} %get-tuple-element.33), channel_id=1, source_target_pairs={{0,6},{1,7},{2,0},{3,1},{4,2},{5,3},{6,4},{7,5},{8,14},{9,15},{10,... | collective-permute-start | bytes 110600 | tf_op jit(solution)/shard_map/ppermute | solution.py:178

commit v3 on v2

--- a/solution.py
+++ b/solution.py
@@ -41,9 +41,8 @@
     return lax.ppermute(array, ("ka", "occ"), route(columns, by))
 
 
-def piece_kernel(later, chosen, pairs, flags, occupied, left, own_energy, *refs):
-    mates = refs[:2]
-    refs = refs[2:]
+def piece_kernel(sources, later, chosen, pairs, flags, occupied, left, own_energy, *refs):
+    mates, refs = refs[:sources], refs[sources:]
     if later:
         before, refs = refs[:4], refs[4:]
     keep, send, piece, products, combined, rounded, turned, total = refs
@@ -53,15 +52,11 @@
     share = rows // (2 * orbitals)
     count = pairs.shape[0]
     mine = chosen[0]
-    first = flags[0] == 0
-
-    @pl.when(first)
-    def _():
-        piece[...] = mates[0][...]
-
-    @pl.when(jnp.logical_not(first))
-    def _():
-        piece[...] = mates[1][...]
+    for number, mate in enumerate(mates):
+
+        @pl.when(flags[0] == number)
+        def _():
+            piece[...] = mate[...]
 
     contract = (((1,), (1,)), ((), ()))
     for orbital in range(orbitals):
@@ -146,9 +141,9 @@
     scalars = pl.BlockSpec(memory_space=pltpu.SMEM)
     whole = pl.BlockSpec(memory_space=pltpu.VMEM)
     return pl.pallas_call(
-        functools.partial(piece_kernel, bool(before)),
+        functools.partial(piece_kernel, len(mates), bool(before)),
         out_shape=(block, block),
-        in_specs=[scalars] * 4 + [whole] * (4 + len(before)),
+        in_specs=[scalars] * 4 + [whole] * (2 + len(mates) + len(before)),
         out_specs=(whole, whole),
         scratch_shapes=[
             pltpu.VMEM((rows + HEAD, auxiliary), jnp.bfloat16),
@@ -195,44 +190,52 @@
     start = lax.axis_index("occ") * share
 
     def outgoing(momentum):
-        cut = lax.dynamic_slice_in_dim(factors[momentum], start, share, 1)
-        cut = jnp.transpose(cut, (2, 0, 1, 3)).reshape(2 * orbitals * share, auxiliary)
-        energy = lax.dynamic_slice_in_dim(virtual_energy[momentum], start, share, 0)
-        head = jnp.pad(energy[None, :], ((0, HEAD - 1), (0, auxiliary - share)))
+        cut = lax.dynamic_slice(
+            factors, (momentum, 0, start, 0, 0), (1, orbitals, share, 2, auxiliary)
+        )
+        cut = jnp.transpose(cut[0], (2, 0, 1, 3)).reshape(2 * orbitals * share, auxiliary)
+        energy = lax.dynamic_slice(virtual_energy, (momentum, start), (1, share))
+        head = jnp.pad(energy, ((0, HEAD - 1), (0, auxiliary - share)))
         return jnp.concatenate([cut, head], axis=0)
 
+    pairs = all_pairs_of(pair_lists)
     straight = outgoing(0)
     relayed = outgoing(1)
+    straight, relayed, pairs, factors = lax.optimization_barrier((straight, relayed, pairs, factors))
     cross_one = moved(straight, (3,), 1)
-    cross_two = moved(straight, (2, 3), 2)
+    cross_two = moved(straight, (2,), 2)
     hop_plus = lax.ppermute(relayed, ("ka", "occ"), ring_route(1))
     hop_minus = lax.ppermute(relayed, ("ka", "occ"), ring_route(-1))
+    left = jnp.transpose(factors, (0, 1, 3, 2, 4)).reshape(momenta, orbitals, 2 * virtuals, auxiliary)
     straight, hop_plus, hop_minus = lax.optimization_barrier((straight, hop_plus, hop_minus))
     up = moved(hop_plus, (0,), 0)
     back = moved(hop_minus, range(COLUMNS), -1)
     near_one = moved(straight, (0, 1, 2), 1)
+    straight, cross_one, cross_two, near_one = lax.optimization_barrier((straight, cross_one, cross_two, near_one))
+    late_two = moved(straight, (3,), 2)
     near_two = moved(straight, (0, 1), 2)
 
-    left = jnp.transpose(factors, (0, 1, 3, 2, 4)).reshape(momenta, orbitals, 2 * virtuals, auxiliary)
     own_energy = virtual_energy.astype(jnp.float32)[:, None, :]
-    pairs = all_pairs_of(pair_lists)
     core = lax.axis_index("occ") % CORES
     column = lax.axis_index("ka") % COLUMNS
     chosen = (conserve[0][:, None] + jnp.arange(momenta, dtype=jnp.int32)[None, :]) % momenta
 
-    def density(round_index, momentum, mates, from_second, before, swapped):
-        flags = jnp.stack([from_second.astype(jnp.int32), core.astype(jnp.int32), swapped])
+    def density(round_index, momentum, mates, source, before, swapped):
+        flags = jnp.stack([source.astype(jnp.int32), core.astype(jnp.int32), swapped])
         return piece_density(
             chosen[round_index, momentum].reshape(1), pairs[round_index], flags,
             occupied_energy, left, own_energy, mates, before,
         )
 
     zero = jnp.int32(0)
+    early_a = density(0, 0, (cross_one, near_one), column != 0, (), zero)
     early_b = density(0, 1, (up, hop_plus), column != 0, (), zero)
-    early_a = density(0, 0, (cross_one, near_one), column != 0, (), zero)
     before = (*early_a, *early_b)
-    late_b = density(1, 1, (back, back), column != column, before, (chosen[0, 0] != chosen[1, 1]).astype(jnp.int32))
-    late_a = density(1, 0, (cross_two, near_two), column > 1, before, (chosen[0, 0] != chosen[1, 0]).astype(jnp.int32))
+    late_b = density(1, 1, (back,), zero, before, (chosen[0, 0] != chosen[1, 1]).astype(jnp.int32))
+    source = jnp.clip(column, 0, 2)
+    late_a = density(
+        1, 0, (cross_two, late_two, near_two), source, before, (chosen[0, 0] != chosen[1, 0]).astype(jnp.int32)
+    )
     of_b = summed(*late_b)
     of_a = summed(*late_a)
     stacked = jnp.stack([of_a, of_b])

time: 138 us -> 132 us (0.957)
  the two profiles are of different devices: /device:TPU:1 before, /device:TPU:10 now
where the time goes in v3:
time: 132 us; the launch traced here: 131 us
  starting transfers between devices  67.4 us (51%)
  Pallas kernels  20.6 us (16%)
  waiting for transfers between devices  20.1 us (15%)
  local copies, waits for them, and re-layouts  18.4 us (14%)
  between operations  3.38 us (3%)
  other arithmetic  1.54 us (1%)
    ppermute x7, starting transfers between devices, moved(): return lax.ppermute(array, ('ka', 'occ'), route(columns, by))  50.7 us
    pallas_call x4, Pallas kernels, piece_density(): pl.pallas_call(functools.partial(piece_kernel, len(mates), bool(before)),...  20.6 us
    ppermute x1, waiting for transfers between devices, local(): hop_plus = lax.ppermute(relayed, ('ka', 'occ'), ring_route(1))  10.7 us
    transpose x1, local copies, waits for them, and re-layouts, local(): jnp.transpose(factors, (0, 1, 3, 2, 4))  9.31 us
    ppermute x6, starting transfers between devices, summed(): total = total + lax.ppermute(part, 'occ', ring)  8.76 us
    ppermute x6, waiting for transfers between devices, summed(): total = total + lax.ppermute(part, 'occ', ring)  5.86 us
    ppermute x3, starting transfers between devices, all_pairs_of(): lax.ppermute(gathered, 'occ', [(i, i ^ reach) for i in range(LINE * CORES)])  5.24 us
    unnamed x17, local copies, waits for them, and re-layouts  4.48 us
  transfers between devices with their start and end apart: 20, of which 7 were waited for; matrix products, arithmetic and copies ran while one was open for 11% of the time, Pallas kernels for 16%

profile of v3, /device:TPU:10, one launch (start us, length us, event | category | flops | bytes accessed | tf_op | source)
XLA Modules:
  0.0 131.3 jit_solution(14553017364795148388)
XLA Ops:
  0.0 0.8 copy.32
  0.8 0.8 constant_dynamic-slice_fusion.3
  1.6 2.1 %constant_dynamic-slice_fusion = (bf16[1,8,24,2,768]{4,3,2,1,0:T(2,128)(2,1)S(1)}, bf16[1,8,24,2,768]{4,3,2,1,0:T(2,128)(2,1)S(1)}) fusion(bf16[2,8,192,2,768]{4,3,2,1,0:T(2,128)(2,1)} %param.5, s32[]{:T(128)S(6)} %select_n.73), kind=kLoop, calls=%fused_computation.22 | loop fusion | bytes 2359300 | tf_op jit(solution)/shard_map/dynamic_slice | solution.py:193
  3.7 0.1 copy.41
  3.7 0.1 pad_add_fusion
  3.8 1.9 %collective-permute-start.1 = (s32[2,4,2]{1,2,0:T(2,128)S(1)}, s32[2,4,2]{1,2,0:T(2,128)S(1)}, u32[]{:S(2)}, u32[]{:S(2)}) collective-permute-start(s32[2,4,2]{1,2,0:T(2,128)S(1)} %pad_add_fusion), channel_id=1, source_target_pairs={{0,2},{1,3},{2,0},{3,1},{4,6},{5,7},{6,4},{7,5},{8,10},{9,11},{10,... | collective-permute-start | bytes 200 | tf_op jit(solution)/shard_map/ppermute | solution.py:181
  5.8 0.1 copy.42
  5.8 1.6 %collective-permute-done.1 = s32[2,4,2]{1,2,0:T(2,128)S(1)} collective-permute-done((s32[2,4,2]{1,2,0:T(2,128)S(1)}, s32[2,4,2]{1,2,0:T(2,128)S(1)}, u32[]{:S(2)}, u32[]{:S(2)}) %collective-permute-start.1) | collective-permute-done | bytes 96 | tf_op jit(solution)/shard_map/ppermute | solution.py:181
  7.4 0.1 pad_add_fusion.1
  7.5 3.3 %collective-permute-start.2 = (s32[2,8,2]{1,2,0:T(2,128)S(1)}, s32[2,8,2]{1,2,0:T(2,128)S(1)}, u32[]{:S(2)}, u32[]{:S(2)}) collective-permute-start(s32[2,8,2]{1,2,0:T(2,128)S(1)} %pad_add_fusion.1), channel_id=1, source_target_pairs={{0,4},{1,5},{2,6},{3,7},{4,0},{5,1},{6,2},{7,3},{8,12},{9,13},{10,... | collective-permute-start | bytes 392 | tf_op jit(solution)/shard_map/ppermute | solution.py:181
  10.8 0.9 fusion.2
  11.7 0.7 collective-permute-done.2
  12.4 0.1 pad_add_fusion.2
  12.5 1.5 %collective-permute-start.3 = (bf16[392,768]{1,0:T(8,128)(2,1)S(1)}, bf16[392,768]{1,0:T(8,128)(2,1)S(1)}, u32[]{:S(2)}, u32[]{:S(2)}) collective-permute-start(bf16[392,768]{1,0:T(8,128)(2,1)S(1)} %get-tuple-element.27), channel_id=1, source_target_pairs={{0,8},{1,9},{2,10},{3,11},{4,12},{5,13},{6,14},{7,15},{8,16},{9,17... | collective-permute-start | bytes 1806344 | tf_op jit(solution)/shard_map/ppermute | solution.py:207
  14.0 0.5 collective-permute-start.4
  14.5 0.7 collective-permute-start.5
  15.2 0.7 collective-permute-start.6
  15.9 10.7 %collective-permute-done.3.refs_1_ = bf16[392,768]{1,0:T(8,128)(2,1)S(1)} collective-permute-done((bf16[392,768]{1,0:T(8,128)(2,1)S(1)}, bf16[392,768]{1,0:T(8,128)(2,1)S(1)}, u32[]{:S(2)}, u32[]{:S(2)}) %collective-permute-start.3) | collective-permute-done | bytes 602144 | tf_op jit(solution)/shard_map/ppermute | solution.py:207
  26.6 1.2 collective-permute-done.4
  27.8 3.1 %collective-permute-start.7 = (bf16[392,768]{1,0:T(8,128)(2,1)}, bf16[392,768]{1,0:T(8,128)(2,1)S(1)}, u32[]{:S(2)}, u32[]{:S(2)}) collective-permute-start(bf16[392,768]{1,0:T(8,128)(2,1)} %get-tuple-element.30), channel_id=1, source_target_pairs={{0,8},{1,9},{2,10},{3,11},{4,12},{5,13},{6,14},{7,15},{8,16},{9,17... | collective-permute-start | bytes 1806344 | tf_op jit(solution)/shard_map/ppermute | solution.py:41
  30.9 0.1 and_select_fusion
  31.0 0.7 fusion.12
  34.1 0.1 pad_add_fusion.5.flags
  34.2 1.5 %collective-permute-start.10 = (bf16[392,768]{1,0:T(8,128)(2,1)S(1)}, bf16[392,768]{1,0:T(8,128)(2,1)}, u32[]{:S(2)}, u32[]{:S(2)}) collective-permute-start(bf16[392,768]{1,0:T(8,128)(2,1)S(1)} %collective-permute-done.3.refs_1_), channel_id=1, source_target_pairs={{0,38},{1,39},{2,36},{3,37},{4,34},{5,35},{6,32},{7,33},{32,70},{3... | collective-permute-start | bytes 1806344 | tf_op jit(solution)/shard_map/ppermute | solution.py:41
  35.7 0.1 pad_add_fusion.4.flags
  35.8 29.5 %collective-permute-start.15 = (bf16[392,768]{1,0:T(8,128)(2,1)}, bf16[392,768]{1,0:T(8,128)(2,1)S(1)}, u32[]{:S(2)}, u32[]{:S(2)}) collective-permute-start(bf16[392,768]{1,0:T(8,128)(2,1)} %copy-done.6), channel_id=1, source_target_pairs={{0,24},{1,25},{2,26},{3,27},{4,28},{5,29},{6,30},{7,31},{8,38},{9,... | collective-permute-start | bytes 1806344 | tf_op jit(solution)/shard_map/ppermute | solution.py:41
  65.2 0.1 pad_add_fusion.3.flags
  65.4 1.3 collective-permute-start.8
  66.7 13.9 %collective-permute-start.9 = (bf16[392,768]{1,0:T(8,128)(2,1)}, bf16[392,768]{1,0:T(8,128)(2,1)}, u32[]{:S(2)}, u32[]{:S(2)}) collective-permute-start(bf16[392,768]{1,0:T(8,128)(2,1)} %get-tuple-element.30), channel_id=1, source_target_pairs={{0,16},{1,17},{2,18},{3,19},{4,20},{5,21},{6,22},{7,23},{8,24},{9,... | collective-permute-start | bytes 1806344 | tf_op jit(solution)/shard_map/ppermute | solution.py:41
  80.6 0.1 copy.36.pairs
  80.7 9.3 %copy.33 = bf16[2,8,2,192,768]{4,3,2,1,0:T(8,128)(2,1)} copy(bf16[2,8,2,192,768]{4,2,3,1,0:T(2,128)(2,1)} %bitcast.68) | data formatting | bytes 18874368 | tf_op jit(solution)/shard_map/transpose | solution.py:209
  90.0 0.1 copy.34.pairs
  90.1 3.7 %copy-done = bf16[2,8,2,192,768]{4,3,2,1,0:T(8,128)(2,1)S(1)} copy-done((bf16[2,8,2,192,768]{4,3,2,1,0:T(8,128)(2,1)S(1)}, bf16[2,8,2,192,768]{4,3,2,1,0:T(8,128)(2,1)}, u32[]{:S(2)}) %copy-start) | copy-done | bytes 9437208
  93.8 4.8 %shard_map.55 = (f32[4,2,24,192]{3,2,1,0:T(8,128)S(1)}, f32[4,2,24,192]{3,2,1,0:T(8,128)S(1)}) custom-call(s32[1]{0:T(128)} %bitcast.15.chosen, s32[16,2]{1,0:T(8,128)S(1)} %copy.34.pairs, s32[3]{0:T(128)S(1)} %pad_add_fusion.4.flags, f32[8]{0:T(128)S(1)} %copy-done.4, bf16[2,8,384,768]{3,2,1,0:T(8,128)(2,1)S(1)} %bitcast.64, ...), custom_call_target="tpu_custom_call" | custom-call | flops 1925185536 | bytes 5308416 | tf_op jit(solution)/shard_map/pallas_call | solution.py:143
  98.7 5.2 %shard_map.56 = (f32[4,2,24,192]{3,2,1,0:T(8,128)S(1)}, f32[4,2,24,192]{3,2,1,0:T(8,128)S(1)}) custom-call(s32[1]{0:T(128)} %bitcast.18.chosen, s32[16,2]{1,0:T(8,128)S(1)} %copy.34.pairs, s32[3]{0:T(128)S(1)} %pad_add_fusion.4.flags, f32[8]{0:T(128)S(1)} %copy-done.4, bf16[2,8,384,768]{3,2,1,0:T(8,128)(2,1)S(1)} %bitcast.65, ...), custom_call_target="tpu_custom_call" | custom-call | flops 1925185536 | bytes 5308416 | tf_op jit(solution)/shard_map/pallas_call | solution.py:143
  103.9 5.1 %shard_map.58 = (f32[4,2,24,192]{3,2,1,0:T(8,128)S(1)}, f32[4,2,24,192]{3,2,1,0:T(8,128)S(1)}) custom-call(s32[1]{0:T(128)} %bitcast.24.chosen, s32[16,2]{1,0:T(8,128)S(1)} %copy.36.pairs, s32[3]{0:T(128)S(1)} %pad_add_fusion.5.flags, f32[8]{0:T(128)S(1)} %copy-done.4, bf16[2,8,384,768]{3,2,1,0:T(8,128)(2,1)S(1)} %bitcast.66, ...), custom_call_target="tpu_custom_call" | custom-call | flops 1925185536 | bytes 5308416 | tf_op jit(solution)/shard_map/pallas_call | solution.py:143
  109.0 0.1 collective-permute-start.16
  109.1 5.5 %shard_map.57 = (f32[4,2,24,192]{3,2,1,0:T(8,128)S(1)}, f32[4,2,24,192]{3,2,1,0:T(8,128)S(1)}) custom-call(s32[1]{0:T(128)} %bitcast.2.chosen, s32[16,2]{1,0:T(8,128)S(1)} %copy.36.pairs, s32[3]{0:T(128)S(1)} %pad_add_fusion.3.flags, f32[8]{0:T(128)S(1)} %copy-done.4, bf16[2,8,384,768]{3,2,1,0:T(8,128)(2,1)S(1)} %bitcast.67, ...), custom_call_target="tpu_custom_call" | custom-call | flops 1925185536 | bytes 5308416 | tf_op jit(solution)/shard_map/pallas_call | solution.py:143
  114.6 0.6 collective-permute-start.11
  115.9 3.7 %collective-permute-start.19 = (f32[2,24,192]{2,1,0:T(8,128)S(1)}, f32[2,24,192]{2,1,0:T(8,128)S(1)}, u32[]{:S(2)}, u32[]{:S(2)}) collective-permute-start(f32[2,24,192]{2,1,0:T(8,128)S(1)} %get-tuple-element.49), channel_id=1, source_target_pairs={{0,6},{1,7},{2,0},{3,1},{4,2},{5,3},{6,4},{7,5},{8,14},{9,15},{10,... | collective-permute-start | bytes 110600 | tf_op jit(solution)/shard_map/ppermute | solution.py:173
  119.6 0.7 collective-permute-start.17
  120.3 3.2 %collective-permute-start.14 = (f32[2,24,192]{2,1,0:T(8,128)S(1)}, f32[2,24,192]{2,1,0:T(8,128)S(1)}, u32[]{:S(2)}, u32[]{:S(2)}) collective-permute-start(f32[2,24,192]{2,1,0:T(8,128)S(1)} %get-tuple-element.46), channel_id=1, source_target_pairs={{0,6},{1,7},{2,0},{3,1},{4,2},{5,3},{6,4},{7,5},{8,14},{9,15},{10,... | collective-permute-start | bytes 110600 | tf_op jit(solution)/shard_map/ppermute | solution.py:173
  123.6 1.1 collective-permute-start.13
  124.7 0.0 collective-permute-start.12
  124.7 1.4 %collective-permute-done.18 = f32[2,24,192]{2,1,0:T(8,128)S(1)} collective-permute-done((f32[2,24,192]{2,1,0:T(8,128)S(1)}, f32[2,24,192]{2,1,0:T(8,128)S(1)}, u32[]{:S(2)}, u32[]{:S(2)}) %collective-permute-start.18) | collective-permute-done | bytes 36896 | tf_op jit(solution)/shard_map/ppermute | solution.py:173
  126.1 2.9 %collective-permute-done.13 = f32[2,24,192]{2,1,0:T(8,128)S(1)} collective-permute-done((f32[2,24,192]{2,1,0:T(8,128)S(1)}, f32[2,24,192]{2,1,0:T(8,128)S(1)}, u32[]{:S(2)}, u32[]{:S(2)}) %collective-permute-start.13) | collective-permute-done | bytes 36896 | tf_op jit(solution)/shard_map/ppermute | solution.py:173
  129.1 1.5 %collective-permute-done.12 = f32[2,24,192]{2,1,0:T(8,128)S(1)} collective-permute-done((f32[2,24,192]{2,1,0:T(8,128)S(1)}, f32[2,24,192]{2,1,0:T(8,128)S(1)}, u32[]{:S(2)}, u32[]{:S(2)}) %collective-permute-start.12) | collective-permute-done | bytes 36896 | tf_op jit(solution)/shard_map/ppermute | solution.py:173
  130.6 0.7 copy.38
  (41 shorter events, 0.2 us)
Async XLA Ops:
  0.8 3.0 %collective-permute-start = (s32[2,2,2]{1,2,0:T(2,128)S(1)}, s32[2,2,2]{1,2,0:T(2,128)S(1)}, u32[]{:S(2)}, u32[]{:S(2)}) collective-permute-start(s32[2,2,2]{1,2,0:T(2,128)S(1)} %copy.32), channel_id=1, source_target_pairs={{0,1},{1,0},{2,3},{3,2},{4,5},{5,4},{6,7},{7,6},{8,9},{9,8},{10,11... | collective-permute-start | bytes 104 | tf_op jit(solution)/shard_map/ppermute | solution.py:181
  3.8 3.6 %collective-permute-start.1 = (s32[2,4,2]{1,2,0:T(2,128)S(1)}, s32[2,4,2]{1,2,0:T(2,128)S(1)}, u32[]{:S(2)}, u32[]{:S(2)}) collective-permute-start(s32[2,4,2]{1,2,0:T(2,128)S(1)} %pad_add_fusion), channel_id=1, source_target_pairs={{0,2},{1,3},{2,0},{3,1},{4,6},{5,7},{6,4},{7,5},{8,10},{9,11},{10,... | collective-permute-start | bytes 200 | tf_op jit(solution)/shard_map/ppermute | solution.py:181
  7.5 4.9 %collective-permute-start.2 = (s32[2,8,2]{1,2,0:T(2,128)S(1)}, s32[2,8,2]{1,2,0:T(2,128)S(1)}, u32[]{:S(2)}, u32[]{:S(2)}) collective-permute-start(s32[2,8,2]{1,2,0:T(2,128)S(1)} %pad_add_fusion.1), channel_id=1, source_target_pairs={{0,4},{1,5},{2,6},{3,7},{4,0},{5,1},{6,2},{7,3},{8,12},{9,13},{10,... | collective-permute-start | bytes 392 | tf_op jit(solution)/shard_map/ppermute | solution.py:181
  10.8 3.7 %copy-start.7 = (s32[2,2]{1,0:T(2,128)S(1)}, s32[2,2]{1,0:T(2,128)}, u32[]{:S(2)}) copy-start(s32[2,2]{1,0:T(2,128)} %param.8) | copy-start | bytes 52
  10.8 54.5 %copy-start.5 = (bf16[2,192]{1,0:T(2,128)(2,1)S(1)}, bf16[2,192]{1,0:T(2,128)(2,1)}, u32[]{:S(2)}) copy-start(bf16[2,192]{1,0:T(2,128)(2,1)} %param.7) | copy-start | bytes 2308
  12.5 14.1 %collective-permute-start.3 = (bf16[392,768]{1,0:T(8,128)(2,1)S(1)}, bf16[392,768]{1,0:T(8,128)(2,1)S(1)}, u32[]{:S(2)}, u32[]{:S(2)}) collective-permute-start(bf16[392,768]{1,0:T(8,128)(2,1)S(1)} %get-tuple-element.27), channel_id=1, source_target_pairs={{0,8},{1,9},{2,10},{3,11},{4,12},{5,13},{6,14},{7,15},{8,16},{9,17... | collective-permute-start | bytes 1806344 | tf_op jit(solution)/shard_map/ppermute | solution.py:207
  14.0 13.8 %collective-permute-start.4 = (bf16[392,768]{1,0:T(8,128)(2,1)S(1)}, bf16[392,768]{1,0:T(8,128)(2,1)S(1)}, u32[]{:S(2)}, u32[]{:S(2)}) collective-permute-start(bf16[392,768]{1,0:T(8,128)(2,1)S(1)} %get-tuple-element.27), channel_id=1, source_target_pairs={{0,24},{1,25},{2,26},{3,27},{4,28},{5,29},{6,30},{7,31},{8,0},{9,1... | collective-permute-start | bytes 1806344 | tf_op jit(solution)/shard_map/ppermute | solution.py:208
  14.5 50.8 %collective-permute-start.5 = (bf16[392,768]{1,0:T(8,128)(2,1)}, bf16[392,768]{1,0:T(8,128)(2,1)S(1)}, u32[]{:S(2)}, u32[]{:S(2)}) collective-permute-start(bf16[392,768]{1,0:T(8,128)(2,1)} %get-tuple-element.30), channel_id=1, source_target_pairs={{24,38},{25,39},{26,36},{27,37},{28,34},{29,35},{30,32},{31,33},{5... | collective-permute-start | bytes 1806344 | tf_op jit(solution)/shard_map/ppermute | solution.py:41
  15.2 50.1 %collective-permute-start.6 = (bf16[392,768]{1,0:T(8,128)(2,1)}, bf16[392,768]{1,0:T(8,128)(2,1)S(1)}, u32[]{:S(2)}, u32[]{:S(2)}) collective-permute-start(bf16[392,768]{1,0:T(8,128)(2,1)} %get-tuple-element.30), channel_id=1, source_target_pairs={{16,38},{17,39},{18,36},{19,37},{20,34},{21,35},{22,32},{23,33},{4... | collective-permute-start | bytes 1806344 | tf_op jit(solution)/shard_map/ppermute | solution.py:41
  27.8 6.3 %copy-start.6 = (bf16[392,768]{1,0:T(8,128)(2,1)}, bf16[392,768]{1,0:T(8,128)(2,1)S(1)}, u32[]{:S(2)}) copy-start(bf16[392,768]{1,0:T(8,128)(2,1)S(1)} %collective-permute-done.4) | copy-start | bytes 1806340
  27.8 37.5 %collective-permute-start.7 = (bf16[392,768]{1,0:T(8,128)(2,1)}, bf16[392,768]{1,0:T(8,128)(2,1)S(1)}, u32[]{:S(2)}, u32[]{:S(2)}) collective-permute-start(bf16[392,768]{1,0:T(8,128)(2,1)} %get-tuple-element.30), channel_id=1, source_target_pairs={{0,8},{1,9},{2,10},{3,11},{4,12},{5,13},{6,14},{7,15},{8,16},{9,17... | collective-permute-start | bytes 1806344 | tf_op jit(solution)/shard_map/ppermute | solution.py:41
  34.2 64.4 %collective-permute-start.10 = (bf16[392,768]{1,0:T(8,128)(2,1)S(1)}, bf16[392,768]{1,0:T(8,128)(2,1)}, u32[]{:S(2)}, u32[]{:S(2)}) collective-permute-start(bf16[392,768]{1,0:T(8,128)(2,1)S(1)} %collective-permute-done.3.refs_1_), channel_id=1, source_target_pairs={{0,38},{1,39},{2,36},{3,37},{4,34},{5,35},{6,32},{7,33},{32,70},{3... | collective-permute-start | bytes 1806344 | tf_op jit(solution)/shard_map/ppermute | solution.py:41
  35.8 68.1 %collective-permute-start.15 = (bf16[392,768]{1,0:T(8,128)(2,1)}, bf16[392,768]{1,0:T(8,128)(2,1)S(1)}, u32[]{:S(2)}, u32[]{:S(2)}) collective-permute-start(bf16[392,768]{1,0:T(8,128)(2,1)} %copy-done.6), channel_id=1, source_target_pairs={{0,24},{1,25},{2,26},{3,27},{4,28},{5,29},{6,30},{7,31},{8,38},{9,... | collective-permute-start | bytes 1806344 | tf_op jit(solution)/shard_map/ppermute | solution.py:41
  65.3 24.7 %copy-start.2 = (bf16[392,768]{1,0:T(8,128)(2,1)}, bf16[392,768]{1,0:T(8,128)(2,1)S(1)}, u32[]{:S(2)}) copy-start(bf16[392,768]{1,0:T(8,128)(2,1)S(1)} %collective-permute-done.6.refs_0_) | copy-start | bytes 1806340
  65.4 43.7 %collective-permute-start.8 = (bf16[392,768]{1,0:T(8,128)(2,1)}, bf16[392,768]{1,0:T(8,128)(2,1)}, u32[]{:S(2)}, u32[]{:S(2)}) collective-permute-start(bf16[392,768]{1,0:T(8,128)(2,1)} %get-tuple-element.30), channel_id=1, source_target_pairs={{24,46},{25,47},{26,44},{27,45},{28,42},{29,43},{30,40},{31,41},{5... | collective-permute-start | bytes 1806344 | tf_op jit(solution)/shard_map/ppermute | solution.py:41
  66.7 42.4 %collective-permute-start.9 = (bf16[392,768]{1,0:T(8,128)(2,1)}, bf16[392,768]{1,0:T(8,128)(2,1)}, u32[]{:S(2)}, u32[]{:S(2)}) collective-permute-start(bf16[392,768]{1,0:T(8,128)(2,1)} %get-tuple-element.30), channel_id=1, source_target_pairs={{0,16},{1,17},{2,18},{3,19},{4,20},{5,21},{6,22},{7,23},{8,24},{9,... | collective-permute-start | bytes 1806344 | tf_op jit(solution)/shard_map/ppermute | solution.py:41
  80.7 9.4 %copy-start.4 = (f32[8]{0:T(128)S(1)}, f32[8]{0:T(128)}, u32[]{:S(2)}) copy-start(f32[8]{0:T(128)} %occupied.7) | copy-start | bytes 100
  90.1 3.7 %copy-start = (bf16[2,8,2,192,768]{4,3,2,1,0:T(8,128)(2,1)S(1)}, bf16[2,8,2,192,768]{4,3,2,1,0:T(8,128)(2,1)}, u32[]{:S(2)}) copy-start(bf16[2,8,2,192,768]{4,3,2,1,0:T(8,128)(2,1)} %copy.33) | copy-start | bytes 28311556
  93.8 4.9 %copy-start.1 = (bf16[2,8,2,192,768]{4,3,2,1,0:T(8,128)(2,1)S(1)}, bf16[2,8,2,192,768]{4,3,2,1,0:T(8,128)(2,1)}, u32[]{:S(2)}) copy-start(bf16[2,8,2,192,768]{4,3,2,1,0:T(8,128)(2,1)} %copy.33) | copy-start | bytes 28311556
  103.9 5.2 %copy-start.3 = (bf16[392,768]{1,0:T(8,128)(2,1)S(1)}, bf16[392,768]{1,0:T(8,128)(2,1)}, u32[]{:S(2)}) copy-start(bf16[392,768]{1,0:T(8,128)(2,1)} %copy-done.2) | copy-start | bytes 1806340
  109.0 6.8 %collective-permute-start.16 = (f32[4,2,24,192]{3,2,1,0:T(8,128)S(1)}, f32[4,2,24,192]{3,2,1,0:T(8,128)S(1)}, u32[]{:S(2)}, u32[]{:S(2)}) collective-permute-start(f32[4,2,24,192]{3,2,1,0:T(8,128)S(1)} %get-tuple-element.42), channel_id=1, source_target_pairs={{0,1},{1,0},{2,3},{3,2},{4,5},{5,4},{6,7},{7,6},{8,9},{9,8},{10,11... | collective-permute-start | bytes 442376 | tf_op jit(solution)/shard_map/ppermute | solution.py:168
  114.6 5.7 %collective-permute-start.11 = (f32[4,2,24,192]{3,2,1,0:T(8,128)S(1)}, f32[4,2,24,192]{3,2,1,0:T(8,128)S(1)}, u32[]{:S(2)}, u32[]{:S(2)}) collective-permute-start(f32[4,2,24,192]{3,2,1,0:T(8,128)S(1)} %get-tuple-element.39), channel_id=1, source_target_pairs={{0,1},{1,0},{2,3},{3,2},{4,5},{5,4},{6,7},{7,6},{8,9},{9,8},{10,11... | collective-permute-start | bytes 442376 | tf_op jit(solution)/shard_map/ppermute | solution.py:168
  115.9 8.8 %collective-permute-start.19 = (f32[2,24,192]{2,1,0:T(8,128)S(1)}, f32[2,24,192]{2,1,0:T(8,128)S(1)}, u32[]{:S(2)}, u32[]{:S(2)}) collective-permute-start(f32[2,24,192]{2,1,0:T(8,128)S(1)} %get-tuple-element.49), channel_id=1, source_target_pairs={{0,6},{1,7},{2,0},{3,1},{4,2},{5,3},{6,4},{7,5},{8,14},{9,15},{10,... | collective-permute-start | bytes 110600 | tf_op jit(solution)/shard_map/ppermute | solution.py:173
  119.6 6.5 %collective-permute-start.18 = (f32[2,24,192]{2,1,0:T(8,128)S(1)}, f32[2,24,192]{2,1,0:T(8,128)S(1)}, u32[]{:S(2)}, u32[]{:S(2)}) collective-permute-start(f32[2,24,192]{2,1,0:T(8,128)S(1)} %get-tuple-element.50), channel_id=1, source_target_pairs={{0,4},{1,5},{2,6},{3,7},{4,0},{5,1},{6,2},{7,3},{8,12},{9,13},{10,... | collective-permute-start | bytes 110600 | tf_op jit(solution)/shard_map/ppermute | solution.py:173
  119.6 6.5 %collective-permute-start.17 = (f32[2,24,192]{2,1,0:T(8,128)S(1)}, f32[2,24,192]{2,1,0:T(8,128)S(1)}, u32[]{:S(2)}, u32[]{:S(2)}) collective-permute-start(f32[2,24,192]{2,1,0:T(8,128)S(1)} %get-tuple-element.48), channel_id=1, source_target_pairs={{0,2},{1,3},{2,4},{3,5},{4,6},{5,7},{6,0},{7,1},{8,10},{9,11},{10,... | collective-permute-start | bytes 110600 | tf_op jit(solution)/shard_map/ppermute | solution.py:173
  120.3 5.8 %collective-permute-start.14 = (f32[2,24,192]{2,1,0:T(8,128)S(1)}, f32[2,24,192]{2,1,0:T(8,128)S(1)}, u32[]{:S(2)}, u32[]{:S(2)}) collective-permute-start(f32[2,24,192]{2,1,0:T(8,128)S(1)} %get-tuple-element.46), channel_id=1, source_target_pairs={{0,6},{1,7},{2,0},{3,1},{4,2},{5,3},{6,4},{7,5},{8,14},{9,15},{10,... | collective-permute-start | bytes 110600 | tf_op jit(solution)/shard_map/ppermute | solution.py:173
  123.6 5.5 %collective-permute-start.13 = (f32[2,24,192]{2,1,0:T(8,128)S(1)}, f32[2,24,192]{2,1,0:T(8,128)S(1)}, u32[]{:S(2)}, u32[]{:S(2)}) collective-permute-start(f32[2,24,192]{2,1,0:T(8,128)S(1)} %get-tuple-element.47), channel_id=1, source_target_pairs={{0,4},{1,5},{2,6},{3,7},{4,0},{5,1},{6,2},{7,3},{8,12},{9,13},{10,... | collective-permute-start | bytes 110600 | tf_op jit(solution)/shard_map/ppermute | solution.py:173
  124.7 5.9 %collective-permute-start.12 = (f32[2,24,192]{2,1,0:T(8,128)S(1)}, f32[2,24,192]{2,1,0:T(8,128)S(1)}, u32[]{:S(2)}, u32[]{:S(2)}) collective-permute-start(f32[2,24,192]{2,1,0:T(8,128)S(1)} %get-tuple-element.45), channel_id=1, source_target_pairs={{0,2},{1,3},{2,4},{3,5},{4,6},{5,7},{6,0},{7,1},{8,10},{9,11},{10,... | collective-permute-start | bytes 110600 | tf_op jit(solution)/shard_map/ppermute | solution.py:173

commit v4 on v3

--- a/solution.py
+++ b/solution.py
@@ -174,14 +174,12 @@
     return total
 
 
-def all_pairs_of(pair_lists):
-    gathered = pair_lists
-    reach = 1
-    while reach < LINE * CORES:
-        other = lax.ppermute(gathered, "occ", [(i, i ^ reach) for i in range(LINE * CORES)])
-        gathered = jnp.concatenate([gathered, other], axis=1)
-        reach *= 2
-    return gathered
+def line_pairs_of(pair_lists):
+    parts = [pair_lists]
+    for reach in range(1, LINE):
+        swap = [(i, i ^ (CORES * reach)) for i in range(LINE * CORES)]
+        parts.append(lax.ppermute(pair_lists, "occ", swap))
+    return jnp.concatenate(parts, axis=1)
 
 
 def local(factors, occupied_energy, virtual_energy, conserve, pair_lists):
@@ -198,16 +196,20 @@
         head = jnp.pad(energy, ((0, HEAD - 1), (0, auxiliary - share)))
         return jnp.concatenate([cut, head], axis=0)
 
-    pairs = all_pairs_of(pair_lists)
+    line_pairs = line_pairs_of(pair_lists)
     straight = outgoing(0)
     relayed = outgoing(1)
-    straight, relayed, pairs, factors = lax.optimization_barrier((straight, relayed, pairs, factors))
+    straight, relayed, line_pairs, factors = lax.optimization_barrier((straight, relayed, line_pairs, factors))
     cross_one = moved(straight, (3,), 1)
     cross_two = moved(straight, (2,), 2)
     hop_plus = lax.ppermute(relayed, ("ka", "occ"), ring_route(1))
     hop_minus = lax.ppermute(relayed, ("ka", "occ"), ring_route(-1))
     left = jnp.transpose(factors, (0, 1, 3, 2, 4)).reshape(momenta, orbitals, 2 * virtuals, auxiliary)
-    straight, hop_plus, hop_minus = lax.optimization_barrier((straight, hop_plus, hop_minus))
+    other_pairs = lax.ppermute(line_pairs, "occ", [(i, i ^ 1) for i in range(LINE * CORES)])
+    pairs = jnp.concatenate([line_pairs, other_pairs], axis=1)
+    straight, hop_plus, hop_minus, left, pairs = lax.optimization_barrier(
+        (straight, hop_plus, hop_minus, left, pairs)
+    )
     up = moved(hop_plus, (0,), 0)
     back = moved(hop_minus, range(COLUMNS), -1)
     near_one = moved(straight, (0, 1, 2), 1)

time: 132 us -> 121 us (0.917)
  waiting for transfers between devices: 20.1 us -> 9.57 us
  starting transfers between devices: 67.4 us -> 65.4 us
    ppermute x1, waiting for transfers between devices: 10.7 us -> 1.83 us  [local(): hop_plus = lax.ppermute(relayed, ('ka', 'occ'), ring_route(1))]
    ppermute x7, starting transfers between devices: 50.7 us -> 47.8 us  [moved(): return lax.ppermute(array, ('ka', 'occ'), route(columns, by))]
    ppermute x3 -> x4, waiting for transfers between devices: 2.29 us -> 0.01 us  [the longest x3 0.01 us: line_pairs_of(): parts.append(lax.ppermute(pair_lists, 'occ', swap))]
    ppermute x6, starting transfers between devices: 8.76 us -> 10.2 us  [summed(): total = total + lax.ppermute(part, 'occ', ring)]
    unnamed x17 -> x15, local copies, waits for them, and re-layouts: 4.48 us -> 5.29 us
    ppermute x3 -> x4, starting transfers between devices: 5.24 us -> 5.31 us  [the longest x3 5.21 us: line_pairs_of(): parts.append(lax.ppermute(pair_lists, 'occ', swap))]
  transfers between devices with their start and end apart: 20 -> 21, of which waited for: 7 -> 6; matrix products, arithmetic and copies ran while one was open for 11% -> 12% of each run, Pallas kernels for 16% -> 17%
where the time goes in v4:
time: 121 us; the launch traced here: 120 us
  starting transfers between devices  65.4 us (54%)
  Pallas kernels  20.6 us (17%)
  local copies, waits for them, and re-layouts  19.2 us (16%)
  waiting for transfers between devices  9.57 us (8%)
  between operations  3.44 us (3%)
  other arithmetic  1.46 us (1%)
    ppermute x7, starting transfers between devices, moved(): return lax.ppermute(array, ('ka', 'occ'), route(columns, by))  47.8 us
    pallas_call x4, Pallas kernels, piece_density(): pl.pallas_call(functools.partial(piece_kernel, len(mates), bool(before)),...  20.6 us
    ppermute x6, starting transfers between devices, summed(): total = total + lax.ppermute(part, 'occ', ring)  10.2 us
    transpose x1, local copies, waits for them, and re-layouts, local(): jnp.transpose(factors, (0, 1, 3, 2, 4))  9.3 us
    ppermute x6, waiting for transfers between devices, summed(): total = total + lax.ppermute(part, 'occ', ring)  5.86 us
    unnamed x15, local copies, waits for them, and re-layouts  5.29 us
    ppermute x3, starting transfers between devices, line_pairs_of(): parts.append(lax.ppermute(pair_lists, 'occ', swap))  5.21 us
  transfers between devices with their start and end apart: 21, of which 6 were waited for; matrix products, arithmetic and copies ran while one was open for 12% of the time, Pallas kernels for 17%

profile of v4, /device:TPU:10, one launch (start us, length us, event | category | flops | bytes accessed | tf_op | source)
XLA Modules:
  0.0 119.7 jit_solution(7647591860624801198)
XLA Ops:
  0.0 0.8 copy.32
  0.8 4.6 %collective-permute-start.2 = (s32[2,2,2]{1,2,0:T(2,128)S(1)}, s32[2,2,2]{1,2,0:T(2,128)S(1)}, u32[]{:S(2)}, u32[]{:S(2)}) collective-permute-start(s32[2,2,2]{1,2,0:T(2,128)S(1)} %copy.32), channel_id=1, source_target_pairs={{0,6},{1,7},{2,4},{3,5},{4,2},{5,3},{6,0},{7,1},{8,14},{9,15},{10,... | collective-permute-start | bytes 104 | tf_op jit(solution)/shard_map/ppermute | solution.py:181
  5.4 0.6 collective-permute-start
  6.0 0.8 constant_dynamic-slice_fusion.3
  6.8 2.1 %constant_dynamic-slice_fusion = (bf16[1,8,24,2,768]{4,3,2,1,0:T(2,128)(2,1)S(1)}, bf16[1,8,24,2,768]{4,3,2,1,0:T(2,128)(2,1)S(1)}) fusion(bf16[2,8,192,2,768]{4,3,2,1,0:T(2,128)(2,1)} %param.5, s32[]{:T(128)S(6)} %select_n.73), kind=kLoop, calls=%fused_computation.22 | loop fusion | bytes 2359300 | tf_op jit(solution)/shard_map/dynamic_slice | solution.py:191
  8.9 0.1 copy.41
  8.9 0.1 copy.42
  9.0 0.9 fusion.2
  9.9 0.1 pad_add_fusion
  10.0 1.5 %collective-permute-start.3 = (bf16[392,768]{1,0:T(8,128)(2,1)S(1)}, bf16[392,768]{1,0:T(8,128)(2,1)S(1)}, u32[]{:S(2)}, u32[]{:S(2)}) collective-permute-start(bf16[392,768]{1,0:T(8,128)(2,1)S(1)} %get-tuple-element.27), channel_id=1, source_target_pairs={{0,8},{1,9},{2,10},{3,11},{4,12},{5,13},{6,14},{7,15},{8,16},{9,17... | collective-permute-start | bytes 1806344 | tf_op jit(solution)/shard_map/ppermute | solution.py:205
  11.5 0.5 collective-permute-start.4
  12.1 0.7 collective-permute-start.6
  12.8 0.7 collective-permute-start.7
  13.5 0.1 collective-permute-start.5
  13.6 0.0 copy-start.5
  13.6 9.3 %copy.33 = bf16[2,8,2,192,768]{4,3,2,1,0:T(8,128)(2,1)} copy(bf16[2,8,2,192,768]{4,2,3,1,0:T(2,128)(2,1)} %bitcast.68) | data formatting | bytes 18874368 | tf_op jit(solution)/shard_map/transpose | solution.py:207
  22.9 0.1 pad_add_fusion.1
  23.0 1.8 %collective-permute-done.3.refs_1_ = bf16[392,768]{1,0:T(8,128)(2,1)S(1)} collective-permute-done((bf16[392,768]{1,0:T(8,128)(2,1)S(1)}, bf16[392,768]{1,0:T(8,128)(2,1)S(1)}, u32[]{:S(2)}, u32[]{:S(2)}) %collective-permute-start.3) | collective-permute-done | bytes 602144 | tf_op jit(solution)/shard_map/ppermute | solution.py:205
  24.8 1.3 %collective-permute-done.4 = bf16[392,768]{1,0:T(8,128)(2,1)} collective-permute-done((bf16[392,768]{1,0:T(8,128)(2,1)S(1)}, bf16[392,768]{1,0:T(8,128)(2,1)}, u32[]{:S(2)}, u32[]{:S(2)}) %collective-permute-start.4) | collective-permute-done | bytes 602144 | tf_op jit(solution)/shard_map/ppermute | solution.py:206
  26.1 8.2 %collective-permute-start.8 = (bf16[392,768]{1,0:T(8,128)(2,1)}, bf16[392,768]{1,0:T(8,128)(2,1)S(1)}, u32[]{:S(2)}, u32[]{:S(2)}) collective-permute-start(bf16[392,768]{1,0:T(8,128)(2,1)} %get-tuple-element.34), channel_id=1, source_target_pairs={{0,8},{1,9},{2,10},{3,11},{4,12},{5,13},{6,14},{7,15},{8,16},{9,17... | collective-permute-start | bytes 1806344 | tf_op jit(solution)/shard_map/ppermute | solution.py:41
  34.4 0.1 and_select_fusion
  34.5 0.7 fusion.12
  37.6 0.1 pad_add_fusion.4.flags
  37.6 1.5 %collective-permute-start.11 = (bf16[392,768]{1,0:T(8,128)(2,1)S(1)}, bf16[392,768]{1,0:T(8,128)(2,1)}, u32[]{:S(2)}, u32[]{:S(2)}) collective-permute-start(bf16[392,768]{1,0:T(8,128)(2,1)S(1)} %collective-permute-done.3.refs_1_), channel_id=1, source_target_pairs={{0,38},{1,39},{2,36},{3,37},{4,34},{5,35},{6,32},{7,33},{32,70},{3... | collective-permute-start | bytes 1806344 | tf_op jit(solution)/shard_map/ppermute | solution.py:41
  39.1 0.1 pad_add_fusion.3.flags
  39.2 23.9 %collective-permute-start.16 = (bf16[392,768]{1,0:T(8,128)(2,1)}, bf16[392,768]{1,0:T(8,128)(2,1)S(1)}, u32[]{:S(2)}, u32[]{:S(2)}) collective-permute-start(bf16[392,768]{1,0:T(8,128)(2,1)} %collective-permute-done.4), channel_id=1, source_target_pairs={{0,24},{1,25},{2,26},{3,27},{4,28},{5,29},{6,30},{7,31},{8,38},{9,... | collective-permute-start | bytes 1806344 | tf_op jit(solution)/shard_map/ppermute | solution.py:41
  63.1 0.1 pad_add_fusion.2.flags
  63.2 0.8 copy-done.2
  64.0 1.3 %collective-permute-start.9 = (bf16[392,768]{1,0:T(8,128)(2,1)}, bf16[392,768]{1,0:T(8,128)(2,1)}, u32[]{:S(2)}, u32[]{:S(2)}) collective-permute-start(bf16[392,768]{1,0:T(8,128)(2,1)} %get-tuple-element.34), channel_id=1, source_target_pairs={{24,46},{25,47},{26,44},{27,45},{28,42},{29,43},{30,40},{31,41},{5... | collective-permute-start | bytes 1806344 | tf_op jit(solution)/shard_map/ppermute | solution.py:41
  65.3 11.4 %collective-permute-start.10 = (bf16[392,768]{1,0:T(8,128)(2,1)}, bf16[392,768]{1,0:T(8,128)(2,1)}, u32[]{:S(2)}, u32[]{:S(2)}) collective-permute-start(bf16[392,768]{1,0:T(8,128)(2,1)} %get-tuple-element.34), channel_id=1, source_target_pairs={{0,16},{1,17},{2,18},{3,19},{4,20},{5,21},{6,22},{7,23},{8,24},{9,... | collective-permute-start | bytes 1806344 | tf_op jit(solution)/shard_map/ppermute | solution.py:41
  76.8 0.1 copy.36.pairs
  76.9 0.1 copy.34.pairs
  76.9 3.7 %copy-done = bf16[2,8,2,192,768]{4,3,2,1,0:T(8,128)(2,1)S(1)} copy-done((bf16[2,8,2,192,768]{4,3,2,1,0:T(8,128)(2,1)S(1)}, bf16[2,8,2,192,768]{4,3,2,1,0:T(8,128)(2,1)}, u32[]{:S(2)}) %copy-start) | copy-done | bytes 9437208
  80.6 4.8 %shard_map.55 = (f32[4,2,24,192]{3,2,1,0:T(8,128)S(1)}, f32[4,2,24,192]{3,2,1,0:T(8,128)S(1)}) custom-call(s32[1]{0:T(128)} %bitcast.15.chosen, s32[16,2]{1,0:T(8,128)S(1)} %copy.34.pairs, s32[3]{0:T(128)S(1)} %pad_add_fusion.3.flags, f32[8]{0:T(128)S(1)} %copy-done.4, bf16[2,8,384,768]{3,2,1,0:T(8,128)(2,1)S(1)} %bitcast.64, ...), custom_call_target="tpu_custom_call" | custom-call | flops 1925185536 | bytes 5308416 | tf_op jit(solution)/shard_map/pallas_call | solution.py:143
  85.5 5.4 %shard_map.56 = (f32[4,2,24,192]{3,2,1,0:T(8,128)S(1)}, f32[4,2,24,192]{3,2,1,0:T(8,128)S(1)}) custom-call(s32[1]{0:T(128)} %bitcast.18.chosen, s32[16,2]{1,0:T(8,128)S(1)} %copy.34.pairs, s32[3]{0:T(128)S(1)} %pad_add_fusion.3.flags, f32[8]{0:T(128)S(1)} %copy-done.4, bf16[2,8,384,768]{3,2,1,0:T(8,128)(2,1)S(1)} %bitcast.65, ...), custom_call_target="tpu_custom_call" | custom-call | flops 1925185536 | bytes 5308416 | tf_op jit(solution)/shard_map/pallas_call | solution.py:143
  90.9 4.9 %shard_map.58 = (f32[4,2,24,192]{3,2,1,0:T(8,128)S(1)}, f32[4,2,24,192]{3,2,1,0:T(8,128)S(1)}) custom-call(s32[1]{0:T(128)} %bitcast.24.chosen, s32[16,2]{1,0:T(8,128)S(1)} %copy.36.pairs, s32[3]{0:T(128)S(1)} %pad_add_fusion.4.flags, f32[8]{0:T(128)S(1)} %copy-done.4, bf16[2,8,384,768]{3,2,1,0:T(8,128)(2,1)S(1)} %bitcast.66, ...), custom_call_target="tpu_custom_call" | custom-call | flops 1925185536 | bytes 5308416 | tf_op jit(solution)/shard_map/pallas_call | solution.py:143
  95.8 0.1 collective-permute-start.17
  95.9 0.5 collective-permute-done.9.refs_1_
  96.5 5.4 %shard_map.57 = (f32[4,2,24,192]{3,2,1,0:T(8,128)S(1)}, f32[4,2,24,192]{3,2,1,0:T(8,128)S(1)}) custom-call(s32[1]{0:T(128)} %bitcast.2.chosen, s32[16,2]{1,0:T(8,128)S(1)} %copy.36.pairs, s32[3]{0:T(128)S(1)} %pad_add_fusion.2.flags, f32[8]{0:T(128)S(1)} %copy-done.4, bf16[2,8,384,768]{3,2,1,0:T(8,128)(2,1)S(1)} %bitcast.67, ...), custom_call_target="tpu_custom_call" | custom-call | flops 1925185536 | bytes 5308416 | tf_op jit(solution)/shard_map/pallas_call | solution.py:143
  101.9 0.1 collective-permute-start.12
  102.8 5.1 %collective-permute-start.20 = (f32[2,24,192]{2,1,0:T(8,128)S(1)}, f32[2,24,192]{2,1,0:T(8,128)S(1)}, u32[]{:S(2)}, u32[]{:S(2)}) collective-permute-start(f32[2,24,192]{2,1,0:T(8,128)S(1)} %get-tuple-element.53), channel_id=1, source_target_pairs={{0,6},{1,7},{2,0},{3,1},{4,2},{5,3},{6,4},{7,5},{8,14},{9,15},{10,... | collective-permute-start | bytes 110600 | tf_op jit(solution)/shard_map/ppermute | solution.py:173
  107.9 0.8 collective-permute-start.18
  108.8 3.1 %collective-permute-start.15 = (f32[2,24,192]{2,1,0:T(8,128)S(1)}, f32[2,24,192]{2,1,0:T(8,128)S(1)}, u32[]{:S(2)}, u32[]{:S(2)}) collective-permute-start(f32[2,24,192]{2,1,0:T(8,128)S(1)} %get-tuple-element.50), channel_id=1, source_target_pairs={{0,6},{1,7},{2,0},{3,1},{4,2},{5,3},{6,4},{7,5},{8,14},{9,15},{10,... | collective-permute-start | bytes 110600 | tf_op jit(solution)/shard_map/ppermute | solution.py:173
  111.9 1.1 collective-permute-start.14
  113.0 1.4 %collective-permute-done.19 = f32[2,24,192]{2,1,0:T(8,128)S(1)} collective-permute-done((f32[2,24,192]{2,1,0:T(8,128)S(1)}, f32[2,24,192]{2,1,0:T(8,128)S(1)}, u32[]{:S(2)}, u32[]{:S(2)}) %collective-permute-start.19) | collective-permute-done | bytes 36896 | tf_op jit(solution)/shard_map/ppermute | solution.py:173
  114.5 2.9 %collective-permute-done.14 = f32[2,24,192]{2,1,0:T(8,128)S(1)} collective-permute-done((f32[2,24,192]{2,1,0:T(8,128)S(1)}, f32[2,24,192]{2,1,0:T(8,128)S(1)}, u32[]{:S(2)}, u32[]{:S(2)}) %collective-permute-start.14) | collective-permute-done | bytes 36896 | tf_op jit(solution)/shard_map/ppermute | solution.py:173
  117.4 1.5 %collective-permute-done.13 = f32[2,24,192]{2,1,0:T(8,128)S(1)} collective-permute-done((f32[2,24,192]{2,1,0:T(8,128)S(1)}, f32[2,24,192]{2,1,0:T(8,128)S(1)}, u32[]{:S(2)}, u32[]{:S(2)}) %collective-permute-start.13) | collective-permute-done | bytes 36896 | tf_op jit(solution)/shard_map/ppermute | solution.py:173
  119.0 0.7 copy.38
  (40 shorter events, 0.2 us)
Async XLA Ops:
  0.8 9.2 %collective-permute-start.2 = (s32[2,2,2]{1,2,0:T(2,128)S(1)}, s32[2,2,2]{1,2,0:T(2,128)S(1)}, u32[]{:S(2)}, u32[]{:S(2)}) collective-permute-start(s32[2,2,2]{1,2,0:T(2,128)S(1)} %copy.32), channel_id=1, source_target_pairs={{0,6},{1,7},{2,4},{3,5},{4,2},{5,3},{6,0},{7,1},{8,14},{9,15},{10,... | collective-permute-start | bytes 104 | tf_op jit(solution)/shard_map/ppermute | solution.py:181
  5.4 4.5 %collective-permute-start.1 = (s32[2,2,2]{1,2,0:T(2,128)S(1)}, s32[2,2,2]{1,2,0:T(2,128)S(1)}, u32[]{:S(2)}, u32[]{:S(2)}) collective-permute-start(s32[2,2,2]{1,2,0:T(2,128)S(1)} %copy.32), channel_id=1, source_target_pairs={{0,4},{1,5},{2,6},{3,7},{4,0},{5,1},{6,2},{7,3},{8,12},{9,13},{10,... | collective-permute-start | bytes 104 | tf_op jit(solution)/shard_map/ppermute | solution.py:181
  5.4 4.5 %collective-permute-start = (s32[2,2,2]{1,2,0:T(2,128)S(1)}, s32[2,2,2]{1,2,0:T(2,128)S(1)}, u32[]{:S(2)}, u32[]{:S(2)}) collective-permute-start(s32[2,2,2]{1,2,0:T(2,128)S(1)} %copy.32), channel_id=1, source_target_pairs={{0,2},{1,3},{2,0},{3,1},{4,6},{5,7},{6,4},{7,5},{8,10},{9,11},{10,... | collective-permute-start | bytes 104 | tf_op jit(solution)/shard_map/ppermute | solution.py:181
  9.0 3.1 %copy-start.6 = (s32[2,2]{1,0:T(2,128)S(1)}, s32[2,2]{1,0:T(2,128)}, u32[]{:S(2)}) copy-start(s32[2,2]{1,0:T(2,128)} %param.8) | copy-start | bytes 52
  10.0 14.8 %collective-permute-start.3 = (bf16[392,768]{1,0:T(8,128)(2,1)S(1)}, bf16[392,768]{1,0:T(8,128)(2,1)S(1)}, u32[]{:S(2)}, u32[]{:S(2)}) collective-permute-start(bf16[392,768]{1,0:T(8,128)(2,1)S(1)} %get-tuple-element.27), channel_id=1, source_target_pairs={{0,8},{1,9},{2,10},{3,11},{4,12},{5,13},{6,14},{7,15},{8,16},{9,17... | collective-permute-start | bytes 1806344 | tf_op jit(solution)/shard_map/ppermute | solution.py:205
  11.5 14.6 %collective-permute-start.4 = (bf16[392,768]{1,0:T(8,128)(2,1)S(1)}, bf16[392,768]{1,0:T(8,128)(2,1)}, u32[]{:S(2)}, u32[]{:S(2)}) collective-permute-start(bf16[392,768]{1,0:T(8,128)(2,1)S(1)} %get-tuple-element.27), channel_id=1, source_target_pairs={{0,24},{1,25},{2,26},{3,27},{4,28},{5,29},{6,30},{7,31},{8,0},{9,1... | collective-permute-start | bytes 1806344 | tf_op jit(solution)/shard_map/ppermute | solution.py:206
  12.1 51.1 %collective-permute-start.6 = (bf16[392,768]{1,0:T(8,128)(2,1)}, bf16[392,768]{1,0:T(8,128)(2,1)S(1)}, u32[]{:S(2)}, u32[]{:S(2)}) collective-permute-start(bf16[392,768]{1,0:T(8,128)(2,1)} %get-tuple-element.34), channel_id=1, source_target_pairs={{24,38},{25,39},{26,36},{27,37},{28,34},{29,35},{30,32},{31,33},{5... | collective-permute-start | bytes 1806344 | tf_op jit(solution)/shard_map/ppermute | solution.py:41
  12.8 50.4 %collective-permute-start.7 = (bf16[392,768]{1,0:T(8,128)(2,1)}, bf16[392,768]{1,0:T(8,128)(2,1)S(1)}, u32[]{:S(2)}, u32[]{:S(2)}) collective-permute-start(bf16[392,768]{1,0:T(8,128)(2,1)} %get-tuple-element.34), channel_id=1, source_target_pairs={{16,38},{17,39},{18,36},{19,37},{20,34},{21,35},{22,32},{23,33},{4... | collective-permute-start | bytes 1806344 | tf_op jit(solution)/shard_map/ppermute | solution.py:41
  13.5 9.4 %collective-permute-start.5 = (s32[2,8,2]{1,2,0:T(2,128)S(1)}, s32[2,8,2]{1,2,0:T(2,128)S(1)}, u32[]{:S(2)}, u32[]{:S(2)}) collective-permute-start(s32[2,8,2]{1,2,0:T(2,128)S(1)} %pad_add_fusion), channel_id=1, source_target_pairs={{0,1},{1,0},{2,3},{3,2},{4,5},{5,4},{6,7},{7,6},{8,9},{9,8},{10,11... | collective-permute-start | bytes 392 | tf_op jit(solution)/shard_map/ppermute | solution.py:208
  13.6 49.6 %copy-start.5 = (bf16[2,192]{1,0:T(2,128)(2,1)S(1)}, bf16[2,192]{1,0:T(2,128)(2,1)}, u32[]{:S(2)}) copy-start(bf16[2,192]{1,0:T(2,128)(2,1)} %param.7) | copy-start | bytes 2308
  13.6 63.4 %copy-start.4 = (f32[8]{0:T(128)S(1)}, f32[8]{0:T(128)}, u32[]{:S(2)}) copy-start(f32[8]{0:T(128)} %occupied.7) | copy-start | bytes 100
  26.1 37.9 %collective-permute-start.8 = (bf16[392,768]{1,0:T(8,128)(2,1)}, bf16[392,768]{1,0:T(8,128)(2,1)S(1)}, u32[]{:S(2)}, u32[]{:S(2)}) collective-permute-start(bf16[392,768]{1,0:T(8,128)(2,1)} %get-tuple-element.34), channel_id=1, source_target_pairs={{0,8},{1,9},{2,10},{3,11},{4,12},{5,13},{6,14},{7,15},{8,16},{9,17... | collective-permute-start | bytes 1806344 | tf_op jit(solution)/shard_map/ppermute | solution.py:41
  37.6 47.9 %collective-permute-start.11 = (bf16[392,768]{1,0:T(8,128)(2,1)S(1)}, bf16[392,768]{1,0:T(8,128)(2,1)}, u32[]{:S(2)}, u32[]{:S(2)}) collective-permute-start(bf16[392,768]{1,0:T(8,128)(2,1)S(1)} %collective-permute-done.3.refs_1_), channel_id=1, source_target_pairs={{0,38},{1,39},{2,36},{3,37},{4,34},{5,35},{6,32},{7,33},{32,70},{3... | collective-permute-start | bytes 1806344 | tf_op jit(solution)/shard_map/ppermute | solution.py:41
  39.2 51.7 %collective-permute-start.16 = (bf16[392,768]{1,0:T(8,128)(2,1)}, bf16[392,768]{1,0:T(8,128)(2,1)S(1)}, u32[]{:S(2)}, u32[]{:S(2)}) collective-permute-start(bf16[392,768]{1,0:T(8,128)(2,1)} %collective-permute-done.4), channel_id=1, source_target_pairs={{0,24},{1,25},{2,26},{3,27},{4,28},{5,29},{6,30},{7,31},{8,38},{9,... | collective-permute-start | bytes 1806344 | tf_op jit(solution)/shard_map/ppermute | solution.py:41
  63.2 0.8 copy-start.2
  64.0 32.4 %collective-permute-start.9 = (bf16[392,768]{1,0:T(8,128)(2,1)}, bf16[392,768]{1,0:T(8,128)(2,1)}, u32[]{:S(2)}, u32[]{:S(2)}) collective-permute-start(bf16[392,768]{1,0:T(8,128)(2,1)} %get-tuple-element.34), channel_id=1, source_target_pairs={{24,46},{25,47},{26,44},{27,45},{28,42},{29,43},{30,40},{31,41},{5... | collective-permute-start | bytes 1806344 | tf_op jit(solution)/shard_map/ppermute | solution.py:41
  65.3 31.1 %collective-permute-start.10 = (bf16[392,768]{1,0:T(8,128)(2,1)}, bf16[392,768]{1,0:T(8,128)(2,1)}, u32[]{:S(2)}, u32[]{:S(2)}) collective-permute-start(bf16[392,768]{1,0:T(8,128)(2,1)} %get-tuple-element.34), channel_id=1, source_target_pairs={{0,16},{1,17},{2,18},{3,19},{4,20},{5,21},{6,22},{7,23},{8,24},{9,... | collective-permute-start | bytes 1806344 | tf_op jit(solution)/shard_map/ppermute | solution.py:41
  76.9 3.7 %copy-start = (bf16[2,8,2,192,768]{4,3,2,1,0:T(8,128)(2,1)S(1)}, bf16[2,8,2,192,768]{4,3,2,1,0:T(8,128)(2,1)}, u32[]{:S(2)}) copy-start(bf16[2,8,2,192,768]{4,3,2,1,0:T(8,128)(2,1)} %copy.33) | copy-start | bytes 28311556
  80.6 4.9 %copy-start.1 = (bf16[2,8,2,192,768]{4,3,2,1,0:T(8,128)(2,1)S(1)}, bf16[2,8,2,192,768]{4,3,2,1,0:T(8,128)(2,1)}, u32[]{:S(2)}) copy-start(bf16[2,8,2,192,768]{4,3,2,1,0:T(8,128)(2,1)} %copy.33) | copy-start | bytes 28311556
  90.9 5.6 %copy-start.3 = (bf16[392,768]{1,0:T(8,128)(2,1)S(1)}, bf16[392,768]{1,0:T(8,128)(2,1)}, u32[]{:S(2)}) copy-start(bf16[392,768]{1,0:T(8,128)(2,1)} %copy-done.2) | copy-start | bytes 1806340
  95.8 6.9 %collective-permute-start.17 = (f32[4,2,24,192]{3,2,1,0:T(8,128)S(1)}, f32[4,2,24,192]{3,2,1,0:T(8,128)S(1)}, u32[]{:S(2)}, u32[]{:S(2)}) collective-permute-start(f32[4,2,24,192]{3,2,1,0:T(8,128)S(1)} %get-tuple-element.46), channel_id=1, source_target_pairs={{0,1},{1,0},{2,3},{3,2},{4,5},{5,4},{6,7},{7,6},{8,9},{9,8},{10,11... | collective-permute-start | bytes 442376 | tf_op jit(solution)/shard_map/ppermute | solution.py:168
  101.9 6.8 %collective-permute-start.12 = (f32[4,2,24,192]{3,2,1,0:T(8,128)S(1)}, f32[4,2,24,192]{3,2,1,0:T(8,128)S(1)}, u32[]{:S(2)}, u32[]{:S(2)}) collective-permute-start(f32[4,2,24,192]{3,2,1,0:T(8,128)S(1)} %get-tuple-element.43), channel_id=1, source_target_pairs={{0,1},{1,0},{2,3},{3,2},{4,5},{5,4},{6,7},{7,6},{8,9},{9,8},{10,11... | collective-permute-start | bytes 442376 | tf_op jit(solution)/shard_map/ppermute | solution.py:168
  102.8 10.2 %collective-permute-start.20 = (f32[2,24,192]{2,1,0:T(8,128)S(1)}, f32[2,24,192]{2,1,0:T(8,128)S(1)}, u32[]{:S(2)}, u32[]{:S(2)}) collective-permute-start(f32[2,24,192]{2,1,0:T(8,128)S(1)} %get-tuple-element.53), channel_id=1, source_target_pairs={{0,6},{1,7},{2,0},{3,1},{4,2},{5,3},{6,4},{7,5},{8,14},{9,15},{10,... | collective-permute-start | bytes 110600 | tf_op jit(solution)/shard_map/ppermute | solution.py:173
  107.9 6.5 %collective-permute-start.19 = (f32[2,24,192]{2,1,0:T(8,128)S(1)}, f32[2,24,192]{2,1,0:T(8,128)S(1)}, u32[]{:S(2)}, u32[]{:S(2)}) collective-permute-start(f32[2,24,192]{2,1,0:T(8,128)S(1)} %get-tuple-element.54), channel_id=1, source_target_pairs={{0,4},{1,5},{2,6},{3,7},{4,0},{5,1},{6,2},{7,3},{8,12},{9,13},{10,... | collective-permute-start | bytes 110600 | tf_op jit(solution)/shard_map/ppermute | solution.py:173
  107.9 6.5 %collective-permute-start.18 = (f32[2,24,192]{2,1,0:T(8,128)S(1)}, f32[2,24,192]{2,1,0:T(8,128)S(1)}, u32[]{:S(2)}, u32[]{:S(2)}) collective-permute-start(f32[2,24,192]{2,1,0:T(8,128)S(1)} %get-tuple-element.52), channel_id=1, source_target_pairs={{0,2},{1,3},{2,4},{3,5},{4,6},{5,7},{6,0},{7,1},{8,10},{9,11},{10,... | collective-permute-start | bytes 110600 | tf_op jit(solution)/shard_map/ppermute | solution.py:173
  108.8 5.7 %collective-permute-start.15 = (f32[2,24,192]{2,1,0:T(8,128)S(1)}, f32[2,24,192]{2,1,0:T(8,128)S(1)}, u32[]{:S(2)}, u32[]{:S(2)}) collective-permute-start(f32[2,24,192]{2,1,0:T(8,128)S(1)} %get-tuple-element.50), channel_id=1, source_target_pairs={{0,6},{1,7},{2,0},{3,1},{4,2},{5,3},{6,4},{7,5},{8,14},{9,15},{10,... | collective-permute-start | bytes 110600 | tf_op jit(solution)/shard_map/ppermute | solution.py:173
  111.9 5.5 %collective-permute-start.14 = (f32[2,24,192]{2,1,0:T(8,128)S(1)}, f32[2,24,192]{2,1,0:T(8,128)S(1)}, u32[]{:S(2)}, u32[]{:S(2)}) collective-permute-start(f32[2,24,192]{2,1,0:T(8,128)S(1)} %get-tuple-element.51), channel_id=1, source_target_pairs={{0,4},{1,5},{2,6},{3,7},{4,0},{5,1},{6,2},{7,3},{8,12},{9,13},{10,... | collective-permute-start | bytes 110600 | tf_op jit(solution)/shard_map/ppermute | solution.py:173
  113.0 5.9 %collective-permute-start.13 = (f32[2,24,192]{2,1,0:T(8,128)S(1)}, f32[2,24,192]{2,1,0:T(8,128)S(1)}, u32[]{:S(2)}, u32[]{:S(2)}) collective-permute-start(f32[2,24,192]{2,1,0:T(8,128)S(1)} %get-tuple-element.49), channel_id=1, source_target_pairs={{0,2},{1,3},{2,4},{3,5},{4,6},{5,7},{6,0},{7,1},{8,10},{9,11},{10,... | collective-permute-start | bytes 110600 | tf_op jit(solution)/shard_map/ppermute | solution.py:173

commit v5 on v4

v5 whole, which is shorter than its diff:
```python
import functools

import jax
import jax.numpy as jnp
from jax import lax
from jax.experimental import pallas as pl
from jax.experimental.pallas import tpu as pltpu
from jax.sharding import PartitionSpec as P

ROWS, COLUMNS, LINE, CORES = 8, 4, 4, 2
HEAD = 8


def device_index(row, column, place, core):
    return ((row % ROWS) * COLUMNS + column) * LINE * CORES + place * CORES + core


def moved(array, moves):
    pairs = []
    for row in range(ROWS):
        for column, (goal, crosses) in moves.items():
            for place in range(LINE):
                for core in range(CORES):
                    source = device_index(row, column, place, core)
                    end = LINE - 1 - place if crosses else place
                    pairs.append((source, device_index(row + crosses, goal, end, core)))
    return lax.ppermute(array, ("ka", "occ"), pairs)


def piece_kernel(
    sources, before_count, kind, order, conserve, pairs, here, occupied, own_energy, left, *refs
):
    mates, refs = refs[:sources], refs[sources:]
    before, refs = refs[:before_count], refs[before_count:]
    outs, refs = refs[:-8], refs[-8:]
    piece, own, products, combined, rounded, turned, total, arrived = refs
    orbitals = products.shape[0]
    virtuals = products.shape[3]
    rows = products.shape[2]
    share = rows // (2 * orbitals)
    devices, _, each, _ = pairs.shape
    count = devices * each
    column = here[0]
    core = here[1]

    def by_column(values):
        result = jnp.int32(values[-1])
        for number in range(len(values) - 2, -1, -1):
            result = jnp.where(column == number, jnp.int32(values[number]), result)
        return result

    round_index = by_column(order[0])
    momentum = by_column(order[1])
    source = by_column(order[2])
    mine = lax.rem(conserve[0, round_index] + momentum, jnp.int32(2))

    def copy_of(orbital):
        return pltpu.make_async_copy(left.at[mine, orbital], own.at[orbital], arrived.at[orbital])

    for orbital in range(orbitals):
        copy_of(orbital).start()
    for number, mate in enumerate(mates):

        @pl.when(source == number)
        def _():
            piece[...] = mate[...]

    contract = (((1,), (1,)), ((), ()))
    for orbital in range(orbitals):
        copy_of(orbital).wait()
        for part in range(2):
            products[orbital, part] = lax.dot_general(
                piece[:rows],
                own[orbital, part * virtuals : (part + 1) * virtuals],
                contract,
                preferred_element_type=jnp.float32,
            )

    width = 2 * 128
    energy_row = piece[rows : rows + 1, :width].astype(jnp.float32)
    first_row = piece[rows + 1 : rows + 2, :width].astype(jnp.float32)
    lane = lax.broadcasted_iota(jnp.int32, (share, width), 1)
    row = lax.broadcasted_iota(jnp.int32, (share, width), 0)
    wanted = (lane - row).astype(jnp.float32) == jnp.broadcast_to(first_row, (share, width))
    spread = jnp.broadcast_to(energy_row, (share, width))
    energy_mate = jnp.sum(jnp.where(wanted, spread, 0.0), axis=1, keepdims=True)
    energy_sum = own_energy[mine] + energy_mate

    def exchange(lead, trail):
        top = pl.ds(pl.multiple_of(trail * share, 8), share)
        bottom = pl.ds(pl.multiple_of((orbitals + trail) * share, 8), share)
        real = products[lead, 0, top] + products[lead, 1, bottom]
        imaginary = products[lead, 1, top] - products[lead, 0, bottom]
        return real, imaginary

    def one_pair(holder, number):
        lead = pairs[holder, round_index, number, 0]
        trail = pairs[holder, round_index, number, 1]
        inverse = 1.0 / (energy_sum - (occupied[lead] + occupied[trail]))
        real, imaginary = exchange(lead, trail)
        swapped_real, swapped_imaginary = exchange(trail, lead)
        real, imaginary = real * inverse, imaginary * inverse
        return (
            2.0 * real - swapped_real * inverse,
            2.0 * imaginary - swapped_imaginary * inverse,
            real,
            imaginary,
        )

    def two_pairs(index, carry):
        low = one_pair(index, 0)
        high = one_pair(index, 1)
        c_re, c_im, a_re, a_im = (
            jnp.concatenate([x, y], axis=0).astype(jnp.bfloat16) for x, y in zip(low, high)
        )
        top = pl.ds(pl.multiple_of(index * 2 * share, 16), 2 * share)
        bottom = pl.ds(pl.multiple_of((count + index * 2) * share, 16), 2 * share)
        combined[top] = c_re
        combined[bottom] = c_im
        rounded[top] = a_re
        rounded[bottom] = a_im
        turned[top] = -a_im
        turned[bottom] = a_re
        return carry

    lax.fori_loop(0, devices, two_pairs, 0)
    contract_rows = (((0,), (0,)), ((), ()))
    for part, right in enumerate((rounded, turned)):
        total[part] = lax.dot_general(
            combined[...], right[...], contract_rows, preferred_element_type=jnp.float32
        )
    done = lax.rem(conserve[0, 1], jnp.int32(2))
    for place in range(LINE):
        for number, offset in enumerate((core, 1 - core)):
            cut = pl.ds(pl.multiple_of((place * CORES + offset) * share, 8), share)
            value = total[:, cut]
            if kind == "first":
                for local_index in range(2):
                    outs[number][local_index, place] = jnp.where(mine == local_index, value, 0.0)
            elif kind == "second":
                for local_index in range(2):
                    outs[number][local_index, place] = before[number][local_index, place] + jnp.where(
                        mine == local_index, value, 0.0
                    )
            elif kind == "third":
                for slot, which in enumerate((done, 1 - done)):
                    outs[2 * slot + number][place] = before[number][which, place] + jnp.where(
                        mine == which, value, 0.0
                    )
            else:
                outs[number][place] = before[number][place] + value


def piece_density(kind, order, conserve, pairs, here, occupied, own_energy, left, mates, before):
    momenta, orbitals, both, auxiliary = left.shape
    virtuals = both // 2
    share = virtuals // (LINE * CORES)
    count = pairs.shape[0] * pairs.shape[2]
    rows = 2 * orbitals * share
    whole_block = jax.ShapeDtypeStruct((momenta, LINE, 2, share, virtuals), jnp.float32)
    block = jax.ShapeDtypeStruct((LINE, 2, share, virtuals), jnp.float32)
    out_shape = {
        "first": (whole_block,) * 2,
        "second": (whole_block,) * 2,
        "third": (block,) * 4,
        "fourth": (block,) * 2,
    }[kind]
    scalars = pl.BlockSpec(memory_space=pltpu.SMEM)
    whole = pl.BlockSpec(memory_space=pltpu.VMEM)
    return pl.pallas_call(
        functools.partial(piece_kernel, len(mates), len(before), kind, order),
        out_shape=out_shape,
        in_specs=[scalars] * 4
        + [whole, pl.BlockSpec(memory_space=pl.ANY)]
        + [whole] * (len(mates) + len(before)),
        out_specs=(whole,) * len(out_shape),
        scratch_shapes=[
            pltpu.VMEM((rows + HEAD, auxiliary), jnp.bfloat16),
            pltpu.VMEM((orbitals, both, auxiliary), jnp.bfloat16),
            pltpu.VMEM((orbitals, 2, rows, virtuals), jnp.float32),
            pltpu.VMEM((2 * count * share, virtuals), jnp.bfloat16),
            pltpu.VMEM((2 * count * share, virtuals), jnp.bfloat16),
            pltpu.VMEM((2 * count * share, virtuals), jnp.bfloat16),
            pltpu.VMEM((2, virtuals, virtuals), jnp.float32),
            pltpu.SemaphoreType.DMA((orbitals,)),
        ],
        compiler_params=pltpu.CompilerParams(vmem_limit_bytes=40 << 20),
        cost_estimate=pl.CostEstimate(
            flops=4 * rows * virtuals * auxiliary * orbitals + 8 * count * share * virtuals * virtuals,
            bytes_accessed=orbitals * both * auxiliary * 2 + 2 * rows * auxiliary,
            transcendentals=0,
        ),
    )(conserve, pairs, here, occupied, own_energy, left, *mates, *before)


def summed(keep, send):
    place = lax.axis_index("occ") // CORES
    devices = LINE * CORES
    held = keep + lax.ppermute(send, "occ", [(i, i ^ 1) for i in range(devices)])
    total = lax.dynamic_index_in_dim(held, place, 0, keepdims=False)
    for hop in range(1, LINE):
        part = lax.dynamic_index_in_dim(held, (place + hop) % LINE, 0, keepdims=False)
        ring = [(i, (i + CORES * hop) % devices) for i in range(devices)]
        total = total + lax.ppermute(part, "occ", ring)
    return total


def with_partner(array, reach):
    other = lax.ppermute(array, "occ", [(i, i ^ reach) for i in range(LINE * CORES)])
    return jnp.concatenate([array, other], axis=0)


def local(factors, occupied_energy, virtual_energy, conserve, pair_lists):
    momenta, orbitals, virtuals, _, auxiliary = factors.shape
    share = virtuals // (LINE * CORES)
    start = lax.axis_index("occ") * share
    column = lax.axis_index("ka") % COLUMNS
    here = jnp.stack([column, lax.axis_index("occ") % CORES]).astype(jnp.int32)

    def outgoing(momentum):
        cut = lax.dynamic_slice(
            factors, (momentum, 0, start, 0, 0), (1, orbitals, share, 2, auxiliary)
        )
        cut = jnp.transpose(cut[0], (2, 0, 1, 3)).reshape(2 * orbitals * share, auxiliary)
        energy = jnp.pad(virtual_energy[momentum : momentum + 1], ((0, 0), (0, auxiliary - virtuals)))
        first = jnp.broadcast_to(start.astype(jnp.bfloat16), (HEAD - 1, auxiliary))
        return jnp.concatenate([cut, energy, first], axis=0)

    pairs = with_partner(with_partner(pair_lists[None], CORES), 2 * CORES)
    m0 = outgoing(0)
    m1 = outgoing(1)
    mixed = jnp.where(column == 3, m1, m0)
    m0, m1, mixed, pairs, factors, here = lax.optimization_barrier((m0, m1, mixed, pairs, factors, here))
    one = moved(m0, {0: (1, False), 1: (2, False), 2: (3, False), 3: (0, True)})
    two = moved(mixed, {2: (0, True), 3: (1, False)})
    three = moved(m1, {0: (1, False), 1: (2, False), 2: (3, False)})
    left = jnp.transpose(factors, (0, 1, 3, 2, 4)).reshape(momenta, orbitals, 2 * virtuals, auxiliary)
    pairs = with_partner(pairs, 1)
    own_energy = virtual_energy.astype(jnp.float32)[:, None, :]
    four_out = jnp.where(column == 0, one, m1)
    five_out = jnp.where(column == 1, two, m1)
    four_out, five_out, one, two, three, left, pairs, m0, own_energy = lax.optimization_barrier(
        (four_out, five_out, one, two, three, left, pairs, m0, own_energy)
    )
    four = moved(four_out, {3: (0, True), 0: (1, False), 1: (3, False)})
    five = moved(five_out, {2: (0, True), 1: (1, True), 0: (2, False)})
    six = moved(m0, {0: (2, False), 1: (3, False)})

    def density(kind, order, mates, before):
        return piece_density(
            kind, order, conserve, pairs, here, occupied_energy, own_energy, left, mates, before
        )

    total = density("first", ((0,), (0,), (0,)), (one,), ())
    total = density("second", ((1, 0), (0, 1), (0, 1)), (two, three), total)
    keep_a, send_a, keep_b, send_b = density(
        "third", ((0, 1), (1, 0), (0, 0, 1)), (four, six), total
    )
    keep_b, send_b = density("fourth", ((1,), (1,), (0, 0, 0, 1)), (five, four), (keep_b, send_b))
    done = summed(keep_a, send_a)
    last = summed(keep_b, send_b)
    result = jnp.where(conserve[0, 1] % 2 == 0, jnp.stack([done, last]), jnp.stack([last, done]))
    return jnp.transpose(result, (0, 2, 1, 3))


def solution(mesh):
    in_specs = (
        P("ka", None, None, None, None),
        P(),
        P("ka", None),
        P("ka", None),
        P(None, "occ", None),
    )
    out_specs = P("ka", "occ", None, None)
    return jax.shard_map(local, mesh=mesh, in_specs=in_specs, out_specs=out_specs, check_vma=False)
```

time: 121 us -> 128 us (1.058)
  the two profiles are of different devices: /device:TPU:10 before, /device:TPU:1 now
where the time goes in v5:
time: 128 us; the launch traced here: 127 us
  waiting for transfers between devices  44.7 us (35%)
  starting transfers between devices  33.2 us (26%)
  Pallas kernels  27 us (21%)
  local copies, waits for them, and re-layouts  17.6 us (14%)
  other arithmetic  2.53 us (2%)
  between operations  2.21 us (2%)
    ppermute x6, waiting for transfers between devices, moved(): return lax.ppermute(array, ('ka', 'occ'), pairs)  38.3 us
    pallas_call x4, Pallas kernels, piece_density(): pl.pallas_call(functools.partial(piece_kernel, len(mates), len(before), k...  27 us
    ppermute x6, starting transfers between devices, moved(): return lax.ppermute(array, ('ka', 'occ'), pairs)  17.7 us
    transpose x1, local copies, waits for them, and re-layouts, local(): jnp.transpose(factors, (0, 1, 3, 2, 4))  9.29 us
    ppermute x3, starting transfers between devices, with_partner(): lax.ppermute(array, 'occ', [(i, i ^ reach) for i in range(LINE * CORES)])  8.58 us
    ppermute x6, starting transfers between devices, summed(): total = total + lax.ppermute(part, 'occ', ring)  5.91 us
    ppermute x6, waiting for transfers between devices, summed(): total = total + lax.ppermute(part, 'occ', ring)  5.42 us
    unnamed x10, local copies, waits for them, and re-layouts  3.69 us
  transfers between devices with their start and end apart: 17, of which 6 were waited for; matrix products, arithmetic and copies ran while one was open for 12% of the time, Pallas kernels for 16%

profile of v5, /device:TPU:1, one launch (start us, length us, event | category | flops | bytes accessed | tf_op | source)
XLA Modules:
  0.0 127.3 jit_solution(2136522203468567944)
XLA Ops:
  0.0 2.5 %collective-permute-start = (s32[1,2,2,2]{3,2,1,0:T(2,128)}, s32[1,2,2,2]{3,2,1,0:T(2,128)S(1)}, u32[]{:S(2)}, u32[]{:S(2)}) collective-permute-start(s32[1,2,2,2]{3,2,1,0:T(2,128)} %bitcast.59), channel_id=1, source_target_pairs={{0,2},{1,3},{2,0},{3,1},{4,6},{5,7},{6,4},{7,5},{8,10},{9,11},{10,... | collective-permute-start | bytes 104 | tf_op jit(solution)/shard_map/ppermute | solution.py:209
  2.5 0.8 fusion.14
  3.2 2.1 %constant_dynamic-slice_fusion = (bf16[1,8,24,2,768]{4,3,2,1,0:T(2,128)(2,1)S(1)}, bf16[1,8,24,2,768]{4,3,2,1,0:T(2,128)(2,1)S(1)}) fusion(bf16[2,8,192,2,768]{4,3,2,1,0:T(2,128)(2,1)} %param.5, s32[]{:T(128)S(6)} %select_n.91), kind=kLoop, calls=%fused_computation.31 | loop fusion | bytes 2359300 | tf_op jit(solution)/shard_map/dynamic_slice | solution.py:221
  5.3 0.1 copy.28
  5.4 0.1 copy.27
  5.4 0.1 pad.27.clone
  5.5 1.1 broadcast_select_fusion.1
  6.7 3.1 %collective-permute-start.1 = (s32[2,2,2,2]{3,2,1,0:T(2,128)S(1)}, s32[2,2,2,2]{3,2,1,0:T(2,128)S(1)}, u32[]{:S(2)}, u32[]{:S(2)}) collective-permute-start(s32[2,2,2,2]{3,2,1,0:T(2,128)S(1)} %pad_add_fusion.1), channel_id=1, source_target_pairs={{0,4},{1,5},{2,6},{3,7},{4,0},{5,1},{6,2},{7,3},{8,12},{9,13},{10,... | collective-permute-start | bytes 200 | tf_op jit(solution)/shard_map/ppermute | solution.py:209
  9.7 0.1 pad_add_fusion.3.here
  9.8 0.9 collective-permute-done.1
  10.7 1.3 %collective-permute-start.3 = (bf16[392,768]{1,0:T(8,128)(2,1)S(1)}, bf16[392,768]{1,0:T(8,128)(2,1)S(1)}, u32[]{:S(2)}, u32[]{:S(2)}) collective-permute-start(bf16[392,768]{1,0:T(8,128)(2,1)S(1)} %get-tuple-element.32), channel_id=1, source_target_pairs={{16,38},{17,39},{18,36},{19,37},{20,34},{21,35},{22,32},{23,33},{2... | collective-permute-start | bytes 1806344 | tf_op jit(solution)/shard_map/ppermute | solution.py:27
  12.0 1.3 %collective-permute-start.2 = (bf16[392,768]{1,0:T(8,128)(2,1)}, bf16[392,768]{1,0:T(8,128)(2,1)S(1)}, u32[]{:S(2)}, u32[]{:S(2)}) collective-permute-start(bf16[392,768]{1,0:T(8,128)(2,1)} %get-tuple-element.40), channel_id=1, source_target_pairs={{0,8},{1,9},{2,10},{3,11},{4,12},{5,13},{6,14},{7,15},{8,16},{9,17... | collective-permute-start | bytes 1806344 | tf_op jit(solution)/shard_map/ppermute | solution.py:27
  13.3 7.8 %collective-permute-start.4 = (bf16[392,768]{1,0:T(8,128)(2,1)S(1)}, bf16[392,768]{1,0:T(8,128)(2,1)S(1)}, u32[]{:S(2)}, u32[]{:S(2)}) collective-permute-start(bf16[392,768]{1,0:T(8,128)(2,1)S(1)} %get-tuple-element.31), channel_id=1, source_target_pairs={{0,8},{1,9},{2,10},{3,11},{4,12},{5,13},{6,14},{7,15},{8,16},{9,17... | collective-permute-start | bytes 1806344 | tf_op jit(solution)/shard_map/ppermute | solution.py:27
  21.1 3.0 %collective-permute-start.5 = (s32[4,2,2,2]{3,2,1,0:T(2,128)S(1)}, s32[4,2,2,2]{3,2,1,0:T(2,128)S(1)}, u32[]{:S(2)}, u32[]{:S(2)}) collective-permute-start(s32[4,2,2,2]{3,2,1,0:T(2,128)S(1)} %pad_add_fusion), channel_id=1, source_target_pairs={{0,1},{1,0},{2,3},{3,2},{4,5},{5,4},{6,7},{7,6},{8,9},{9,8},{10,11... | collective-permute-start | bytes 392 | tf_op jit(solution)/shard_map/ppermute | solution.py:209
  24.2 0.1 copy.18
  24.3 9.3 %copy.17 = bf16[2,8,2,192,768]{4,3,2,1,0:T(8,128)(2,1)} copy(bf16[2,8,2,192,768]{4,2,3,1,0:T(2,128)(2,1)} %bitcast.56) | data formatting | bytes 18874368 | tf_op jit(solution)/shard_map/transpose | solution.py:237
  33.6 0.0 collective-permute-done.5
  33.6 0.1 copy.19
  33.7 0.1 pad_add_fusion.2
  33.8 17.5 %collective-permute-done.3.refs_0_ = bf16[392,768]{1,0:T(8,128)(2,1)S(1)} collective-permute-done((bf16[392,768]{1,0:T(8,128)(2,1)S(1)}, bf16[392,768]{1,0:T(8,128)(2,1)S(1)}, u32[]{:S(2)}, u32[]{:S(2)}) %collective-permute-start.3) | collective-permute-done | bytes 602144 | tf_op jit(solution)/shard_map/ppermute | solution.py:27
  51.2 0.4 collective-permute-done.2.refs_0_
  51.6 1.1 broadcast_select_fusion
  52.8 0.0 collective-permute-done.4.refs_1_
  52.8 1.9 %collective-permute-start.6 = (bf16[392,768]{1,0:T(8,128)(2,1)}, bf16[392,768]{1,0:T(8,128)(2,1)S(1)}, u32[]{:S(2)}, u32[]{:S(2)}) collective-permute-start(bf16[392,768]{1,0:T(8,128)(2,1)} %get-tuple-element.39), channel_id=1, source_target_pairs={{24,38},{25,39},{26,36},{27,37},{28,34},{29,35},{30,32},{31,33},{0... | collective-permute-start | bytes 1806344 | tf_op jit(solution)/shard_map/ppermute | solution.py:27
  54.7 3.5 %collective-permute-start.7 = (bf16[392,768]{1,0:T(8,128)(2,1)}, bf16[392,768]{1,0:T(8,128)(2,1)S(1)}, u32[]{:S(2)}, u32[]{:S(2)}) collective-permute-start(bf16[392,768]{1,0:T(8,128)(2,1)} %get-tuple-element.40), channel_id=1, source_target_pairs={{0,16},{1,17},{2,18},{3,19},{4,20},{5,21},{6,22},{7,23},{8,24},{9,... | collective-permute-start | bytes 1806344 | tf_op jit(solution)/shard_map/ppermute | solution.py:27
  58.2 1.9 %collective-permute-start.12 = (bf16[392,768]{1,0:T(8,128)(2,1)}, bf16[392,768]{1,0:T(8,128)(2,1)}, u32[]{:S(2)}, u32[]{:S(2)}) collective-permute-start(bf16[392,768]{1,0:T(8,128)(2,1)} %get-tuple-element.50), channel_id=1, source_target_pairs={{16,38},{17,39},{18,36},{19,37},{20,34},{21,35},{22,32},{23,33},{8... | collective-permute-start | bytes 1806344 | tf_op jit(solution)/shard_map/ppermute | solution.py:27
  60.1 0.1 copy.22.pairs
  60.3 3.7 %copy-done = bf16[2,8,2,192,768]{4,3,2,1,0:T(8,128)(2,1)S(1)} copy-done((bf16[2,8,2,192,768]{4,3,2,1,0:T(8,128)(2,1)S(1)}, bf16[2,8,2,192,768]{4,3,2,1,0:T(8,128)(2,1)}, u32[]{:S(2)}) %copy-start) | copy-done | bytes 9437208
  63.9 6.6 %shard_map.55 = (f32[2,4,2,24,192]{4,3,2,1,0:T(8,128)S(1)}, f32[2,4,2,24,192]{4,3,2,1,0:T(8,128)S(1)}) custom-call(s32[2,2]{1,0:T(2,128)S(1)} %copy-done.1, s32[8,2,2,2]{3,2,1,0:T(2,128)S(1)} %copy.22.pairs, s32[2]{0:T(128)S(1)} %pad_add_fusion.3.here, f32[8]{0:T(128)S(1)} %copy-done.2, f32[2,1,192]{2,1,0:T(1,128)S(1)} %reshape.12.own_energy, ...), custom_call_target="tpu_custom_call" | custom-call | flops 1925185536 | bytes 5308416 | tf_op jit(solution)/shard_map/pallas_call | solution.py:170
  70.6 6.7 %shard_map.56 = (f32[2,4,2,24,192]{4,3,2,1,0:T(8,128)S(1)}, f32[2,4,2,24,192]{4,3,2,1,0:T(8,128)S(1)}) custom-call(s32[2,2]{1,0:T(2,128)S(1)} %copy-done.1, s32[8,2,2,2]{3,2,1,0:T(2,128)S(1)} %copy.22.pairs, s32[2]{0:T(128)S(1)} %pad_add_fusion.3.here, f32[8]{0:T(128)S(1)} %copy-done.2, f32[2,1,192]{2,1,0:T(1,128)S(1)} %reshape.12.own_energy, ...), custom_call_target="tpu_custom_call" | custom-call | flops 1925185536 | bytes 5308416 | tf_op jit(solution)/shard_map/pallas_call | solution.py:170
  77.3 20.4 %collective-permute-done.6.refs_0_.refs_1_ = bf16[392,768]{1,0:T(8,128)(2,1)S(1)} collective-permute-done((bf16[392,768]{1,0:T(8,128)(2,1)}, bf16[392,768]{1,0:T(8,128)(2,1)S(1)}, u32[]{:S(2)}, u32[]{:S(2)}) %collective-permute-start.6) | collective-permute-done | bytes 602144 | tf_op jit(solution)/shard_map/ppermute | solution.py:27
  97.7 6.9 %shard_map.57 = (f32[4,2,24,192]{3,2,1,0:T(8,128)S(1)}, f32[4,2,24,192]{3,2,1,0:T(8,128)S(1)}, f32[4,2,24,192]{3,2,1,0:T(8,128)S(1)}, f32[4,2,24,192]{3,2,1,0:T(8,128)S(1)}) custom-call(s32[2,2]{1,0:T(2,128)S(1)} %copy-done.1, s32[8,2,2,2]{3,2,1,0:T(2,128)S(1)} %copy.22.pairs, s32[2]{0:T(128)S(1)} %pad_add_fusion.3.here, f32[8]{0:T(128)S(1)} %copy-done.2, ...), custom_call_target="tpu_custom_call" | custom-call | flops 1925185536 | bytes 5308416 | tf_op jit(solution)/shard_map/pallas_call | solution.py:170
  104.6 6.9 %shard_map.58 = (f32[4,2,24,192]{3,2,1,0:T(8,128)S(1)}, f32[4,2,24,192]{3,2,1,0:T(8,128)S(1)}) custom-call(s32[2,2]{1,0:T(2,128)S(1)} %copy-done.1, s32[8,2,2,2]{3,2,1,0:T(2,128)S(1)} %copy.22.pairs, s32[2]{0:T(128)S(1)} %pad_add_fusion.3.here, f32[8]{0:T(128)S(1)} %copy-done.2, f32[2,1,192]{2,1,0:T(1,128)S(1)} %reshape.12.own_energy, ...), custom_call_target="tpu_custom_call" | custom-call | flops 1925185536 | bytes 5308416 | tf_op jit(solution)/shard_map/pallas_call | solution.py:170
  111.5 0.9 collective-permute-start.13
  112.4 0.1 collective-permute-start.8
  112.5 0.6 slice.9
  115.1 0.0 collective-permute-done.13
  115.1 2.0 %collective-permute-start.16 = (f32[2,24,192]{2,1,0:T(8,128)S(1)}, f32[2,24,192]{2,1,0:T(8,128)S(1)}, u32[]{:S(2)}, u32[]{:S(2)}) collective-permute-start(f32[2,24,192]{2,1,0:T(8,128)S(1)} %get-tuple-element.66), channel_id=1, source_target_pairs={{0,6},{1,7},{2,0},{3,1},{4,2},{5,3},{6,4},{7,5},{8,14},{9,15},{10,... | collective-permute-start | bytes 110600 | tf_op jit(solution)/shard_map/ppermute | solution.py:204
  117.1 0.4 collective-permute-start.14
  117.5 0.0 collective-permute-done.8
  117.6 3.0 %collective-permute-start.11 = (f32[2,24,192]{2,1,0:T(8,128)S(1)}, f32[2,24,192]{2,1,0:T(8,128)S(1)}, u32[]{:S(2)}, u32[]{:S(2)}) collective-permute-start(f32[2,24,192]{2,1,0:T(8,128)S(1)} %get-tuple-element.63), channel_id=1, source_target_pairs={{0,6},{1,7},{2,0},{3,1},{4,2},{5,3},{6,4},{7,5},{8,14},{9,15},{10,... | collective-permute-start | bytes 110600 | tf_op jit(solution)/shard_map/ppermute | solution.py:204
  120.5 0.6 collective-permute-start.10
  121.1 0.0 collective-permute-done.16
  121.1 0.0 collective-permute-start.9
  121.1 0.9 collective-permute-done.15
  122.0 0.0 collective-permute-done.14
  122.1 4.5 %collective-permute-done.10 = f32[2,24,192]{2,1,0:T(8,128)S(1)} collective-permute-done((f32[2,24,192]{2,1,0:T(8,128)S(1)}, f32[2,24,192]{2,1,0:T(8,128)S(1)}, u32[]{:S(2)}, u32[]{:S(2)}) %collective-permute-start.10) | collective-permute-done | bytes 36896 | tf_op jit(solution)/shard_map/ppermute | solution.py:204
  126.6 0.7 copy.24
  (26 shorter events, 0.2 us)
Async XLA Ops:
  0.0 6.6 %collective-permute-start = (s32[1,2,2,2]{3,2,1,0:T(2,128)}, s32[1,2,2,2]{3,2,1,0:T(2,128)S(1)}, u32[]{:S(2)}, u32[]{:S(2)}) collective-permute-start(s32[1,2,2,2]{3,2,1,0:T(2,128)} %bitcast.59), channel_id=1, source_target_pairs={{0,2},{1,3},{2,0},{3,1},{4,6},{5,7},{6,4},{7,5},{8,10},{9,11},{10,... | collective-permute-start | bytes 104 | tf_op jit(solution)/shard_map/ppermute | solution.py:209
  5.5 1.1 copy-start.4
  5.5 15.6 %copy-start.3 = (bf16[2,192]{1,0:T(2,128)(2,1)S(1)}, bf16[2,192]{1,0:T(2,128)(2,1)}, u32[]{:S(2)}) copy-start(bf16[2,192]{1,0:T(2,128)(2,1)} %param.7) | copy-start | bytes 2308
  6.7 4.1 %collective-permute-start.1 = (s32[2,2,2,2]{3,2,1,0:T(2,128)S(1)}, s32[2,2,2,2]{3,2,1,0:T(2,128)S(1)}, u32[]{:S(2)}, u32[]{:S(2)}) collective-permute-start(s32[2,2,2,2]{3,2,1,0:T(2,128)S(1)} %pad_add_fusion.1), channel_id=1, source_target_pairs={{0,4},{1,5},{2,6},{3,7},{4,0},{5,1},{6,2},{7,3},{8,12},{9,13},{10,... | collective-permute-start | bytes 200 | tf_op jit(solution)/shard_map/ppermute | solution.py:209
  10.7 40.5 %collective-permute-start.3 = (bf16[392,768]{1,0:T(8,128)(2,1)S(1)}, bf16[392,768]{1,0:T(8,128)(2,1)S(1)}, u32[]{:S(2)}, u32[]{:S(2)}) collective-permute-start(bf16[392,768]{1,0:T(8,128)(2,1)S(1)} %get-tuple-element.32), channel_id=1, source_target_pairs={{16,38},{17,39},{18,36},{19,37},{20,34},{21,35},{22,32},{23,33},{2... | collective-permute-start | bytes 1806344 | tf_op jit(solution)/shard_map/ppermute | solution.py:27
  12.0 39.6 %collective-permute-start.2 = (bf16[392,768]{1,0:T(8,128)(2,1)}, bf16[392,768]{1,0:T(8,128)(2,1)S(1)}, u32[]{:S(2)}, u32[]{:S(2)}) collective-permute-start(bf16[392,768]{1,0:T(8,128)(2,1)} %get-tuple-element.40), channel_id=1, source_target_pairs={{0,8},{1,9},{2,10},{3,11},{4,12},{5,13},{6,14},{7,15},{8,16},{9,17... | collective-permute-start | bytes 1806344 | tf_op jit(solution)/shard_map/ppermute | solution.py:27
  13.3 39.5 %collective-permute-start.4 = (bf16[392,768]{1,0:T(8,128)(2,1)S(1)}, bf16[392,768]{1,0:T(8,128)(2,1)S(1)}, u32[]{:S(2)}, u32[]{:S(2)}) collective-permute-start(bf16[392,768]{1,0:T(8,128)(2,1)S(1)} %get-tuple-element.31), channel_id=1, source_target_pairs={{0,8},{1,9},{2,10},{3,11},{4,12},{5,13},{6,14},{7,15},{8,16},{9,17... | collective-permute-start | bytes 1806344 | tf_op jit(solution)/shard_map/ppermute | solution.py:27
  21.1 12.4 %collective-permute-start.5 = (s32[4,2,2,2]{3,2,1,0:T(2,128)S(1)}, s32[4,2,2,2]{3,2,1,0:T(2,128)S(1)}, u32[]{:S(2)}, u32[]{:S(2)}) collective-permute-start(s32[4,2,2,2]{3,2,1,0:T(2,128)S(1)} %pad_add_fusion), channel_id=1, source_target_pairs={{0,1},{1,0},{2,3},{3,2},{4,5},{5,4},{6,7},{7,6},{8,9},{9,8},{10,11... | collective-permute-start | bytes 392 | tf_op jit(solution)/shard_map/ppermute | solution.py:209
  33.7 26.5 %copy-start.1 = (s32[2,2]{1,0:T(2,128)S(1)}, s32[2,2]{1,0:T(2,128)}, u32[]{:S(2)}) copy-start(s32[2,2]{1,0:T(2,128)} %conserve.7) | copy-start | bytes 52
  33.8 26.5 %copy-start.2 = (f32[8]{0:T(128)S(1)}, f32[8]{0:T(128)}, u32[]{:S(2)}) copy-start(f32[8]{0:T(128)} %occupied.7) | copy-start | bytes 100
  52.8 44.9 %collective-permute-start.6 = (bf16[392,768]{1,0:T(8,128)(2,1)}, bf16[392,768]{1,0:T(8,128)(2,1)S(1)}, u32[]{:S(2)}, u32[]{:S(2)}) collective-permute-start(bf16[392,768]{1,0:T(8,128)(2,1)} %get-tuple-element.39), channel_id=1, source_target_pairs={{24,38},{25,39},{26,36},{27,37},{28,34},{29,35},{30,32},{31,33},{0... | collective-permute-start | bytes 1806344 | tf_op jit(solution)/shard_map/ppermute | solution.py:27
  54.7 43.0 %collective-permute-start.7 = (bf16[392,768]{1,0:T(8,128)(2,1)}, bf16[392,768]{1,0:T(8,128)(2,1)S(1)}, u32[]{:S(2)}, u32[]{:S(2)}) collective-permute-start(bf16[392,768]{1,0:T(8,128)(2,1)} %get-tuple-element.40), channel_id=1, source_target_pairs={{0,16},{1,17},{2,18},{3,19},{4,20},{5,21},{6,22},{7,23},{8,24},{9,... | collective-permute-start | bytes 1806344 | tf_op jit(solution)/shard_map/ppermute | solution.py:27
  58.2 46.4 %collective-permute-start.12 = (bf16[392,768]{1,0:T(8,128)(2,1)}, bf16[392,768]{1,0:T(8,128)(2,1)}, u32[]{:S(2)}, u32[]{:S(2)}) collective-permute-start(bf16[392,768]{1,0:T(8,128)(2,1)} %get-tuple-element.50), channel_id=1, source_target_pairs={{16,38},{17,39},{18,36},{19,37},{20,34},{21,35},{22,32},{23,33},{8... | collective-permute-start | bytes 1806344 | tf_op jit(solution)/shard_map/ppermute | solution.py:27
  60.2 3.7 %copy-start = (bf16[2,8,2,192,768]{4,3,2,1,0:T(8,128)(2,1)S(1)}, bf16[2,8,2,192,768]{4,3,2,1,0:T(8,128)(2,1)}, u32[]{:S(2)}) copy-start(bf16[2,8,2,192,768]{4,3,2,1,0:T(8,128)(2,1)} %copy.17) | copy-start | bytes 28311556
  111.5 3.6 %collective-permute-start.13 = (f32[4,2,24,192]{3,2,1,0:T(8,128)S(1)}, f32[4,2,24,192]{3,2,1,0:T(8,128)S(1)}, u32[]{:S(2)}, u32[]{:S(2)}) collective-permute-start(f32[4,2,24,192]{3,2,1,0:T(8,128)S(1)} %get-tuple-element.54), channel_id=1, source_target_pairs={{0,1},{1,0},{2,3},{3,2},{4,5},{5,4},{6,7},{7,6},{8,9},{9,8},{10,11... | collective-permute-start | bytes 442376 | tf_op jit(solution)/shard_map/ppermute | solution.py:199
  112.4 5.1 %collective-permute-start.8 = (f32[4,2,24,192]{3,2,1,0:T(8,128)S(1)}, f32[4,2,24,192]{3,2,1,0:T(8,128)S(1)}, u32[]{:S(2)}, u32[]{:S(2)}) collective-permute-start(f32[4,2,24,192]{3,2,1,0:T(8,128)S(1)} %get-tuple-element.49), channel_id=1, source_target_pairs={{0,1},{1,0},{2,3},{3,2},{4,5},{5,4},{6,7},{7,6},{8,9},{9,8},{10,11... | collective-permute-start | bytes 442376 | tf_op jit(solution)/shard_map/ppermute | solution.py:199
  115.1 6.0 %collective-permute-start.16 = (f32[2,24,192]{2,1,0:T(8,128)S(1)}, f32[2,24,192]{2,1,0:T(8,128)S(1)}, u32[]{:S(2)}, u32[]{:S(2)}) collective-permute-start(f32[2,24,192]{2,1,0:T(8,128)S(1)} %get-tuple-element.66), channel_id=1, source_target_pairs={{0,6},{1,7},{2,0},{3,1},{4,2},{5,3},{6,4},{7,5},{8,14},{9,15},{10,... | collective-permute-start | bytes 110600 | tf_op jit(solution)/shard_map/ppermute | solution.py:204
  117.1 4.9 %collective-permute-start.15 = (f32[2,24,192]{2,1,0:T(8,128)S(1)}, f32[2,24,192]{2,1,0:T(8,128)S(1)}, u32[]{:S(2)}, u32[]{:S(2)}) collective-permute-start(f32[2,24,192]{2,1,0:T(8,128)S(1)} %get-tuple-element.67), channel_id=1, source_target_pairs={{0,4},{1,5},{2,6},{3,7},{4,0},{5,1},{6,2},{7,3},{8,12},{9,13},{10,... | collective-permute-start | bytes 110600 | tf_op jit(solution)/shard_map/ppermute | solution.py:204
  117.1 4.9 %collective-permute-start.14 = (f32[2,24,192]{2,1,0:T(8,128)S(1)}, f32[2,24,192]{2,1,0:T(8,128)S(1)}, u32[]{:S(2)}, u32[]{:S(2)}) collective-permute-start(f32[2,24,192]{2,1,0:T(8,128)S(1)} %get-tuple-element.65), channel_id=1, source_target_pairs={{0,2},{1,3},{2,4},{3,5},{4,6},{5,7},{6,0},{7,1},{8,10},{9,11},{10,... | collective-permute-start | bytes 110600 | tf_op jit(solution)/shard_map/ppermute | solution.py:204
  117.6 4.5 %collective-permute-start.11 = (f32[2,24,192]{2,1,0:T(8,128)S(1)}, f32[2,24,192]{2,1,0:T(8,128)S(1)}, u32[]{:S(2)}, u32[]{:S(2)}) collective-permute-start(f32[2,24,192]{2,1,0:T(8,128)S(1)} %get-tuple-element.63), channel_id=1, source_target_pairs={{0,6},{1,7},{2,0},{3,1},{4,2},{5,3},{6,4},{7,5},{8,14},{9,15},{10,... | collective-permute-start | bytes 110600 | tf_op jit(solution)/shard_map/ppermute | solution.py:204
  120.5 6.0 %collective-permute-start.10 = (f32[2,24,192]{2,1,0:T(8,128)S(1)}, f32[2,24,192]{2,1,0:T(8,128)S(1)}, u32[]{:S(2)}, u32[]{:S(2)}) collective-permute-start(f32[2,24,192]{2,1,0:T(8,128)S(1)} %get-tuple-element.64), channel_id=1, source_target_pairs={{0,4},{1,5},{2,6},{3,7},{4,0},{5,1},{6,2},{7,3},{8,12},{9,13},{10,... | collective-permute-start | bytes 110600 | tf_op jit(solution)/shard_map/ppermute | solution.py:204
  121.1 5.5 %collective-permute-start.9 = (f32[2,24,192]{2,1,0:T(8,128)S(1)}, f32[2,24,192]{2,1,0:T(8,128)S(1)}, u32[]{:S(2)}, u32[]{:S(2)}) collective-permute-start(f32[2,24,192]{2,1,0:T(8,128)S(1)} %get-tuple-element.62), channel_id=1, source_target_pairs={{0,2},{1,3},{2,4},{3,5},{4,6},{5,7},{6,0},{7,1},{8,10},{9,11},{10,... | collective-permute-start | bytes 110600 | tf_op jit(solution)/shard_map/ppermute | solution.py:204

commit v6 on v5

--- a/solution.py
+++ b/solution.py
@@ -27,13 +27,17 @@
     return lax.ppermute(array, ("ka", "occ"), pairs)
 
 
+def finished(column, conserve):
+    return jnp.where(column == 0, lax.rem(conserve[0, 0], 2), 1 - lax.rem(conserve[0, 1], 2))
+
+
 def piece_kernel(
     sources, before_count, kind, order, conserve, pairs, here, occupied, own_energy, left, *refs
 ):
     mates, refs = refs[:sources], refs[sources:]
     before, refs = refs[:before_count], refs[before_count:]
-    outs, refs = refs[:-8], refs[-8:]
-    piece, own, products, combined, rounded, turned, total, arrived = refs
+    outs, refs = refs[:-6], refs[-6:]
+    piece, products, combined, rounded, turned, total = refs
     orbitals = products.shape[0]
     virtuals = products.shape[3]
     rows = products.shape[2]
@@ -54,11 +58,6 @@
     source = by_column(order[2])
     mine = lax.rem(conserve[0, round_index] + momentum, jnp.int32(2))
 
-    def copy_of(orbital):
-        return pltpu.make_async_copy(left.at[mine, orbital], own.at[orbital], arrived.at[orbital])
-
-    for orbital in range(orbitals):
-        copy_of(orbital).start()
     for number, mate in enumerate(mates):
 
         @pl.when(source == number)
@@ -67,11 +66,10 @@
 
     contract = (((1,), (1,)), ((), ()))
     for orbital in range(orbitals):
-        copy_of(orbital).wait()
         for part in range(2):
             products[orbital, part] = lax.dot_general(
                 piece[:rows],
-                own[orbital, part * virtuals : (part + 1) * virtuals],
+                left[mine, orbital, part * virtuals : (part + 1) * virtuals],
                 contract,
                 preferred_element_type=jnp.float32,
             )
@@ -129,7 +127,7 @@
         total[part] = lax.dot_general(
             combined[...], right[...], contract_rows, preferred_element_type=jnp.float32
         )
-    done = lax.rem(conserve[0, 1], jnp.int32(2))
+    done = finished(column, conserve)
     for place in range(LINE):
         for number, offset in enumerate((core, 1 - core)):
             cut = pl.ds(pl.multiple_of((place * CORES + offset) * share, 8), share)
@@ -171,18 +169,15 @@
         functools.partial(piece_kernel, len(mates), len(before), kind, order),
         out_shape=out_shape,
         in_specs=[scalars] * 4
-        + [whole, pl.BlockSpec(memory_space=pl.ANY)]
-        + [whole] * (len(mates) + len(before)),
+        + [whole] * (2 + len(mates) + len(before)),
         out_specs=(whole,) * len(out_shape),
         scratch_shapes=[
             pltpu.VMEM((rows + HEAD, auxiliary), jnp.bfloat16),
-            pltpu.VMEM((orbitals, both, auxiliary), jnp.bfloat16),
             pltpu.VMEM((orbitals, 2, rows, virtuals), jnp.float32),
             pltpu.VMEM((2 * count * share, virtuals), jnp.bfloat16),
             pltpu.VMEM((2 * count * share, virtuals), jnp.bfloat16),
             pltpu.VMEM((2 * count * share, virtuals), jnp.bfloat16),
             pltpu.VMEM((2, virtuals, virtuals), jnp.float32),
-            pltpu.SemaphoreType.DMA((orbitals,)),
         ],
         compiler_params=pltpu.CompilerParams(vmem_limit_bytes=40 << 20),
         cost_estimate=pl.CostEstimate(
@@ -229,37 +224,40 @@
     pairs = with_partner(with_partner(pair_lists[None], CORES), 2 * CORES)
     m0 = outgoing(0)
     m1 = outgoing(1)
-    mixed = jnp.where(column == 3, m1, m0)
-    m0, m1, mixed, pairs, factors, here = lax.optimization_barrier((m0, m1, mixed, pairs, factors, here))
-    one = moved(m0, {0: (1, False), 1: (2, False), 2: (3, False), 3: (0, True)})
-    two = moved(mixed, {2: (0, True), 3: (1, False)})
-    three = moved(m1, {0: (1, False), 1: (2, False), 2: (3, False)})
+    m0, m1, pairs, factors, here = lax.optimization_barrier((m0, m1, pairs, factors, here))
+    plus = moved(m1, {c: ((c + 1) % COLUMNS, False) for c in range(COLUMNS)})
+    minus = moved(m1, {c: ((c - 1) % COLUMNS, False) for c in range(COLUMNS)})
     left = jnp.transpose(factors, (0, 1, 3, 2, 4)).reshape(momenta, orbitals, 2 * virtuals, auxiliary)
+    m0, left = lax.optimization_barrier((m0, left))
+    cross_one = moved(m0, {3: (0, True)})
+    cross_two = moved(m0, {2: (0, True)})
     pairs = with_partner(pairs, 1)
     own_energy = virtual_energy.astype(jnp.float32)[:, None, :]
-    four_out = jnp.where(column == 0, one, m1)
-    five_out = jnp.where(column == 1, two, m1)
-    four_out, five_out, one, two, three, left, pairs, m0, own_energy = lax.optimization_barrier(
-        (four_out, five_out, one, two, three, left, pairs, m0, own_energy)
-    )
-    four = moved(four_out, {3: (0, True), 0: (1, False), 1: (3, False)})
-    five = moved(five_out, {2: (0, True), 1: (1, True), 0: (2, False)})
-    six = moved(m0, {0: (2, False), 1: (3, False)})
+    m0, plus, minus, pairs, own_energy = lax.optimization_barrier((m0, plus, minus, pairs, own_energy))
+    up = moved(plus, {0: (0, True)})
+    back = moved(minus, {0: (3, False), 1: (0, True), 2: (1, True), 3: (2, False)})
+    near_one = moved(m0, {0: (1, False), 1: (2, False), 2: (3, False)})
+    m0, cross_one, cross_two, near_one = lax.optimization_barrier((m0, cross_one, cross_two, near_one))
+    onward = moved(cross_one, {0: (1, False)})
+    near_two = moved(m0, {0: (2, False), 1: (3, False)})
 
     def density(kind, order, mates, before):
         return piece_density(
             kind, order, conserve, pairs, here, occupied_energy, own_energy, left, mates, before
         )
 
-    total = density("first", ((0,), (0,), (0,)), (one,), ())
-    total = density("second", ((1, 0), (0, 1), (0, 1)), (two, three), total)
+    total = density("first", ((0,), (0,), (0, 1)), (cross_one, near_one), ())
+    total = density("second", ((1,), (1,), (0,)), (back,), total)
     keep_a, send_a, keep_b, send_b = density(
-        "third", ((0, 1), (1, 0), (0, 0, 1)), (four, six), total
+        "third", ((1, 0), (0, 1), (0, 1)), (cross_two, plus), total
     )
-    keep_b, send_b = density("fourth", ((1,), (1,), (0, 0, 0, 1)), (five, four), (keep_b, send_b))
+    keep_b, send_b = density(
+        "fourth", ((0, 1), (1, 0), (0, 1, 2)), (up, onward, near_two), (keep_b, send_b)
+    )
     done = summed(keep_a, send_a)
     last = summed(keep_b, send_b)
-    result = jnp.where(conserve[0, 1] % 2 == 0, jnp.stack([done, last]), jnp.stack([last, done]))
+    done_first = finished(column, conserve) == 0
+    result = jnp.where(done_first, jnp.stack([done, last]), jnp.stack([last, done]))
     return jnp.transpose(result, (0, 2, 1, 3))
 
 

time: 128 us -> 139 us (1.086)
  the two profiles are of different devices: /device:TPU:1 before, /device:TPU:4 now
where the time goes in v6:
time: 139 us; the launch traced here: 138 us
  waiting for transfers between devices  64.6 us (46%)
  starting transfers between devices  31 us (22%)
  local copies, waits for them, and re-layouts  19.7 us (14%)
  Pallas kernels  18 us (13%)
  between operations  4.28 us (3%)
    ppermute x9, waiting for transfers between devices, moved(): return lax.ppermute(array, ('ka', 'occ'), pairs)  60.1 us
    pallas_call x4, Pallas kernels, piece_density(): pl.pallas_call(functools.partial(piece_kernel, len(mates), len(before), k...  18 us
    ppermute x9, starting transfers between devices, moved(): return lax.ppermute(array, ('ka', 'occ'), pairs)  17 us
    transpose x1, local copies, waits for them, and re-layouts, local(): jnp.transpose(factors, (0, 1, 3, 2, 4))  9.33 us
    ppermute x6, starting transfers between devices, summed(): total = total + lax.ppermute(part, 'occ', ring)  8.58 us
    unnamed x16, local copies, waits for them, and re-layouts  6.45 us
    ppermute x3, starting transfers between devices, with_partner(): lax.ppermute(array, 'occ', [(i, i ^ reach) for i in range(LINE * CORES)])  5.19 us
    ppermute x6, waiting for transfers between devices, summed(): total = total + lax.ppermute(part, 'occ', ring)  3.02 us
  transfers between devices with their start and end apart: 20, of which 7 were waited for; matrix products, arithmetic and copies ran while one was open for 9% of the time, Pallas kernels for 13%

profile of v6, /device:TPU:4, one launch (start us, length us, event | category | flops | bytes accessed | tf_op | source)
XLA Modules:
  0.0 138.1 jit_solution(13428309412323755124)
XLA Ops:
  0.0 1.9 %collective-permute-start = (s32[1,2,2,2]{3,2,1,0:T(2,128)}, s32[1,2,2,2]{3,2,1,0:T(2,128)S(1)}, u32[]{:S(2)}, u32[]{:S(2)}) collective-permute-start(s32[1,2,2,2]{3,2,1,0:T(2,128)} %bitcast.60), channel_id=1, source_target_pairs={{0,2},{1,3},{2,0},{3,1},{4,6},{5,7},{6,4},{7,5},{8,10},{9,11},{10,... | collective-permute-start | bytes 104 | tf_op jit(solution)/shard_map/ppermute | solution.py:204
  1.9 2.1 %constant_dynamic-slice_fusion = (bf16[1,8,24,2,768]{4,3,2,1,0:T(2,128)(2,1)S(1)}, bf16[1,8,24,2,768]{4,3,2,1,0:T(2,128)(2,1)S(1)}) fusion(bf16[2,8,192,2,768]{4,3,2,1,0:T(2,128)(2,1)} %param.5, s32[]{:T(128)S(6)} %select_n.69), kind=kLoop, calls=%fused_computation.28 | loop fusion | bytes 2359300 | tf_op jit(solution)/shard_map/dynamic_slice | solution.py:216
  4.0 0.1 copy.27
  4.1 0.1 copy.28
  4.1 0.5 copy-done.6
  4.7 0.1 pad.27.clone
  4.7 0.3 fusion.6
  5.0 0.3 copy-done.7
  5.4 3.3 %collective-permute-start.1 = (s32[2,2,2,2]{3,2,1,0:T(2,128)S(1)}, s32[2,2,2,2]{3,2,1,0:T(2,128)S(1)}, u32[]{:S(2)}, u32[]{:S(2)}) collective-permute-start(s32[2,2,2,2]{3,2,1,0:T(2,128)S(1)} %pad_add_fusion.1), channel_id=1, source_target_pairs={{0,4},{1,5},{2,6},{3,7},{4,0},{5,1},{6,2},{7,3},{8,12},{9,13},{10,... | collective-permute-start | bytes 200 | tf_op jit(solution)/shard_map/ppermute | solution.py:204
  8.6 0.1 pad_add_fusion.3.here
  8.7 1.5 %collective-permute-done.1 = s32[2,2,2,2]{3,2,1,0:T(2,128)S(1)} collective-permute-done((s32[2,2,2,2]{3,2,1,0:T(2,128)S(1)}, s32[2,2,2,2]{3,2,1,0:T(2,128)S(1)}, u32[]{:S(2)}, u32[]{:S(2)}) %collective-permute-start.1) | collective-permute-done | bytes 96 | tf_op jit(solution)/shard_map/ppermute | solution.py:204
  10.2 1.2 collective-permute-start.2
  11.4 0.8 collective-permute-start.3
  12.2 0.1 copy.18
  12.4 9.3 %copy.17 = bf16[2,8,2,192,768]{4,3,2,1,0:T(8,128)(2,1)} copy(bf16[2,8,2,192,768]{4,2,3,1,0:T(2,128)(2,1)} %bitcast.57) | data formatting | bytes 18874368 | tf_op jit(solution)/shard_map/transpose | solution.py:230
  21.7 1.5 %collective-permute-start.5 = (bf16[392,768]{1,0:T(8,128)(2,1)S(1)}, bf16[392,768]{1,0:T(8,128)(2,1)}, u32[]{:S(2)}, u32[]{:S(2)}) collective-permute-start(bf16[392,768]{1,0:T(8,128)(2,1)S(1)} %get-tuple-element.52), channel_id=1, source_target_pairs={{24,38},{25,39},{26,36},{27,37},{28,34},{29,35},{30,32},{31,33},{5... | collective-permute-start | bytes 1806344 | tf_op jit(solution)/shard_map/ppermute | solution.py:27
  23.2 7.5 %collective-permute-start.6 = (bf16[392,768]{1,0:T(8,128)(2,1)S(1)}, bf16[392,768]{1,0:T(8,128)(2,1)S(1)}, u32[]{:S(2)}, u32[]{:S(2)}) collective-permute-start(bf16[392,768]{1,0:T(8,128)(2,1)S(1)} %get-tuple-element.52), channel_id=1, source_target_pairs={{16,38},{17,39},{18,36},{19,37},{20,34},{21,35},{22,32},{23,33},{4... | collective-permute-start | bytes 1806344 | tf_op jit(solution)/shard_map/ppermute | solution.py:27
  30.7 0.1 copy.19
  30.8 0.1 pad_add_fusion.2
  30.9 3.3 %collective-permute-start.7 = (bf16[392,768]{1,0:T(8,128)(2,1)S(1)}, bf16[392,768]{1,0:T(8,128)(2,1)S(1)}, u32[]{:S(2)}, u32[]{:S(2)}) collective-permute-start(bf16[392,768]{1,0:T(8,128)(2,1)S(1)} %get-tuple-element.52), channel_id=1, source_target_pairs={{0,8},{1,9},{2,10},{3,11},{4,12},{5,13},{6,14},{7,15},{8,16},{9,17... | collective-permute-start | bytes 1806344 | tf_op jit(solution)/shard_map/ppermute | solution.py:27
  34.2 0.1 collective-permute-start.8
  34.3 0.7 collective-permute-start.13
  35.0 35.4 %collective-permute-done.6.refs_0_ = bf16[392,768]{1,0:T(8,128)(2,1)S(1)} collective-permute-done((bf16[392,768]{1,0:T(8,128)(2,1)S(1)}, bf16[392,768]{1,0:T(8,128)(2,1)S(1)}, u32[]{:S(2)}, u32[]{:S(2)}) %collective-permute-start.6) | collective-permute-done | bytes 602144 | tf_op jit(solution)/shard_map/ppermute | solution.py:27
  70.3 0.9 copy-done.1
  71.2 0.7 collective-permute-start.14
  71.9 1.3 collective-permute-start.15
  73.2 0.1 copy.22.pairs
  73.3 3.7 %copy-done = bf16[2,8,2,192,768]{4,3,2,1,0:T(8,128)(2,1)S(1)} copy-done((bf16[2,8,2,192,768]{4,3,2,1,0:T(8,128)(2,1)S(1)}, bf16[2,8,2,192,768]{4,3,2,1,0:T(8,128)(2,1)}, u32[]{:S(2)}) %copy-start) | copy-done | bytes 9437208
  77.0 1.1 copy-done.2
  78.1 4.6 %shard_map.55 = (f32[2,4,2,24,192]{4,3,2,1,0:T(8,128)S(1)}, f32[2,4,2,24,192]{4,3,2,1,0:T(8,128)S(1)}) custom-call(s32[2,2]{1,0:T(2,128)S(1)} %copy-done.3, s32[8,2,2,2]{3,2,1,0:T(2,128)S(1)} %copy.22.pairs, s32[2]{0:T(128)S(1)} %pad_add_fusion.3.here, f32[8]{0:T(128)S(1)} %copy-done.4, f32[2,1,192]{2,1,0:T(1,128)S(1)} %reshape.12.own_energy, ...), custom_call_target="tpu_custom_call" | custom-call | flops 1925185536 | bytes 5308416 | tf_op jit(solution)/shard_map/pallas_call | solution.py:168
  82.6 0.3 collective-permute-done.8.refs_0_
  83.0 4.6 %shard_map.56 = (f32[2,4,2,24,192]{4,3,2,1,0:T(8,128)S(1)}, f32[2,4,2,24,192]{4,3,2,1,0:T(8,128)S(1)}) custom-call(s32[2,2]{1,0:T(2,128)S(1)} %copy-done.3, s32[8,2,2,2]{3,2,1,0:T(2,128)S(1)} %copy.22.pairs, s32[2]{0:T(128)S(1)} %pad_add_fusion.3.here, f32[8]{0:T(128)S(1)} %copy-done.4, f32[2,1,192]{2,1,0:T(1,128)S(1)} %reshape.12.own_energy, ...), custom_call_target="tpu_custom_call" | custom-call | flops 1925185536 | bytes 5308416 | tf_op jit(solution)/shard_map/pallas_call | solution.py:168
  87.5 4.6 %shard_map.57 = (f32[4,2,24,192]{3,2,1,0:T(8,128)S(1)}, f32[4,2,24,192]{3,2,1,0:T(8,128)S(1)}, f32[4,2,24,192]{3,2,1,0:T(8,128)S(1)}, f32[4,2,24,192]{3,2,1,0:T(8,128)S(1)}) custom-call(s32[2,2]{1,0:T(2,128)S(1)} %copy-done.3, s32[8,2,2,2]{3,2,1,0:T(2,128)S(1)} %copy.22.pairs, s32[2]{0:T(128)S(1)} %pad_add_fusion.3.here, f32[8]{0:T(128)S(1)} %copy-done.4, ...), custom_call_target="tpu_custom_call" | custom-call | flops 1925185536 | bytes 5308416 | tf_op jit(solution)/shard_map/pallas_call | solution.py:168
  92.1 0.1 collective-permute-start.9
  92.2 24.4 %collective-permute-done.15.refs_2_ = bf16[392,768]{1,0:T(8,128)(2,1)S(1)} collective-permute-done((bf16[392,768]{1,0:T(8,128)(2,1)}, bf16[392,768]{1,0:T(8,128)(2,1)S(1)}, u32[]{:S(2)}, u32[]{:S(2)}) %collective-permute-start.15) | collective-permute-done | bytes 602144 | tf_op jit(solution)/shard_map/ppermute | solution.py:27
  116.6 4.3 %shard_map.58 = (f32[4,2,24,192]{3,2,1,0:T(8,128)S(1)}, f32[4,2,24,192]{3,2,1,0:T(8,128)S(1)}) custom-call(s32[2,2]{1,0:T(2,128)S(1)} %copy-done.3, s32[8,2,2,2]{3,2,1,0:T(2,128)S(1)} %copy.22.pairs, s32[2]{0:T(128)S(1)} %pad_add_fusion.3.here, f32[8]{0:T(128)S(1)} %copy-done.4, f32[2,1,192]{2,1,0:T(1,128)S(1)} %reshape.12.own_energy, ...), custom_call_target="tpu_custom_call" | custom-call | flops 1925185536 | bytes 5308416 | tf_op jit(solution)/shard_map/pallas_call | solution.py:168
  121.0 0.1 collective-permute-start.16
  121.1 0.6 fusion.14
  125.7 0.1 collective-permute-start.10
  125.8 0.7 collective-permute-start.11
  126.5 3.2 %collective-permute-start.12 = (f32[2,24,192]{2,1,0:T(8,128)S(1)}, f32[2,24,192]{2,1,0:T(8,128)S(1)}, u32[]{:S(2)}, u32[]{:S(2)}) collective-permute-start(f32[2,24,192]{2,1,0:T(8,128)S(1)} %get-tuple-element.60), channel_id=1, source_target_pairs={{0,6},{1,7},{2,0},{3,1},{4,2},{5,3},{6,4},{7,5},{8,14},{9,15},{10,... | collective-permute-start | bytes 110600 | tf_op jit(solution)/shard_map/ppermute | solution.py:199
  129.7 0.6 collective-permute-start.17
  130.3 1.6 %collective-permute-start.18 = (f32[2,24,192]{2,1,0:T(8,128)S(1)}, f32[2,24,192]{2,1,0:T(8,128)S(1)}, u32[]{:S(2)}, u32[]{:S(2)}) collective-permute-start(f32[2,24,192]{2,1,0:T(8,128)S(1)} %get-tuple-element.64), channel_id=1, source_target_pairs={{0,4},{1,5},{2,6},{3,7},{4,0},{5,1},{6,2},{7,3},{8,12},{9,13},{10,... | collective-permute-start | bytes 110600 | tf_op jit(solution)/shard_map/ppermute | solution.py:199
  131.9 0.3 collective-permute-done.10
  132.2 2.5 %collective-permute-start.19 = (f32[2,24,192]{2,1,0:T(8,128)S(1)}, f32[2,24,192]{2,1,0:T(8,128)S(1)}, u32[]{:S(2)}, u32[]{:S(2)}) collective-permute-start(f32[2,24,192]{2,1,0:T(8,128)S(1)} %get-tuple-element.63), channel_id=1, source_target_pairs={{0,6},{1,7},{2,0},{3,1},{4,2},{5,3},{6,4},{7,5},{8,14},{9,15},{10,... | collective-permute-start | bytes 110600 | tf_op jit(solution)/shard_map/ppermute | solution.py:199
  134.7 1.4 %collective-permute-done.17 = f32[2,24,192]{2,1,0:T(8,128)S(1)} collective-permute-done((f32[2,24,192]{2,1,0:T(8,128)S(1)}, f32[2,24,192]{2,1,0:T(8,128)S(1)}, u32[]{:S(2)}, u32[]{:S(2)}) %collective-permute-start.17) | collective-permute-done | bytes 36896 | tf_op jit(solution)/shard_map/ppermute | solution.py:199
  136.1 1.3 collective-permute-done.18
  137.5 0.7 copy.24
  (37 shorter events, 0.2 us)
Async XLA Ops:
  0.0 5.0 %collective-permute-start = (s32[1,2,2,2]{3,2,1,0:T(2,128)}, s32[1,2,2,2]{3,2,1,0:T(2,128)S(1)}, u32[]{:S(2)}, u32[]{:S(2)}) collective-permute-start(s32[1,2,2,2]{3,2,1,0:T(2,128)} %bitcast.60), channel_id=1, source_target_pairs={{0,2},{1,3},{2,0},{3,1},{4,6},{5,7},{6,4},{7,5},{8,10},{9,11},{10,... | collective-permute-start | bytes 104 | tf_op jit(solution)/shard_map/ppermute | solution.py:204
  4.0 0.7 copy-start.6
  4.7 0.7 copy-start.7
  5.0 25.9 %copy-start.5 = (bf16[392,768]{1,0:T(8,128)(2,1)}, bf16[392,768]{1,0:T(8,128)(2,1)S(1)}, u32[]{:S(2)}) copy-start(bf16[392,768]{1,0:T(8,128)(2,1)S(1)} %get-tuple-element.52) | copy-start | bytes 1806340
  5.4 4.9 %collective-permute-start.1 = (s32[2,2,2,2]{3,2,1,0:T(2,128)S(1)}, s32[2,2,2,2]{3,2,1,0:T(2,128)S(1)}, u32[]{:S(2)}, u32[]{:S(2)}) collective-permute-start(s32[2,2,2,2]{3,2,1,0:T(2,128)S(1)} %pad_add_fusion.1), channel_id=1, source_target_pairs={{0,4},{1,5},{2,6},{3,7},{4,0},{5,1},{6,2},{7,3},{8,12},{9,13},{10,... | collective-permute-start | bytes 200 | tf_op jit(solution)/shard_map/ppermute | solution.py:204
  10.2 20.7 %collective-permute-start.2 = (bf16[392,768]{1,0:T(8,128)(2,1)S(1)}, bf16[392,768]{1,0:T(8,128)(2,1)S(1)}, u32[]{:S(2)}, u32[]{:S(2)}) collective-permute-start(bf16[392,768]{1,0:T(8,128)(2,1)S(1)} %get-tuple-element.34), channel_id=1, source_target_pairs={{0,8},{1,9},{2,10},{3,11},{4,12},{5,13},{6,14},{7,15},{8,16},{9,17... | collective-permute-start | bytes 1806344 | tf_op jit(solution)/shard_map/ppermute | solution.py:27
  11.4 19.5 %collective-permute-start.3 = (bf16[392,768]{1,0:T(8,128)(2,1)S(1)}, bf16[392,768]{1,0:T(8,128)(2,1)}, u32[]{:S(2)}, u32[]{:S(2)}) collective-permute-start(bf16[392,768]{1,0:T(8,128)(2,1)S(1)} %get-tuple-element.34), channel_id=1, source_target_pairs={{0,24},{1,25},{2,26},{3,27},{4,28},{5,29},{6,30},{7,31},{8,0},{9,1... | collective-permute-start | bytes 1806344 | tf_op jit(solution)/shard_map/ppermute | solution.py:27
  12.2 18.4 %collective-permute-start.4 = (s32[4,2,2,2]{3,2,1,0:T(2,128)S(1)}, s32[4,2,2,2]{3,2,1,0:T(2,128)S(1)}, u32[]{:S(2)}, u32[]{:S(2)}) collective-permute-start(s32[4,2,2,2]{3,2,1,0:T(2,128)S(1)} %pad_add_fusion), channel_id=1, source_target_pairs={{0,1},{1,0},{2,3},{3,2},{4,5},{5,4},{6,7},{7,6},{8,9},{9,8},{10,11... | collective-permute-start | bytes 392 | tf_op jit(solution)/shard_map/ppermute | solution.py:204
  12.4 60.9 %copy-start.3 = (s32[2,2]{1,0:T(2,128)S(1)}, s32[2,2]{1,0:T(2,128)}, u32[]{:S(2)}) copy-start(s32[2,2]{1,0:T(2,128)} %conserve.7) | copy-start | bytes 52
  12.4 60.9 %copy-start.4 = (f32[8]{0:T(128)S(1)}, f32[8]{0:T(128)}, u32[]{:S(2)}) copy-start(f32[8]{0:T(128)} %occupied.7) | copy-start | bytes 100
  21.7 13.3 %collective-permute-start.5 = (bf16[392,768]{1,0:T(8,128)(2,1)S(1)}, bf16[392,768]{1,0:T(8,128)(2,1)}, u32[]{:S(2)}, u32[]{:S(2)}) collective-permute-start(bf16[392,768]{1,0:T(8,128)(2,1)S(1)} %get-tuple-element.52), channel_id=1, source_target_pairs={{24,38},{25,39},{26,36},{27,37},{28,34},{29,35},{30,32},{31,33},{5... | collective-permute-start | bytes 1806344 | tf_op jit(solution)/shard_map/ppermute | solution.py:27
  23.2 47.2 %collective-permute-start.6 = (bf16[392,768]{1,0:T(8,128)(2,1)S(1)}, bf16[392,768]{1,0:T(8,128)(2,1)S(1)}, u32[]{:S(2)}, u32[]{:S(2)}) collective-permute-start(bf16[392,768]{1,0:T(8,128)(2,1)S(1)} %get-tuple-element.52), channel_id=1, source_target_pairs={{16,38},{17,39},{18,36},{19,37},{20,34},{21,35},{22,32},{23,33},{4... | collective-permute-start | bytes 1806344 | tf_op jit(solution)/shard_map/ppermute | solution.py:27
  30.9 39.4 %collective-permute-start.7 = (bf16[392,768]{1,0:T(8,128)(2,1)S(1)}, bf16[392,768]{1,0:T(8,128)(2,1)S(1)}, u32[]{:S(2)}, u32[]{:S(2)}) collective-permute-start(bf16[392,768]{1,0:T(8,128)(2,1)S(1)} %get-tuple-element.52), channel_id=1, source_target_pairs={{0,8},{1,9},{2,10},{3,11},{4,12},{5,13},{6,14},{7,15},{8,16},{9,17... | collective-permute-start | bytes 1806344 | tf_op jit(solution)/shard_map/ppermute | solution.py:27
  34.2 48.8 %collective-permute-start.8 = (bf16[392,768]{1,0:T(8,128)(2,1)}, bf16[392,768]{1,0:T(8,128)(2,1)}, u32[]{:S(2)}, u32[]{:S(2)}) collective-permute-start(bf16[392,768]{1,0:T(8,128)(2,1)} %collective-permute-done.3), channel_id=1, source_target_pairs={{0,24},{1,25},{2,26},{3,27},{4,28},{5,29},{6,30},{7,31},{8,38},{9,... | collective-permute-start | bytes 1806344 | tf_op jit(solution)/shard_map/ppermute | solution.py:27
  34.3 57.9 %collective-permute-start.13 = (bf16[392,768]{1,0:T(8,128)(2,1)S(1)}, bf16[392,768]{1,0:T(8,128)(2,1)S(1)}, u32[]{:S(2)}, u32[]{:S(2)}) collective-permute-start(bf16[392,768]{1,0:T(8,128)(2,1)S(1)} %collective-permute-done.2.refs_1_), channel_id=1, source_target_pairs={{0,38},{1,39},{2,36},{3,37},{4,34},{5,35},{6,32},{7,33},{32,70},{3... | collective-permute-start | bytes 1806344 | tf_op jit(solution)/shard_map/ppermute | solution.py:27
  70.3 0.9 copy-start.1
  71.2 21.0 %collective-permute-start.14 = (bf16[392,768]{1,0:T(8,128)(2,1)}, bf16[392,768]{1,0:T(8,128)(2,1)S(1)}, u32[]{:S(2)}, u32[]{:S(2)}) collective-permute-start(bf16[392,768]{1,0:T(8,128)(2,1)} %collective-permute-done.5.refs_0_), channel_id=1, source_target_pairs={{0,8},{1,9},{2,10},{3,11},{4,12},{5,13},{6,14},{7,15},{32,40},{33,... | collective-permute-start | bytes 1806344 | tf_op jit(solution)/shard_map/ppermute | solution.py:27
  71.9 44.7 %collective-permute-start.15 = (bf16[392,768]{1,0:T(8,128)(2,1)}, bf16[392,768]{1,0:T(8,128)(2,1)S(1)}, u32[]{:S(2)}, u32[]{:S(2)}) collective-permute-start(bf16[392,768]{1,0:T(8,128)(2,1)} %copy-done.5), channel_id=1, source_target_pairs={{0,16},{1,17},{2,18},{3,19},{4,20},{5,21},{6,22},{7,23},{8,24},{9,... | collective-permute-start | bytes 1806344 | tf_op jit(solution)/shard_map/ppermute | solution.py:27
  73.3 3.7 %copy-start = (bf16[2,8,2,192,768]{4,3,2,1,0:T(8,128)(2,1)S(1)}, bf16[2,8,2,192,768]{4,3,2,1,0:T(8,128)(2,1)}, u32[]{:S(2)}) copy-start(bf16[2,8,2,192,768]{4,3,2,1,0:T(8,128)(2,1)} %copy.17) | copy-start | bytes 28311556
  77.0 1.1 copy-start.2
  92.1 33.5 %collective-permute-start.9 = (f32[4,2,24,192]{3,2,1,0:T(8,128)S(1)}, f32[4,2,24,192]{3,2,1,0:T(8,128)S(1)}, u32[]{:S(2)}, u32[]{:S(2)}) collective-permute-start(f32[4,2,24,192]{3,2,1,0:T(8,128)S(1)} %get-tuple-element.51), channel_id=1, source_target_pairs={{0,1},{1,0},{2,3},{3,2},{4,5},{5,4},{6,7},{7,6},{8,9},{9,8},{10,11... | collective-permute-start | bytes 442376 | tf_op jit(solution)/shard_map/ppermute | solution.py:194
  121.0 8.7 %collective-permute-start.16 = (f32[4,2,24,192]{3,2,1,0:T(8,128)S(1)}, f32[4,2,24,192]{3,2,1,0:T(8,128)S(1)}, u32[]{:S(2)}, u32[]{:S(2)}) collective-permute-start(f32[4,2,24,192]{3,2,1,0:T(8,128)S(1)} %get-tuple-element.56), channel_id=1, source_target_pairs={{0,1},{1,0},{2,3},{3,2},{4,5},{5,4},{6,7},{7,6},{8,9},{9,8},{10,11... | collective-permute-start | bytes 442376 | tf_op jit(solution)/shard_map/ppermute | solution.py:194
  125.7 6.5 %collective-permute-start.10 = (f32[2,24,192]{2,1,0:T(8,128)S(1)}, f32[2,24,192]{2,1,0:T(8,128)S(1)}, u32[]{:S(2)}, u32[]{:S(2)}) collective-permute-start(f32[2,24,192]{2,1,0:T(8,128)S(1)} %get-tuple-element.59), channel_id=1, source_target_pairs={{0,2},{1,3},{2,4},{3,5},{4,6},{5,7},{6,0},{7,1},{8,10},{9,11},{10,... | collective-permute-start | bytes 110600 | tf_op jit(solution)/shard_map/ppermute | solution.py:199
  125.8 8.9 %collective-permute-start.11 = (f32[2,24,192]{2,1,0:T(8,128)S(1)}, f32[2,24,192]{2,1,0:T(8,128)S(1)}, u32[]{:S(2)}, u32[]{:S(2)}) collective-permute-start(f32[2,24,192]{2,1,0:T(8,128)S(1)} %get-tuple-element.61), channel_id=1, source_target_pairs={{0,4},{1,5},{2,6},{3,7},{4,0},{5,1},{6,2},{7,3},{8,12},{9,13},{10,... | collective-permute-start | bytes 110600 | tf_op jit(solution)/shard_map/ppermute | solution.py:199
  126.5 8.3 %collective-permute-start.12 = (f32[2,24,192]{2,1,0:T(8,128)S(1)}, f32[2,24,192]{2,1,0:T(8,128)S(1)}, u32[]{:S(2)}, u32[]{:S(2)}) collective-permute-start(f32[2,24,192]{2,1,0:T(8,128)S(1)} %get-tuple-element.60), channel_id=1, source_target_pairs={{0,6},{1,7},{2,0},{3,1},{4,2},{5,3},{6,4},{7,5},{8,14},{9,15},{10,... | collective-permute-start | bytes 110600 | tf_op jit(solution)/shard_map/ppermute | solution.py:199
  129.7 6.4 %collective-permute-start.17 = (f32[2,24,192]{2,1,0:T(8,128)S(1)}, f32[2,24,192]{2,1,0:T(8,128)S(1)}, u32[]{:S(2)}, u32[]{:S(2)}) collective-permute-start(f32[2,24,192]{2,1,0:T(8,128)S(1)} %get-tuple-element.62), channel_id=1, source_target_pairs={{0,2},{1,3},{2,4},{3,5},{4,6},{5,7},{6,0},{7,1},{8,10},{9,11},{10,... | collective-permute-start | bytes 110600 | tf_op jit(solution)/shard_map/ppermute | solution.py:199
  130.3 7.1 %collective-permute-start.18 = (f32[2,24,192]{2,1,0:T(8,128)S(1)}, f32[2,24,192]{2,1,0:T(8,128)S(1)}, u32[]{:S(2)}, u32[]{:S(2)}) collective-permute-start(f32[2,24,192]{2,1,0:T(8,128)S(1)} %get-tuple-element.64), channel_id=1, source_target_pairs={{0,4},{1,5},{2,6},{3,7},{4,0},{5,1},{6,2},{7,3},{8,12},{9,13},{10,... | collective-permute-start | bytes 110600 | tf_op jit(solution)/shard_map/ppermute | solution.py:199
  132.2 5.2 %collective-permute-start.19 = (f32[2,24,192]{2,1,0:T(8,128)S(1)}, f32[2,24,192]{2,1,0:T(8,128)S(1)}, u32[]{:S(2)}, u32[]{:S(2)}) collective-permute-start(f32[2,24,192]{2,1,0:T(8,128)S(1)} %get-tuple-element.63), channel_id=1, source_target_pairs={{0,6},{1,7},{2,0},{3,1},{4,2},{5,3},{6,4},{7,5},{8,14},{9,15},{10,... | collective-permute-start | bytes 110600 | tf_op jit(solution)/shard_map/ppermute | solution.py:199

commit v7 on v6

--- a/solution.py
+++ b/solution.py
@@ -18,21 +18,34 @@
 def moved(array, moves):
     pairs = []
     for row in range(ROWS):
-        for column, (goal, crosses) in moves.items():
+        for column, (goal, next_row) in moves.items():
+            goal_row = next_row(row)
             for place in range(LINE):
                 for core in range(CORES):
                     source = device_index(row, column, place, core)
-                    end = LINE - 1 - place if crosses else place
-                    pairs.append((source, device_index(row + crosses, goal, end, core)))
+                    end = place if (goal_row - row) % 2 == 0 else LINE - 1 - place
+                    pairs.append((source, device_index(goal_row, goal, end, core)))
     return lax.ppermute(array, ("ka", "occ"), pairs)
 
 
-def finished(column, conserve):
-    return jnp.where(column == 0, lax.rem(conserve[0, 0], 2), 1 - lax.rem(conserve[0, 1], 2))
+def same(row):
+    return row
+
+
+def onto_next(row):
+    return row + 1
+
+
+def beside_next(row):
+    return row + 2 * (row % 2)
+
+
+def across(row):
+    return row ^ 1
 
 
 def piece_kernel(
-    sources, before_count, kind, order, conserve, pairs, here, occupied, own_energy, left, *refs
+    sources, before_count, order, conserve, pairs, here, occupied, own_energy, left, *refs
 ):
     mates, refs = refs[:sources], refs[sources:]
     before, refs = refs[:before_count], refs[before_count:]
@@ -127,46 +140,28 @@
         total[part] = lax.dot_general(
             combined[...], right[...], contract_rows, preferred_element_type=jnp.float32
         )
-    done = finished(column, conserve)
     for place in range(LINE):
         for number, offset in enumerate((core, 1 - core)):
             cut = pl.ds(pl.multiple_of((place * CORES + offset) * share, 8), share)
             value = total[:, cut]
-            if kind == "first":
-                for local_index in range(2):
-                    outs[number][local_index, place] = jnp.where(mine == local_index, value, 0.0)
-            elif kind == "second":
-                for local_index in range(2):
-                    outs[number][local_index, place] = before[number][local_index, place] + jnp.where(
-                        mine == local_index, value, 0.0
-                    )
-            elif kind == "third":
-                for slot, which in enumerate((done, 1 - done)):
-                    outs[2 * slot + number][place] = before[number][which, place] + jnp.where(
-                        mine == which, value, 0.0
-                    )
-            else:
-                outs[number][place] = before[number][place] + value
-
-
-def piece_density(kind, order, conserve, pairs, here, occupied, own_energy, left, mates, before):
+            for local_index in range(2):
+                added = jnp.where(mine == local_index, value, 0.0)
+                if before:
+                    added = added + before[number][place, local_index]
+                outs[number][place, local_index] = added
+
+
+def piece_density(order, conserve, pairs, here, occupied, own_energy, left, mates, before):
     momenta, orbitals, both, auxiliary = left.shape
     virtuals = both // 2
     share = virtuals // (LINE * CORES)
     count = pairs.shape[0] * pairs.shape[2]
     rows = 2 * orbitals * share
-    whole_block = jax.ShapeDtypeStruct((momenta, LINE, 2, share, virtuals), jnp.float32)
-    block = jax.ShapeDtypeStruct((LINE, 2, share, virtuals), jnp.float32)
-    out_shape = {
-        "first": (whole_block,) * 2,
-        "second": (whole_block,) * 2,
-        "third": (block,) * 4,
-        "fourth": (block,) * 2,
-    }[kind]
+    out_shape = (jax.ShapeDtypeStruct((LINE, momenta, 2, share, virtuals), jnp.float32),) * 2
     scalars = pl.BlockSpec(memory_space=pltpu.SMEM)
     whole = pl.BlockSpec(memory_space=pltpu.VMEM)
     return pl.pallas_call(
-        functools.partial(piece_kernel, len(mates), len(before), kind, order),
+        functools.partial(piece_kernel, len(mates), len(before), order),
         out_shape=out_shape,
         in_specs=[scalars] * 4
         + [whole] * (2 + len(mates) + len(before)),
@@ -179,7 +174,7 @@
             pltpu.VMEM((2 * count * share, virtuals), jnp.bfloat16),
             pltpu.VMEM((2, virtuals, virtuals), jnp.float32),
         ],
-        compiler_params=pltpu.CompilerParams(vmem_limit_bytes=40 << 20),
+        compiler_params=pltpu.CompilerParams(vmem_limit_bytes=32 << 20),
         cost_estimate=pl.CostEstimate(
             flops=4 * rows * virtuals * auxiliary * orbitals + 8 * count * share * virtuals * virtuals,
             bytes_accessed=orbitals * both * auxiliary * 2 + 2 * rows * auxiliary,
@@ -221,44 +216,37 @@
         first = jnp.broadcast_to(start.astype(jnp.bfloat16), (HEAD - 1, auxiliary))
         return jnp.concatenate([cut, energy, first], axis=0)
 
-    pairs = with_partner(with_partner(pair_lists[None], CORES), 2 * CORES)
+    pairs = with_partner(pair_lists[None], CORES)
     m0 = outgoing(0)
     m1 = outgoing(1)
     m0, m1, pairs, factors, here = lax.optimization_barrier((m0, m1, pairs, factors, here))
-    plus = moved(m1, {c: ((c + 1) % COLUMNS, False) for c in range(COLUMNS)})
-    minus = moved(m1, {c: ((c - 1) % COLUMNS, False) for c in range(COLUMNS)})
+    plus = moved(m1, {0: (1, same), 1: (2, same), 2: (3, same), 3: (0, beside_next)})
+    minus = moved(m1, {0: (3, same), 1: (0, same), 2: (1, beside_next), 3: (2, beside_next)})
+    pairs = with_partner(pairs, 2 * CORES)
     left = jnp.transpose(factors, (0, 1, 3, 2, 4)).reshape(momenta, orbitals, 2 * virtuals, auxiliary)
-    m0, left = lax.optimization_barrier((m0, left))
-    cross_one = moved(m0, {3: (0, True)})
-    cross_two = moved(m0, {2: (0, True)})
+    m0, left, pairs = lax.optimization_barrier((m0, left, pairs))
+    cross_one = moved(m0, {3: (0, onto_next)})
+    cross_two = moved(m0, {2: (0, onto_next)})
     pairs = with_partner(pairs, 1)
     own_energy = virtual_energy.astype(jnp.float32)[:, None, :]
     m0, plus, minus, pairs, own_energy = lax.optimization_barrier((m0, plus, minus, pairs, own_energy))
-    up = moved(plus, {0: (0, True)})
-    back = moved(minus, {0: (3, False), 1: (0, True), 2: (1, True), 3: (2, False)})
-    near_one = moved(m0, {0: (1, False), 1: (2, False), 2: (3, False)})
-    m0, cross_one, cross_two, near_one = lax.optimization_barrier((m0, cross_one, cross_two, near_one))
-    onward = moved(cross_one, {0: (1, False)})
-    near_two = moved(m0, {0: (2, False), 1: (3, False)})
-
-    def density(kind, order, mates, before):
+    up = moved(plus, {0: (0, across)})
+    back = moved(minus, {0: (3, same), 1: (0, across), 2: (1, across), 3: (2, same)})
+    near_one = moved(m0, {0: (1, same), 1: (2, same), 2: (3, same)})
+    m0, cross_one, near_one = lax.optimization_barrier((m0, cross_one, near_one))
+    onward = moved(cross_one, {0: (1, same)})
+    near_two = moved(m0, {0: (2, same), 1: (3, same)})
+
+    def density(order, mates, before):
         return piece_density(
-            kind, order, conserve, pairs, here, occupied_energy, own_energy, left, mates, before
-        )
-
-    total = density("first", ((0,), (0,), (0, 1)), (cross_one, near_one), ())
-    total = density("second", ((1,), (1,), (0,)), (back,), total)
-    keep_a, send_a, keep_b, send_b = density(
-        "third", ((1, 0), (0, 1), (0, 1)), (cross_two, plus), total
-    )
-    keep_b, send_b = density(
-        "fourth", ((0, 1), (1, 0), (0, 1, 2)), (up, onward, near_two), (keep_b, send_b)
-    )
-    done = summed(keep_a, send_a)
-    last = summed(keep_b, send_b)
-    done_first = finished(column, conserve) == 0
-    result = jnp.where(done_first, jnp.stack([done, last]), jnp.stack([last, done]))
-    return jnp.transpose(result, (0, 2, 1, 3))
+            order, conserve, pairs, here, occupied_energy, own_energy, left, mates, before
+        )
+
+    total = density(((0,), (0,), (0, 1)), (cross_one, near_one), ())
+    total = density(((1, 0), (0, 1), (0, 1)), (cross_two, plus), total)
+    total = density(((1,), (1,), (0,)), (back,), total)
+    total = density(((0, 1), (1, 0), (0, 1, 2)), (up, onward, near_two), total)
+    return jnp.transpose(summed(*total), (0, 2, 1, 3))
 
 
 def solution(mesh):

time: 139 us -> 110 us (0.79)
  the two profiles are of different devices: /device:TPU:4 before, /device:TPU:10 now
where the time goes in v7:
time: 110 us
  starting transfers between devices  45.8 us (42%)
  waiting for transfers between devices  25.5 us (23%)
  local copies, waits for them, and re-layouts  18.8 us (17%)
  Pallas kernels  18.1 us (16%)
  other arithmetic  1.31 us (1%)
    ppermute x9, starting transfers between devices, moved(): return lax.ppermute(array, ('ka', 'occ'), pairs)  36.5 us
    pallas_call x4, Pallas kernels, piece_density(): pl.pallas_call(functools.partial(piece_kernel, len(mates), len(before), o...  18.1 us
    ppermute x9, waiting for transfers between devices, moved(): return lax.ppermute(array, ('ka', 'occ'), pairs)  16.8 us
    transpose x1, local copies, waits for them, and re-layouts, local(): jnp.transpose(factors, (0, 1, 3, 2, 4))  9.32 us
    ppermute x3, waiting for transfers between devices, summed(): total = total + lax.ppermute(part, 'occ', ring)  7.01 us
    unnamed x14, local copies, waits for them, and re-layouts  6.13 us
    ppermute x3, starting transfers between devices, with_partner(): lax.ppermute(array, 'occ', [(i, i ^ reach) for i in range(LINE * CORES)])  5.28 us
    ppermute x3, starting transfers between devices, summed(): total = total + lax.ppermute(part, 'occ', ring)  3.9 us
  transfers between devices with their start and end apart: 16, of which 5 were waited for; matrix products, arithmetic and copies ran while one was open for 12% of the time, Pallas kernels for 12%

profile of v7, /device:TPU:10, one launch (start us, length us, event | category | flops | bytes accessed | tf_op | source)
XLA Modules:
  0.0 109.7 jit_solution(1832891490147662959)
XLA Ops:
  0.0 1.9 %collective-permute-start = (s32[1,2,2,2]{3,2,1,0:T(2,128)}, s32[1,2,2,2]{3,2,1,0:T(2,128)S(1)}, u32[]{:S(2)}, u32[]{:S(2)}) collective-permute-start(s32[1,2,2,2]{3,2,1,0:T(2,128)} %bitcast.40), channel_id=1, source_target_pairs={{0,2},{1,3},{2,0},{3,1},{4,6},{5,7},{6,4},{7,5},{8,10},{9,11},{10,... | collective-permute-start | bytes 104 | tf_op jit(solution)/shard_map/ppermute | solution.py:199
  1.9 2.1 %constant_dynamic-slice_fusion = (bf16[1,8,24,2,768]{4,3,2,1,0:T(2,128)(2,1)S(1)}, bf16[1,8,24,2,768]{4,3,2,1,0:T(2,128)(2,1)S(1)}) fusion(bf16[2,8,192,2,768]{4,3,2,1,0:T(2,128)(2,1)} %param.5, s32[]{:T(128)S(6)} %select_n.44), kind=kLoop, calls=%fused_computation.19 | loop fusion | bytes 2359300 | tf_op jit(solution)/shard_map/dynamic_slice | solution.py:211
  4.0 0.0 copy-start.5
  4.0 0.1 copy.27
  4.1 0.1 copy.28
  4.1 0.5 copy-done.5
  4.7 0.1 pad_add_fusion.3.here
  4.7 0.1 pad.22.clone
  4.8 1.1 fusion.6
  5.9 0.0 collective-permute-done
  5.9 1.6 %collective-permute-start.2 = (bf16[392,768]{1,0:T(8,128)(2,1)S(1)}, bf16[392,768]{1,0:T(8,128)(2,1)S(1)}, u32[]{:S(2)}, u32[]{:S(2)}) collective-permute-start(bf16[392,768]{1,0:T(8,128)(2,1)S(1)} %get-tuple-element.33), channel_id=1, source_target_pairs={{0,8},{1,9},{2,10},{3,11},{4,12},{5,13},{6,14},{7,15},{8,16},{9,17... | collective-permute-start | bytes 1806344 | tf_op jit(solution)/shard_map/ppermute | solution.py:28
  7.5 0.5 collective-permute-start.3
  8.0 3.3 %collective-permute-start.1 = (s32[2,2,2,2]{3,2,1,0:T(2,128)S(1)}, s32[2,2,2,2]{3,2,1,0:T(2,128)S(1)}, u32[]{:S(2)}, u32[]{:S(2)}) collective-permute-start(s32[2,2,2,2]{3,2,1,0:T(2,128)S(1)} %pad_add_fusion.1), channel_id=1, source_target_pairs={{0,4},{1,5},{2,6},{3,7},{4,0},{5,1},{6,2},{7,3},{8,12},{9,13},{10,... | collective-permute-start | bytes 200 | tf_op jit(solution)/shard_map/ppermute | solution.py:199
  11.3 9.3 %copy.17 = bf16[2,8,2,192,768]{4,3,2,1,0:T(8,128)(2,1)} copy(bf16[2,8,2,192,768]{4,2,3,1,0:T(2,128)(2,1)} %bitcast.37) | data formatting | bytes 18874368 | tf_op jit(solution)/shard_map/transpose | solution.py:226
  20.6 0.1 collective-permute-start.4
  20.7 0.1 copy.18
  20.8 1.5 %collective-permute-start.6 = (bf16[392,768]{1,0:T(8,128)(2,1)}, bf16[392,768]{1,0:T(8,128)(2,1)}, u32[]{:S(2)}, u32[]{:S(2)}) collective-permute-start(bf16[392,768]{1,0:T(8,128)(2,1)} %get-tuple-element.42), channel_id=1, source_target_pairs={{24,38},{25,39},{26,36},{27,37},{28,34},{29,35},{30,32},{31,33},{5... | collective-permute-start | bytes 1806344 | tf_op jit(solution)/shard_map/ppermute | solution.py:28
  22.3 0.0 collective-permute-done.4
  22.3 0.1 copy.19
  22.5 0.1 pad_add_fusion.2
  22.5 0.0 collective-permute-done.2.refs_1_
  22.5 0.0 collective-permute-done.3
  22.5 3.4 %collective-permute-start.7 = (bf16[392,768]{1,0:T(8,128)(2,1)}, bf16[392,768]{1,0:T(8,128)(2,1)S(1)}, u32[]{:S(2)}, u32[]{:S(2)}) collective-permute-start(bf16[392,768]{1,0:T(8,128)(2,1)} %get-tuple-element.42), channel_id=1, source_target_pairs={{0,8},{1,9},{2,10},{3,11},{4,12},{5,13},{6,14},{7,15},{8,16},{9,17... | collective-permute-start | bytes 1806344 | tf_op jit(solution)/shard_map/ppermute | solution.py:28
  25.9 0.7 collective-permute-start.11
  26.6 6.3 %collective-permute-start.10 = (bf16[392,768]{1,0:T(8,128)(2,1)}, bf16[392,768]{1,0:T(8,128)(2,1)}, u32[]{:S(2)}, u32[]{:S(2)}) collective-permute-start(bf16[392,768]{1,0:T(8,128)(2,1)} %collective-permute-done.3), channel_id=1, source_target_pairs={{0,24},{1,25},{2,26},{3,27},{4,28},{5,29},{6,30},{7,31},{8,38},{9,... | collective-permute-start | bytes 1806344 | tf_op jit(solution)/shard_map/ppermute | solution.py:28
  33.0 0.7 collective-permute-start.5
  33.7 0.0 collective-permute-done.6.refs_0_
  33.7 6.9 %collective-permute-done.7.refs_1_ = bf16[392,768]{1,0:T(8,128)(2,1)S(1)} collective-permute-done((bf16[392,768]{1,0:T(8,128)(2,1)}, bf16[392,768]{1,0:T(8,128)(2,1)S(1)}, u32[]{:S(2)}, u32[]{:S(2)}) %collective-permute-start.7) | collective-permute-done | bytes 602144 | tf_op jit(solution)/shard_map/ppermute | solution.py:28
  40.6 0.8 copy-done.1
  41.5 1.3 %collective-permute-start.8 = (bf16[392,768]{1,0:T(8,128)(2,1)}, bf16[392,768]{1,0:T(8,128)(2,1)S(1)}, u32[]{:S(2)}, u32[]{:S(2)}) collective-permute-start(bf16[392,768]{1,0:T(8,128)(2,1)} %collective-permute-done.6.refs_0_), channel_id=1, source_target_pairs={{0,8},{1,9},{2,10},{3,11},{4,12},{5,13},{6,14},{7,15},{32,40},{33,... | collective-permute-start | bytes 1806344 | tf_op jit(solution)/shard_map/ppermute | solution.py:28
  42.8 20.5 %collective-permute-start.9 = (bf16[392,768]{1,0:T(8,128)(2,1)}, bf16[392,768]{1,0:T(8,128)(2,1)S(1)}, u32[]{:S(2)}, u32[]{:S(2)}) collective-permute-start(bf16[392,768]{1,0:T(8,128)(2,1)} %get-tuple-element.42), channel_id=1, source_target_pairs={{0,16},{1,17},{2,18},{3,19},{4,20},{5,21},{6,22},{7,23},{8,24},{9,... | collective-permute-start | bytes 1806344 | tf_op jit(solution)/shard_map/ppermute | solution.py:28
  63.3 0.1 copy.23.pairs
  63.4 3.7 %copy-done = bf16[2,8,2,192,768]{4,3,2,1,0:T(8,128)(2,1)S(1)} copy-done((bf16[2,8,2,192,768]{4,3,2,1,0:T(8,128)(2,1)S(1)}, bf16[2,8,2,192,768]{4,3,2,1,0:T(8,128)(2,1)}, u32[]{:S(2)}) %copy-start) | copy-done | bytes 9437208
  67.1 1.1 copy-done.2
  68.2 4.6 %shard_map.55 = (f32[4,2,2,24,192]{4,3,2,1,0:T(8,128)S(1)}, f32[4,2,2,24,192]{4,3,2,1,0:T(8,128)S(1)}) custom-call(s32[2,2]{1,0:T(2,128)S(1)} %copy-done.3, s32[8,2,2,2]{3,2,1,0:T(2,128)S(1)} %copy.23.pairs, s32[2]{0:T(128)S(1)} %pad_add_fusion.3.here, f32[8]{0:T(128)S(1)} %copy-done.4, f32[2,1,192]{2,1,0:T(1,128)S(1)} %reshape.12.own_energy, ...), custom_call_target="tpu_custom_call" | custom-call | flops 1925185536 | bytes 5308416 | tf_op jit(solution)/shard_map/pallas_call | solution.py:163
  72.8 4.6 %shard_map.56 = (f32[4,2,2,24,192]{4,3,2,1,0:T(8,128)S(1)}, f32[4,2,2,24,192]{4,3,2,1,0:T(8,128)S(1)}) custom-call(s32[2,2]{1,0:T(2,128)S(1)} %copy-done.3, s32[8,2,2,2]{3,2,1,0:T(2,128)S(1)} %copy.23.pairs, s32[2]{0:T(128)S(1)} %pad_add_fusion.3.here, f32[8]{0:T(128)S(1)} %copy-done.4, f32[2,1,192]{2,1,0:T(1,128)S(1)} %reshape.12.own_energy, ...), custom_call_target="tpu_custom_call" | custom-call | flops 1925185536 | bytes 5308416 | tf_op jit(solution)/shard_map/pallas_call | solution.py:163
  77.3 9.9 %collective-permute-done.10.refs_0_ = bf16[392,768]{1,0:T(8,128)(2,1)} collective-permute-done((bf16[392,768]{1,0:T(8,128)(2,1)}, bf16[392,768]{1,0:T(8,128)(2,1)}, u32[]{:S(2)}, u32[]{:S(2)}) %collective-permute-start.10) | collective-permute-done | bytes 602144 | tf_op jit(solution)/shard_map/ppermute | solution.py:28
  87.2 4.6 %shard_map.57 = (f32[4,2,2,24,192]{4,3,2,1,0:T(8,128)S(1)}, f32[4,2,2,24,192]{4,3,2,1,0:T(8,128)S(1)}) custom-call(s32[2,2]{1,0:T(2,128)S(1)} %copy-done.3, s32[8,2,2,2]{3,2,1,0:T(2,128)S(1)} %copy.23.pairs, s32[2]{0:T(128)S(1)} %pad_add_fusion.3.here, f32[8]{0:T(128)S(1)} %copy-done.4, f32[2,1,192]{2,1,0:T(1,128)S(1)} %reshape.12.own_energy, ...), custom_call_target="tpu_custom_call" | custom-call | flops 1925185536 | bytes 5308416 | tf_op jit(solution)/shard_map/pallas_call | solution.py:163
  91.8 4.4 %shard_map.58 = (f32[4,2,2,24,192]{4,3,2,1,0:T(8,128)S(1)}, f32[4,2,2,24,192]{4,3,2,1,0:T(8,128)S(1)}) custom-call(s32[2,2]{1,0:T(2,128)S(1)} %copy-done.3, s32[8,2,2,2]{3,2,1,0:T(2,128)S(1)} %copy.23.pairs, s32[2]{0:T(128)S(1)} %pad_add_fusion.3.here, f32[8]{0:T(128)S(1)} %copy-done.4, f32[2,1,192]{2,1,0:T(1,128)S(1)} %reshape.12.own_energy, ...), custom_call_target="tpu_custom_call" | custom-call | flops 1925185536 | bytes 5308416 | tf_op jit(solution)/shard_map/pallas_call | solution.py:163
  96.2 0.1 collective-permute-start.12
  96.4 1.6 %collective-permute-done.12 = f32[4,2,2,24,192]{4,3,2,1,0:T(8,128)S(1)} collective-permute-done((f32[4,2,2,24,192]{4,3,2,1,0:T(8,128)S(1)}, f32[4,2,2,24,192]{4,3,2,1,0:T(8,128)S(1)}, u32[]{:S(2)}, u32[]{:S(2)}) %collective-permute-start.12) | collective-permute-done | bytes 294944 | tf_op jit(solution)/shard_map/ppermute | solution.py:189
  98.0 0.1 add.62
  98.1 0.1 collective-permute-start.13
  98.2 0.9 collective-permute-start.14
  99.1 2.9 %collective-permute-start.15 = (f32[2,2,24,192]{3,2,1,0:T(8,128)S(1)}, f32[2,2,24,192]{3,2,1,0:T(8,128)S(1)}, u32[]{:S(2)}, u32[]{:S(2)}) collective-permute-start(f32[2,2,24,192]{3,2,1,0:T(8,128)S(1)} %get-tuple-element.56), channel_id=1, source_target_pairs={{0,6},{1,7},{2,0},{3,1},{4,2},{5,3},{6,4},{7,5},{8,14},{9,15},{10,... | collective-permute-start | bytes 221192 | tf_op jit(solution)/shard_map/ppermute | solution.py:194
  102.0 3.7 %collective-permute-done.13 = f32[2,2,24,192]{3,2,1,0:T(8,128)S(1)} collective-permute-done((f32[2,2,24,192]{3,2,1,0:T(8,128)S(1)}, f32[2,2,24,192]{3,2,1,0:T(8,128)S(1)}, u32[]{:S(2)}, u32[]{:S(2)}) %collective-permute-start.13) | collective-permute-done | bytes 73760 | tf_op jit(solution)/shard_map/ppermute | solution.py:194
  105.7 3.3 %collective-permute-done.14 = f32[2,2,24,192]{3,2,1,0:T(8,128)S(1)} collective-permute-done((f32[2,2,24,192]{3,2,1,0:T(8,128)S(1)}, f32[2,2,24,192]{3,2,1,0:T(8,128)S(1)}, u32[]{:S(2)}, u32[]{:S(2)}) %collective-permute-start.14) | collective-permute-done | bytes 73760 | tf_op jit(solution)/shard_map/ppermute | solution.py:194
  109.0 0.7 copy.24
  (22 shorter events, 0.1 us)
Async XLA Ops:
  0.0 5.9 %collective-permute-start = (s32[1,2,2,2]{3,2,1,0:T(2,128)}, s32[1,2,2,2]{3,2,1,0:T(2,128)S(1)}, u32[]{:S(2)}, u32[]{:S(2)}) collective-permute-start(s32[1,2,2,2]{3,2,1,0:T(2,128)} %bitcast.40), channel_id=1, source_target_pairs={{0,2},{1,3},{2,0},{3,1},{4,6},{5,7},{6,4},{7,5},{8,10},{9,11},{10,... | collective-permute-start | bytes 104 | tf_op jit(solution)/shard_map/ppermute | solution.py:199
  4.0 0.7 copy-start.5
  4.7 1.2 %copy-start.6 = (s32[2,2,2]{2,1,0:T(2,128)S(1)}, s32[2,2,2]{2,1,0:T(2,128)}, u32[]{:S(2)}) copy-start(s32[2,2,2]{2,1,0:T(2,128)} %param.9) | copy-start | bytes 100
  5.9 16.6 %collective-permute-start.2 = (bf16[392,768]{1,0:T(8,128)(2,1)S(1)}, bf16[392,768]{1,0:T(8,128)(2,1)S(1)}, u32[]{:S(2)}, u32[]{:S(2)}) collective-permute-start(bf16[392,768]{1,0:T(8,128)(2,1)S(1)} %get-tuple-element.33), channel_id=1, source_target_pairs={{0,8},{1,9},{2,10},{3,11},{4,12},{5,13},{6,14},{7,15},{8,16},{9,17... | collective-permute-start | bytes 1806344 | tf_op jit(solution)/shard_map/ppermute | solution.py:28
  7.5 15.1 %collective-permute-start.3 = (bf16[392,768]{1,0:T(8,128)(2,1)S(1)}, bf16[392,768]{1,0:T(8,128)(2,1)}, u32[]{:S(2)}, u32[]{:S(2)}) collective-permute-start(bf16[392,768]{1,0:T(8,128)(2,1)S(1)} %get-tuple-element.33), channel_id=1, source_target_pairs={{0,24},{1,25},{2,26},{3,27},{4,28},{5,29},{6,30},{7,31},{8,0},{9,1... | collective-permute-start | bytes 1806344 | tf_op jit(solution)/shard_map/ppermute | solution.py:28
  8.0 12.6 %collective-permute-start.1 = (s32[2,2,2,2]{3,2,1,0:T(2,128)S(1)}, s32[2,2,2,2]{3,2,1,0:T(2,128)S(1)}, u32[]{:S(2)}, u32[]{:S(2)}) collective-permute-start(s32[2,2,2,2]{3,2,1,0:T(2,128)S(1)} %pad_add_fusion.1), channel_id=1, source_target_pairs={{0,4},{1,5},{2,6},{3,7},{4,0},{5,1},{6,2},{7,3},{8,12},{9,13},{10,... | collective-permute-start | bytes 200 | tf_op jit(solution)/shard_map/ppermute | solution.py:199
  11.3 52.1 %copy-start.3 = (s32[2,2]{1,0:T(2,128)S(1)}, s32[2,2]{1,0:T(2,128)}, u32[]{:S(2)}) copy-start(s32[2,2]{1,0:T(2,128)} %conserve.7) | copy-start | bytes 52
  11.3 52.1 %copy-start.4 = (f32[8]{0:T(128)S(1)}, f32[8]{0:T(128)}, u32[]{:S(2)}) copy-start(f32[8]{0:T(128)} %occupied.7) | copy-start | bytes 100
  20.6 1.7 %collective-permute-start.4 = (s32[4,2,2,2]{3,2,1,0:T(2,128)S(1)}, s32[4,2,2,2]{3,2,1,0:T(2,128)S(1)}, u32[]{:S(2)}, u32[]{:S(2)}) collective-permute-start(s32[4,2,2,2]{3,2,1,0:T(2,128)S(1)} %pad_add_fusion), channel_id=1, source_target_pairs={{0,1},{1,0},{2,3},{3,2},{4,5},{5,4},{6,7},{7,6},{8,9},{9,8},{10,11... | collective-permute-start | bytes 392 | tf_op jit(solution)/shard_map/ppermute | solution.py:199
  20.8 12.8 %collective-permute-start.6 = (bf16[392,768]{1,0:T(8,128)(2,1)}, bf16[392,768]{1,0:T(8,128)(2,1)}, u32[]{:S(2)}, u32[]{:S(2)}) collective-permute-start(bf16[392,768]{1,0:T(8,128)(2,1)} %get-tuple-element.42), channel_id=1, source_target_pairs={{24,38},{25,39},{26,36},{27,37},{28,34},{29,35},{30,32},{31,33},{5... | collective-permute-start | bytes 1806344 | tf_op jit(solution)/shard_map/ppermute | solution.py:28
  22.5 18.1 %collective-permute-start.7 = (bf16[392,768]{1,0:T(8,128)(2,1)}, bf16[392,768]{1,0:T(8,128)(2,1)S(1)}, u32[]{:S(2)}, u32[]{:S(2)}) collective-permute-start(bf16[392,768]{1,0:T(8,128)(2,1)} %get-tuple-element.42), channel_id=1, source_target_pairs={{0,8},{1,9},{2,10},{3,11},{4,12},{5,13},{6,14},{7,15},{8,16},{9,17... | collective-permute-start | bytes 1806344 | tf_op jit(solution)/shard_map/ppermute | solution.py:28
  25.9 46.8 %collective-permute-start.11 = (bf16[392,768]{1,0:T(8,128)(2,1)}, bf16[392,768]{1,0:T(8,128)(2,1)S(1)}, u32[]{:S(2)}, u32[]{:S(2)}) collective-permute-start(bf16[392,768]{1,0:T(8,128)(2,1)} %get-tuple-element.42), channel_id=1, source_target_pairs={{16,38},{17,39},{18,36},{19,37},{20,34},{21,35},{22,32},{23,33},{4... | collective-permute-start | bytes 1806344 | tf_op jit(solution)/shard_map/ppermute | solution.py:28
  26.6 60.5 %collective-permute-start.10 = (bf16[392,768]{1,0:T(8,128)(2,1)}, bf16[392,768]{1,0:T(8,128)(2,1)}, u32[]{:S(2)}, u32[]{:S(2)}) collective-permute-start(bf16[392,768]{1,0:T(8,128)(2,1)} %collective-permute-done.3), channel_id=1, source_target_pairs={{0,24},{1,25},{2,26},{3,27},{4,28},{5,29},{6,30},{7,31},{8,38},{9,... | collective-permute-start | bytes 1806344 | tf_op jit(solution)/shard_map/ppermute | solution.py:28
  33.0 58.8 %collective-permute-start.5 = (bf16[392,768]{1,0:T(8,128)(2,1)S(1)}, bf16[392,768]{1,0:T(8,128)(2,1)S(1)}, u32[]{:S(2)}, u32[]{:S(2)}) collective-permute-start(bf16[392,768]{1,0:T(8,128)(2,1)S(1)} %collective-permute-done.2.refs_1_), channel_id=1, source_target_pairs={{0,38},{1,39},{2,36},{3,37},{4,34},{5,35},{6,32},{7,33},{32,6},{33... | collective-permute-start | bytes 1806344 | tf_op jit(solution)/shard_map/ppermute | solution.py:28
  40.6 0.8 copy-start.1
  41.5 50.3 %collective-permute-start.8 = (bf16[392,768]{1,0:T(8,128)(2,1)}, bf16[392,768]{1,0:T(8,128)(2,1)S(1)}, u32[]{:S(2)}, u32[]{:S(2)}) collective-permute-start(bf16[392,768]{1,0:T(8,128)(2,1)} %collective-permute-done.6.refs_0_), channel_id=1, source_target_pairs={{0,8},{1,9},{2,10},{3,11},{4,12},{5,13},{6,14},{7,15},{32,40},{33,... | collective-permute-start | bytes 1806344 | tf_op jit(solution)/shard_map/ppermute | solution.py:28
  42.8 49.0 %collective-permute-start.9 = (bf16[392,768]{1,0:T(8,128)(2,1)}, bf16[392,768]{1,0:T(8,128)(2,1)S(1)}, u32[]{:S(2)}, u32[]{:S(2)}) collective-permute-start(bf16[392,768]{1,0:T(8,128)(2,1)} %get-tuple-element.42), channel_id=1, source_target_pairs={{0,16},{1,17},{2,18},{3,19},{4,20},{5,21},{6,22},{7,23},{8,24},{9,... | collective-permute-start | bytes 1806344 | tf_op jit(solution)/shard_map/ppermute | solution.py:28
  63.4 3.7 %copy-start = (bf16[2,8,2,192,768]{4,3,2,1,0:T(8,128)(2,1)S(1)}, bf16[2,8,2,192,768]{4,3,2,1,0:T(8,128)(2,1)}, u32[]{:S(2)}) copy-start(bf16[2,8,2,192,768]{4,3,2,1,0:T(8,128)(2,1)} %copy.17) | copy-start | bytes 28311556
  67.1 1.1 copy-start.2
  96.2 1.8 %collective-permute-start.12 = (f32[4,2,2,24,192]{4,3,2,1,0:T(8,128)S(1)}, f32[4,2,2,24,192]{4,3,2,1,0:T(8,128)S(1)}, u32[]{:S(2)}, u32[]{:S(2)}) collective-permute-start(f32[4,2,2,24,192]{4,3,2,1,0:T(8,128)S(1)} %get-tuple-element.52), channel_id=1, source_target_pairs={{0,1},{1,0},{2,3},{3,2},{4,5},{5,4},{6,7},{7,6},{8,9},{9,8},{10,11... | collective-permute-start | bytes 884744 | tf_op jit(solution)/shard_map/ppermute | solution.py:189
  98.1 7.6 %collective-permute-start.13 = (f32[2,2,24,192]{3,2,1,0:T(8,128)S(1)}, f32[2,2,24,192]{3,2,1,0:T(8,128)S(1)}, u32[]{:S(2)}, u32[]{:S(2)}) collective-permute-start(f32[2,2,24,192]{3,2,1,0:T(8,128)S(1)} %get-tuple-element.55), channel_id=1, source_target_pairs={{0,2},{1,3},{2,4},{3,5},{4,6},{5,7},{6,0},{7,1},{8,10},{9,11},{10,... | collective-permute-start | bytes 221192 | tf_op jit(solution)/shard_map/ppermute | solution.py:194
  98.2 10.8 %collective-permute-start.14 = (f32[2,2,24,192]{3,2,1,0:T(8,128)S(1)}, f32[2,2,24,192]{3,2,1,0:T(8,128)S(1)}, u32[]{:S(2)}, u32[]{:S(2)}) collective-permute-start(f32[2,2,24,192]{3,2,1,0:T(8,128)S(1)} %get-tuple-element.57), channel_id=1, source_target_pairs={{0,4},{1,5},{2,6},{3,7},{4,0},{5,1},{6,2},{7,3},{8,12},{9,13},{10,... | collective-permute-start | bytes 221192 | tf_op jit(solution)/shard_map/ppermute | solution.py:194
  99.1 9.9 %collective-permute-start.15 = (f32[2,2,24,192]{3,2,1,0:T(8,128)S(1)}, f32[2,2,24,192]{3,2,1,0:T(8,128)S(1)}, u32[]{:S(2)}, u32[]{:S(2)}) collective-permute-start(f32[2,2,24,192]{3,2,1,0:T(8,128)S(1)} %get-tuple-element.56), channel_id=1, source_target_pairs={{0,6},{1,7},{2,0},{3,1},{4,2},{5,3},{6,4},{7,5},{8,14},{9,15},{10,... | collective-permute-start | bytes 221192 | tf_op jit(solution)/shard_map/ppermute | solution.py:194

commit v8 on v7

--- a/solution.py
+++ b/solution.py
@@ -45,7 +45,7 @@
 
 
 def piece_kernel(
-    sources, before_count, order, conserve, pairs, here, occupied, own_energy, left, *refs
+    sources, before_count, orders, held, conserve, pairs, here, occupied, own_energy, left, *refs
 ):
     mates, refs = refs[:sources], refs[sources:]
     before, refs = refs[:before_count], refs[before_count:]
@@ -66,10 +66,17 @@
             result = jnp.where(column == number, jnp.int32(values[number]), result)
         return result
 
-    round_index = by_column(order[0])
-    momentum = by_column(order[1])
-    source = by_column(order[2])
-    mine = lax.rem(conserve[0, round_index] + momentum, jnp.int32(2))
+    round_index = by_column(orders[-1][0])
+    momentum = by_column(orders[-1][1])
+    source = by_column(held)
+    def own_index(round_index, momentum):
+        return lax.rem(conserve[0, round_index] + momentum, jnp.int32(2))
+
+    mine = own_index(round_index, momentum)
+    earlier = [
+        (before[2 * number : 2 * number + 2], own_index(by_column(rounds), by_column(parts)))
+        for number, (rounds, parts) in enumerate(orders[:-1])
+    ]
 
     for number, mate in enumerate(mates):
 
@@ -144,24 +151,28 @@
         for number, offset in enumerate((core, 1 - core)):
             cut = pl.ds(pl.multiple_of((place * CORES + offset) * share, 8), share)
             value = total[:, cut]
+            if not earlier:
+                outs[number][place] = value
+                continue
             for local_index in range(2):
                 added = jnp.where(mine == local_index, value, 0.0)
-                if before:
-                    added = added + before[number][place, local_index]
+                for (term, which) in earlier:
+                    added = added + jnp.where(which == local_index, term[number][place], 0.0)
                 outs[number][place, local_index] = added
 
 
-def piece_density(order, conserve, pairs, here, occupied, own_energy, left, mates, before):
+def piece_density(orders, held, conserve, pairs, here, occupied, own_energy, left, mates, before):
     momenta, orbitals, both, auxiliary = left.shape
     virtuals = both // 2
     share = virtuals // (LINE * CORES)
     count = pairs.shape[0] * pairs.shape[2]
     rows = 2 * orbitals * share
-    out_shape = (jax.ShapeDtypeStruct((LINE, momenta, 2, share, virtuals), jnp.float32),) * 2
+    leading = (LINE, momenta) if before else (LINE,)
+    out_shape = (jax.ShapeDtypeStruct((*leading, 2, share, virtuals), jnp.float32),) * 2
     scalars = pl.BlockSpec(memory_space=pltpu.SMEM)
     whole = pl.BlockSpec(memory_space=pltpu.VMEM)
     return pl.pallas_call(
-        functools.partial(piece_kernel, len(mates), len(before), order),
+        functools.partial(piece_kernel, len(mates), len(before), orders, held),
         out_shape=out_shape,
         in_specs=[scalars] * 4
         + [whole] * (2 + len(mates) + len(before)),
@@ -223,29 +234,34 @@
     plus = moved(m1, {0: (1, same), 1: (2, same), 2: (3, same), 3: (0, beside_next)})
     minus = moved(m1, {0: (3, same), 1: (0, same), 2: (1, beside_next), 3: (2, beside_next)})
     pairs = with_partner(pairs, 2 * CORES)
-    left = jnp.transpose(factors, (0, 1, 3, 2, 4)).reshape(momenta, orbitals, 2 * virtuals, auxiliary)
-    m0, left, pairs = lax.optimization_barrier((m0, left, pairs))
+    m0, pairs, factors = lax.optimization_barrier((m0, pairs, factors))
     cross_one = moved(m0, {3: (0, onto_next)})
     cross_two = moved(m0, {2: (0, onto_next)})
     pairs = with_partner(pairs, 1)
     own_energy = virtual_energy.astype(jnp.float32)[:, None, :]
-    m0, plus, minus, pairs, own_energy = lax.optimization_barrier((m0, plus, minus, pairs, own_energy))
+    m0, plus, minus, factors, pairs, own_energy = lax.optimization_barrier(
+        (m0, plus, minus, factors, pairs, own_energy)
+    )
     up = moved(plus, {0: (0, across)})
     back = moved(minus, {0: (3, same), 1: (0, across), 2: (1, across), 3: (2, same)})
     near_one = moved(m0, {0: (1, same), 1: (2, same), 2: (3, same)})
-    m0, cross_one, near_one = lax.optimization_barrier((m0, cross_one, near_one))
+    left = jnp.transpose(factors, (0, 1, 3, 2, 4)).reshape(momenta, orbitals, 2 * virtuals, auxiliary)
+    m0, cross_one, near_one, left = lax.optimization_barrier((m0, cross_one, near_one, left))
     onward = moved(cross_one, {0: (1, same)})
     near_two = moved(m0, {0: (2, same), 1: (3, same)})
 
-    def density(order, mates, before):
+    def density(orders, held, mates, before):
         return piece_density(
-            order, conserve, pairs, here, occupied_energy, own_energy, left, mates, before
-        )
-
-    total = density(((0,), (0,), (0, 1)), (cross_one, near_one), ())
-    total = density(((1, 0), (0, 1), (0, 1)), (cross_two, plus), total)
-    total = density(((1,), (1,), (0,)), (back,), total)
-    total = density(((0, 1), (1, 0), (0, 1, 2)), (up, onward, near_two), total)
+            orders, held, conserve, pairs, here, occupied_energy, own_energy, left, mates, before
+        )
+
+    orders = (((0,), (0,)), ((1, 0), (0, 1)), ((1,), (1,)), ((0, 1), (1, 0)))
+    terms = density(orders[:1], (0, 1), (cross_one, near_one), ())
+    *terms, cross_two, plus = lax.optimization_barrier((*terms, cross_two, plus))
+    terms += density(orders[1:2], (0, 1), (cross_two, plus), ())
+    *terms, back = lax.optimization_barrier((*terms, back))
+    terms += density(orders[2:3], (0,), (back,), ())
+    total = density(orders, (0, 1, 2), (up, onward, near_two), terms)
     return jnp.transpose(summed(*total), (0, 2, 1, 3))
 
 

time: 110 us -> 108 us (0.982)
  starting transfers between devices: 45.8 us -> 37.3 us
  waiting for transfers between devices: 25.5 us -> 31.3 us
    ppermute x9, starting transfers between devices: 36.5 us -> 28.1 us  [moved(): return lax.ppermute(array, ('ka', 'occ'), pairs)]
    ppermute x9, waiting for transfers between devices: 16.8 us -> 20.7 us  [moved(): return lax.ppermute(array, ('ka', 'occ'), pairs)]
    ppermute x3, waiting for transfers between devices: 0.01 us -> 1.94 us  [with_partner(): lax.ppermute(array, 'occ', [(i, i ^ reach) for i in range(LINE * CORES)])]
    unnamed x14 -> x16, local copies, waits for them, and re-layouts: 6.13 us -> 6.13 us
  transfers between devices with their start and end apart: 16 -> 16, of which waited for: 5 -> 8; matrix products, arithmetic and copies ran while one was open for 12% -> 12% of each run, Pallas kernels for 12% -> 12%
where the time goes in v8:
time: 108 us; the launch traced here: 107 us
  starting transfers between devices  37.3 us (35%)
  waiting for transfers between devices  31.3 us (29%)
  local copies, waits for them, and re-layouts  18.8 us (17%)
  Pallas kernels  18.1 us (17%)
  other arithmetic  1.32 us (1%)
    ppermute x9, starting transfers between devices, moved(): return lax.ppermute(array, ('ka', 'occ'), pairs)  28.1 us
    ppermute x9, waiting for transfers between devices, moved(): return lax.ppermute(array, ('ka', 'occ'), pairs)  20.7 us
    pallas_call x4, Pallas kernels, piece_density(): pl.pallas_call(functools.partial(piece_kernel, len(mates), len(before), o...  18.1 us
    transpose x1, local copies, waits for them, and re-layouts, local(): jnp.transpose(factors, (0, 1, 3, 2, 4))  9.32 us
    ppermute x3, waiting for transfers between devices, summed(): total = total + lax.ppermute(part, 'occ', ring)  7.01 us
    unnamed x16, local copies, waits for them, and re-layouts  6.13 us
    ppermute x3, starting transfers between devices, with_partner(): lax.ppermute(array, 'occ', [(i, i ^ reach) for i in range(LINE * CORES)])  5.19 us
    ppermute x3, starting transfers between devices, summed(): total = total + lax.ppermute(part, 'occ', ring)  3.9 us
  transfers between devices with their start and end apart: 16, of which 8 were waited for; matrix products, arithmetic and copies ran while one was open for 12% of the time, Pallas kernels for 12%

profile of v8, /device:TPU:10, one launch (start us, length us, event | category | flops | bytes accessed | tf_op | source)
XLA Modules:
  0.0 107.1 jit_solution(10875259961119719538)
XLA Ops:
  0.0 1.9 %collective-permute-start = (s32[1,2,2,2]{3,2,1,0:T(2,128)}, s32[1,2,2,2]{3,2,1,0:T(2,128)S(1)}, u32[]{:S(2)}, u32[]{:S(2)}) collective-permute-start(s32[1,2,2,2]{3,2,1,0:T(2,128)} %bitcast.40), channel_id=1, source_target_pairs={{0,2},{1,3},{2,0},{3,1},{4,6},{5,7},{6,4},{7,5},{8,10},{9,11},{10,... | collective-permute-start | bytes 104 | tf_op jit(solution)/shard_map/ppermute | solution.py:210
  1.9 2.1 %constant_dynamic-slice_fusion = (bf16[1,8,24,2,768]{4,3,2,1,0:T(2,128)(2,1)S(1)}, bf16[1,8,24,2,768]{4,3,2,1,0:T(2,128)(2,1)S(1)}) fusion(bf16[2,8,192,2,768]{4,3,2,1,0:T(2,128)(2,1)} %param.5, s32[]{:T(128)S(6)} %select_n.44), kind=kLoop, calls=%fused_computation.19 | loop fusion | bytes 2359300 | tf_op jit(solution)/shard_map/dynamic_slice | solution.py:222
  4.0 0.0 copy-start.5
  4.0 0.1 copy.27
  4.1 0.1 copy.28
  4.1 0.5 copy-done.5
  4.7 0.1 pad_add_fusion.3.here
  4.7 0.1 pad.22.clone
  4.8 1.1 %fusion.6 = (bf16[392,768]{1,0:T(8,128)(2,1)S(1)}, bf16[392,768]{1,0:T(8,128)(2,1)}) fusion(bf16[1,192]{1,0:T(2,128)(2,1)S(1)} %get-tuple-element.82, bf16[384,768]{1,0:T(8,128)(2,1)S(1)} %bitcast.39, bf16[392]{0:T(512)(128)(2,1)S(1)} %pad.22.clone, bf16[1,192]{1,0:T(2,128)(2,1)S(1)} %get-tuple-element.83, bf16[384,768]{1,0:T(8,128)(2,1)S(1)} %bitcast.38), kind=kLoop, calls=%fused_computation.8 | loop fusion | flops 4816896 | bytes 2385424 | tf_op jit(solution)/shard_map/concatenate | solution.py:228
  5.9 1.6 %collective-permute-start.2 = (bf16[392,768]{1,0:T(8,128)(2,1)S(1)}, bf16[392,768]{1,0:T(8,128)(2,1)S(1)}, u32[]{:S(2)}, u32[]{:S(2)}) collective-permute-start(bf16[392,768]{1,0:T(8,128)(2,1)S(1)} %get-tuple-element.44), channel_id=1, source_target_pairs={{0,8},{1,9},{2,10},{3,11},{4,12},{5,13},{6,14},{7,15},{8,16},{9,17... | collective-permute-start | bytes 1806344 | tf_op jit(solution)/shard_map/ppermute | solution.py:28
  7.5 0.5 collective-permute-start.3
  8.0 3.3 %collective-permute-start.1 = (s32[2,2,2,2]{3,2,1,0:T(2,128)S(1)}, s32[2,2,2,2]{3,2,1,0:T(2,128)S(1)}, u32[]{:S(2)}, u32[]{:S(2)}) collective-permute-start(s32[2,2,2,2]{3,2,1,0:T(2,128)S(1)} %pad_add_fusion.1), channel_id=1, source_target_pairs={{0,4},{1,5},{2,6},{3,7},{4,0},{5,1},{6,2},{7,3},{8,12},{9,13},{10,... | collective-permute-start | bytes 200 | tf_op jit(solution)/shard_map/ppermute | solution.py:210
  11.3 1.6 %collective-permute-done.1 = s32[2,2,2,2]{3,2,1,0:T(2,128)S(1)} collective-permute-done((s32[2,2,2,2]{3,2,1,0:T(2,128)S(1)}, s32[2,2,2,2]{3,2,1,0:T(2,128)S(1)}, u32[]{:S(2)}, u32[]{:S(2)}) %collective-permute-start.1) | collective-permute-done | bytes 96 | tf_op jit(solution)/shard_map/ppermute | solution.py:210
  12.9 0.0 collective-permute-start.4
  12.9 0.1 copy.17
  13.0 0.7 collective-permute-start.5
  13.7 0.4 collective-permute-done.4
  14.1 0.1 copy.18
  14.2 0.1 pad_add_fusion.2
  14.2 6.8 %collective-permute-done.2.refs_1_ = bf16[392,768]{1,0:T(8,128)(2,1)S(1)} collective-permute-done((bf16[392,768]{1,0:T(8,128)(2,1)S(1)}, bf16[392,768]{1,0:T(8,128)(2,1)S(1)}, u32[]{:S(2)}, u32[]{:S(2)}) %collective-permute-start.2) | collective-permute-done | bytes 602144 | tf_op jit(solution)/shard_map/ppermute | solution.py:28
  21.0 1.2 %collective-permute-done.3 = bf16[392,768]{1,0:T(8,128)(2,1)S(1)} collective-permute-done((bf16[392,768]{1,0:T(8,128)(2,1)S(1)}, bf16[392,768]{1,0:T(8,128)(2,1)S(1)}, u32[]{:S(2)}, u32[]{:S(2)}) %collective-permute-start.3) | collective-permute-done | bytes 602144 | tf_op jit(solution)/shard_map/ppermute | solution.py:28
  22.3 3.1 %collective-permute-start.6 = (bf16[392,768]{1,0:T(8,128)(2,1)}, bf16[392,768]{1,0:T(8,128)(2,1)S(1)}, u32[]{:S(2)}, u32[]{:S(2)}) collective-permute-start(bf16[392,768]{1,0:T(8,128)(2,1)} %get-tuple-element.55), channel_id=1, source_target_pairs={{0,8},{1,9},{2,10},{3,11},{4,12},{5,13},{6,14},{7,15},{8,16},{9,17... | collective-permute-start | bytes 1806344 | tf_op jit(solution)/shard_map/ppermute | solution.py:28
  25.4 1.5 %collective-permute-start.10 = (bf16[392,768]{1,0:T(8,128)(2,1)}, bf16[392,768]{1,0:T(8,128)(2,1)}, u32[]{:S(2)}, u32[]{:S(2)}) collective-permute-start(bf16[392,768]{1,0:T(8,128)(2,1)} %get-tuple-element.55), channel_id=1, source_target_pairs={{16,38},{17,39},{18,36},{19,37},{20,34},{21,35},{22,32},{23,33},{4... | collective-permute-start | bytes 1806344 | tf_op jit(solution)/shard_map/ppermute | solution.py:28
  26.9 6.0 %collective-permute-start.11 = (bf16[392,768]{1,0:T(8,128)(2,1)}, bf16[392,768]{1,0:T(8,128)(2,1)S(1)}, u32[]{:S(2)}, u32[]{:S(2)}) collective-permute-start(bf16[392,768]{1,0:T(8,128)(2,1)} %copy-done.7), channel_id=1, source_target_pairs={{0,24},{1,25},{2,26},{3,27},{4,28},{5,29},{6,30},{7,31},{8,38},{9,... | collective-permute-start | bytes 1806344 | tf_op jit(solution)/shard_map/ppermute | solution.py:28
  32.9 9.3 %copy.19 = bf16[2,8,2,192,768]{4,3,2,1,0:T(8,128)(2,1)} copy(bf16[2,8,2,192,768]{4,2,3,1,0:T(2,128)(2,1)} %bitcast.37) | data formatting | bytes 18874368 | tf_op jit(solution)/shard_map/transpose | solution.py:248
  42.2 0.7 collective-permute-start.7
  42.9 0.0 collective-permute-done.5.refs_0_
  42.9 0.0 collective-permute-done.6.refs_1_
  42.9 0.8 copy-done.1
  43.8 1.3 %collective-permute-start.8 = (bf16[392,768]{1,0:T(8,128)(2,1)S(1)}, bf16[392,768]{1,0:T(8,128)(2,1)S(1)}, u32[]{:S(2)}, u32[]{:S(2)}) collective-permute-start(bf16[392,768]{1,0:T(8,128)(2,1)S(1)} %collective-permute-done.5.refs_0_), channel_id=1, source_target_pairs={{0,8},{1,9},{2,10},{3,11},{4,12},{5,13},{6,14},{7,15},{32,40},{33,... | collective-permute-start | bytes 1806344 | tf_op jit(solution)/shard_map/ppermute | solution.py:28
  45.1 12.8 %collective-permute-start.9 = (bf16[392,768]{1,0:T(8,128)(2,1)}, bf16[392,768]{1,0:T(8,128)(2,1)}, u32[]{:S(2)}, u32[]{:S(2)}) collective-permute-start(bf16[392,768]{1,0:T(8,128)(2,1)} %get-tuple-element.55), channel_id=1, source_target_pairs={{0,16},{1,17},{2,18},{3,19},{4,20},{5,21},{6,22},{7,23},{8,24},{9,... | collective-permute-start | bytes 1806344 | tf_op jit(solution)/shard_map/ppermute | solution.py:28
  57.8 0.1 copy.23.pairs
  58.0 3.7 %copy-done = bf16[2,8,2,192,768]{4,3,2,1,0:T(8,128)(2,1)S(1)} copy-done((bf16[2,8,2,192,768]{4,3,2,1,0:T(8,128)(2,1)S(1)}, bf16[2,8,2,192,768]{4,3,2,1,0:T(8,128)(2,1)}, u32[]{:S(2)}) %copy-start) | copy-done | bytes 9437208
  61.6 1.1 copy-done.2
  62.7 4.3 %shard_map.55 = (f32[4,2,24,192]{3,2,1,0:T(8,128)S(1)}, f32[4,2,24,192]{3,2,1,0:T(8,128)S(1)}) custom-call(s32[2,2]{1,0:T(2,128)S(1)} %copy-done.3, s32[8,2,2,2]{3,2,1,0:T(2,128)S(1)} %copy.23.pairs, s32[2]{0:T(128)S(1)} %pad_add_fusion.3.here, f32[8]{0:T(128)S(1)} %copy-done.4, f32[2,1,192]{2,1,0:T(1,128)S(1)} %reshape.12.own_energy, ...), custom_call_target="tpu_custom_call" | custom-call | flops 1925185536 | bytes 5308416 | tf_op jit(solution)/shard_map/pallas_call | solution.py:174
  67.0 4.8 %shard_map.56 = (f32[4,2,24,192]{3,2,1,0:T(8,128)S(1)}, f32[4,2,24,192]{3,2,1,0:T(8,128)S(1)}) custom-call(s32[2,2]{1,0:T(2,128)S(1)} %copy-done.3, s32[8,2,2,2]{3,2,1,0:T(2,128)S(1)} %copy.23.pairs, s32[2]{0:T(128)S(1)} %pad_add_fusion.3.here, f32[8]{0:T(128)S(1)} %copy-done.4, f32[2,1,192]{2,1,0:T(1,128)S(1)} %reshape.12.own_energy, ...), custom_call_target="tpu_custom_call" | custom-call | flops 1925185536 | bytes 5308416 | tf_op jit(solution)/shard_map/pallas_call | solution.py:174
  71.8 12.7 %collective-permute-done.11.refs_0_ = bf16[392,768]{1,0:T(8,128)(2,1)S(1)} collective-permute-done((bf16[392,768]{1,0:T(8,128)(2,1)}, bf16[392,768]{1,0:T(8,128)(2,1)S(1)}, u32[]{:S(2)}, u32[]{:S(2)}) %collective-permute-start.11) | collective-permute-done | bytes 602144 | tf_op jit(solution)/shard_map/ppermute | solution.py:28
  84.5 4.3 %shard_map.57 = (f32[4,2,24,192]{3,2,1,0:T(8,128)S(1)}, f32[4,2,24,192]{3,2,1,0:T(8,128)S(1)}) custom-call(s32[2,2]{1,0:T(2,128)S(1)} %copy-done.3, s32[8,2,2,2]{3,2,1,0:T(2,128)S(1)} %copy.23.pairs, s32[2]{0:T(128)S(1)} %pad_add_fusion.3.here, f32[8]{0:T(128)S(1)} %copy-done.4, f32[2,1,192]{2,1,0:T(1,128)S(1)} %reshape.12.own_energy, ...), custom_call_target="tpu_custom_call" | custom-call | flops 1925185536 | bytes 5308416 | tf_op jit(solution)/shard_map/pallas_call | solution.py:174
  88.8 4.8 %shard_map.58 = (f32[4,2,2,24,192]{4,3,2,1,0:T(8,128)S(1)}, f32[4,2,2,24,192]{4,3,2,1,0:T(8,128)S(1)}) custom-call(s32[2,2]{1,0:T(2,128)S(1)} %copy-done.3, s32[8,2,2,2]{3,2,1,0:T(2,128)S(1)} %copy.23.pairs, s32[2]{0:T(128)S(1)} %pad_add_fusion.3.here, f32[8]{0:T(128)S(1)} %copy-done.4, f32[2,1,192]{2,1,0:T(1,128)S(1)} %reshape.12.own_energy, ...), custom_call_target="tpu_custom_call" | custom-call | flops 1925185536 | bytes 5308416 | tf_op jit(solution)/shard_map/pallas_call | solution.py:174
  93.6 0.1 collective-permute-start.12
  93.7 1.6 %collective-permute-done.12 = f32[4,2,2,24,192]{4,3,2,1,0:T(8,128)S(1)} collective-permute-done((f32[4,2,2,24,192]{4,3,2,1,0:T(8,128)S(1)}, f32[4,2,2,24,192]{4,3,2,1,0:T(8,128)S(1)}, u32[]{:S(2)}, u32[]{:S(2)}) %collective-permute-start.12) | collective-permute-done | bytes 294944 | tf_op jit(solution)/shard_map/ppermute | solution.py:200
  95.4 0.1 add.62
  95.5 0.1 collective-permute-start.13
  95.6 2.5 %collective-permute-start.14 = (f32[2,2,24,192]{3,2,1,0:T(8,128)S(1)}, f32[2,2,24,192]{3,2,1,0:T(8,128)S(1)}, u32[]{:S(2)}, u32[]{:S(2)}) collective-permute-start(f32[2,2,24,192]{3,2,1,0:T(8,128)S(1)} %get-tuple-element.79), channel_id=1, source_target_pairs={{0,4},{1,5},{2,6},{3,7},{4,0},{5,1},{6,2},{7,3},{8,12},{9,13},{10,... | collective-permute-start | bytes 221192 | tf_op jit(solution)/shard_map/ppermute | solution.py:205
  98.0 1.4 %collective-permute-start.15 = (f32[2,2,24,192]{3,2,1,0:T(8,128)S(1)}, f32[2,2,24,192]{3,2,1,0:T(8,128)S(1)}, u32[]{:S(2)}, u32[]{:S(2)}) collective-permute-start(f32[2,2,24,192]{3,2,1,0:T(8,128)S(1)} %get-tuple-element.78), channel_id=1, source_target_pairs={{0,6},{1,7},{2,0},{3,1},{4,2},{5,3},{6,4},{7,5},{8,14},{9,15},{10,... | collective-permute-start | bytes 221192 | tf_op jit(solution)/shard_map/ppermute | solution.py:205
  99.4 3.7 %collective-permute-done.13 = f32[2,2,24,192]{3,2,1,0:T(8,128)S(1)} collective-permute-done((f32[2,2,24,192]{3,2,1,0:T(8,128)S(1)}, f32[2,2,24,192]{3,2,1,0:T(8,128)S(1)}, u32[]{:S(2)}, u32[]{:S(2)}) %collective-permute-start.13) | collective-permute-done | bytes 73760 | tf_op jit(solution)/shard_map/ppermute | solution.py:205
  103.1 3.3 %collective-permute-done.14 = f32[2,2,24,192]{3,2,1,0:T(8,128)S(1)} collective-permute-done((f32[2,2,24,192]{3,2,1,0:T(8,128)S(1)}, f32[2,2,24,192]{3,2,1,0:T(8,128)S(1)}, u32[]{:S(2)}, u32[]{:S(2)}) %collective-permute-start.14) | collective-permute-done | bytes 73760 | tf_op jit(solution)/shard_map/ppermute | solution.py:205
  106.4 0.7 copy.24
  (24 shorter events, 0.1 us)
Async XLA Ops:
  0.0 5.9 %collective-permute-start = (s32[1,2,2,2]{3,2,1,0:T(2,128)}, s32[1,2,2,2]{3,2,1,0:T(2,128)S(1)}, u32[]{:S(2)}, u32[]{:S(2)}) collective-permute-start(s32[1,2,2,2]{3,2,1,0:T(2,128)} %bitcast.40), channel_id=1, source_target_pairs={{0,2},{1,3},{2,0},{3,1},{4,6},{5,7},{6,4},{7,5},{8,10},{9,11},{10,... | collective-permute-start | bytes 104 | tf_op jit(solution)/shard_map/ppermute | solution.py:210
  4.0 0.7 copy-start.5
  4.7 1.2 %copy-start.6 = (s32[2,2,2]{2,1,0:T(2,128)S(1)}, s32[2,2,2]{2,1,0:T(2,128)}, u32[]{:S(2)}) copy-start(s32[2,2,2]{2,1,0:T(2,128)} %param.9) | copy-start | bytes 100
  5.9 15.1 %collective-permute-start.2 = (bf16[392,768]{1,0:T(8,128)(2,1)S(1)}, bf16[392,768]{1,0:T(8,128)(2,1)S(1)}, u32[]{:S(2)}, u32[]{:S(2)}) collective-permute-start(bf16[392,768]{1,0:T(8,128)(2,1)S(1)} %get-tuple-element.44), channel_id=1, source_target_pairs={{0,8},{1,9},{2,10},{3,11},{4,12},{5,13},{6,14},{7,15},{8,16},{9,17... | collective-permute-start | bytes 1806344 | tf_op jit(solution)/shard_map/ppermute | solution.py:28
  7.5 14.8 %collective-permute-start.3 = (bf16[392,768]{1,0:T(8,128)(2,1)S(1)}, bf16[392,768]{1,0:T(8,128)(2,1)S(1)}, u32[]{:S(2)}, u32[]{:S(2)}) collective-permute-start(bf16[392,768]{1,0:T(8,128)(2,1)S(1)} %get-tuple-element.44), channel_id=1, source_target_pairs={{0,24},{1,25},{2,26},{3,27},{4,28},{5,29},{6,30},{7,31},{8,0},{9,1... | collective-permute-start | bytes 1806344 | tf_op jit(solution)/shard_map/ppermute | solution.py:28
  8.0 4.9 %collective-permute-start.1 = (s32[2,2,2,2]{3,2,1,0:T(2,128)S(1)}, s32[2,2,2,2]{3,2,1,0:T(2,128)S(1)}, u32[]{:S(2)}, u32[]{:S(2)}) collective-permute-start(s32[2,2,2,2]{3,2,1,0:T(2,128)S(1)} %pad_add_fusion.1), channel_id=1, source_target_pairs={{0,4},{1,5},{2,6},{3,7},{4,0},{5,1},{6,2},{7,3},{8,12},{9,13},{10,... | collective-permute-start | bytes 200 | tf_op jit(solution)/shard_map/ppermute | solution.py:210
  12.9 1.2 %collective-permute-start.4 = (s32[4,2,2,2]{3,2,1,0:T(2,128)S(1)}, s32[4,2,2,2]{3,2,1,0:T(2,128)S(1)}, u32[]{:S(2)}, u32[]{:S(2)}) collective-permute-start(s32[4,2,2,2]{3,2,1,0:T(2,128)S(1)} %pad_add_fusion), channel_id=1, source_target_pairs={{0,1},{1,0},{2,3},{3,2},{4,5},{5,4},{6,7},{7,6},{8,9},{9,8},{10,11... | collective-permute-start | bytes 392 | tf_op jit(solution)/shard_map/ppermute | solution.py:210
  13.0 29.9 %collective-permute-start.5 = (bf16[392,768]{1,0:T(8,128)(2,1)}, bf16[392,768]{1,0:T(8,128)(2,1)S(1)}, u32[]{:S(2)}, u32[]{:S(2)}) collective-permute-start(bf16[392,768]{1,0:T(8,128)(2,1)} %get-tuple-element.55), channel_id=1, source_target_pairs={{24,38},{25,39},{26,36},{27,37},{28,34},{29,35},{30,32},{31,33},{5... | collective-permute-start | bytes 1806344 | tf_op jit(solution)/shard_map/ppermute | solution.py:28
  22.3 3.1 %copy-start.7 = (bf16[392,768]{1,0:T(8,128)(2,1)}, bf16[392,768]{1,0:T(8,128)(2,1)S(1)}, u32[]{:S(2)}) copy-start(bf16[392,768]{1,0:T(8,128)(2,1)S(1)} %collective-permute-done.3) | copy-start | bytes 1806340
  22.3 20.7 %collective-permute-start.6 = (bf16[392,768]{1,0:T(8,128)(2,1)}, bf16[392,768]{1,0:T(8,128)(2,1)S(1)}, u32[]{:S(2)}, u32[]{:S(2)}) collective-permute-start(bf16[392,768]{1,0:T(8,128)(2,1)} %get-tuple-element.55), channel_id=1, source_target_pairs={{0,8},{1,9},{2,10},{3,11},{4,12},{5,13},{6,14},{7,15},{8,16},{9,17... | collective-permute-start | bytes 1806344 | tf_op jit(solution)/shard_map/ppermute | solution.py:28
  25.4 41.6 %collective-permute-start.10 = (bf16[392,768]{1,0:T(8,128)(2,1)}, bf16[392,768]{1,0:T(8,128)(2,1)}, u32[]{:S(2)}, u32[]{:S(2)}) collective-permute-start(bf16[392,768]{1,0:T(8,128)(2,1)} %get-tuple-element.55), channel_id=1, source_target_pairs={{16,38},{17,39},{18,36},{19,37},{20,34},{21,35},{22,32},{23,33},{4... | collective-permute-start | bytes 1806344 | tf_op jit(solution)/shard_map/ppermute | solution.py:28
  26.9 57.6 %collective-permute-start.11 = (bf16[392,768]{1,0:T(8,128)(2,1)}, bf16[392,768]{1,0:T(8,128)(2,1)S(1)}, u32[]{:S(2)}, u32[]{:S(2)}) collective-permute-start(bf16[392,768]{1,0:T(8,128)(2,1)} %copy-done.7), channel_id=1, source_target_pairs={{0,24},{1,25},{2,26},{3,27},{4,28},{5,29},{6,30},{7,31},{8,38},{9,... | collective-permute-start | bytes 1806344 | tf_op jit(solution)/shard_map/ppermute | solution.py:28
  32.9 25.1 %copy-start.3 = (s32[2,2]{1,0:T(2,128)S(1)}, s32[2,2]{1,0:T(2,128)}, u32[]{:S(2)}) copy-start(s32[2,2]{1,0:T(2,128)} %conserve.7) | copy-start | bytes 52
  32.9 25.1 %copy-start.4 = (f32[8]{0:T(128)S(1)}, f32[8]{0:T(128)}, u32[]{:S(2)}) copy-start(f32[8]{0:T(128)} %occupied.7) | copy-start | bytes 100
  42.2 46.5 %collective-permute-start.7 = (bf16[392,768]{1,0:T(8,128)(2,1)S(1)}, bf16[392,768]{1,0:T(8,128)(2,1)S(1)}, u32[]{:S(2)}, u32[]{:S(2)}) collective-permute-start(bf16[392,768]{1,0:T(8,128)(2,1)S(1)} %collective-permute-done.2.refs_1_), channel_id=1, source_target_pairs={{0,38},{1,39},{2,36},{3,37},{4,34},{5,35},{6,32},{7,33},{32,6},{33... | collective-permute-start | bytes 1806344 | tf_op jit(solution)/shard_map/ppermute | solution.py:28
  42.9 0.8 copy-start.1
  43.8 45.0 %collective-permute-start.8 = (bf16[392,768]{1,0:T(8,128)(2,1)S(1)}, bf16[392,768]{1,0:T(8,128)(2,1)S(1)}, u32[]{:S(2)}, u32[]{:S(2)}) collective-permute-start(bf16[392,768]{1,0:T(8,128)(2,1)S(1)} %collective-permute-done.5.refs_0_), channel_id=1, source_target_pairs={{0,8},{1,9},{2,10},{3,11},{4,12},{5,13},{6,14},{7,15},{32,40},{33,... | collective-permute-start | bytes 1806344 | tf_op jit(solution)/shard_map/ppermute | solution.py:28
  45.1 43.7 %collective-permute-start.9 = (bf16[392,768]{1,0:T(8,128)(2,1)}, bf16[392,768]{1,0:T(8,128)(2,1)}, u32[]{:S(2)}, u32[]{:S(2)}) collective-permute-start(bf16[392,768]{1,0:T(8,128)(2,1)} %get-tuple-element.55), channel_id=1, source_target_pairs={{0,16},{1,17},{2,18},{3,19},{4,20},{5,21},{6,22},{7,23},{8,24},{9,... | collective-permute-start | bytes 1806344 | tf_op jit(solution)/shard_map/ppermute | solution.py:28
  57.9 3.7 %copy-start = (bf16[2,8,2,192,768]{4,3,2,1,0:T(8,128)(2,1)S(1)}, bf16[2,8,2,192,768]{4,3,2,1,0:T(8,128)(2,1)}, u32[]{:S(2)}) copy-start(bf16[2,8,2,192,768]{4,3,2,1,0:T(8,128)(2,1)} %copy.19) | copy-start | bytes 28311556
  61.6 1.1 copy-start.2
  93.6 1.8 %collective-permute-start.12 = (f32[4,2,2,24,192]{4,3,2,1,0:T(8,128)S(1)}, f32[4,2,2,24,192]{4,3,2,1,0:T(8,128)S(1)}, u32[]{:S(2)}, u32[]{:S(2)}) collective-permute-start(f32[4,2,2,24,192]{4,3,2,1,0:T(8,128)S(1)} %get-tuple-element.74), channel_id=1, source_target_pairs={{0,1},{1,0},{2,3},{3,2},{4,5},{5,4},{6,7},{7,6},{8,9},{9,8},{10,11... | collective-permute-start | bytes 884744 | tf_op jit(solution)/shard_map/ppermute | solution.py:200
  95.5 7.6 %collective-permute-start.13 = (f32[2,2,24,192]{3,2,1,0:T(8,128)S(1)}, f32[2,2,24,192]{3,2,1,0:T(8,128)S(1)}, u32[]{:S(2)}, u32[]{:S(2)}) collective-permute-start(f32[2,2,24,192]{3,2,1,0:T(8,128)S(1)} %get-tuple-element.77), channel_id=1, source_target_pairs={{0,2},{1,3},{2,4},{3,5},{4,6},{5,7},{6,0},{7,1},{8,10},{9,11},{10,... | collective-permute-start | bytes 221192 | tf_op jit(solution)/shard_map/ppermute | solution.py:205
  95.6 10.8 %collective-permute-start.14 = (f32[2,2,24,192]{3,2,1,0:T(8,128)S(1)}, f32[2,2,24,192]{3,2,1,0:T(8,128)S(1)}, u32[]{:S(2)}, u32[]{:S(2)}) collective-permute-start(f32[2,2,24,192]{3,2,1,0:T(8,128)S(1)} %get-tuple-element.79), channel_id=1, source_target_pairs={{0,4},{1,5},{2,6},{3,7},{4,0},{5,1},{6,2},{7,3},{8,12},{9,13},{10,... | collective-permute-start | bytes 221192 | tf_op jit(solution)/shard_map/ppermute | solution.py:205
  98.0 8.4 %collective-permute-start.15 = (f32[2,2,24,192]{3,2,1,0:T(8,128)S(1)}, f32[2,2,24,192]{3,2,1,0:T(8,128)S(1)}, u32[]{:S(2)}, u32[]{:S(2)}) collective-permute-start(f32[2,2,24,192]{3,2,1,0:T(8,128)S(1)} %get-tuple-element.78), channel_id=1, source_target_pairs={{0,6},{1,7},{2,0},{3,1},{4,2},{5,3},{6,4},{7,5},{8,14},{9,15},{10,... | collective-permute-start | bytes 221192 | tf_op jit(solution)/shard_map/ppermute | solution.py:205

commit v9 on v8

--- a/solution.py
+++ b/solution.py
@@ -246,7 +246,7 @@
     back = moved(minus, {0: (3, same), 1: (0, across), 2: (1, across), 3: (2, same)})
     near_one = moved(m0, {0: (1, same), 1: (2, same), 2: (3, same)})
     left = jnp.transpose(factors, (0, 1, 3, 2, 4)).reshape(momenta, orbitals, 2 * virtuals, auxiliary)
-    m0, cross_one, near_one, left = lax.optimization_barrier((m0, cross_one, near_one, left))
+    m0, cross_one, cross_two, left = lax.optimization_barrier((m0, cross_one, cross_two, left))
     onward = moved(cross_one, {0: (1, same)})
     near_two = moved(m0, {0: (2, same), 1: (3, same)})
 

time: 108 us -> 112 us (1.037)
  the two profiles are of different devices: /device:TPU:10 before, /device:TPU:4 now
where the time goes in v9:
time: 112 us
  waiting for transfers between devices  40.3 us (36%)
  starting transfers between devices  34 us (30%)
  Pallas kernels  18.3 us (16%)
  local copies, waits for them, and re-layouts  17.7 us (16%)
  other arithmetic  1.32 us (1%)
    ppermute x9, waiting for transfers between devices, moved(): return lax.ppermute(array, ('ka', 'occ'), pairs)  30.1 us
    ppermute x9, starting transfers between devices, moved(): return lax.ppermute(array, ('ka', 'occ'), pairs)  24.8 us
    pallas_call x4, Pallas kernels, piece_density(): pl.pallas_call(functools.partial(piece_kernel, len(mates), len(before), o...  18.3 us
    transpose x1, local copies, waits for them, and re-layouts, local(): jnp.transpose(factors, (0, 1, 3, 2, 4))  9.33 us
    ppermute x3, waiting for transfers between devices, summed(): total = total + lax.ppermute(part, 'occ', ring)  7.02 us
    ppermute x3, starting transfers between devices, with_partner(): lax.ppermute(array, 'occ', [(i, i ^ reach) for i in range(LINE * CORES)])  5.19 us
    unnamed x12, local copies, waits for them, and re-layouts  5.07 us
    ppermute x3, starting transfers between devices, summed(): total = total + lax.ppermute(part, 'occ', ring)  3.9 us
  transfers between devices with their start and end apart: 16, of which 6 were waited for; matrix products, arithmetic and copies ran while one was open for 12% of the time, Pallas kernels for 12%

profile of v9, /device:TPU:4, one launch (start us, length us, event | category | flops | bytes accessed | tf_op | source)
XLA Modules:
  0.0 111.9 jit_solution(10798033256653479614)
XLA Ops:
  0.0 1.9 %collective-permute-start = (s32[1,2,2,2]{3,2,1,0:T(2,128)}, s32[1,2,2,2]{3,2,1,0:T(2,128)S(1)}, u32[]{:S(2)}, u32[]{:S(2)}) collective-permute-start(s32[1,2,2,2]{3,2,1,0:T(2,128)} %bitcast.40), channel_id=1, source_target_pairs={{0,2},{1,3},{2,0},{3,1},{4,6},{5,7},{6,4},{7,5},{8,10},{9,11},{10,... | collective-permute-start | bytes 104 | tf_op jit(solution)/shard_map/ppermute | solution.py:210
  1.9 2.1 %constant_dynamic-slice_fusion = (bf16[1,8,24,2,768]{4,3,2,1,0:T(2,128)(2,1)S(1)}, bf16[1,8,24,2,768]{4,3,2,1,0:T(2,128)(2,1)S(1)}) fusion(bf16[2,8,192,2,768]{4,3,2,1,0:T(2,128)(2,1)} %param.5, s32[]{:T(128)S(6)} %select_n.44), kind=kLoop, calls=%fused_computation.19 | loop fusion | bytes 2359300 | tf_op jit(solution)/shard_map/dynamic_slice | solution.py:222
  4.0 0.0 copy-start.3
  4.0 0.1 copy.27
  4.1 0.1 copy.28
  4.1 0.5 copy-done.3
  4.7 0.1 pad_add_fusion.3.here
  4.7 0.1 pad.22.clone
  4.8 1.1 fusion.6
  5.9 0.0 collective-permute-done
  5.9 1.3 %collective-permute-start.2 = (bf16[392,768]{1,0:T(8,128)(2,1)S(1)}, bf16[392,768]{1,0:T(8,128)(2,1)S(1)}, u32[]{:S(2)}, u32[]{:S(2)}) collective-permute-start(bf16[392,768]{1,0:T(8,128)(2,1)S(1)} %get-tuple-element.44), channel_id=1, source_target_pairs={{0,8},{1,9},{2,10},{3,11},{4,12},{5,13},{6,14},{7,15},{8,16},{9,17... | collective-permute-start | bytes 1806344 | tf_op jit(solution)/shard_map/ppermute | solution.py:28
  7.2 0.8 collective-permute-start.3
  8.0 3.3 %collective-permute-start.1 = (s32[2,2,2,2]{3,2,1,0:T(2,128)S(1)}, s32[2,2,2,2]{3,2,1,0:T(2,128)S(1)}, u32[]{:S(2)}, u32[]{:S(2)}) collective-permute-start(s32[2,2,2,2]{3,2,1,0:T(2,128)S(1)} %pad_add_fusion.1), channel_id=1, source_target_pairs={{0,4},{1,5},{2,6},{3,7},{4,0},{5,1},{6,2},{7,3},{8,12},{9,13},{10,... | collective-permute-start | bytes 200 | tf_op jit(solution)/shard_map/ppermute | solution.py:210
  11.3 1.6 %collective-permute-done.1 = s32[2,2,2,2]{3,2,1,0:T(2,128)S(1)} collective-permute-done((s32[2,2,2,2]{3,2,1,0:T(2,128)S(1)}, s32[2,2,2,2]{3,2,1,0:T(2,128)S(1)}, u32[]{:S(2)}, u32[]{:S(2)}) %collective-permute-start.1) | collective-permute-done | bytes 96 | tf_op jit(solution)/shard_map/ppermute | solution.py:210
  12.9 0.1 copy.17
  13.0 0.7 collective-permute-start.5
  13.7 9.3 %collective-permute-start.6 = (bf16[392,768]{1,0:T(8,128)(2,1)}, bf16[392,768]{1,0:T(8,128)(2,1)S(1)}, u32[]{:S(2)}, u32[]{:S(2)}) collective-permute-start(bf16[392,768]{1,0:T(8,128)(2,1)} %get-tuple-element.55), channel_id=1, source_target_pairs={{16,38},{17,39},{18,36},{19,37},{20,34},{21,35},{22,32},{23,33},{4... | collective-permute-start | bytes 1806344 | tf_op jit(solution)/shard_map/ppermute | solution.py:28
  23.0 0.0 collective-permute-done.4
  23.0 0.1 copy.18
  23.1 0.1 pad_add_fusion.2
  23.2 0.8 copy-done.5
  24.1 2.5 %collective-permute-start.10 = (bf16[392,768]{1,0:T(8,128)(2,1)}, bf16[392,768]{1,0:T(8,128)(2,1)}, u32[]{:S(2)}, u32[]{:S(2)}) collective-permute-start(bf16[392,768]{1,0:T(8,128)(2,1)} %get-tuple-element.55), channel_id=1, source_target_pairs={{0,8},{1,9},{2,10},{3,11},{4,12},{5,13},{6,14},{7,15},{8,16},{9,17... | collective-permute-start | bytes 1806344 | tf_op jit(solution)/shard_map/ppermute | solution.py:28
  26.5 6.8 %collective-permute-start.11 = (bf16[392,768]{1,0:T(8,128)(2,1)}, bf16[392,768]{1,0:T(8,128)(2,1)S(1)}, u32[]{:S(2)}, u32[]{:S(2)}) collective-permute-start(bf16[392,768]{1,0:T(8,128)(2,1)} %copy-done.5), channel_id=1, source_target_pairs={{0,24},{1,25},{2,26},{3,27},{4,28},{5,29},{6,30},{7,31},{8,38},{9,... | collective-permute-start | bytes 1806344 | tf_op jit(solution)/shard_map/ppermute | solution.py:28
  33.3 9.3 %copy.19 = bf16[2,8,2,192,768]{4,3,2,1,0:T(8,128)(2,1)} copy(bf16[2,8,2,192,768]{4,2,3,1,0:T(2,128)(2,1)} %bitcast.37) | data formatting | bytes 18874368 | tf_op jit(solution)/shard_map/transpose | solution.py:248
  42.6 0.7 collective-permute-start.7
  43.3 0.0 collective-permute-done.5.refs_0_
  43.4 19.6 %collective-permute-done.6.refs_0_ = bf16[392,768]{1,0:T(8,128)(2,1)S(1)} collective-permute-done((bf16[392,768]{1,0:T(8,128)(2,1)}, bf16[392,768]{1,0:T(8,128)(2,1)S(1)}, u32[]{:S(2)}, u32[]{:S(2)}) %collective-permute-start.6) | collective-permute-done | bytes 602144 | tf_op jit(solution)/shard_map/ppermute | solution.py:28
  63.0 1.5 %collective-permute-start.8 = (bf16[392,768]{1,0:T(8,128)(2,1)S(1)}, bf16[392,768]{1,0:T(8,128)(2,1)}, u32[]{:S(2)}, u32[]{:S(2)}) collective-permute-start(bf16[392,768]{1,0:T(8,128)(2,1)S(1)} %collective-permute-done.5.refs_0_), channel_id=1, source_target_pairs={{0,8},{1,9},{2,10},{3,11},{4,12},{5,13},{6,14},{7,15},{32,40},{33,... | collective-permute-start | bytes 1806344 | tf_op jit(solution)/shard_map/ppermute | solution.py:28
  64.5 1.3 %collective-permute-start.9 = (bf16[392,768]{1,0:T(8,128)(2,1)}, bf16[392,768]{1,0:T(8,128)(2,1)}, u32[]{:S(2)}, u32[]{:S(2)}) collective-permute-start(bf16[392,768]{1,0:T(8,128)(2,1)} %get-tuple-element.55), channel_id=1, source_target_pairs={{0,16},{1,17},{2,18},{3,19},{4,20},{5,21},{6,22},{7,23},{8,24},{9,... | collective-permute-start | bytes 1806344 | tf_op jit(solution)/shard_map/ppermute | solution.py:28
  65.7 0.1 copy.23.pairs
  65.9 3.7 %copy-done = bf16[2,8,2,192,768]{4,3,2,1,0:T(8,128)(2,1)S(1)} copy-done((bf16[2,8,2,192,768]{4,3,2,1,0:T(8,128)(2,1)S(1)}, bf16[2,8,2,192,768]{4,3,2,1,0:T(8,128)(2,1)}, u32[]{:S(2)}) %copy-start) | copy-done | bytes 9437208
  69.5 4.6 %shard_map.55 = (f32[4,2,24,192]{3,2,1,0:T(8,128)S(1)}, f32[4,2,24,192]{3,2,1,0:T(8,128)S(1)}) custom-call(s32[2,2]{1,0:T(2,128)S(1)} %copy-done.1, s32[8,2,2,2]{3,2,1,0:T(2,128)S(1)} %copy.23.pairs, s32[2]{0:T(128)S(1)} %pad_add_fusion.3.here, f32[8]{0:T(128)S(1)} %copy-done.2, f32[2,1,192]{2,1,0:T(1,128)S(1)} %reshape.12.own_energy, ...), custom_call_target="tpu_custom_call" | custom-call | flops 1925185536 | bytes 5308416 | tf_op jit(solution)/shard_map/pallas_call | solution.py:174
  74.1 4.5 %shard_map.56 = (f32[4,2,24,192]{3,2,1,0:T(8,128)S(1)}, f32[4,2,24,192]{3,2,1,0:T(8,128)S(1)}) custom-call(s32[2,2]{1,0:T(2,128)S(1)} %copy-done.1, s32[8,2,2,2]{3,2,1,0:T(2,128)S(1)} %copy.23.pairs, s32[2]{0:T(128)S(1)} %pad_add_fusion.3.here, f32[8]{0:T(128)S(1)} %copy-done.2, f32[2,1,192]{2,1,0:T(1,128)S(1)} %reshape.12.own_energy, ...), custom_call_target="tpu_custom_call" | custom-call | flops 1925185536 | bytes 5308416 | tf_op jit(solution)/shard_map/pallas_call | solution.py:174
  78.6 4.3 %shard_map.57 = (f32[4,2,24,192]{3,2,1,0:T(8,128)S(1)}, f32[4,2,24,192]{3,2,1,0:T(8,128)S(1)}) custom-call(s32[2,2]{1,0:T(2,128)S(1)} %copy-done.1, s32[8,2,2,2]{3,2,1,0:T(2,128)S(1)} %copy.23.pairs, s32[2]{0:T(128)S(1)} %pad_add_fusion.3.here, f32[8]{0:T(128)S(1)} %copy-done.2, f32[2,1,192]{2,1,0:T(1,128)S(1)} %reshape.12.own_energy, ...), custom_call_target="tpu_custom_call" | custom-call | flops 1925185536 | bytes 5308416 | tf_op jit(solution)/shard_map/pallas_call | solution.py:174
  82.9 0.0 collective-permute-done.7.refs_0_
  82.9 0.0 collective-permute-done.8.refs_1_
  82.9 10.5 %collective-permute-done.9.refs_2_ = bf16[392,768]{1,0:T(8,128)(2,1)} collective-permute-done((bf16[392,768]{1,0:T(8,128)(2,1)}, bf16[392,768]{1,0:T(8,128)(2,1)}, u32[]{:S(2)}, u32[]{:S(2)}) %collective-permute-start.9) | collective-permute-done | bytes 602144 | tf_op jit(solution)/shard_map/ppermute | solution.py:28
  93.4 5.0 %shard_map.58 = (f32[4,2,2,24,192]{4,3,2,1,0:T(8,128)S(1)}, f32[4,2,2,24,192]{4,3,2,1,0:T(8,128)S(1)}) custom-call(s32[2,2]{1,0:T(2,128)S(1)} %copy-done.1, s32[8,2,2,2]{3,2,1,0:T(2,128)S(1)} %copy.23.pairs, s32[2]{0:T(128)S(1)} %pad_add_fusion.3.here, f32[8]{0:T(128)S(1)} %copy-done.2, f32[2,1,192]{2,1,0:T(1,128)S(1)} %reshape.12.own_energy, ...), custom_call_target="tpu_custom_call" | custom-call | flops 1925185536 | bytes 5308416 | tf_op jit(solution)/shard_map/pallas_call | solution.py:174
  98.3 0.1 collective-permute-start.12
  98.5 1.6 %collective-permute-done.12 = f32[4,2,2,24,192]{4,3,2,1,0:T(8,128)S(1)} collective-permute-done((f32[4,2,2,24,192]{4,3,2,1,0:T(8,128)S(1)}, f32[4,2,2,24,192]{4,3,2,1,0:T(8,128)S(1)}, u32[]{:S(2)}, u32[]{:S(2)}) %collective-permute-start.12) | collective-permute-done | bytes 294944 | tf_op jit(solution)/shard_map/ppermute | solution.py:200
  100.2 0.1 add.62
  100.3 0.1 collective-permute-start.13
  100.3 3.0 %collective-permute-start.14 = (f32[2,2,24,192]{3,2,1,0:T(8,128)S(1)}, f32[2,2,24,192]{3,2,1,0:T(8,128)S(1)}, u32[]{:S(2)}, u32[]{:S(2)}) collective-permute-start(f32[2,2,24,192]{3,2,1,0:T(8,128)S(1)} %get-tuple-element.79), channel_id=1, source_target_pairs={{0,4},{1,5},{2,6},{3,7},{4,0},{5,1},{6,2},{7,3},{8,12},{9,13},{10,... | collective-permute-start | bytes 221192 | tf_op jit(solution)/shard_map/ppermute | solution.py:205
  103.4 0.8 collective-permute-start.15
  104.2 3.7 %collective-permute-done.13 = f32[2,2,24,192]{3,2,1,0:T(8,128)S(1)} collective-permute-done((f32[2,2,24,192]{3,2,1,0:T(8,128)S(1)}, f32[2,2,24,192]{3,2,1,0:T(8,128)S(1)}, u32[]{:S(2)}, u32[]{:S(2)}) %collective-permute-start.13) | collective-permute-done | bytes 73760 | tf_op jit(solution)/shard_map/ppermute | solution.py:205
  107.9 3.3 %collective-permute-done.14 = f32[2,2,24,192]{3,2,1,0:T(8,128)S(1)} collective-permute-done((f32[2,2,24,192]{3,2,1,0:T(8,128)S(1)}, f32[2,2,24,192]{3,2,1,0:T(8,128)S(1)}, u32[]{:S(2)}, u32[]{:S(2)}) %collective-permute-start.14) | collective-permute-done | bytes 73760 | tf_op jit(solution)/shard_map/ppermute | solution.py:205
  111.2 0.0 collective-permute-done.15
  111.2 0.7 copy.24
  (20 shorter events, 0.1 us)
Async XLA Ops:
  0.0 5.9 %collective-permute-start = (s32[1,2,2,2]{3,2,1,0:T(2,128)}, s32[1,2,2,2]{3,2,1,0:T(2,128)S(1)}, u32[]{:S(2)}, u32[]{:S(2)}) collective-permute-start(s32[1,2,2,2]{3,2,1,0:T(2,128)} %bitcast.40), channel_id=1, source_target_pairs={{0,2},{1,3},{2,0},{3,1},{4,6},{5,7},{6,4},{7,5},{8,10},{9,11},{10,... | collective-permute-start | bytes 104 | tf_op jit(solution)/shard_map/ppermute | solution.py:210
  4.0 0.7 copy-start.3
  4.7 1.2 %copy-start.4 = (s32[2,2,2]{2,1,0:T(2,128)S(1)}, s32[2,2,2]{2,1,0:T(2,128)}, u32[]{:S(2)}) copy-start(s32[2,2,2]{2,1,0:T(2,128)} %param.9) | copy-start | bytes 100
  5.9 17.3 %collective-permute-start.2 = (bf16[392,768]{1,0:T(8,128)(2,1)S(1)}, bf16[392,768]{1,0:T(8,128)(2,1)S(1)}, u32[]{:S(2)}, u32[]{:S(2)}) collective-permute-start(bf16[392,768]{1,0:T(8,128)(2,1)S(1)} %get-tuple-element.44), channel_id=1, source_target_pairs={{0,8},{1,9},{2,10},{3,11},{4,12},{5,13},{6,14},{7,15},{8,16},{9,17... | collective-permute-start | bytes 1806344 | tf_op jit(solution)/shard_map/ppermute | solution.py:28
  7.2 16.0 %collective-permute-start.3 = (bf16[392,768]{1,0:T(8,128)(2,1)S(1)}, bf16[392,768]{1,0:T(8,128)(2,1)S(1)}, u32[]{:S(2)}, u32[]{:S(2)}) collective-permute-start(bf16[392,768]{1,0:T(8,128)(2,1)S(1)} %get-tuple-element.44), channel_id=1, source_target_pairs={{0,24},{1,25},{2,26},{3,27},{4,28},{5,29},{6,30},{7,31},{8,0},{9,1... | collective-permute-start | bytes 1806344 | tf_op jit(solution)/shard_map/ppermute | solution.py:28
  8.0 4.9 %collective-permute-start.1 = (s32[2,2,2,2]{3,2,1,0:T(2,128)S(1)}, s32[2,2,2,2]{3,2,1,0:T(2,128)S(1)}, u32[]{:S(2)}, u32[]{:S(2)}) collective-permute-start(s32[2,2,2,2]{3,2,1,0:T(2,128)S(1)} %pad_add_fusion.1), channel_id=1, source_target_pairs={{0,4},{1,5},{2,6},{3,7},{4,0},{5,1},{6,2},{7,3},{8,12},{9,13},{10,... | collective-permute-start | bytes 200 | tf_op jit(solution)/shard_map/ppermute | solution.py:210
  12.9 10.1 %collective-permute-start.4 = (s32[4,2,2,2]{3,2,1,0:T(2,128)S(1)}, s32[4,2,2,2]{3,2,1,0:T(2,128)S(1)}, u32[]{:S(2)}, u32[]{:S(2)}) collective-permute-start(s32[4,2,2,2]{3,2,1,0:T(2,128)S(1)} %pad_add_fusion), channel_id=1, source_target_pairs={{0,1},{1,0},{2,3},{3,2},{4,5},{5,4},{6,7},{7,6},{8,9},{9,8},{10,11... | collective-permute-start | bytes 392 | tf_op jit(solution)/shard_map/ppermute | solution.py:210
  13.0 30.3 %collective-permute-start.5 = (bf16[392,768]{1,0:T(8,128)(2,1)}, bf16[392,768]{1,0:T(8,128)(2,1)S(1)}, u32[]{:S(2)}, u32[]{:S(2)}) collective-permute-start(bf16[392,768]{1,0:T(8,128)(2,1)} %get-tuple-element.55), channel_id=1, source_target_pairs={{24,38},{25,39},{26,36},{27,37},{28,34},{29,35},{30,32},{31,33},{5... | collective-permute-start | bytes 1806344 | tf_op jit(solution)/shard_map/ppermute | solution.py:28
  13.7 49.3 %collective-permute-start.6 = (bf16[392,768]{1,0:T(8,128)(2,1)}, bf16[392,768]{1,0:T(8,128)(2,1)S(1)}, u32[]{:S(2)}, u32[]{:S(2)}) collective-permute-start(bf16[392,768]{1,0:T(8,128)(2,1)} %get-tuple-element.55), channel_id=1, source_target_pairs={{16,38},{17,39},{18,36},{19,37},{20,34},{21,35},{22,32},{23,33},{4... | collective-permute-start | bytes 1806344 | tf_op jit(solution)/shard_map/ppermute | solution.py:28
  23.2 0.9 copy-start.5
  24.1 41.8 %collective-permute-start.10 = (bf16[392,768]{1,0:T(8,128)(2,1)}, bf16[392,768]{1,0:T(8,128)(2,1)}, u32[]{:S(2)}, u32[]{:S(2)}) collective-permute-start(bf16[392,768]{1,0:T(8,128)(2,1)} %get-tuple-element.55), channel_id=1, source_target_pairs={{0,8},{1,9},{2,10},{3,11},{4,12},{5,13},{6,14},{7,15},{8,16},{9,17... | collective-permute-start | bytes 1806344 | tf_op jit(solution)/shard_map/ppermute | solution.py:28
  26.5 52.1 %collective-permute-start.11 = (bf16[392,768]{1,0:T(8,128)(2,1)}, bf16[392,768]{1,0:T(8,128)(2,1)S(1)}, u32[]{:S(2)}, u32[]{:S(2)}) collective-permute-start(bf16[392,768]{1,0:T(8,128)(2,1)} %copy-done.5), channel_id=1, source_target_pairs={{0,24},{1,25},{2,26},{3,27},{4,28},{5,29},{6,30},{7,31},{8,38},{9,... | collective-permute-start | bytes 1806344 | tf_op jit(solution)/shard_map/ppermute | solution.py:28
  33.3 32.5 %copy-start.1 = (s32[2,2]{1,0:T(2,128)S(1)}, s32[2,2]{1,0:T(2,128)}, u32[]{:S(2)}) copy-start(s32[2,2]{1,0:T(2,128)} %conserve.7) | copy-start | bytes 52
  33.3 32.5 %copy-start.2 = (f32[8]{0:T(128)S(1)}, f32[8]{0:T(128)}, u32[]{:S(2)}) copy-start(f32[8]{0:T(128)} %occupied.7) | copy-start | bytes 100
  42.6 40.3 %collective-permute-start.7 = (bf16[392,768]{1,0:T(8,128)(2,1)S(1)}, bf16[392,768]{1,0:T(8,128)(2,1)S(1)}, u32[]{:S(2)}, u32[]{:S(2)}) collective-permute-start(bf16[392,768]{1,0:T(8,128)(2,1)S(1)} %collective-permute-done.2.refs_1_), channel_id=1, source_target_pairs={{0,38},{1,39},{2,36},{3,37},{4,34},{5,35},{6,32},{7,33},{32,6},{33... | collective-permute-start | bytes 1806344 | tf_op jit(solution)/shard_map/ppermute | solution.py:28
  63.0 20.0 %collective-permute-start.8 = (bf16[392,768]{1,0:T(8,128)(2,1)S(1)}, bf16[392,768]{1,0:T(8,128)(2,1)}, u32[]{:S(2)}, u32[]{:S(2)}) collective-permute-start(bf16[392,768]{1,0:T(8,128)(2,1)S(1)} %collective-permute-done.5.refs_0_), channel_id=1, source_target_pairs={{0,8},{1,9},{2,10},{3,11},{4,12},{5,13},{6,14},{7,15},{32,40},{33,... | collective-permute-start | bytes 1806344 | tf_op jit(solution)/shard_map/ppermute | solution.py:28
  64.5 28.9 %collective-permute-start.9 = (bf16[392,768]{1,0:T(8,128)(2,1)}, bf16[392,768]{1,0:T(8,128)(2,1)}, u32[]{:S(2)}, u32[]{:S(2)}) collective-permute-start(bf16[392,768]{1,0:T(8,128)(2,1)} %get-tuple-element.55), channel_id=1, source_target_pairs={{0,16},{1,17},{2,18},{3,19},{4,20},{5,21},{6,22},{7,23},{8,24},{9,... | collective-permute-start | bytes 1806344 | tf_op jit(solution)/shard_map/ppermute | solution.py:28
  65.9 3.7 %copy-start = (bf16[2,8,2,192,768]{4,3,2,1,0:T(8,128)(2,1)S(1)}, bf16[2,8,2,192,768]{4,3,2,1,0:T(8,128)(2,1)}, u32[]{:S(2)}) copy-start(bf16[2,8,2,192,768]{4,3,2,1,0:T(8,128)(2,1)} %copy.19) | copy-start | bytes 28311556
  98.3 1.8 %collective-permute-start.12 = (f32[4,2,2,24,192]{4,3,2,1,0:T(8,128)S(1)}, f32[4,2,2,24,192]{4,3,2,1,0:T(8,128)S(1)}, u32[]{:S(2)}, u32[]{:S(2)}) collective-permute-start(f32[4,2,2,24,192]{4,3,2,1,0:T(8,128)S(1)} %get-tuple-element.74), channel_id=1, source_target_pairs={{0,1},{1,0},{2,3},{3,2},{4,5},{5,4},{6,7},{7,6},{8,9},{9,8},{10,11... | collective-permute-start | bytes 884744 | tf_op jit(solution)/shard_map/ppermute | solution.py:200
  100.3 7.6 %collective-permute-start.13 = (f32[2,2,24,192]{3,2,1,0:T(8,128)S(1)}, f32[2,2,24,192]{3,2,1,0:T(8,128)S(1)}, u32[]{:S(2)}, u32[]{:S(2)}) collective-permute-start(f32[2,2,24,192]{3,2,1,0:T(8,128)S(1)} %get-tuple-element.77), channel_id=1, source_target_pairs={{0,2},{1,3},{2,4},{3,5},{4,6},{5,7},{6,0},{7,1},{8,10},{9,11},{10,... | collective-permute-start | bytes 221192 | tf_op jit(solution)/shard_map/ppermute | solution.py:205
  100.3 10.8 %collective-permute-start.14 = (f32[2,2,24,192]{3,2,1,0:T(8,128)S(1)}, f32[2,2,24,192]{3,2,1,0:T(8,128)S(1)}, u32[]{:S(2)}, u32[]{:S(2)}) collective-permute-start(f32[2,2,24,192]{3,2,1,0:T(8,128)S(1)} %get-tuple-element.79), channel_id=1, source_target_pairs={{0,4},{1,5},{2,6},{3,7},{4,0},{5,1},{6,2},{7,3},{8,12},{9,13},{10,... | collective-permute-start | bytes 221192 | tf_op jit(solution)/shard_map/ppermute | solution.py:205
  103.4 7.8 %collective-permute-start.15 = (f32[2,2,24,192]{3,2,1,0:T(8,128)S(1)}, f32[2,2,24,192]{3,2,1,0:T(8,128)S(1)}, u32[]{:S(2)}, u32[]{:S(2)}) collective-permute-start(f32[2,2,24,192]{3,2,1,0:T(8,128)S(1)} %get-tuple-element.78), channel_id=1, source_target_pairs={{0,6},{1,7},{2,0},{3,1},{4,2},{5,3},{6,4},{7,5},{8,14},{9,15},{10,... | collective-permute-start | bytes 221192 | tf_op jit(solution)/shard_map/ppermute | solution.py:205

commit v10 on v9

--- a/solution.py
+++ b/solution.py
@@ -236,7 +236,7 @@
     pairs = with_partner(pairs, 2 * CORES)
     m0, pairs, factors = lax.optimization_barrier((m0, pairs, factors))
     cross_one = moved(m0, {3: (0, onto_next)})
-    cross_two = moved(m0, {2: (0, onto_next)})
+    two = moved(m0, {0: (2, same), 1: (3, same), 2: (0, onto_next)})
     pairs = with_partner(pairs, 1)
     own_energy = virtual_energy.astype(jnp.float32)[:, None, :]
     m0, plus, minus, factors, pairs, own_energy = lax.optimization_barrier(
@@ -246,22 +246,21 @@
     back = moved(minus, {0: (3, same), 1: (0, across), 2: (1, across), 3: (2, same)})
     near_one = moved(m0, {0: (1, same), 1: (2, same), 2: (3, same)})
     left = jnp.transpose(factors, (0, 1, 3, 2, 4)).reshape(momenta, orbitals, 2 * virtuals, auxiliary)
-    m0, cross_one, cross_two, left = lax.optimization_barrier((m0, cross_one, cross_two, left))
+    cross_one, left = lax.optimization_barrier((cross_one, left))
     onward = moved(cross_one, {0: (1, same)})
-    near_two = moved(m0, {0: (2, same), 1: (3, same)})
 
     def density(orders, held, mates, before):
         return piece_density(
             orders, held, conserve, pairs, here, occupied_energy, own_energy, left, mates, before
         )
 
-    orders = (((0,), (0,)), ((1, 0), (0, 1)), ((1,), (1,)), ((0, 1), (1, 0)))
-    terms = density(orders[:1], (0, 1), (cross_one, near_one), ())
-    *terms, cross_two, plus = lax.optimization_barrier((*terms, cross_two, plus))
-    terms += density(orders[1:2], (0, 1), (cross_two, plus), ())
+    orders = (((1, 0), (0, 1)), ((0,), (0,)), ((1,), (1,)), ((0, 1), (1, 0)))
+    terms = density(orders[:1], (0, 1), (two, plus), ())
+    *terms, cross_one, near_one = lax.optimization_barrier((*terms, cross_one, near_one))
+    terms += density(orders[1:2], (0, 1), (cross_one, near_one), ())
     *terms, back = lax.optimization_barrier((*terms, back))
     terms += density(orders[2:3], (0,), (back,), ())
-    total = density(orders, (0, 1, 2), (up, onward, near_two), terms)
+    total = density(orders, (0, 1, 2), (up, onward, two), terms)
     return jnp.transpose(summed(*total), (0, 2, 1, 3))
 
 

time: 112 us -> 111 us (level)
  the two profiles are of different devices: /device:TPU:4 before, /device:TPU:1 now
where the time goes in v10:
time: 111 us
  starting transfers between devices  59.5 us (54%)
  Pallas kernels  18.1 us (16%)
  local copies, waits for them, and re-layouts  17.1 us (15%)
  waiting for transfers between devices  14.3 us (13%)
  other arithmetic  1.37 us (1%)
    ppermute x8, starting transfers between devices, moved(): return lax.ppermute(array, ('ka', 'occ'), pairs)  37.6 us
    pallas_call x4, Pallas kernels, piece_density(): pl.pallas_call(functools.partial(piece_kernel, len(mates), len(before), o...  18.1 us
    transpose x1, local copies, waits for them, and re-layouts, local(): jnp.transpose(factors, (0, 1, 3, 2, 4))  9.31 us
    ppermute x3, starting transfers between devices, with_partner(): lax.ppermute(array, 'occ', [(i, i ^ reach) for i in range(LINE * CORES)])  8.21 us
    ppermute x3, starting transfers between devices, summed(): total = total + lax.ppermute(part, 'occ', ring)  7.56 us
    ppermute x3, waiting for transfers between devices, summed(): total = total + lax.ppermute(part, 'occ', ring)  7.03 us
    ppermute x1, starting transfers between devices, summed(): lax.ppermute(send, 'occ', [(i, i ^ 1) for i in range(devices)])  6.14 us
    ppermute x8, waiting for transfers between devices, moved(): return lax.ppermute(array, ('ka', 'occ'), pairs)  4.24 us
  transfers between devices with their start and end apart: 15, of which 7 were waited for; matrix products, arithmetic and copies ran while one was open for 13% of the time, Pallas kernels for 12%

profile of v10, /device:TPU:1, one launch (start us, length us, event | category | flops | bytes accessed | tf_op | source)
XLA Modules:
  0.0 110.6 jit_solution(3646778968587036226)
XLA Ops:
  0.0 2.5 %collective-permute-start = (s32[1,2,2,2]{3,2,1,0:T(2,128)}, s32[1,2,2,2]{3,2,1,0:T(2,128)S(1)}, u32[]{:S(2)}, u32[]{:S(2)}) collective-permute-start(s32[1,2,2,2]{3,2,1,0:T(2,128)} %bitcast.40), channel_id=1, source_target_pairs={{0,2},{1,3},{2,0},{3,1},{4,6},{5,7},{6,4},{7,5},{8,10},{9,11},{10,... | collective-permute-start | bytes 104 | tf_op jit(solution)/shard_map/ppermute | solution.py:210
  2.5 0.8 fusion.10
  3.2 2.1 %constant_dynamic-slice_fusion = (bf16[1,8,24,2,768]{4,3,2,1,0:T(2,128)(2,1)S(1)}, bf16[1,8,24,2,768]{4,3,2,1,0:T(2,128)(2,1)S(1)}) fusion(bf16[2,8,192,2,768]{4,3,2,1,0:T(2,128)(2,1)} %param.5, s32[]{:T(128)S(6)} %select_n.44), kind=kLoop, calls=%fused_computation.19 | loop fusion | bytes 2359300 | tf_op jit(solution)/shard_map/dynamic_slice | solution.py:222
  5.3 0.1 copy.28
  5.4 0.1 copy.27
  5.4 0.0 copy-start.4
  5.5 0.1 pad_add_fusion.3.here
  5.5 0.1 pad.22.clone
  5.6 1.1 %fusion.6 = (bf16[392,768]{1,0:T(8,128)(2,1)S(1)}, bf16[392,768]{1,0:T(8,128)(2,1)}) fusion(bf16[1,192]{1,0:T(2,128)(2,1)S(1)} %get-tuple-element.78, bf16[384,768]{1,0:T(8,128)(2,1)S(1)} %bitcast.38, bf16[392]{0:T(512)(128)(2,1)S(1)} %pad.22.clone, bf16[1,192]{1,0:T(2,128)(2,1)S(1)} %get-tuple-element.79, bf16[384,768]{1,0:T(8,128)(2,1)S(1)} %bitcast.39), kind=kLoop, calls=%fused_computation.8 | loop fusion | flops 4816896 | bytes 2385424 | tf_op jit(solution)/shard_map/concatenate | solution.py:228
  6.7 0.0 collective-permute-done
  6.7 2.6 %collective-permute-start.3 = (bf16[392,768]{1,0:T(8,128)(2,1)S(1)}, bf16[392,768]{1,0:T(8,128)(2,1)S(1)}, u32[]{:S(2)}, u32[]{:S(2)}) collective-permute-start(bf16[392,768]{1,0:T(8,128)(2,1)S(1)} %get-tuple-element.42), channel_id=1, source_target_pairs={{0,24},{1,25},{2,26},{3,27},{4,28},{5,29},{6,30},{7,31},{8,0},{9,1... | collective-permute-start | bytes 1806344 | tf_op jit(solution)/shard_map/ppermute | solution.py:28
  9.3 3.0 %collective-permute-start.1 = (s32[2,2,2,2]{3,2,1,0:T(2,128)S(1)}, s32[2,2,2,2]{3,2,1,0:T(2,128)S(1)}, u32[]{:S(2)}, u32[]{:S(2)}) collective-permute-start(s32[2,2,2,2]{3,2,1,0:T(2,128)S(1)} %pad_add_fusion.1), channel_id=1, source_target_pairs={{0,4},{1,5},{2,6},{3,7},{4,0},{5,1},{6,2},{7,3},{8,12},{9,13},{10,... | collective-permute-start | bytes 200 | tf_op jit(solution)/shard_map/ppermute | solution.py:210
  12.3 1.0 collective-permute-done.1
  13.3 1.3 %collective-permute-start.5 = (bf16[392,768]{1,0:T(8,128)(2,1)}, bf16[392,768]{1,0:T(8,128)(2,1)S(1)}, u32[]{:S(2)}, u32[]{:S(2)}) collective-permute-start(bf16[392,768]{1,0:T(8,128)(2,1)} %get-tuple-element.54), channel_id=1, source_target_pairs={{24,38},{25,39},{26,36},{27,37},{28,34},{29,35},{30,32},{31,33},{5... | collective-permute-start | bytes 1806344 | tf_op jit(solution)/shard_map/ppermute | solution.py:28
  14.6 3.0 %collective-permute-start.8 = (bf16[392,768]{1,0:T(8,128)(2,1)}, bf16[392,768]{1,0:T(8,128)(2,1)S(1)}, u32[]{:S(2)}, u32[]{:S(2)}) collective-permute-start(bf16[392,768]{1,0:T(8,128)(2,1)} %get-tuple-element.54), channel_id=1, source_target_pairs={{0,16},{1,17},{2,18},{3,19},{4,20},{5,21},{6,22},{7,23},{8,24},{9,... | collective-permute-start | bytes 1806344 | tf_op jit(solution)/shard_map/ppermute | solution.py:28
  17.6 2.8 %collective-permute-start.4 = (s32[4,2,2,2]{3,2,1,0:T(2,128)S(1)}, s32[4,2,2,2]{3,2,1,0:T(2,128)S(1)}, u32[]{:S(2)}, u32[]{:S(2)}) collective-permute-start(s32[4,2,2,2]{3,2,1,0:T(2,128)S(1)} %pad_add_fusion), channel_id=1, source_target_pairs={{0,1},{1,0},{2,3},{3,2},{4,5},{5,4},{6,7},{7,6},{8,9},{9,8},{10,11... | collective-permute-start | bytes 392 | tf_op jit(solution)/shard_map/ppermute | solution.py:210
  20.4 0.1 copy.17
  20.5 0.7 collective-permute-done.4
  21.2 0.1 copy.18
  21.3 0.1 pad_add_fusion.2
  21.4 0.0 collective-permute-done.3
  21.4 4.2 %collective-permute-done.2.refs_1_ = bf16[392,768]{1,0:T(8,128)(2,1)S(1)} collective-permute-done((bf16[392,768]{1,0:T(8,128)(2,1)S(1)}, bf16[392,768]{1,0:T(8,128)(2,1)S(1)}, u32[]{:S(2)}, u32[]{:S(2)}) %collective-permute-start.2) | collective-permute-done | bytes 602144 | tf_op jit(solution)/shard_map/ppermute | solution.py:28
  25.6 6.2 %collective-permute-start.9 = (bf16[392,768]{1,0:T(8,128)(2,1)}, bf16[392,768]{1,0:T(8,128)(2,1)}, u32[]{:S(2)}, u32[]{:S(2)}) collective-permute-start(bf16[392,768]{1,0:T(8,128)(2,1)} %get-tuple-element.54), channel_id=1, source_target_pairs={{0,8},{1,9},{2,10},{3,11},{4,12},{5,13},{6,14},{7,15},{8,16},{9,17... | collective-permute-start | bytes 1806344 | tf_op jit(solution)/shard_map/ppermute | solution.py:28
  31.8 22.5 %collective-permute-start.6 = (bf16[392,768]{1,0:T(8,128)(2,1)S(1)}, bf16[392,768]{1,0:T(8,128)(2,1)S(1)}, u32[]{:S(2)}, u32[]{:S(2)}) collective-permute-start(bf16[392,768]{1,0:T(8,128)(2,1)S(1)} %collective-permute-done.2.refs_1_), channel_id=1, source_target_pairs={{0,38},{1,39},{2,36},{3,37},{4,34},{5,35},{6,32},{7,33},{32,6},{33... | collective-permute-start | bytes 1806344 | tf_op jit(solution)/shard_map/ppermute | solution.py:28
  54.3 0.0 copy-start.1
  54.3 0.0 copy-start.2
  54.3 9.3 %copy.19 = bf16[2,8,2,192,768]{4,3,2,1,0:T(8,128)(2,1)} copy(bf16[2,8,2,192,768]{4,2,3,1,0:T(2,128)(2,1)} %bitcast.37) | data formatting | bytes 18874368 | tf_op jit(solution)/shard_map/transpose | solution.py:248
  63.6 2.1 %collective-permute-start.7 = (bf16[392,768]{1,0:T(8,128)(2,1)S(1)}, bf16[392,768]{1,0:T(8,128)(2,1)}, u32[]{:S(2)}, u32[]{:S(2)}) collective-permute-start(bf16[392,768]{1,0:T(8,128)(2,1)S(1)} %collective-permute-done.5.refs_0_), channel_id=1, source_target_pairs={{0,8},{1,9},{2,10},{3,11},{4,12},{5,13},{6,14},{7,15},{32,40},{33,... | collective-permute-start | bytes 1806344 | tf_op jit(solution)/shard_map/ppermute | solution.py:28
  65.7 0.1 copy.23.pairs
  65.8 0.0 collective-permute-done.8.refs_0_.refs_2_
  65.9 3.7 %copy-done = bf16[2,8,2,192,768]{4,3,2,1,0:T(8,128)(2,1)S(1)} copy-done((bf16[2,8,2,192,768]{4,3,2,1,0:T(8,128)(2,1)S(1)}, bf16[2,8,2,192,768]{4,3,2,1,0:T(8,128)(2,1)}, u32[]{:S(2)}) %copy-start) | copy-done | bytes 9437208
  69.5 4.3 %shard_map.55 = (f32[4,2,24,192]{3,2,1,0:T(8,128)S(1)}, f32[4,2,24,192]{3,2,1,0:T(8,128)S(1)}) custom-call(s32[2,2]{1,0:T(2,128)S(1)} %copy-done.1, s32[8,2,2,2]{3,2,1,0:T(2,128)S(1)} %copy.23.pairs, s32[2]{0:T(128)S(1)} %pad_add_fusion.3.here, f32[8]{0:T(128)S(1)} %copy-done.2, f32[2,1,192]{2,1,0:T(1,128)S(1)} %reshape.12.own_energy, ...), custom_call_target="tpu_custom_call" | custom-call | flops 1925185536 | bytes 5308416 | tf_op jit(solution)/shard_map/pallas_call | solution.py:174
  73.9 0.0 collective-permute-done.9.refs_1_
  73.9 4.7 %shard_map.56 = (f32[4,2,24,192]{3,2,1,0:T(8,128)S(1)}, f32[4,2,24,192]{3,2,1,0:T(8,128)S(1)}) custom-call(s32[2,2]{1,0:T(2,128)S(1)} %copy-done.1, s32[8,2,2,2]{3,2,1,0:T(2,128)S(1)} %copy.23.pairs, s32[2]{0:T(128)S(1)} %pad_add_fusion.3.here, f32[8]{0:T(128)S(1)} %copy-done.2, f32[2,1,192]{2,1,0:T(1,128)S(1)} %reshape.12.own_energy, ...), custom_call_target="tpu_custom_call" | custom-call | flops 1925185536 | bytes 5308416 | tf_op jit(solution)/shard_map/pallas_call | solution.py:174
  78.6 0.0 collective-permute-done.10.refs_0_
  78.6 4.3 %shard_map.57 = (f32[4,2,24,192]{3,2,1,0:T(8,128)S(1)}, f32[4,2,24,192]{3,2,1,0:T(8,128)S(1)}) custom-call(s32[2,2]{1,0:T(2,128)S(1)} %copy-done.1, s32[8,2,2,2]{3,2,1,0:T(2,128)S(1)} %copy.23.pairs, s32[2]{0:T(128)S(1)} %pad_add_fusion.3.here, f32[8]{0:T(128)S(1)} %copy-done.2, f32[2,1,192]{2,1,0:T(1,128)S(1)} %reshape.12.own_energy, ...), custom_call_target="tpu_custom_call" | custom-call | flops 1925185536 | bytes 5308416 | tf_op jit(solution)/shard_map/pallas_call | solution.py:174
  82.9 0.0 collective-permute-done.6.refs_0_
  82.9 4.8 %shard_map.58 = (f32[4,2,2,24,192]{4,3,2,1,0:T(8,128)S(1)}, f32[4,2,2,24,192]{4,3,2,1,0:T(8,128)S(1)}) custom-call(s32[2,2]{1,0:T(2,128)S(1)} %copy-done.1, s32[8,2,2,2]{3,2,1,0:T(2,128)S(1)} %copy.23.pairs, s32[2]{0:T(128)S(1)} %pad_add_fusion.3.here, f32[8]{0:T(128)S(1)} %copy-done.2, f32[2,1,192]{2,1,0:T(1,128)S(1)} %reshape.12.own_energy, ...), custom_call_target="tpu_custom_call" | custom-call | flops 1925185536 | bytes 5308416 | tf_op jit(solution)/shard_map/pallas_call | solution.py:174
  87.7 6.1 %collective-permute-start.11 = (f32[4,2,2,24,192]{4,3,2,1,0:T(8,128)S(1)}, f32[4,2,2,24,192]{4,3,2,1,0:T(8,128)S(1)}, u32[]{:S(2)}, u32[]{:S(2)}) collective-permute-start(f32[4,2,2,24,192]{4,3,2,1,0:T(8,128)S(1)} %get-tuple-element.70), channel_id=1, source_target_pairs={{0,1},{1,0},{2,3},{3,2},{4,5},{5,4},{6,7},{7,6},{8,9},{9,8},{10,11... | collective-permute-start | bytes 884744 | tf_op jit(solution)/shard_map/ppermute | solution.py:200
  93.9 1.3 %collective-permute-done.11 = f32[4,2,2,24,192]{4,3,2,1,0:T(8,128)S(1)} collective-permute-done((f32[4,2,2,24,192]{4,3,2,1,0:T(8,128)S(1)}, f32[4,2,2,24,192]{4,3,2,1,0:T(8,128)S(1)}, u32[]{:S(2)}, u32[]{:S(2)}) %collective-permute-start.11) | collective-permute-done | bytes 294944 | tf_op jit(solution)/shard_map/ppermute | solution.py:200
  95.2 0.1 add.62
  95.3 5.7 %collective-permute-start.12 = (f32[2,2,24,192]{3,2,1,0:T(8,128)S(1)}, f32[2,2,24,192]{3,2,1,0:T(8,128)S(1)}, u32[]{:S(2)}, u32[]{:S(2)}) collective-permute-start(f32[2,2,24,192]{3,2,1,0:T(8,128)S(1)} %get-tuple-element.73), channel_id=1, source_target_pairs={{0,2},{1,3},{2,4},{3,5},{4,6},{5,7},{6,0},{7,1},{8,10},{9,11},{10,... | collective-permute-start | bytes 221192 | tf_op jit(solution)/shard_map/ppermute | solution.py:205
  101.0 0.1 collective-permute-start.14
  101.0 1.8 %collective-permute-start.13 = (f32[2,2,24,192]{3,2,1,0:T(8,128)S(1)}, f32[2,2,24,192]{3,2,1,0:T(8,128)S(1)}, u32[]{:S(2)}, u32[]{:S(2)}) collective-permute-start(f32[2,2,24,192]{3,2,1,0:T(8,128)S(1)} %get-tuple-element.75), channel_id=1, source_target_pairs={{0,4},{1,5},{2,6},{3,7},{4,0},{5,1},{6,2},{7,3},{8,12},{9,13},{10,... | collective-permute-start | bytes 221192 | tf_op jit(solution)/shard_map/ppermute | solution.py:205
  102.9 1.0 collective-permute-done.12
  103.8 2.3 %collective-permute-done.14 = f32[2,2,24,192]{3,2,1,0:T(8,128)S(1)} collective-permute-done((f32[2,2,24,192]{3,2,1,0:T(8,128)S(1)}, f32[2,2,24,192]{3,2,1,0:T(8,128)S(1)}, u32[]{:S(2)}, u32[]{:S(2)}) %collective-permute-start.14) | collective-permute-done | bytes 73760 | tf_op jit(solution)/shard_map/ppermute | solution.py:205
  106.1 3.8 %collective-permute-done.13 = f32[2,2,24,192]{3,2,1,0:T(8,128)S(1)} collective-permute-done((f32[2,2,24,192]{3,2,1,0:T(8,128)S(1)}, f32[2,2,24,192]{3,2,1,0:T(8,128)S(1)}, u32[]{:S(2)}, u32[]{:S(2)}) %collective-permute-start.13) | collective-permute-done | bytes 73760 | tf_op jit(solution)/shard_map/ppermute | solution.py:205
  109.9 0.7 copy.24
  (18 shorter events, 0.1 us)
Async XLA Ops:
  0.0 6.7 %collective-permute-start = (s32[1,2,2,2]{3,2,1,0:T(2,128)}, s32[1,2,2,2]{3,2,1,0:T(2,128)S(1)}, u32[]{:S(2)}, u32[]{:S(2)}) collective-permute-start(s32[1,2,2,2]{3,2,1,0:T(2,128)} %bitcast.40), channel_id=1, source_target_pairs={{0,2},{1,3},{2,0},{3,1},{4,6},{5,7},{6,4},{7,5},{8,10},{9,11},{10,... | collective-permute-start | bytes 104 | tf_op jit(solution)/shard_map/ppermute | solution.py:210
  5.4 1.3 %copy-start.4 = (s32[2,2,2]{2,1,0:T(2,128)S(1)}, s32[2,2,2]{2,1,0:T(2,128)}, u32[]{:S(2)}) copy-start(s32[2,2,2]{2,1,0:T(2,128)} %param.9) | copy-start | bytes 100
  5.6 14.8 %copy-start.3 = (bf16[2,192]{1,0:T(2,128)(2,1)S(1)}, bf16[2,192]{1,0:T(2,128)(2,1)}, u32[]{:S(2)}) copy-start(bf16[2,192]{1,0:T(2,128)(2,1)} %param.7) | copy-start | bytes 2308
  6.7 14.7 %collective-permute-start.3 = (bf16[392,768]{1,0:T(8,128)(2,1)S(1)}, bf16[392,768]{1,0:T(8,128)(2,1)S(1)}, u32[]{:S(2)}, u32[]{:S(2)}) collective-permute-start(bf16[392,768]{1,0:T(8,128)(2,1)S(1)} %get-tuple-element.42), channel_id=1, source_target_pairs={{0,24},{1,25},{2,26},{3,27},{4,28},{5,29},{6,30},{7,31},{8,0},{9,1... | collective-permute-start | bytes 1806344 | tf_op jit(solution)/shard_map/ppermute | solution.py:28
  9.3 16.3 %collective-permute-start.2 = (bf16[392,768]{1,0:T(8,128)(2,1)S(1)}, bf16[392,768]{1,0:T(8,128)(2,1)S(1)}, u32[]{:S(2)}, u32[]{:S(2)}) collective-permute-start(bf16[392,768]{1,0:T(8,128)(2,1)S(1)} %get-tuple-element.42), channel_id=1, source_target_pairs={{0,8},{1,9},{2,10},{3,11},{4,12},{5,13},{6,14},{7,15},{8,16},{9,17... | collective-permute-start | bytes 1806344 | tf_op jit(solution)/shard_map/ppermute | solution.py:28
  9.3 4.0 %collective-permute-start.1 = (s32[2,2,2,2]{3,2,1,0:T(2,128)S(1)}, s32[2,2,2,2]{3,2,1,0:T(2,128)S(1)}, u32[]{:S(2)}, u32[]{:S(2)}) collective-permute-start(s32[2,2,2,2]{3,2,1,0:T(2,128)S(1)} %pad_add_fusion.1), channel_id=1, source_target_pairs={{0,4},{1,5},{2,6},{3,7},{4,0},{5,1},{6,2},{7,3},{8,12},{9,13},{10,... | collective-permute-start | bytes 200 | tf_op jit(solution)/shard_map/ppermute | solution.py:210
  13.3 50.3 %collective-permute-start.5 = (bf16[392,768]{1,0:T(8,128)(2,1)}, bf16[392,768]{1,0:T(8,128)(2,1)S(1)}, u32[]{:S(2)}, u32[]{:S(2)}) collective-permute-start(bf16[392,768]{1,0:T(8,128)(2,1)} %get-tuple-element.54), channel_id=1, source_target_pairs={{24,38},{25,39},{26,36},{27,37},{28,34},{29,35},{30,32},{31,33},{5... | collective-permute-start | bytes 1806344 | tf_op jit(solution)/shard_map/ppermute | solution.py:28
  14.6 51.3 %collective-permute-start.8 = (bf16[392,768]{1,0:T(8,128)(2,1)}, bf16[392,768]{1,0:T(8,128)(2,1)S(1)}, u32[]{:S(2)}, u32[]{:S(2)}) collective-permute-start(bf16[392,768]{1,0:T(8,128)(2,1)} %get-tuple-element.54), channel_id=1, source_target_pairs={{0,16},{1,17},{2,18},{3,19},{4,20},{5,21},{6,22},{7,23},{8,24},{9,... | collective-permute-start | bytes 1806344 | tf_op jit(solution)/shard_map/ppermute | solution.py:28
  17.6 3.6 %collective-permute-start.4 = (s32[4,2,2,2]{3,2,1,0:T(2,128)S(1)}, s32[4,2,2,2]{3,2,1,0:T(2,128)S(1)}, u32[]{:S(2)}, u32[]{:S(2)}) collective-permute-start(s32[4,2,2,2]{3,2,1,0:T(2,128)S(1)} %pad_add_fusion), channel_id=1, source_target_pairs={{0,1},{1,0},{2,3},{3,2},{4,5},{5,4},{6,7},{7,6},{8,9},{9,8},{10,11... | collective-permute-start | bytes 392 | tf_op jit(solution)/shard_map/ppermute | solution.py:210
  21.4 4.2 %copy-start.5 = (bf16[392,768]{1,0:T(8,128)(2,1)}, bf16[392,768]{1,0:T(8,128)(2,1)S(1)}, u32[]{:S(2)}) copy-start(bf16[392,768]{1,0:T(8,128)(2,1)S(1)} %collective-permute-done.3) | copy-start | bytes 1806340
  25.6 48.2 %collective-permute-start.9 = (bf16[392,768]{1,0:T(8,128)(2,1)}, bf16[392,768]{1,0:T(8,128)(2,1)}, u32[]{:S(2)}, u32[]{:S(2)}) collective-permute-start(bf16[392,768]{1,0:T(8,128)(2,1)} %get-tuple-element.54), channel_id=1, source_target_pairs={{0,8},{1,9},{2,10},{3,11},{4,12},{5,13},{6,14},{7,15},{8,16},{9,17... | collective-permute-start | bytes 1806344 | tf_op jit(solution)/shard_map/ppermute | solution.py:28
  31.8 46.8 %collective-permute-start.10 = (bf16[392,768]{1,0:T(8,128)(2,1)}, bf16[392,768]{1,0:T(8,128)(2,1)S(1)}, u32[]{:S(2)}, u32[]{:S(2)}) collective-permute-start(bf16[392,768]{1,0:T(8,128)(2,1)} %copy-done.5), channel_id=1, source_target_pairs={{0,24},{1,25},{2,26},{3,27},{4,28},{5,29},{6,30},{7,31},{8,38},{9,... | collective-permute-start | bytes 1806344 | tf_op jit(solution)/shard_map/ppermute | solution.py:28
  31.8 51.1 %collective-permute-start.6 = (bf16[392,768]{1,0:T(8,128)(2,1)S(1)}, bf16[392,768]{1,0:T(8,128)(2,1)S(1)}, u32[]{:S(2)}, u32[]{:S(2)}) collective-permute-start(bf16[392,768]{1,0:T(8,128)(2,1)S(1)} %collective-permute-done.2.refs_1_), channel_id=1, source_target_pairs={{0,38},{1,39},{2,36},{3,37},{4,34},{5,35},{6,32},{7,33},{32,6},{33... | collective-permute-start | bytes 1806344 | tf_op jit(solution)/shard_map/ppermute | solution.py:28
  54.3 11.6 %copy-start.1 = (s32[2,2]{1,0:T(2,128)S(1)}, s32[2,2]{1,0:T(2,128)}, u32[]{:S(2)}) copy-start(s32[2,2]{1,0:T(2,128)} %conserve.7) | copy-start | bytes 52
  54.3 11.6 %copy-start.2 = (f32[8]{0:T(128)S(1)}, f32[8]{0:T(128)}, u32[]{:S(2)}) copy-start(f32[8]{0:T(128)} %occupied.7) | copy-start | bytes 100
  63.6 19.3 %collective-permute-start.7 = (bf16[392,768]{1,0:T(8,128)(2,1)S(1)}, bf16[392,768]{1,0:T(8,128)(2,1)}, u32[]{:S(2)}, u32[]{:S(2)}) collective-permute-start(bf16[392,768]{1,0:T(8,128)(2,1)S(1)} %collective-permute-done.5.refs_0_), channel_id=1, source_target_pairs={{0,8},{1,9},{2,10},{3,11},{4,12},{5,13},{6,14},{7,15},{32,40},{33,... | collective-permute-start | bytes 1806344 | tf_op jit(solution)/shard_map/ppermute | solution.py:28
  65.9 3.7 %copy-start = (bf16[2,8,2,192,768]{4,3,2,1,0:T(8,128)(2,1)S(1)}, bf16[2,8,2,192,768]{4,3,2,1,0:T(8,128)(2,1)}, u32[]{:S(2)}) copy-start(bf16[2,8,2,192,768]{4,3,2,1,0:T(8,128)(2,1)} %copy.19) | copy-start | bytes 28311556
  87.7 7.5 %collective-permute-start.11 = (f32[4,2,2,24,192]{4,3,2,1,0:T(8,128)S(1)}, f32[4,2,2,24,192]{4,3,2,1,0:T(8,128)S(1)}, u32[]{:S(2)}, u32[]{:S(2)}) collective-permute-start(f32[4,2,2,24,192]{4,3,2,1,0:T(8,128)S(1)} %get-tuple-element.70), channel_id=1, source_target_pairs={{0,1},{1,0},{2,3},{3,2},{4,5},{5,4},{6,7},{7,6},{8,9},{9,8},{10,11... | collective-permute-start | bytes 884744 | tf_op jit(solution)/shard_map/ppermute | solution.py:200
  95.3 8.5 %collective-permute-start.12 = (f32[2,2,24,192]{3,2,1,0:T(8,128)S(1)}, f32[2,2,24,192]{3,2,1,0:T(8,128)S(1)}, u32[]{:S(2)}, u32[]{:S(2)}) collective-permute-start(f32[2,2,24,192]{3,2,1,0:T(8,128)S(1)} %get-tuple-element.73), channel_id=1, source_target_pairs={{0,2},{1,3},{2,4},{3,5},{4,6},{5,7},{6,0},{7,1},{8,10},{9,11},{10,... | collective-permute-start | bytes 221192 | tf_op jit(solution)/shard_map/ppermute | solution.py:205
  101.0 5.1 %collective-permute-start.14 = (f32[2,2,24,192]{3,2,1,0:T(8,128)S(1)}, f32[2,2,24,192]{3,2,1,0:T(8,128)S(1)}, u32[]{:S(2)}, u32[]{:S(2)}) collective-permute-start(f32[2,2,24,192]{3,2,1,0:T(8,128)S(1)} %get-tuple-element.74), channel_id=1, source_target_pairs={{0,6},{1,7},{2,0},{3,1},{4,2},{5,3},{6,4},{7,5},{8,14},{9,15},{10,... | collective-permute-start | bytes 221192 | tf_op jit(solution)/shard_map/ppermute | solution.py:205
  101.0 8.8 %collective-permute-start.13 = (f32[2,2,24,192]{3,2,1,0:T(8,128)S(1)}, f32[2,2,24,192]{3,2,1,0:T(8,128)S(1)}, u32[]{:S(2)}, u32[]{:S(2)}) collective-permute-start(f32[2,2,24,192]{3,2,1,0:T(8,128)S(1)} %get-tuple-element.75), channel_id=1, source_target_pairs={{0,4},{1,5},{2,6},{3,7},{4,0},{5,1},{6,2},{7,3},{8,12},{9,13},{10,... | collective-permute-start | bytes 221192 | tf_op jit(solution)/shard_map/ppermute | solution.py:205

commit v11 on v10

--- a/solution.py
+++ b/solution.py
@@ -236,7 +236,7 @@
     pairs = with_partner(pairs, 2 * CORES)
     m0, pairs, factors = lax.optimization_barrier((m0, pairs, factors))
     cross_one = moved(m0, {3: (0, onto_next)})
-    two = moved(m0, {0: (2, same), 1: (3, same), 2: (0, onto_next)})
+    two = moved(m0, {0: (2, same), 2: (0, onto_next)})
     pairs = with_partner(pairs, 1)
     own_energy = virtual_energy.astype(jnp.float32)[:, None, :]
     m0, plus, minus, factors, pairs, own_energy = lax.optimization_barrier(
@@ -247,7 +247,7 @@
     near_one = moved(m0, {0: (1, same), 1: (2, same), 2: (3, same)})
     left = jnp.transpose(factors, (0, 1, 3, 2, 4)).reshape(momenta, orbitals, 2 * virtuals, auxiliary)
     cross_one, left = lax.optimization_barrier((cross_one, left))
-    onward = moved(cross_one, {0: (1, same)})
+    onward = moved(jnp.where(column == 0, cross_one, m0), {0: (1, same), 1: (3, same)})
 
     def density(orders, held, mates, before):
         return piece_density(
@@ -260,7 +260,7 @@
     terms += density(orders[1:2], (0, 1), (cross_one, near_one), ())
     *terms, back = lax.optimization_barrier((*terms, back))
     terms += density(orders[2:3], (0,), (back,), ())
-    total = density(orders, (0, 1, 2), (up, onward, two), terms)
+    total = density(orders, (0, 1, 2, 1), (up, onward, two), terms)
     return jnp.transpose(summed(*total), (0, 2, 1, 3))
 
 

time: 111 us -> 116 us (1.045)
  the two profiles are of different devices: /device:TPU:1 before, /device:TPU:10 now
where the time goes in v11:
time: 116 us; the launch traced here: 114 us
  starting transfers between devices  46.7 us (40%)
  waiting for transfers between devices  28.4 us (24%)
  Pallas kernels  18.1 us (16%)
  local copies, waits for them, and re-layouts  16.8 us (14%)
  other arithmetic  3.34 us (3%)
    ppermute x8, starting transfers between devices, moved(): return lax.ppermute(array, ('ka', 'occ'), pairs)  37.4 us
    ppermute x8, waiting for transfers between devices, moved(): return lax.ppermute(array, ('ka', 'occ'), pairs)  18.7 us
    pallas_call x4, Pallas kernels, piece_density(): pl.pallas_call(functools.partial(piece_kernel, len(mates), len(before), o...  18.1 us
    transpose x1, local copies, waits for them, and re-layouts, local(): jnp.transpose(factors, (0, 1, 3, 2, 4))  9.31 us
    ppermute x3, waiting for transfers between devices, summed(): total = total + lax.ppermute(part, 'occ', ring)  7.01 us
    ppermute x3, starting transfers between devices, with_partner(): lax.ppermute(array, 'occ', [(i, i ^ reach) for i in range(LINE * CORES)])  5.37 us
    unnamed x12, local copies, waits for them, and re-layouts  4.22 us
    ppermute x3, starting transfers between devices, summed(): total = total + lax.ppermute(part, 'occ', ring)  3.9 us
  transfers between devices with their start and end apart: 15, of which 6 were waited for; matrix products, arithmetic and copies ran while one was open for 13% of the time, Pallas kernels for 12%

profile of v11, /device:TPU:10, one launch (start us, length us, event | category | flops | bytes accessed | tf_op | source)
XLA Modules:
  0.0 113.8 jit_solution(12600085045516134312)
XLA Ops:
  0.0 1.9 %collective-permute-start = (s32[1,2,2,2]{3,2,1,0:T(2,128)}, s32[1,2,2,2]{3,2,1,0:T(2,128)S(1)}, u32[]{:S(2)}, u32[]{:S(2)}) collective-permute-start(s32[1,2,2,2]{3,2,1,0:T(2,128)} %bitcast.40), channel_id=1, source_target_pairs={{0,2},{1,3},{2,0},{3,1},{4,6},{5,7},{6,4},{7,5},{8,10},{9,11},{10,... | collective-permute-start | bytes 104 | tf_op jit(solution)/shard_map/ppermute | solution.py:210
  1.9 2.1 %constant_dynamic-slice_fusion = (bf16[1,8,24,2,768]{4,3,2,1,0:T(2,128)(2,1)S(1)}, bf16[1,8,24,2,768]{4,3,2,1,0:T(2,128)(2,1)S(1)}) fusion(bf16[2,8,192,2,768]{4,3,2,1,0:T(2,128)(2,1)} %param.5, s32[]{:T(128)S(6)} %select_n.52), kind=kLoop, calls=%fused_computation.20 | loop fusion | bytes 2359300 | tf_op jit(solution)/shard_map/dynamic_slice | solution.py:222
  4.0 0.0 copy-start.3
  4.0 0.1 copy.27
  4.1 0.1 copy.28
  4.1 0.5 copy-done.3
  4.7 0.1 pad_add_fusion.3.here
  4.7 0.1 pad.22.clone
  4.8 1.1 fusion.6
  5.9 0.0 collective-permute-done
  6.0 3.4 %collective-permute-start.1 = (s32[2,2,2,2]{3,2,1,0:T(2,128)S(1)}, s32[2,2,2,2]{3,2,1,0:T(2,128)S(1)}, u32[]{:S(2)}, u32[]{:S(2)}) collective-permute-start(s32[2,2,2,2]{3,2,1,0:T(2,128)S(1)} %pad_add_fusion.1), channel_id=1, source_target_pairs={{0,4},{1,5},{2,6},{3,7},{4,0},{5,1},{6,2},{7,3},{8,12},{9,13},{10,... | collective-permute-start | bytes 200 | tf_op jit(solution)/shard_map/ppermute | solution.py:210
  9.3 1.5 %collective-permute-start.2 = (bf16[392,768]{1,0:T(8,128)(2,1)S(1)}, bf16[392,768]{1,0:T(8,128)(2,1)S(1)}, u32[]{:S(2)}, u32[]{:S(2)}) collective-permute-start(bf16[392,768]{1,0:T(8,128)(2,1)S(1)} %get-tuple-element.42), channel_id=1, source_target_pairs={{0,8},{1,9},{2,10},{3,11},{4,12},{5,13},{6,14},{7,15},{8,16},{9,17... | collective-permute-start | bytes 1806344 | tf_op jit(solution)/shard_map/ppermute | solution.py:28
  10.8 0.5 collective-permute-start.3
  11.3 0.0 collective-permute-done.1
  11.4 0.7 collective-permute-start.5
  12.1 0.7 collective-permute-start.8
  12.8 0.1 collective-permute-start.4
  12.9 0.1 copy.17
  13.0 1.0 collective-permute-done.4
  14.0 0.1 copy.18
  14.1 0.1 pad_add_fusion.2
  14.2 11.6 %collective-permute-done.2.refs_1_ = bf16[392,768]{1,0:T(8,128)(2,1)S(1)} collective-permute-done((bf16[392,768]{1,0:T(8,128)(2,1)S(1)}, bf16[392,768]{1,0:T(8,128)(2,1)S(1)}, u32[]{:S(2)}, u32[]{:S(2)}) %collective-permute-start.2) | collective-permute-done | bytes 602144 | tf_op jit(solution)/shard_map/ppermute | solution.py:28
  25.9 0.0 collective-permute-done.3
  25.9 3.4 %collective-permute-start.9 = (bf16[392,768]{1,0:T(8,128)(2,1)}, bf16[392,768]{1,0:T(8,128)(2,1)}, u32[]{:S(2)}, u32[]{:S(2)}) collective-permute-start(bf16[392,768]{1,0:T(8,128)(2,1)} %get-tuple-element.52), channel_id=1, source_target_pairs={{0,8},{1,9},{2,10},{3,11},{4,12},{5,13},{6,14},{7,15},{8,16},{9,17... | collective-permute-start | bytes 1806344 | tf_op jit(solution)/shard_map/ppermute | solution.py:28
  29.3 9.3 %copy.19 = bf16[2,8,2,192,768]{4,3,2,1,0:T(8,128)(2,1)} copy(bf16[2,8,2,192,768]{4,2,3,1,0:T(2,128)(2,1)} %bitcast.37) | data formatting | bytes 18874368 | tf_op jit(solution)/shard_map/transpose | solution.py:248
  38.6 27.9 %collective-permute-start.10 = (bf16[392,768]{1,0:T(8,128)(2,1)}, bf16[392,768]{1,0:T(8,128)(2,1)S(1)}, u32[]{:S(2)}, u32[]{:S(2)}) collective-permute-start(bf16[392,768]{1,0:T(8,128)(2,1)} %copy-done.5), channel_id=1, source_target_pairs={{0,24},{1,25},{2,26},{3,27},{4,28},{5,29},{6,30},{7,31},{8,38},{9,... | collective-permute-start | bytes 1806344 | tf_op jit(solution)/shard_map/ppermute | solution.py:28
  66.5 0.7 collective-permute-start.6
  67.2 0.0 collective-permute-done.5.refs_0_
  67.2 2.0 %broadcast_select_fusion = bf16[392,768]{1,0:T(8,128)(2,1)} fusion(bf16[392,768]{1,0:T(8,128)(2,1)S(1)} %collective-permute-done.5.refs_0_, bf16[392,768]{1,0:T(8,128)(2,1)} %get-tuple-element.52, pred[]{:T(512)S(6)} %eq.9), kind=kLoop, calls=%fused_computation.9 | loop fusion | flops 301056 | bytes 1806337 | tf_op jit(solution)/shard_map/jit(_where)/select_n | solution.py:250
  69.2 1.9 %collective-permute-start.7 = (bf16[392,768]{1,0:T(8,128)(2,1)}, bf16[392,768]{1,0:T(8,128)(2,1)}, u32[]{:S(2)}, u32[]{:S(2)}) collective-permute-start(bf16[392,768]{1,0:T(8,128)(2,1)} %broadcast_select_fusion), channel_id=1, source_target_pairs={{0,8},{1,9},{2,10},{3,11},{4,12},{5,13},{6,14},{7,15},{8,24},{9,25... | collective-permute-start | bytes 1806344 | tf_op jit(solution)/shard_map/ppermute | solution.py:28
  71.1 0.1 copy.23.pairs
  71.3 3.7 %copy-done = bf16[2,8,2,192,768]{4,3,2,1,0:T(8,128)(2,1)S(1)} copy-done((bf16[2,8,2,192,768]{4,3,2,1,0:T(8,128)(2,1)S(1)}, bf16[2,8,2,192,768]{4,3,2,1,0:T(8,128)(2,1)}, u32[]{:S(2)}) %copy-start) | copy-done | bytes 9437208
  74.9 4.3 %shard_map.55 = (f32[4,2,24,192]{3,2,1,0:T(8,128)S(1)}, f32[4,2,24,192]{3,2,1,0:T(8,128)S(1)}) custom-call(s32[2,2]{1,0:T(2,128)S(1)} %copy-done.1, s32[8,2,2,2]{3,2,1,0:T(2,128)S(1)} %copy.23.pairs, s32[2]{0:T(128)S(1)} %pad_add_fusion.3.here, f32[8]{0:T(128)S(1)} %copy-done.2, f32[2,1,192]{2,1,0:T(1,128)S(1)} %reshape.12.own_energy, ...), custom_call_target="tpu_custom_call" | custom-call | flops 1925185536 | bytes 5308416 | tf_op jit(solution)/shard_map/pallas_call | solution.py:174
  79.3 4.7 %shard_map.56 = (f32[4,2,24,192]{3,2,1,0:T(8,128)S(1)}, f32[4,2,24,192]{3,2,1,0:T(8,128)S(1)}) custom-call(s32[2,2]{1,0:T(2,128)S(1)} %copy-done.1, s32[8,2,2,2]{3,2,1,0:T(2,128)S(1)} %copy.23.pairs, s32[2]{0:T(128)S(1)} %pad_add_fusion.3.here, f32[8]{0:T(128)S(1)} %copy-done.2, f32[2,1,192]{2,1,0:T(1,128)S(1)} %reshape.12.own_energy, ...), custom_call_target="tpu_custom_call" | custom-call | flops 1925185536 | bytes 5308416 | tf_op jit(solution)/shard_map/pallas_call | solution.py:174
  84.0 7.1 %collective-permute-done.10.refs_0_ = bf16[392,768]{1,0:T(8,128)(2,1)S(1)} collective-permute-done((bf16[392,768]{1,0:T(8,128)(2,1)}, bf16[392,768]{1,0:T(8,128)(2,1)S(1)}, u32[]{:S(2)}, u32[]{:S(2)}) %collective-permute-start.10) | collective-permute-done | bytes 602144 | tf_op jit(solution)/shard_map/ppermute | solution.py:28
  91.1 4.3 %shard_map.57 = (f32[4,2,24,192]{3,2,1,0:T(8,128)S(1)}, f32[4,2,24,192]{3,2,1,0:T(8,128)S(1)}) custom-call(s32[2,2]{1,0:T(2,128)S(1)} %copy-done.1, s32[8,2,2,2]{3,2,1,0:T(2,128)S(1)} %copy.23.pairs, s32[2]{0:T(128)S(1)} %pad_add_fusion.3.here, f32[8]{0:T(128)S(1)} %copy-done.2, f32[2,1,192]{2,1,0:T(1,128)S(1)} %reshape.12.own_energy, ...), custom_call_target="tpu_custom_call" | custom-call | flops 1925185536 | bytes 5308416 | tf_op jit(solution)/shard_map/pallas_call | solution.py:174
  95.4 0.0 collective-permute-done.6.refs_0_
  95.4 4.8 %shard_map.58 = (f32[4,2,2,24,192]{4,3,2,1,0:T(8,128)S(1)}, f32[4,2,2,24,192]{4,3,2,1,0:T(8,128)S(1)}) custom-call(s32[2,2]{1,0:T(2,128)S(1)} %copy-done.1, s32[8,2,2,2]{3,2,1,0:T(2,128)S(1)} %copy.23.pairs, s32[2]{0:T(128)S(1)} %pad_add_fusion.3.here, f32[8]{0:T(128)S(1)} %copy-done.2, f32[2,1,192]{2,1,0:T(1,128)S(1)} %reshape.12.own_energy, ...), custom_call_target="tpu_custom_call" | custom-call | flops 1925185536 | bytes 5308416 | tf_op jit(solution)/shard_map/pallas_call | solution.py:174
  100.2 0.1 collective-permute-start.11
  100.4 1.6 %collective-permute-done.11 = f32[4,2,2,24,192]{4,3,2,1,0:T(8,128)S(1)} collective-permute-done((f32[4,2,2,24,192]{4,3,2,1,0:T(8,128)S(1)}, f32[4,2,2,24,192]{4,3,2,1,0:T(8,128)S(1)}, u32[]{:S(2)}, u32[]{:S(2)}) %collective-permute-start.11) | collective-permute-done | bytes 294944 | tf_op jit(solution)/shard_map/ppermute | solution.py:200
  102.0 0.1 add.62
  102.1 0.1 collective-permute-start.12
  102.2 2.5 %collective-permute-start.13 = (f32[2,2,24,192]{3,2,1,0:T(8,128)S(1)}, f32[2,2,24,192]{3,2,1,0:T(8,128)S(1)}, u32[]{:S(2)}, u32[]{:S(2)}) collective-permute-start(f32[2,2,24,192]{3,2,1,0:T(8,128)S(1)} %get-tuple-element.75), channel_id=1, source_target_pairs={{0,4},{1,5},{2,6},{3,7},{4,0},{5,1},{6,2},{7,3},{8,12},{9,13},{10,... | collective-permute-start | bytes 221192 | tf_op jit(solution)/shard_map/ppermute | solution.py:205
  104.7 1.3 %collective-permute-start.14 = (f32[2,2,24,192]{3,2,1,0:T(8,128)S(1)}, f32[2,2,24,192]{3,2,1,0:T(8,128)S(1)}, u32[]{:S(2)}, u32[]{:S(2)}) collective-permute-start(f32[2,2,24,192]{3,2,1,0:T(8,128)S(1)} %get-tuple-element.74), channel_id=1, source_target_pairs={{0,6},{1,7},{2,0},{3,1},{4,2},{5,3},{6,4},{7,5},{8,14},{9,15},{10,... | collective-permute-start | bytes 221192 | tf_op jit(solution)/shard_map/ppermute | solution.py:205
  106.0 3.7 %collective-permute-done.12 = f32[2,2,24,192]{3,2,1,0:T(8,128)S(1)} collective-permute-done((f32[2,2,24,192]{3,2,1,0:T(8,128)S(1)}, f32[2,2,24,192]{3,2,1,0:T(8,128)S(1)}, u32[]{:S(2)}, u32[]{:S(2)}) %collective-permute-start.12) | collective-permute-done | bytes 73760 | tf_op jit(solution)/shard_map/ppermute | solution.py:205
  109.7 3.3 %collective-permute-done.13 = f32[2,2,24,192]{3,2,1,0:T(8,128)S(1)} collective-permute-done((f32[2,2,24,192]{3,2,1,0:T(8,128)S(1)}, f32[2,2,24,192]{3,2,1,0:T(8,128)S(1)}, u32[]{:S(2)}, u32[]{:S(2)}) %collective-permute-start.13) | collective-permute-done | bytes 73760 | tf_op jit(solution)/shard_map/ppermute | solution.py:205
  113.0 0.0 collective-permute-done.14
  113.1 0.7 copy.24
  (19 shorter events, 0.1 us)
Async XLA Ops:
  0.0 6.0 %collective-permute-start = (s32[1,2,2,2]{3,2,1,0:T(2,128)}, s32[1,2,2,2]{3,2,1,0:T(2,128)S(1)}, u32[]{:S(2)}, u32[]{:S(2)}) collective-permute-start(s32[1,2,2,2]{3,2,1,0:T(2,128)} %bitcast.40), channel_id=1, source_target_pairs={{0,2},{1,3},{2,0},{3,1},{4,6},{5,7},{6,4},{7,5},{8,10},{9,11},{10,... | collective-permute-start | bytes 104 | tf_op jit(solution)/shard_map/ppermute | solution.py:210
  4.0 0.7 copy-start.3
  4.7 1.3 %copy-start.4 = (s32[2,2,2]{2,1,0:T(2,128)S(1)}, s32[2,2,2]{2,1,0:T(2,128)}, u32[]{:S(2)}) copy-start(s32[2,2,2]{2,1,0:T(2,128)} %param.9) | copy-start | bytes 100
  6.0 5.4 %collective-permute-start.1 = (s32[2,2,2,2]{3,2,1,0:T(2,128)S(1)}, s32[2,2,2,2]{3,2,1,0:T(2,128)S(1)}, u32[]{:S(2)}, u32[]{:S(2)}) collective-permute-start(s32[2,2,2,2]{3,2,1,0:T(2,128)S(1)} %pad_add_fusion.1), channel_id=1, source_target_pairs={{0,4},{1,5},{2,6},{3,7},{4,0},{5,1},{6,2},{7,3},{8,12},{9,13},{10,... | collective-permute-start | bytes 200 | tf_op jit(solution)/shard_map/ppermute | solution.py:210
  9.3 16.5 %collective-permute-start.2 = (bf16[392,768]{1,0:T(8,128)(2,1)S(1)}, bf16[392,768]{1,0:T(8,128)(2,1)S(1)}, u32[]{:S(2)}, u32[]{:S(2)}) collective-permute-start(bf16[392,768]{1,0:T(8,128)(2,1)S(1)} %get-tuple-element.42), channel_id=1, source_target_pairs={{0,8},{1,9},{2,10},{3,11},{4,12},{5,13},{6,14},{7,15},{8,16},{9,17... | collective-permute-start | bytes 1806344 | tf_op jit(solution)/shard_map/ppermute | solution.py:28
  10.8 15.0 %collective-permute-start.3 = (bf16[392,768]{1,0:T(8,128)(2,1)S(1)}, bf16[392,768]{1,0:T(8,128)(2,1)S(1)}, u32[]{:S(2)}, u32[]{:S(2)}) collective-permute-start(bf16[392,768]{1,0:T(8,128)(2,1)S(1)} %get-tuple-element.42), channel_id=1, source_target_pairs={{0,24},{1,25},{2,26},{3,27},{4,28},{5,29},{6,30},{7,31},{8,0},{9,1... | collective-permute-start | bytes 1806344 | tf_op jit(solution)/shard_map/ppermute | solution.py:28
  11.4 55.9 %collective-permute-start.5 = (bf16[392,768]{1,0:T(8,128)(2,1)}, bf16[392,768]{1,0:T(8,128)(2,1)S(1)}, u32[]{:S(2)}, u32[]{:S(2)}) collective-permute-start(bf16[392,768]{1,0:T(8,128)(2,1)} %get-tuple-element.52), channel_id=1, source_target_pairs={{24,38},{25,39},{26,36},{27,37},{28,34},{29,35},{30,32},{31,33},{5... | collective-permute-start | bytes 1806344 | tf_op jit(solution)/shard_map/ppermute | solution.py:28
  12.1 59.2 %collective-permute-start.8 = (bf16[392,768]{1,0:T(8,128)(2,1)}, bf16[392,768]{1,0:T(8,128)(2,1)S(1)}, u32[]{:S(2)}, u32[]{:S(2)}) collective-permute-start(bf16[392,768]{1,0:T(8,128)(2,1)} %get-tuple-element.52), channel_id=1, source_target_pairs={{0,16},{1,17},{2,18},{3,19},{4,20},{5,21},{6,22},{7,23},{16,38},{1... | collective-permute-start | bytes 1806344 | tf_op jit(solution)/shard_map/ppermute | solution.py:28
  12.8 1.3 %collective-permute-start.4 = (s32[4,2,2,2]{3,2,1,0:T(2,128)S(1)}, s32[4,2,2,2]{3,2,1,0:T(2,128)S(1)}, u32[]{:S(2)}, u32[]{:S(2)}) collective-permute-start(s32[4,2,2,2]{3,2,1,0:T(2,128)S(1)} %pad_add_fusion), channel_id=1, source_target_pairs={{0,1},{1,0},{2,3},{3,2},{4,5},{5,4},{6,7},{7,6},{8,9},{9,8},{10,11... | collective-permute-start | bytes 392 | tf_op jit(solution)/shard_map/ppermute | solution.py:210
  25.9 3.4 %copy-start.5 = (bf16[392,768]{1,0:T(8,128)(2,1)}, bf16[392,768]{1,0:T(8,128)(2,1)S(1)}, u32[]{:S(2)}) copy-start(bf16[392,768]{1,0:T(8,128)(2,1)S(1)} %collective-permute-done.3) | copy-start | bytes 1806340
  25.9 53.4 %collective-permute-start.9 = (bf16[392,768]{1,0:T(8,128)(2,1)}, bf16[392,768]{1,0:T(8,128)(2,1)}, u32[]{:S(2)}, u32[]{:S(2)}) collective-permute-start(bf16[392,768]{1,0:T(8,128)(2,1)} %get-tuple-element.52), channel_id=1, source_target_pairs={{0,8},{1,9},{2,10},{3,11},{4,12},{5,13},{6,14},{7,15},{8,16},{9,17... | collective-permute-start | bytes 1806344 | tf_op jit(solution)/shard_map/ppermute | solution.py:28
  38.6 32.7 %copy-start.1 = (s32[2,2]{1,0:T(2,128)S(1)}, s32[2,2]{1,0:T(2,128)}, u32[]{:S(2)}) copy-start(s32[2,2]{1,0:T(2,128)} %conserve.7) | copy-start | bytes 52
  38.6 32.7 %copy-start.2 = (f32[8]{0:T(128)S(1)}, f32[8]{0:T(128)}, u32[]{:S(2)}) copy-start(f32[8]{0:T(128)} %occupied.7) | copy-start | bytes 100
  38.6 52.5 %collective-permute-start.10 = (bf16[392,768]{1,0:T(8,128)(2,1)}, bf16[392,768]{1,0:T(8,128)(2,1)S(1)}, u32[]{:S(2)}, u32[]{:S(2)}) collective-permute-start(bf16[392,768]{1,0:T(8,128)(2,1)} %copy-done.5), channel_id=1, source_target_pairs={{0,24},{1,25},{2,26},{3,27},{4,28},{5,29},{6,30},{7,31},{8,38},{9,... | collective-permute-start | bytes 1806344 | tf_op jit(solution)/shard_map/ppermute | solution.py:28
  66.5 28.9 %collective-permute-start.6 = (bf16[392,768]{1,0:T(8,128)(2,1)S(1)}, bf16[392,768]{1,0:T(8,128)(2,1)S(1)}, u32[]{:S(2)}, u32[]{:S(2)}) collective-permute-start(bf16[392,768]{1,0:T(8,128)(2,1)S(1)} %collective-permute-done.2.refs_1_), channel_id=1, source_target_pairs={{0,38},{1,39},{2,36},{3,37},{4,34},{5,35},{6,32},{7,33},{32,6},{33... | collective-permute-start | bytes 1806344 | tf_op jit(solution)/shard_map/ppermute | solution.py:28
  69.2 26.2 %collective-permute-start.7 = (bf16[392,768]{1,0:T(8,128)(2,1)}, bf16[392,768]{1,0:T(8,128)(2,1)}, u32[]{:S(2)}, u32[]{:S(2)}) collective-permute-start(bf16[392,768]{1,0:T(8,128)(2,1)} %broadcast_select_fusion), channel_id=1, source_target_pairs={{0,8},{1,9},{2,10},{3,11},{4,12},{5,13},{6,14},{7,15},{8,24},{9,25... | collective-permute-start | bytes 1806344 | tf_op jit(solution)/shard_map/ppermute | solution.py:28
  71.3 3.7 %copy-start = (bf16[2,8,2,192,768]{4,3,2,1,0:T(8,128)(2,1)S(1)}, bf16[2,8,2,192,768]{4,3,2,1,0:T(8,128)(2,1)}, u32[]{:S(2)}) copy-start(bf16[2,8,2,192,768]{4,3,2,1,0:T(8,128)(2,1)} %copy.19) | copy-start | bytes 28311556
  100.2 1.8 %collective-permute-start.11 = (f32[4,2,2,24,192]{4,3,2,1,0:T(8,128)S(1)}, f32[4,2,2,24,192]{4,3,2,1,0:T(8,128)S(1)}, u32[]{:S(2)}, u32[]{:S(2)}) collective-permute-start(f32[4,2,2,24,192]{4,3,2,1,0:T(8,128)S(1)} %get-tuple-element.70), channel_id=1, source_target_pairs={{0,1},{1,0},{2,3},{3,2},{4,5},{5,4},{6,7},{7,6},{8,9},{9,8},{10,11... | collective-permute-start | bytes 884744 | tf_op jit(solution)/shard_map/ppermute | solution.py:200
  102.1 7.6 %collective-permute-start.12 = (f32[2,2,24,192]{3,2,1,0:T(8,128)S(1)}, f32[2,2,24,192]{3,2,1,0:T(8,128)S(1)}, u32[]{:S(2)}, u32[]{:S(2)}) collective-permute-start(f32[2,2,24,192]{3,2,1,0:T(8,128)S(1)} %get-tuple-element.73), channel_id=1, source_target_pairs={{0,2},{1,3},{2,4},{3,5},{4,6},{5,7},{6,0},{7,1},{8,10},{9,11},{10,... | collective-permute-start | bytes 221192 | tf_op jit(solution)/shard_map/ppermute | solution.py:205
  102.2 10.8 %collective-permute-start.13 = (f32[2,2,24,192]{3,2,1,0:T(8,128)S(1)}, f32[2,2,24,192]{3,2,1,0:T(8,128)S(1)}, u32[]{:S(2)}, u32[]{:S(2)}) collective-permute-start(f32[2,2,24,192]{3,2,1,0:T(8,128)S(1)} %get-tuple-element.75), channel_id=1, source_target_pairs={{0,4},{1,5},{2,6},{3,7},{4,0},{5,1},{6,2},{7,3},{8,12},{9,13},{10,... | collective-permute-start | bytes 221192 | tf_op jit(solution)/shard_map/ppermute | solution.py:205
  104.7 8.3 %collective-permute-start.14 = (f32[2,2,24,192]{3,2,1,0:T(8,128)S(1)}, f32[2,2,24,192]{3,2,1,0:T(8,128)S(1)}, u32[]{:S(2)}, u32[]{:S(2)}) collective-permute-start(f32[2,2,24,192]{3,2,1,0:T(8,128)S(1)} %get-tuple-element.74), channel_id=1, source_target_pairs={{0,6},{1,7},{2,0},{3,1},{4,2},{5,3},{6,4},{7,5},{8,14},{9,15},{10,... | collective-permute-start | bytes 221192 | tf_op jit(solution)/shard_map/ppermute | solution.py:205

commit v12 on v8

--- a/solution.py
+++ b/solution.py
@@ -255,13 +255,13 @@
             orders, held, conserve, pairs, here, occupied_energy, own_energy, left, mates, before
         )
 
-    orders = (((0,), (0,)), ((1, 0), (0, 1)), ((1,), (1,)), ((0, 1), (1, 0)))
+    orders = (((0,), (0,)), ((1, 0), (0, 1)), ((0, 1), (1, 0)), ((1,), (1,)))
     terms = density(orders[:1], (0, 1), (cross_one, near_one), ())
     *terms, cross_two, plus = lax.optimization_barrier((*terms, cross_two, plus))
     terms += density(orders[1:2], (0, 1), (cross_two, plus), ())
-    *terms, back = lax.optimization_barrier((*terms, back))
-    terms += density(orders[2:3], (0,), (back,), ())
-    total = density(orders, (0, 1, 2), (up, onward, near_two), terms)
+    *terms, up, onward, near_two = lax.optimization_barrier((*terms, up, onward, near_two))
+    terms += density(orders[2:3], (0, 1, 2), (up, onward, near_two), ())
+    total = density(orders, (0,), (back,), terms)
     return jnp.transpose(summed(*total), (0, 2, 1, 3))
 
 

time: 108 us -> 111 us (1.028); the launches traced: 107 us -> 108 us
  starting transfers between devices: 37.3 us -> 40.8 us
  waiting for transfers between devices: 31.3 us -> 29.1 us
    ppermute x9, waiting for transfers between devices: 20.7 us -> 16.4 us  [moved(): return lax.ppermute(array, ('ka', 'occ'), pairs)]
    ppermute x9, starting transfers between devices: 28.1 us -> 31.1 us  [moved(): return lax.ppermute(array, ('ka', 'occ'), pairs)]
    ppermute x3, waiting for transfers between devices: 7.01 us -> 9.13 us  [summed(): total = total + lax.ppermute(part, 'occ', ring)]
    unnamed x16 -> x14, local copies, waits for them, and re-layouts: 6.13 us -> 5.6 us
  transfers between devices with their start and end apart: 16 -> 16, of which waited for: 8 -> 9; matrix products, arithmetic and copies ran while one was open for 12% -> 13% of each run, Pallas kernels for 12% -> 12%
where the time goes in v12:
time: 111 us; the launch traced here: 108 us
  starting transfers between devices  40.8 us (37%)
  waiting for transfers between devices  29.1 us (26%)
  local copies, waits for them, and re-layouts  19 us (17%)
  Pallas kernels  18.1 us (16%)
  other arithmetic  1.3 us (1%)
    ppermute x9, starting transfers between devices, moved(): return lax.ppermute(array, ('ka', 'occ'), pairs)  31.1 us
    pallas_call x4, Pallas kernels, piece_density(): pl.pallas_call(functools.partial(piece_kernel, len(mates), len(before), o...  18.1 us
    ppermute x9, waiting for transfers between devices, moved(): return lax.ppermute(array, ('ka', 'occ'), pairs)  16.4 us
    transpose x1, local copies, waits for them, and re-layouts, local(): jnp.transpose(factors, (0, 1, 3, 2, 4))  9.32 us
    ppermute x3, waiting for transfers between devices, summed(): total = total + lax.ppermute(part, 'occ', ring)  9.13 us
    unnamed x14, local copies, waits for them, and re-layouts  5.6 us
    ppermute x3, starting transfers between devices, with_partner(): lax.ppermute(array, 'occ', [(i, i ^ reach) for i in range(LINE * CORES)])  5.19 us
    ppermute x3, starting transfers between devices, summed(): total = total + lax.ppermute(part, 'occ', ring)  4.36 us
  transfers between devices with their start and end apart: 16, of which 9 were waited for; matrix products, arithmetic and copies ran while one was open for 13% of the time, Pallas kernels for 12%

profile of v12, /device:TPU:10, one launch (start us, length us, event | category | flops | bytes accessed | tf_op | source)
XLA Modules:
  0.0 108.5 jit_solution(642422161694027073)
XLA Ops:
  0.0 1.9 %collective-permute-start = (s32[1,2,2,2]{3,2,1,0:T(2,128)}, s32[1,2,2,2]{3,2,1,0:T(2,128)S(1)}, u32[]{:S(2)}, u32[]{:S(2)}) collective-permute-start(s32[1,2,2,2]{3,2,1,0:T(2,128)} %bitcast.40), channel_id=1, source_target_pairs={{0,2},{1,3},{2,0},{3,1},{4,6},{5,7},{6,4},{7,5},{8,10},{9,11},{10,... | collective-permute-start | bytes 104 | tf_op jit(solution)/shard_map/ppermute | solution.py:210
  1.9 0.8 fusion.10
  2.7 2.1 %constant_dynamic-slice_fusion = (bf16[1,8,24,2,768]{4,3,2,1,0:T(2,128)(2,1)S(1)}, bf16[1,8,24,2,768]{4,3,2,1,0:T(2,128)(2,1)S(1)}) fusion(bf16[2,8,192,2,768]{4,3,2,1,0:T(2,128)(2,1)} %param.5, s32[]{:T(128)S(6)} %select_n.44), kind=kLoop, calls=%fused_computation.19 | loop fusion | bytes 2359300 | tf_op jit(solution)/shard_map/dynamic_slice | solution.py:222
  4.7 0.1 copy.28
  4.8 0.1 copy.27
  4.9 0.1 pad.22.clone
  5.0 0.1 pad_add_fusion.3.here
  5.0 1.1 fusion.6
  6.1 0.0 collective-permute-done
  6.1 1.6 %collective-permute-start.2 = (bf16[392,768]{1,0:T(8,128)(2,1)S(1)}, bf16[392,768]{1,0:T(8,128)(2,1)S(1)}, u32[]{:S(2)}, u32[]{:S(2)}) collective-permute-start(bf16[392,768]{1,0:T(8,128)(2,1)S(1)} %get-tuple-element.46), channel_id=1, source_target_pairs={{0,8},{1,9},{2,10},{3,11},{4,12},{5,13},{6,14},{7,15},{8,16},{9,17... | collective-permute-start | bytes 1806344 | tf_op jit(solution)/shard_map/ppermute | solution.py:28
  7.7 0.5 collective-permute-start.3
  8.2 3.3 %collective-permute-start.1 = (s32[2,2,2,2]{3,2,1,0:T(2,128)S(1)}, s32[2,2,2,2]{3,2,1,0:T(2,128)S(1)}, u32[]{:S(2)}, u32[]{:S(2)}) collective-permute-start(s32[2,2,2,2]{3,2,1,0:T(2,128)S(1)} %pad_add_fusion.1), channel_id=1, source_target_pairs={{0,4},{1,5},{2,6},{3,7},{4,0},{5,1},{6,2},{7,3},{8,12},{9,13},{10,... | collective-permute-start | bytes 200 | tf_op jit(solution)/shard_map/ppermute | solution.py:210
  11.5 1.6 %collective-permute-done.1 = s32[2,2,2,2]{3,2,1,0:T(2,128)S(1)} collective-permute-done((s32[2,2,2,2]{3,2,1,0:T(2,128)S(1)}, s32[2,2,2,2]{3,2,1,0:T(2,128)S(1)}, u32[]{:S(2)}, u32[]{:S(2)}) %collective-permute-start.1) | collective-permute-done | bytes 96 | tf_op jit(solution)/shard_map/ppermute | solution.py:210
  13.1 0.1 copy.17
  13.2 0.7 collective-permute-start.5
  13.9 0.4 collective-permute-done.4
  14.3 0.1 copy.18
  14.4 0.1 pad_add_fusion.2
  14.4 6.8 %collective-permute-done.2.refs_1_ = bf16[392,768]{1,0:T(8,128)(2,1)S(1)} collective-permute-done((bf16[392,768]{1,0:T(8,128)(2,1)S(1)}, bf16[392,768]{1,0:T(8,128)(2,1)S(1)}, u32[]{:S(2)}, u32[]{:S(2)}) %collective-permute-start.2) | collective-permute-done | bytes 602144 | tf_op jit(solution)/shard_map/ppermute | solution.py:28
  21.2 1.3 %collective-permute-done.3 = bf16[392,768]{1,0:T(8,128)(2,1)} collective-permute-done((bf16[392,768]{1,0:T(8,128)(2,1)S(1)}, bf16[392,768]{1,0:T(8,128)(2,1)}, u32[]{:S(2)}, u32[]{:S(2)}) %collective-permute-start.3) | collective-permute-done | bytes 602144 | tf_op jit(solution)/shard_map/ppermute | solution.py:28
  22.6 3.1 %collective-permute-start.6 = (bf16[392,768]{1,0:T(8,128)(2,1)}, bf16[392,768]{1,0:T(8,128)(2,1)S(1)}, u32[]{:S(2)}, u32[]{:S(2)}) collective-permute-start(bf16[392,768]{1,0:T(8,128)(2,1)} %get-tuple-element.67), channel_id=1, source_target_pairs={{0,8},{1,9},{2,10},{3,11},{4,12},{5,13},{6,14},{7,15},{8,16},{9,17... | collective-permute-start | bytes 1806344 | tf_op jit(solution)/shard_map/ppermute | solution.py:28
  25.7 1.5 %collective-permute-start.8 = (bf16[392,768]{1,0:T(8,128)(2,1)}, bf16[392,768]{1,0:T(8,128)(2,1)}, u32[]{:S(2)}, u32[]{:S(2)}) collective-permute-start(bf16[392,768]{1,0:T(8,128)(2,1)} %get-tuple-element.67), channel_id=1, source_target_pairs={{16,38},{17,39},{18,36},{19,37},{20,34},{21,35},{22,32},{23,33},{4... | collective-permute-start | bytes 1806344 | tf_op jit(solution)/shard_map/ppermute | solution.py:28
  27.2 9.3 %copy.19 = bf16[2,8,2,192,768]{4,3,2,1,0:T(8,128)(2,1)} copy(bf16[2,8,2,192,768]{4,2,3,1,0:T(2,128)(2,1)} %bitcast.37) | data formatting | bytes 18874368 | tf_op jit(solution)/shard_map/transpose | solution.py:248
  36.5 0.7 collective-permute-start.9
  37.2 1.3 %collective-permute-done.6.refs_1_ = bf16[392,768]{1,0:T(8,128)(2,1)S(1)} collective-permute-done((bf16[392,768]{1,0:T(8,128)(2,1)}, bf16[392,768]{1,0:T(8,128)(2,1)S(1)}, u32[]{:S(2)}, u32[]{:S(2)}) %collective-permute-start.6) | collective-permute-done | bytes 602144 | tf_op jit(solution)/shard_map/ppermute | solution.py:28
  38.5 0.8 copy-done.1
  39.3 1.3 %collective-permute-start.10 = (bf16[392,768]{1,0:T(8,128)(2,1)S(1)}, bf16[392,768]{1,0:T(8,128)(2,1)S(1)}, u32[]{:S(2)}, u32[]{:S(2)}) collective-permute-start(bf16[392,768]{1,0:T(8,128)(2,1)S(1)} %collective-permute-done.5.refs_0_), channel_id=1, source_target_pairs={{0,8},{1,9},{2,10},{3,11},{4,12},{5,13},{6,14},{7,15},{32,40},{33,... | collective-permute-start | bytes 1806344 | tf_op jit(solution)/shard_map/ppermute | solution.py:28
  40.6 16.5 %collective-permute-start.11 = (bf16[392,768]{1,0:T(8,128)(2,1)}, bf16[392,768]{1,0:T(8,128)(2,1)S(1)}, u32[]{:S(2)}, u32[]{:S(2)}) collective-permute-start(bf16[392,768]{1,0:T(8,128)(2,1)} %get-tuple-element.67), channel_id=1, source_target_pairs={{0,16},{1,17},{2,18},{3,19},{4,20},{5,21},{6,22},{7,23},{8,24},{9,... | collective-permute-start | bytes 1806344 | tf_op jit(solution)/shard_map/ppermute | solution.py:28
  57.2 5.2 %collective-permute-start.7 = (bf16[392,768]{1,0:T(8,128)(2,1)}, bf16[392,768]{1,0:T(8,128)(2,1)}, u32[]{:S(2)}, u32[]{:S(2)}) collective-permute-start(bf16[392,768]{1,0:T(8,128)(2,1)} %collective-permute-done.3), channel_id=1, source_target_pairs={{0,24},{1,25},{2,26},{3,27},{4,28},{5,29},{6,30},{7,31},{8,38},{9,... | collective-permute-start | bytes 1806344 | tf_op jit(solution)/shard_map/ppermute | solution.py:28
  62.4 0.1 copy.23.pairs
  62.5 3.7 %copy-done = bf16[2,8,2,192,768]{4,3,2,1,0:T(8,128)(2,1)S(1)} copy-done((bf16[2,8,2,192,768]{4,3,2,1,0:T(8,128)(2,1)S(1)}, bf16[2,8,2,192,768]{4,3,2,1,0:T(8,128)(2,1)}, u32[]{:S(2)}) %copy-start) | copy-done | bytes 9437208
  66.2 1.1 copy-done.2
  67.3 4.3 %shard_map.55 = (f32[4,2,24,192]{3,2,1,0:T(8,128)S(1)}, f32[4,2,24,192]{3,2,1,0:T(8,128)S(1)}) custom-call(s32[2,2]{1,0:T(2,128)S(1)} %copy-done.3, s32[8,2,2,2]{3,2,1,0:T(2,128)S(1)} %copy.23.pairs, s32[2]{0:T(128)S(1)} %pad_add_fusion.3.here, f32[8]{0:T(128)S(1)} %copy-done.4, f32[2,1,192]{2,1,0:T(1,128)S(1)} %reshape.12.own_energy, ...), custom_call_target="tpu_custom_call" | custom-call | flops 1925185536 | bytes 5308416 | tf_op jit(solution)/shard_map/pallas_call | solution.py:174
  71.6 0.0 collective-permute-done.8.refs_0_
  71.6 4.6 %shard_map.56 = (f32[4,2,24,192]{3,2,1,0:T(8,128)S(1)}, f32[4,2,24,192]{3,2,1,0:T(8,128)S(1)}) custom-call(s32[2,2]{1,0:T(2,128)S(1)} %copy-done.3, s32[8,2,2,2]{3,2,1,0:T(2,128)S(1)} %copy.23.pairs, s32[2]{0:T(128)S(1)} %pad_add_fusion.3.here, f32[8]{0:T(128)S(1)} %copy-done.4, f32[2,1,192]{2,1,0:T(1,128)S(1)} %reshape.12.own_energy, ...), custom_call_target="tpu_custom_call" | custom-call | flops 1925185536 | bytes 5308416 | tf_op jit(solution)/shard_map/pallas_call | solution.py:174
  76.2 0.0 collective-permute-done.10.refs_1_
  76.2 0.0 collective-permute-done.11.refs_2_
  76.2 4.5 %shard_map.57 = (f32[4,2,24,192]{3,2,1,0:T(8,128)S(1)}, f32[4,2,24,192]{3,2,1,0:T(8,128)S(1)}) custom-call(s32[2,2]{1,0:T(2,128)S(1)} %copy-done.3, s32[8,2,2,2]{3,2,1,0:T(2,128)S(1)} %copy.23.pairs, s32[2]{0:T(128)S(1)} %pad_add_fusion.3.here, f32[8]{0:T(128)S(1)} %copy-done.4, f32[2,1,192]{2,1,0:T(1,128)S(1)} %reshape.12.own_energy, ...), custom_call_target="tpu_custom_call" | custom-call | flops 1925185536 | bytes 5308416 | tf_op jit(solution)/shard_map/pallas_call | solution.py:174
  80.7 7.0 %collective-permute-done.7.refs_0_ = bf16[392,768]{1,0:T(8,128)(2,1)} collective-permute-done((bf16[392,768]{1,0:T(8,128)(2,1)}, bf16[392,768]{1,0:T(8,128)(2,1)}, u32[]{:S(2)}, u32[]{:S(2)}) %collective-permute-start.7) | collective-permute-done | bytes 602144 | tf_op jit(solution)/shard_map/ppermute | solution.py:28
  87.7 4.7 %shard_map.58 = (f32[4,2,2,24,192]{4,3,2,1,0:T(8,128)S(1)}, f32[4,2,2,24,192]{4,3,2,1,0:T(8,128)S(1)}) custom-call(s32[2,2]{1,0:T(2,128)S(1)} %copy-done.3, s32[8,2,2,2]{3,2,1,0:T(2,128)S(1)} %copy.23.pairs, s32[2]{0:T(128)S(1)} %pad_add_fusion.3.here, f32[8]{0:T(128)S(1)} %copy-done.4, f32[2,1,192]{2,1,0:T(1,128)S(1)} %reshape.12.own_energy, ...), custom_call_target="tpu_custom_call" | custom-call | flops 1925185536 | bytes 5308416 | tf_op jit(solution)/shard_map/pallas_call | solution.py:174
  92.4 0.1 collective-permute-start.12
  92.6 1.6 %collective-permute-done.12 = f32[4,2,2,24,192]{4,3,2,1,0:T(8,128)S(1)} collective-permute-done((f32[4,2,2,24,192]{4,3,2,1,0:T(8,128)S(1)}, f32[4,2,2,24,192]{4,3,2,1,0:T(8,128)S(1)}, u32[]{:S(2)}, u32[]{:S(2)}) %collective-permute-start.12) | collective-permute-done | bytes 294944 | tf_op jit(solution)/shard_map/ppermute | solution.py:200
  94.2 0.1 add.62
  94.3 2.0 %collective-permute-start.15 = (f32[2,2,24,192]{3,2,1,0:T(8,128)S(1)}, f32[2,2,24,192]{3,2,1,0:T(8,128)S(1)}, u32[]{:S(2)}, u32[]{:S(2)}) collective-permute-start(f32[2,2,24,192]{3,2,1,0:T(8,128)S(1)} %get-tuple-element.82), channel_id=1, source_target_pairs={{0,6},{1,7},{2,0},{3,1},{4,2},{5,3},{6,4},{7,5},{8,14},{9,15},{10,... | collective-permute-start | bytes 221192 | tf_op jit(solution)/shard_map/ppermute | solution.py:205
  96.3 2.4 %collective-permute-start.14 = (f32[2,2,24,192]{3,2,1,0:T(8,128)S(1)}, f32[2,2,24,192]{3,2,1,0:T(8,128)S(1)}, u32[]{:S(2)}, u32[]{:S(2)}) collective-permute-start(f32[2,2,24,192]{3,2,1,0:T(8,128)S(1)} %get-tuple-element.83), channel_id=1, source_target_pairs={{0,4},{1,5},{2,6},{3,7},{4,0},{5,1},{6,2},{7,3},{8,12},{9,13},{10,... | collective-permute-start | bytes 221192 | tf_op jit(solution)/shard_map/ppermute | solution.py:205
  98.6 1.6 %collective-permute-done.15 = f32[2,2,24,192]{3,2,1,0:T(8,128)S(1)} collective-permute-done((f32[2,2,24,192]{3,2,1,0:T(8,128)S(1)}, f32[2,2,24,192]{3,2,1,0:T(8,128)S(1)}, u32[]{:S(2)}, u32[]{:S(2)}) %collective-permute-start.15) | collective-permute-done | bytes 73760 | tf_op jit(solution)/shard_map/ppermute | solution.py:205
  100.3 7.5 %collective-permute-done.14 = f32[2,2,24,192]{3,2,1,0:T(8,128)S(1)} collective-permute-done((f32[2,2,24,192]{3,2,1,0:T(8,128)S(1)}, f32[2,2,24,192]{3,2,1,0:T(8,128)S(1)}, u32[]{:S(2)}, u32[]{:S(2)}) %collective-permute-start.14) | collective-permute-done | bytes 73760 | tf_op jit(solution)/shard_map/ppermute | solution.py:205
  107.8 0.7 copy.24
  (22 shorter events, 0.1 us)
Async XLA Ops:
  0.0 6.1 %collective-permute-start = (s32[1,2,2,2]{3,2,1,0:T(2,128)}, s32[1,2,2,2]{3,2,1,0:T(2,128)S(1)}, u32[]{:S(2)}, u32[]{:S(2)}) collective-permute-start(s32[1,2,2,2]{3,2,1,0:T(2,128)} %bitcast.40), channel_id=1, source_target_pairs={{0,2},{1,3},{2,0},{3,1},{4,6},{5,7},{6,4},{7,5},{8,10},{9,11},{10,... | collective-permute-start | bytes 104 | tf_op jit(solution)/shard_map/ppermute | solution.py:210
  5.0 1.1 %copy-start.6 = (s32[2,2,2]{2,1,0:T(2,128)S(1)}, s32[2,2,2]{2,1,0:T(2,128)}, u32[]{:S(2)}) copy-start(s32[2,2,2]{2,1,0:T(2,128)} %param.9) | copy-start | bytes 100
  5.0 6.5 %copy-start.5 = (bf16[2,192]{1,0:T(2,128)(2,1)S(1)}, bf16[2,192]{1,0:T(2,128)(2,1)}, u32[]{:S(2)}) copy-start(bf16[2,192]{1,0:T(2,128)(2,1)} %param.7) | copy-start | bytes 2308
  6.1 15.1 %collective-permute-start.2 = (bf16[392,768]{1,0:T(8,128)(2,1)S(1)}, bf16[392,768]{1,0:T(8,128)(2,1)S(1)}, u32[]{:S(2)}, u32[]{:S(2)}) collective-permute-start(bf16[392,768]{1,0:T(8,128)(2,1)S(1)} %get-tuple-element.46), channel_id=1, source_target_pairs={{0,8},{1,9},{2,10},{3,11},{4,12},{5,13},{6,14},{7,15},{8,16},{9,17... | collective-permute-start | bytes 1806344 | tf_op jit(solution)/shard_map/ppermute | solution.py:28
  7.7 14.9 %collective-permute-start.3 = (bf16[392,768]{1,0:T(8,128)(2,1)S(1)}, bf16[392,768]{1,0:T(8,128)(2,1)}, u32[]{:S(2)}, u32[]{:S(2)}) collective-permute-start(bf16[392,768]{1,0:T(8,128)(2,1)S(1)} %get-tuple-element.46), channel_id=1, source_target_pairs={{0,24},{1,25},{2,26},{3,27},{4,28},{5,29},{6,30},{7,31},{8,0},{9,1... | collective-permute-start | bytes 1806344 | tf_op jit(solution)/shard_map/ppermute | solution.py:28
  8.2 4.9 %collective-permute-start.1 = (s32[2,2,2,2]{3,2,1,0:T(2,128)S(1)}, s32[2,2,2,2]{3,2,1,0:T(2,128)S(1)}, u32[]{:S(2)}, u32[]{:S(2)}) collective-permute-start(s32[2,2,2,2]{3,2,1,0:T(2,128)S(1)} %pad_add_fusion.1), channel_id=1, source_target_pairs={{0,4},{1,5},{2,6},{3,7},{4,0},{5,1},{6,2},{7,3},{8,12},{9,13},{10,... | collective-permute-start | bytes 200 | tf_op jit(solution)/shard_map/ppermute | solution.py:210
  13.1 1.2 %collective-permute-start.4 = (s32[4,2,2,2]{3,2,1,0:T(2,128)S(1)}, s32[4,2,2,2]{3,2,1,0:T(2,128)S(1)}, u32[]{:S(2)}, u32[]{:S(2)}) collective-permute-start(s32[4,2,2,2]{3,2,1,0:T(2,128)S(1)} %pad_add_fusion), channel_id=1, source_target_pairs={{0,1},{1,0},{2,3},{3,2},{4,5},{5,4},{6,7},{7,6},{8,9},{9,8},{10,11... | collective-permute-start | bytes 392 | tf_op jit(solution)/shard_map/ppermute | solution.py:210
  13.2 24.0 %collective-permute-start.5 = (bf16[392,768]{1,0:T(8,128)(2,1)}, bf16[392,768]{1,0:T(8,128)(2,1)S(1)}, u32[]{:S(2)}, u32[]{:S(2)}) collective-permute-start(bf16[392,768]{1,0:T(8,128)(2,1)} %get-tuple-element.67), channel_id=1, source_target_pairs={{24,38},{25,39},{26,36},{27,37},{28,34},{29,35},{30,32},{31,33},{5... | collective-permute-start | bytes 1806344 | tf_op jit(solution)/shard_map/ppermute | solution.py:28
  22.6 15.9 %collective-permute-start.6 = (bf16[392,768]{1,0:T(8,128)(2,1)}, bf16[392,768]{1,0:T(8,128)(2,1)S(1)}, u32[]{:S(2)}, u32[]{:S(2)}) collective-permute-start(bf16[392,768]{1,0:T(8,128)(2,1)} %get-tuple-element.67), channel_id=1, source_target_pairs={{0,8},{1,9},{2,10},{3,11},{4,12},{5,13},{6,14},{7,15},{8,16},{9,17... | collective-permute-start | bytes 1806344 | tf_op jit(solution)/shard_map/ppermute | solution.py:28
  25.7 45.9 %collective-permute-start.8 = (bf16[392,768]{1,0:T(8,128)(2,1)}, bf16[392,768]{1,0:T(8,128)(2,1)}, u32[]{:S(2)}, u32[]{:S(2)}) collective-permute-start(bf16[392,768]{1,0:T(8,128)(2,1)} %get-tuple-element.67), channel_id=1, source_target_pairs={{16,38},{17,39},{18,36},{19,37},{20,34},{21,35},{22,32},{23,33},{4... | collective-permute-start | bytes 1806344 | tf_op jit(solution)/shard_map/ppermute | solution.py:28
  27.2 35.3 %copy-start.3 = (s32[2,2]{1,0:T(2,128)S(1)}, s32[2,2]{1,0:T(2,128)}, u32[]{:S(2)}) copy-start(s32[2,2]{1,0:T(2,128)} %conserve.7) | copy-start | bytes 52
  27.2 35.3 %copy-start.4 = (f32[8]{0:T(128)S(1)}, f32[8]{0:T(128)}, u32[]{:S(2)}) copy-start(f32[8]{0:T(128)} %occupied.7) | copy-start | bytes 100
  36.5 39.7 %collective-permute-start.9 = (bf16[392,768]{1,0:T(8,128)(2,1)S(1)}, bf16[392,768]{1,0:T(8,128)(2,1)S(1)}, u32[]{:S(2)}, u32[]{:S(2)}) collective-permute-start(bf16[392,768]{1,0:T(8,128)(2,1)S(1)} %collective-permute-done.2.refs_1_), channel_id=1, source_target_pairs={{0,38},{1,39},{2,36},{3,37},{4,34},{5,35},{6,32},{7,33},{32,6},{33... | collective-permute-start | bytes 1806344 | tf_op jit(solution)/shard_map/ppermute | solution.py:28
  38.5 0.8 copy-start.1
  39.3 36.8 %collective-permute-start.10 = (bf16[392,768]{1,0:T(8,128)(2,1)S(1)}, bf16[392,768]{1,0:T(8,128)(2,1)S(1)}, u32[]{:S(2)}, u32[]{:S(2)}) collective-permute-start(bf16[392,768]{1,0:T(8,128)(2,1)S(1)} %collective-permute-done.5.refs_0_), channel_id=1, source_target_pairs={{0,8},{1,9},{2,10},{3,11},{4,12},{5,13},{6,14},{7,15},{32,40},{33,... | collective-permute-start | bytes 1806344 | tf_op jit(solution)/shard_map/ppermute | solution.py:28
  40.6 35.6 %collective-permute-start.11 = (bf16[392,768]{1,0:T(8,128)(2,1)}, bf16[392,768]{1,0:T(8,128)(2,1)S(1)}, u32[]{:S(2)}, u32[]{:S(2)}) collective-permute-start(bf16[392,768]{1,0:T(8,128)(2,1)} %get-tuple-element.67), channel_id=1, source_target_pairs={{0,16},{1,17},{2,18},{3,19},{4,20},{5,21},{6,22},{7,23},{8,24},{9,... | collective-permute-start | bytes 1806344 | tf_op jit(solution)/shard_map/ppermute | solution.py:28
  57.2 30.5 %collective-permute-start.7 = (bf16[392,768]{1,0:T(8,128)(2,1)}, bf16[392,768]{1,0:T(8,128)(2,1)}, u32[]{:S(2)}, u32[]{:S(2)}) collective-permute-start(bf16[392,768]{1,0:T(8,128)(2,1)} %collective-permute-done.3), channel_id=1, source_target_pairs={{0,24},{1,25},{2,26},{3,27},{4,28},{5,29},{6,30},{7,31},{8,38},{9,... | collective-permute-start | bytes 1806344 | tf_op jit(solution)/shard_map/ppermute | solution.py:28
  62.5 3.7 %copy-start = (bf16[2,8,2,192,768]{4,3,2,1,0:T(8,128)(2,1)S(1)}, bf16[2,8,2,192,768]{4,3,2,1,0:T(8,128)(2,1)}, u32[]{:S(2)}) copy-start(bf16[2,8,2,192,768]{4,3,2,1,0:T(8,128)(2,1)} %copy.19) | copy-start | bytes 28311556
  66.2 1.1 copy-start.2
  92.4 1.8 %collective-permute-start.12 = (f32[4,2,2,24,192]{4,3,2,1,0:T(8,128)S(1)}, f32[4,2,2,24,192]{4,3,2,1,0:T(8,128)S(1)}, u32[]{:S(2)}, u32[]{:S(2)}) collective-permute-start(f32[4,2,2,24,192]{4,3,2,1,0:T(8,128)S(1)} %get-tuple-element.78), channel_id=1, source_target_pairs={{0,1},{1,0},{2,3},{3,2},{4,5},{5,4},{6,7},{7,6},{8,9},{9,8},{10,11... | collective-permute-start | bytes 884744 | tf_op jit(solution)/shard_map/ppermute | solution.py:200
  94.3 6.0 %collective-permute-start.15 = (f32[2,2,24,192]{3,2,1,0:T(8,128)S(1)}, f32[2,2,24,192]{3,2,1,0:T(8,128)S(1)}, u32[]{:S(2)}, u32[]{:S(2)}) collective-permute-start(f32[2,2,24,192]{3,2,1,0:T(8,128)S(1)} %get-tuple-element.82), channel_id=1, source_target_pairs={{0,6},{1,7},{2,0},{3,1},{4,2},{5,3},{6,4},{7,5},{8,14},{9,15},{10,... | collective-permute-start | bytes 221192 | tf_op jit(solution)/shard_map/ppermute | solution.py:205
  96.3 11.5 %collective-permute-start.14 = (f32[2,2,24,192]{3,2,1,0:T(8,128)S(1)}, f32[2,2,24,192]{3,2,1,0:T(8,128)S(1)}, u32[]{:S(2)}, u32[]{:S(2)}) collective-permute-start(f32[2,2,24,192]{3,2,1,0:T(8,128)S(1)} %get-tuple-element.83), channel_id=1, source_target_pairs={{0,4},{1,5},{2,6},{3,7},{4,0},{5,1},{6,2},{7,3},{8,12},{9,13},{10,... | collective-permute-start | bytes 221192 | tf_op jit(solution)/shard_map/ppermute | solution.py:205
  98.6 9.1 %collective-permute-start.13 = (f32[2,2,24,192]{3,2,1,0:T(8,128)S(1)}, f32[2,2,24,192]{3,2,1,0:T(8,128)S(1)}, u32[]{:S(2)}, u32[]{:S(2)}) collective-permute-start(f32[2,2,24,192]{3,2,1,0:T(8,128)S(1)} %get-tuple-element.81), channel_id=1, source_target_pairs={{0,2},{1,3},{2,4},{3,5},{4,6},{5,7},{6,0},{7,1},{8,10},{9,11},{10,... | collective-permute-start | bytes 221192 | tf_op jit(solution)/shard_map/ppermute | solution.py:205

commit v13 on v12

--- a/solution.py
+++ b/solution.py
@@ -233,11 +233,10 @@
     m0, m1, pairs, factors, here = lax.optimization_barrier((m0, m1, pairs, factors, here))
     plus = moved(m1, {0: (1, same), 1: (2, same), 2: (3, same), 3: (0, beside_next)})
     minus = moved(m1, {0: (3, same), 1: (0, same), 2: (1, beside_next), 3: (2, beside_next)})
-    pairs = with_partner(pairs, 2 * CORES)
+    pairs = with_partner(with_partner(pairs, 2 * CORES), 1)
     m0, pairs, factors = lax.optimization_barrier((m0, pairs, factors))
     cross_one = moved(m0, {3: (0, onto_next)})
-    cross_two = moved(m0, {2: (0, onto_next)})
-    pairs = with_partner(pairs, 1)
+    two = moved(m0, {0: (2, same), 2: (0, onto_next)})
     own_energy = virtual_energy.astype(jnp.float32)[:, None, :]
     m0, plus, minus, factors, pairs, own_energy = lax.optimization_barrier(
         (m0, plus, minus, factors, pairs, own_energy)
@@ -246,9 +245,8 @@
     back = moved(minus, {0: (3, same), 1: (0, across), 2: (1, across), 3: (2, same)})
     near_one = moved(m0, {0: (1, same), 1: (2, same), 2: (3, same)})
     left = jnp.transpose(factors, (0, 1, 3, 2, 4)).reshape(momenta, orbitals, 2 * virtuals, auxiliary)
-    m0, cross_one, near_one, left = lax.optimization_barrier((m0, cross_one, near_one, left))
-    onward = moved(cross_one, {0: (1, same)})
-    near_two = moved(m0, {0: (2, same), 1: (3, same)})
+    m0, cross_one, left = lax.optimization_barrier((m0, cross_one, left))
+    onward = moved(jnp.where(column == 0, cross_one, m0), {0: (1, same), 1: (3, same)})
 
     def density(orders, held, mates, before):
         return piece_density(
@@ -257,10 +255,10 @@
 
     orders = (((0,), (0,)), ((1, 0), (0, 1)), ((0, 1), (1, 0)), ((1,), (1,)))
     terms = density(orders[:1], (0, 1), (cross_one, near_one), ())
-    *terms, cross_two, plus = lax.optimization_barrier((*terms, cross_two, plus))
-    terms += density(orders[1:2], (0, 1), (cross_two, plus), ())
-    *terms, up, onward, near_two = lax.optimization_barrier((*terms, up, onward, near_two))
-    terms += density(orders[2:3], (0, 1, 2), (up, onward, near_two), ())
+    *terms, two, plus = lax.optimization_barrier((*terms, two, plus))
+    terms += density(orders[1:2], (0, 1), (two, plus), ())
+    *terms, up, onward = lax.optimization_barrier((*terms, up, onward))
+    terms += density(orders[2:3], (0, 1, 2, 1), (up, onward, two), ())
     total = density(orders, (0,), (back,), terms)
     return jnp.transpose(summed(*total), (0, 2, 1, 3))
 

time: 111 us -> 106 us (0.955); the launches traced: 108 us -> 105 us
  starting transfers between devices: 40.8 us -> 30.2 us
  waiting for transfers between devices: 29.1 us -> 36.2 us
  other arithmetic: 1.3 us -> 3.36 us
  local copies, waits for them, and re-layouts: 19 us -> 17 us
    ppermute x9 -> x8, starting transfers between devices: 31.1 us -> 21.1 us  [moved(): return lax.ppermute(array, ('ka', 'occ'), pairs)]
    ppermute x9 -> x8, waiting for transfers between devices: 16.4 us -> 25.6 us  [moved(): return lax.ppermute(array, ('ka', 'occ'), pairs)]
    ppermute x3, waiting for transfers between devices: 9.13 us -> 7.01 us  [summed(): total = total + lax.ppermute(part, 'occ', ring)]
    select_n x0 -> x1, other arithmetic: none -> 2 us  [local(): jnp.where(column == 0, cross_one, m0)]
    unnamed x14 -> x10, local copies, waits for them, and re-layouts: 5.6 us -> 4.22 us
  transfers between devices with their start and end apart: 16 -> 15, of which waited for: 9 -> 8; matrix products, arithmetic and copies ran while one was open for 13% -> 15% of each run, Pallas kernels for 12% -> 13%
where the time goes in v13:
time: 106 us; the launch traced here: 105 us
  waiting for transfers between devices  36.2 us (34%)
  starting transfers between devices  30.2 us (28%)
  Pallas kernels  18.1 us (17%)
  local copies, waits for them, and re-layouts  17 us (16%)
  other arithmetic  3.36 us (3%)
    ppermute x8, waiting for transfers between devices, moved(): return lax.ppermute(array, ('ka', 'occ'), pairs)  25.6 us
    ppermute x8, starting transfers between devices, moved(): return lax.ppermute(array, ('ka', 'occ'), pairs)  21.1 us
    pallas_call x4, Pallas kernels, piece_density(): pl.pallas_call(functools.partial(piece_kernel, len(mates), len(before), o...  18.1 us
    transpose x1, local copies, waits for them, and re-layouts, local(): jnp.transpose(factors, (0, 1, 3, 2, 4))  9.31 us
    ppermute x3, waiting for transfers between devices, summed(): total = total + lax.ppermute(part, 'occ', ring)  7.01 us
    ppermute x3, starting transfers between devices, with_partner(): lax.ppermute(array, 'occ', [(i, i ^ reach) for i in range(LINE * CORES)])  5.19 us
    unnamed x10, local copies, waits for them, and re-layouts  4.22 us
    ppermute x3, starting transfers between devices, summed(): total = total + lax.ppermute(part, 'occ', ring)  3.9 us
  transfers between devices with their start and end apart: 15, of which 8 were waited for; matrix products, arithmetic and copies ran while one was open for 15% of the time, Pallas kernels for 13%

profile of v13, /device:TPU:10, one launch (start us, length us, event | category | flops | bytes accessed | tf_op | source)
XLA Modules:
  0.0 105.1 jit_solution(10695977988548191896)
XLA Ops:
  0.0 1.9 %collective-permute-start = (s32[1,2,2,2]{3,2,1,0:T(2,128)}, s32[1,2,2,2]{3,2,1,0:T(2,128)S(1)}, u32[]{:S(2)}, u32[]{:S(2)}) collective-permute-start(s32[1,2,2,2]{3,2,1,0:T(2,128)} %bitcast.40), channel_id=1, source_target_pairs={{0,2},{1,3},{2,0},{3,1},{4,6},{5,7},{6,4},{7,5},{8,10},{9,11},{10,... | collective-permute-start | bytes 104 | tf_op jit(solution)/shard_map/ppermute | solution.py:210
  1.9 2.1 %constant_dynamic-slice_fusion = (bf16[1,8,24,2,768]{4,3,2,1,0:T(2,128)(2,1)S(1)}, bf16[1,8,24,2,768]{4,3,2,1,0:T(2,128)(2,1)S(1)}) fusion(bf16[2,8,192,2,768]{4,3,2,1,0:T(2,128)(2,1)} %param.5, s32[]{:T(128)S(6)} %select_n.52), kind=kLoop, calls=%fused_computation.20 | loop fusion | bytes 2359300 | tf_op jit(solution)/shard_map/dynamic_slice | solution.py:222
  4.0 0.0 copy-start.3
  4.0 0.1 copy.28
  4.1 0.1 copy.29
  4.1 0.5 copy-done.3
  4.7 0.1 pad_add_fusion.3.here
  4.7 0.1 pad.23.clone
  4.8 1.1 %fusion.6 = (bf16[392,768]{1,0:T(8,128)(2,1)S(1)}, bf16[392,768]{1,0:T(8,128)(2,1)}) fusion(bf16[1,192]{1,0:T(2,128)(2,1)S(1)} %get-tuple-element.82, bf16[384,768]{1,0:T(8,128)(2,1)S(1)} %bitcast.39, bf16[392]{0:T(512)(128)(2,1)S(1)} %pad.23.clone, bf16[1,192]{1,0:T(2,128)(2,1)S(1)} %get-tuple-element.83, bf16[384,768]{1,0:T(8,128)(2,1)S(1)} %bitcast.38), kind=kLoop, calls=%fused_computation.8 | loop fusion | flops 4816896 | bytes 2385424 | tf_op jit(solution)/shard_map/concatenate | solution.py:228
  5.9 0.0 collective-permute-done
  6.0 1.6 %collective-permute-start.3 = (bf16[392,768]{1,0:T(8,128)(2,1)S(1)}, bf16[392,768]{1,0:T(8,128)(2,1)S(1)}, u32[]{:S(2)}, u32[]{:S(2)}) collective-permute-start(bf16[392,768]{1,0:T(8,128)(2,1)S(1)} %get-tuple-element.44), channel_id=1, source_target_pairs={{0,8},{1,9},{2,10},{3,11},{4,12},{5,13},{6,14},{7,15},{8,16},{9,17... | collective-permute-start | bytes 1806344 | tf_op jit(solution)/shard_map/ppermute | solution.py:28
  7.5 3.3 %collective-permute-start.1 = (s32[2,2,2,2]{3,2,1,0:T(2,128)S(1)}, s32[2,2,2,2]{3,2,1,0:T(2,128)S(1)}, u32[]{:S(2)}, u32[]{:S(2)}) collective-permute-start(s32[2,2,2,2]{3,2,1,0:T(2,128)S(1)} %pad_add_fusion.1), channel_id=1, source_target_pairs={{0,4},{1,5},{2,6},{3,7},{4,0},{5,1},{6,2},{7,3},{8,12},{9,13},{10,... | collective-permute-start | bytes 200 | tf_op jit(solution)/shard_map/ppermute | solution.py:210
  10.8 0.5 collective-permute-start.4
  11.3 1.0 collective-permute-done.1
  12.4 0.0 collective-permute-start.2
  12.4 0.1 copy.17
  12.5 0.1 copy.18
  12.6 0.9 collective-permute-done.2
  13.6 0.1 copy.19
  13.7 0.1 pad_add_fusion.2
  13.7 0.7 collective-permute-start.5
  14.5 6.6 %collective-permute-done.3.refs_1_ = bf16[392,768]{1,0:T(8,128)(2,1)S(1)} collective-permute-done((bf16[392,768]{1,0:T(8,128)(2,1)S(1)}, bf16[392,768]{1,0:T(8,128)(2,1)S(1)}, u32[]{:S(2)}, u32[]{:S(2)}) %collective-permute-start.3) | collective-permute-done | bytes 602144 | tf_op jit(solution)/shard_map/ppermute | solution.py:28
  21.1 4.3 %collective-permute-done.4 = bf16[392,768]{1,0:T(8,128)(2,1)} collective-permute-done((bf16[392,768]{1,0:T(8,128)(2,1)S(1)}, bf16[392,768]{1,0:T(8,128)(2,1)}, u32[]{:S(2)}, u32[]{:S(2)}) %collective-permute-start.4) | collective-permute-done | bytes 602144 | tf_op jit(solution)/shard_map/ppermute | solution.py:28
  25.4 3.1 %collective-permute-start.7 = (bf16[392,768]{1,0:T(8,128)(2,1)}, bf16[392,768]{1,0:T(8,128)(2,1)}, u32[]{:S(2)}, u32[]{:S(2)}) collective-permute-start(bf16[392,768]{1,0:T(8,128)(2,1)} %get-tuple-element.64), channel_id=1, source_target_pairs={{0,8},{1,9},{2,10},{3,11},{4,12},{5,13},{6,14},{7,15},{8,16},{9,17... | collective-permute-start | bytes 1806344 | tf_op jit(solution)/shard_map/ppermute | solution.py:28
  28.5 0.7 collective-permute-start.8
  29.2 9.3 %copy.20 = bf16[2,8,2,192,768]{4,3,2,1,0:T(8,128)(2,1)} copy(bf16[2,8,2,192,768]{4,2,3,1,0:T(2,128)(2,1)} %bitcast.37) | data formatting | bytes 18874368 | tf_op jit(solution)/shard_map/transpose | solution.py:247
  38.5 0.8 collective-permute-start.9
  39.4 2.0 %broadcast_select_fusion = bf16[392,768]{1,0:T(8,128)(2,1)} fusion(bf16[392,768]{1,0:T(8,128)(2,1)S(1)} %collective-permute-done.5.refs_0_, bf16[392,768]{1,0:T(8,128)(2,1)} %get-tuple-element.64, pred[]{:T(512)S(6)} %eq.9), kind=kLoop, calls=%fused_computation.9 | loop fusion | flops 301056 | bytes 1806337 | tf_op jit(solution)/shard_map/jit(_where)/select_n | solution.py:249
  41.4 11.5 %collective-permute-start.10 = (bf16[392,768]{1,0:T(8,128)(2,1)}, bf16[392,768]{1,0:T(8,128)(2,1)S(1)}, u32[]{:S(2)}, u32[]{:S(2)}) collective-permute-start(bf16[392,768]{1,0:T(8,128)(2,1)} %broadcast_select_fusion), channel_id=1, source_target_pairs={{0,8},{1,9},{2,10},{3,11},{4,12},{5,13},{6,14},{7,15},{8,24},{9,25... | collective-permute-start | bytes 1806344 | tf_op jit(solution)/shard_map/ppermute | solution.py:28
  52.9 2.1 %collective-permute-start.6 = (bf16[392,768]{1,0:T(8,128)(2,1)}, bf16[392,768]{1,0:T(8,128)(2,1)}, u32[]{:S(2)}, u32[]{:S(2)}) collective-permute-start(bf16[392,768]{1,0:T(8,128)(2,1)} %collective-permute-done.4), channel_id=1, source_target_pairs={{0,24},{1,25},{2,26},{3,27},{4,28},{5,29},{6,30},{7,31},{8,38},{9,... | collective-permute-start | bytes 1806344 | tf_op jit(solution)/shard_map/ppermute | solution.py:28
  55.0 0.1 copy.24.pairs
  55.2 3.7 %copy-done = bf16[2,8,2,192,768]{4,3,2,1,0:T(8,128)(2,1)S(1)} copy-done((bf16[2,8,2,192,768]{4,3,2,1,0:T(8,128)(2,1)S(1)}, bf16[2,8,2,192,768]{4,3,2,1,0:T(8,128)(2,1)}, u32[]{:S(2)}) %copy-start) | copy-done | bytes 9437208
  58.8 4.6 %shard_map.55 = (f32[4,2,24,192]{3,2,1,0:T(8,128)S(1)}, f32[4,2,24,192]{3,2,1,0:T(8,128)S(1)}) custom-call(s32[2,2]{1,0:T(2,128)S(1)} %copy-done.1, s32[8,2,2,2]{3,2,1,0:T(2,128)S(1)} %copy.24.pairs, s32[2]{0:T(128)S(1)} %pad_add_fusion.3.here, f32[8]{0:T(128)S(1)} %copy-done.2, f32[2,1,192]{2,1,0:T(1,128)S(1)} %reshape.12.own_energy, ...), custom_call_target="tpu_custom_call" | custom-call | flops 1925185536 | bytes 5308416 | tf_op jit(solution)/shard_map/pallas_call | solution.py:174
  63.4 4.3 %shard_map.56 = (f32[4,2,24,192]{3,2,1,0:T(8,128)S(1)}, f32[4,2,24,192]{3,2,1,0:T(8,128)S(1)}) custom-call(s32[2,2]{1,0:T(2,128)S(1)} %copy-done.1, s32[8,2,2,2]{3,2,1,0:T(2,128)S(1)} %copy.24.pairs, s32[2]{0:T(128)S(1)} %pad_add_fusion.3.here, f32[8]{0:T(128)S(1)} %copy-done.2, f32[2,1,192]{2,1,0:T(1,128)S(1)} %reshape.12.own_energy, ...), custom_call_target="tpu_custom_call" | custom-call | flops 1925185536 | bytes 5308416 | tf_op jit(solution)/shard_map/pallas_call | solution.py:174
  67.7 0.0 collective-permute-done.9.refs_0_
  67.8 4.5 %shard_map.57 = (f32[4,2,24,192]{3,2,1,0:T(8,128)S(1)}, f32[4,2,24,192]{3,2,1,0:T(8,128)S(1)}) custom-call(s32[2,2]{1,0:T(2,128)S(1)} %copy-done.1, s32[8,2,2,2]{3,2,1,0:T(2,128)S(1)} %copy.24.pairs, s32[2]{0:T(128)S(1)} %pad_add_fusion.3.here, f32[8]{0:T(128)S(1)} %copy-done.2, f32[2,1,192]{2,1,0:T(1,128)S(1)} %reshape.12.own_energy, ...), custom_call_target="tpu_custom_call" | custom-call | flops 1925185536 | bytes 5308416 | tf_op jit(solution)/shard_map/pallas_call | solution.py:174
  72.3 14.6 %collective-permute-done.6.refs_0_ = bf16[392,768]{1,0:T(8,128)(2,1)} collective-permute-done((bf16[392,768]{1,0:T(8,128)(2,1)}, bf16[392,768]{1,0:T(8,128)(2,1)}, u32[]{:S(2)}, u32[]{:S(2)}) %collective-permute-start.6) | collective-permute-done | bytes 602144 | tf_op jit(solution)/shard_map/ppermute | solution.py:28
  86.9 4.7 %shard_map.58 = (f32[4,2,2,24,192]{4,3,2,1,0:T(8,128)S(1)}, f32[4,2,2,24,192]{4,3,2,1,0:T(8,128)S(1)}) custom-call(s32[2,2]{1,0:T(2,128)S(1)} %copy-done.1, s32[8,2,2,2]{3,2,1,0:T(2,128)S(1)} %copy.24.pairs, s32[2]{0:T(128)S(1)} %pad_add_fusion.3.here, f32[8]{0:T(128)S(1)} %copy-done.2, f32[2,1,192]{2,1,0:T(1,128)S(1)} %reshape.12.own_energy, ...), custom_call_target="tpu_custom_call" | custom-call | flops 1925185536 | bytes 5308416 | tf_op jit(solution)/shard_map/pallas_call | solution.py:174
  91.6 0.1 collective-permute-start.11
  91.8 1.6 %collective-permute-done.11 = f32[4,2,2,24,192]{4,3,2,1,0:T(8,128)S(1)} collective-permute-done((f32[4,2,2,24,192]{4,3,2,1,0:T(8,128)S(1)}, f32[4,2,2,24,192]{4,3,2,1,0:T(8,128)S(1)}, u32[]{:S(2)}, u32[]{:S(2)}) %collective-permute-start.11) | collective-permute-done | bytes 294944 | tf_op jit(solution)/shard_map/ppermute | solution.py:200
  93.4 0.1 add.62
  93.5 0.1 collective-permute-start.12
  93.6 1.8 %collective-permute-start.13 = (f32[2,2,24,192]{3,2,1,0:T(8,128)S(1)}, f32[2,2,24,192]{3,2,1,0:T(8,128)S(1)}, u32[]{:S(2)}, u32[]{:S(2)}) collective-permute-start(f32[2,2,24,192]{3,2,1,0:T(8,128)S(1)} %get-tuple-element.79), channel_id=1, source_target_pairs={{0,4},{1,5},{2,6},{3,7},{4,0},{5,1},{6,2},{7,3},{8,12},{9,13},{10,... | collective-permute-start | bytes 221192 | tf_op jit(solution)/shard_map/ppermute | solution.py:205
  95.4 2.0 %collective-permute-start.14 = (f32[2,2,24,192]{3,2,1,0:T(8,128)S(1)}, f32[2,2,24,192]{3,2,1,0:T(8,128)S(1)}, u32[]{:S(2)}, u32[]{:S(2)}) collective-permute-start(f32[2,2,24,192]{3,2,1,0:T(8,128)S(1)} %get-tuple-element.78), channel_id=1, source_target_pairs={{0,6},{1,7},{2,0},{3,1},{4,2},{5,3},{6,4},{7,5},{8,14},{9,15},{10,... | collective-permute-start | bytes 221192 | tf_op jit(solution)/shard_map/ppermute | solution.py:205
  97.4 3.7 %collective-permute-done.12 = f32[2,2,24,192]{3,2,1,0:T(8,128)S(1)} collective-permute-done((f32[2,2,24,192]{3,2,1,0:T(8,128)S(1)}, f32[2,2,24,192]{3,2,1,0:T(8,128)S(1)}, u32[]{:S(2)}, u32[]{:S(2)}) %collective-permute-start.12) | collective-permute-done | bytes 73760 | tf_op jit(solution)/shard_map/ppermute | solution.py:205
  101.1 3.3 %collective-permute-done.13 = f32[2,2,24,192]{3,2,1,0:T(8,128)S(1)} collective-permute-done((f32[2,2,24,192]{3,2,1,0:T(8,128)S(1)}, f32[2,2,24,192]{3,2,1,0:T(8,128)S(1)}, u32[]{:S(2)}, u32[]{:S(2)}) %collective-permute-start.13) | collective-permute-done | bytes 73760 | tf_op jit(solution)/shard_map/ppermute | solution.py:205
  104.4 0.0 collective-permute-done.14
  104.5 0.7 copy.25
  (18 shorter events, 0.1 us)
Async XLA Ops:
  0.0 5.9 %collective-permute-start = (s32[1,2,2,2]{3,2,1,0:T(2,128)}, s32[1,2,2,2]{3,2,1,0:T(2,128)S(1)}, u32[]{:S(2)}, u32[]{:S(2)}) collective-permute-start(s32[1,2,2,2]{3,2,1,0:T(2,128)} %bitcast.40), channel_id=1, source_target_pairs={{0,2},{1,3},{2,0},{3,1},{4,6},{5,7},{6,4},{7,5},{8,10},{9,11},{10,... | collective-permute-start | bytes 104 | tf_op jit(solution)/shard_map/ppermute | solution.py:210
  4.0 0.7 copy-start.3
  4.7 1.3 %copy-start.4 = (s32[2,2,2]{2,1,0:T(2,128)S(1)}, s32[2,2,2]{2,1,0:T(2,128)}, u32[]{:S(2)}) copy-start(s32[2,2,2]{2,1,0:T(2,128)} %param.9) | copy-start | bytes 100
  6.0 15.1 %collective-permute-start.3 = (bf16[392,768]{1,0:T(8,128)(2,1)S(1)}, bf16[392,768]{1,0:T(8,128)(2,1)S(1)}, u32[]{:S(2)}, u32[]{:S(2)}) collective-permute-start(bf16[392,768]{1,0:T(8,128)(2,1)S(1)} %get-tuple-element.44), channel_id=1, source_target_pairs={{0,8},{1,9},{2,10},{3,11},{4,12},{5,13},{6,14},{7,15},{8,16},{9,17... | collective-permute-start | bytes 1806344 | tf_op jit(solution)/shard_map/ppermute | solution.py:28
  7.5 4.9 %collective-permute-start.1 = (s32[2,2,2,2]{3,2,1,0:T(2,128)S(1)}, s32[2,2,2,2]{3,2,1,0:T(2,128)S(1)}, u32[]{:S(2)}, u32[]{:S(2)}) collective-permute-start(s32[2,2,2,2]{3,2,1,0:T(2,128)S(1)} %pad_add_fusion.1), channel_id=1, source_target_pairs={{0,4},{1,5},{2,6},{3,7},{4,0},{5,1},{6,2},{7,3},{8,12},{9,13},{10,... | collective-permute-start | bytes 200 | tf_op jit(solution)/shard_map/ppermute | solution.py:210
  10.8 14.6 %collective-permute-start.4 = (bf16[392,768]{1,0:T(8,128)(2,1)S(1)}, bf16[392,768]{1,0:T(8,128)(2,1)}, u32[]{:S(2)}, u32[]{:S(2)}) collective-permute-start(bf16[392,768]{1,0:T(8,128)(2,1)S(1)} %get-tuple-element.44), channel_id=1, source_target_pairs={{0,24},{1,25},{2,26},{3,27},{4,28},{5,29},{6,30},{7,31},{8,0},{9,1... | collective-permute-start | bytes 1806344 | tf_op jit(solution)/shard_map/ppermute | solution.py:28
  12.4 1.2 %collective-permute-start.2 = (s32[4,2,2,2]{3,2,1,0:T(2,128)S(1)}, s32[4,2,2,2]{3,2,1,0:T(2,128)S(1)}, u32[]{:S(2)}, u32[]{:S(2)}) collective-permute-start(s32[4,2,2,2]{3,2,1,0:T(2,128)S(1)} %pad_add_fusion), channel_id=1, source_target_pairs={{0,1},{1,0},{2,3},{3,2},{4,5},{5,4},{6,7},{7,6},{8,9},{9,8},{10,11... | collective-permute-start | bytes 392 | tf_op jit(solution)/shard_map/ppermute | solution.py:210
  13.7 25.6 %collective-permute-start.5 = (bf16[392,768]{1,0:T(8,128)(2,1)}, bf16[392,768]{1,0:T(8,128)(2,1)S(1)}, u32[]{:S(2)}, u32[]{:S(2)}) collective-permute-start(bf16[392,768]{1,0:T(8,128)(2,1)} %get-tuple-element.64), channel_id=1, source_target_pairs={{24,38},{25,39},{26,36},{27,37},{28,34},{29,35},{30,32},{31,33},{5... | collective-permute-start | bytes 1806344 | tf_op jit(solution)/shard_map/ppermute | solution.py:28
  25.4 29.7 %collective-permute-start.7 = (bf16[392,768]{1,0:T(8,128)(2,1)}, bf16[392,768]{1,0:T(8,128)(2,1)}, u32[]{:S(2)}, u32[]{:S(2)}) collective-permute-start(bf16[392,768]{1,0:T(8,128)(2,1)} %get-tuple-element.64), channel_id=1, source_target_pairs={{0,8},{1,9},{2,10},{3,11},{4,12},{5,13},{6,14},{7,15},{8,16},{9,17... | collective-permute-start | bytes 1806344 | tf_op jit(solution)/shard_map/ppermute | solution.py:28
  28.5 34.9 %collective-permute-start.8 = (bf16[392,768]{1,0:T(8,128)(2,1)}, bf16[392,768]{1,0:T(8,128)(2,1)S(1)}, u32[]{:S(2)}, u32[]{:S(2)}) collective-permute-start(bf16[392,768]{1,0:T(8,128)(2,1)} %get-tuple-element.64), channel_id=1, source_target_pairs={{0,16},{1,17},{2,18},{3,19},{4,20},{5,21},{6,22},{7,23},{16,38},{1... | collective-permute-start | bytes 1806344 | tf_op jit(solution)/shard_map/ppermute | solution.py:28
  38.5 16.6 %copy-start.1 = (s32[2,2]{1,0:T(2,128)S(1)}, s32[2,2]{1,0:T(2,128)}, u32[]{:S(2)}) copy-start(s32[2,2]{1,0:T(2,128)} %conserve.7) | copy-start | bytes 52
  38.5 16.6 %copy-start.2 = (f32[8]{0:T(128)S(1)}, f32[8]{0:T(128)}, u32[]{:S(2)}) copy-start(f32[8]{0:T(128)} %occupied.7) | copy-start | bytes 100
  38.5 29.2 %collective-permute-start.9 = (bf16[392,768]{1,0:T(8,128)(2,1)S(1)}, bf16[392,768]{1,0:T(8,128)(2,1)S(1)}, u32[]{:S(2)}, u32[]{:S(2)}) collective-permute-start(bf16[392,768]{1,0:T(8,128)(2,1)S(1)} %collective-permute-done.3.refs_1_), channel_id=1, source_target_pairs={{0,38},{1,39},{2,36},{3,37},{4,34},{5,35},{6,32},{7,33},{32,6},{33... | collective-permute-start | bytes 1806344 | tf_op jit(solution)/shard_map/ppermute | solution.py:28
  41.4 26.4 %collective-permute-start.10 = (bf16[392,768]{1,0:T(8,128)(2,1)}, bf16[392,768]{1,0:T(8,128)(2,1)S(1)}, u32[]{:S(2)}, u32[]{:S(2)}) collective-permute-start(bf16[392,768]{1,0:T(8,128)(2,1)} %broadcast_select_fusion), channel_id=1, source_target_pairs={{0,8},{1,9},{2,10},{3,11},{4,12},{5,13},{6,14},{7,15},{8,24},{9,25... | collective-permute-start | bytes 1806344 | tf_op jit(solution)/shard_map/ppermute | solution.py:28
  52.9 34.0 %collective-permute-start.6 = (bf16[392,768]{1,0:T(8,128)(2,1)}, bf16[392,768]{1,0:T(8,128)(2,1)}, u32[]{:S(2)}, u32[]{:S(2)}) collective-permute-start(bf16[392,768]{1,0:T(8,128)(2,1)} %collective-permute-done.4), channel_id=1, source_target_pairs={{0,24},{1,25},{2,26},{3,27},{4,28},{5,29},{6,30},{7,31},{8,38},{9,... | collective-permute-start | bytes 1806344 | tf_op jit(solution)/shard_map/ppermute | solution.py:28
  55.2 3.7 %copy-start = (bf16[2,8,2,192,768]{4,3,2,1,0:T(8,128)(2,1)S(1)}, bf16[2,8,2,192,768]{4,3,2,1,0:T(8,128)(2,1)}, u32[]{:S(2)}) copy-start(bf16[2,8,2,192,768]{4,3,2,1,0:T(8,128)(2,1)} %copy.20) | copy-start | bytes 28311556
  91.6 1.8 %collective-permute-start.11 = (f32[4,2,2,24,192]{4,3,2,1,0:T(8,128)S(1)}, f32[4,2,2,24,192]{4,3,2,1,0:T(8,128)S(1)}, u32[]{:S(2)}, u32[]{:S(2)}) collective-permute-start(f32[4,2,2,24,192]{4,3,2,1,0:T(8,128)S(1)} %get-tuple-element.74), channel_id=1, source_target_pairs={{0,1},{1,0},{2,3},{3,2},{4,5},{5,4},{6,7},{7,6},{8,9},{9,8},{10,11... | collective-permute-start | bytes 884744 | tf_op jit(solution)/shard_map/ppermute | solution.py:200
  93.5 7.6 %collective-permute-start.12 = (f32[2,2,24,192]{3,2,1,0:T(8,128)S(1)}, f32[2,2,24,192]{3,2,1,0:T(8,128)S(1)}, u32[]{:S(2)}, u32[]{:S(2)}) collective-permute-start(f32[2,2,24,192]{3,2,1,0:T(8,128)S(1)} %get-tuple-element.77), channel_id=1, source_target_pairs={{0,2},{1,3},{2,4},{3,5},{4,6},{5,7},{6,0},{7,1},{8,10},{9,11},{10,... | collective-permute-start | bytes 221192 | tf_op jit(solution)/shard_map/ppermute | solution.py:205
  93.6 10.8 %collective-permute-start.13 = (f32[2,2,24,192]{3,2,1,0:T(8,128)S(1)}, f32[2,2,24,192]{3,2,1,0:T(8,128)S(1)}, u32[]{:S(2)}, u32[]{:S(2)}) collective-permute-start(f32[2,2,24,192]{3,2,1,0:T(8,128)S(1)} %get-tuple-element.79), channel_id=1, source_target_pairs={{0,4},{1,5},{2,6},{3,7},{4,0},{5,1},{6,2},{7,3},{8,12},{9,13},{10,... | collective-permute-start | bytes 221192 | tf_op jit(solution)/shard_map/ppermute | solution.py:205
  95.4 9.0 %collective-permute-start.14 = (f32[2,2,24,192]{3,2,1,0:T(8,128)S(1)}, f32[2,2,24,192]{3,2,1,0:T(8,128)S(1)}, u32[]{:S(2)}, u32[]{:S(2)}) collective-permute-start(f32[2,2,24,192]{3,2,1,0:T(8,128)S(1)} %get-tuple-element.78), channel_id=1, source_target_pairs={{0,6},{1,7},{2,0},{3,1},{4,2},{5,3},{6,4},{7,5},{8,14},{9,15},{10,... | collective-permute-start | bytes 221192 | tf_op jit(solution)/shard_map/ppermute | solution.py:205

commit v14 on v13

--- a/solution.py
+++ b/solution.py
@@ -253,10 +253,10 @@
             orders, held, conserve, pairs, here, occupied_energy, own_energy, left, mates, before
         )
 
-    orders = (((0,), (0,)), ((1, 0), (0, 1)), ((0, 1), (1, 0)), ((1,), (1,)))
-    terms = density(orders[:1], (0, 1), (cross_one, near_one), ())
-    *terms, two, plus = lax.optimization_barrier((*terms, two, plus))
-    terms += density(orders[1:2], (0, 1), (two, plus), ())
+    orders = (((1, 0), (0, 1)), ((0,), (0,)), ((0, 1), (1, 0)), ((1,), (1,)))
+    terms = density(orders[:1], (0, 1), (two, plus), ())
+    *terms, cross_one, near_one = lax.optimization_barrier((*terms, cross_one, near_one))
+    terms += density(orders[1:2], (0, 1), (cross_one, near_one), ())
     *terms, up, onward = lax.optimization_barrier((*terms, up, onward))
     terms += density(orders[2:3], (0, 1, 2, 1), (up, onward, two), ())
     total = density(orders, (0,), (back,), terms)

time: 106 us -> 111 us (1.047)
  the two profiles are of different devices: /device:TPU:10 before, /device:TPU:30 now
where the time goes in v14:
time: 111 us
  waiting for transfers between devices  43.4 us (39%)
  starting transfers between devices  28.8 us (26%)
  Pallas kernels  18.1 us (16%)
  local copies, waits for them, and re-layouts  17.2 us (15%)
  other arithmetic  3.35 us (3%)
    ppermute x8, waiting for transfers between devices, moved(): return lax.ppermute(array, ('ka', 'occ'), pairs)  31.5 us
    pallas_call x4, Pallas kernels, piece_density(): pl.pallas_call(functools.partial(piece_kernel, len(mates), len(before), o...  18.1 us
    ppermute x8, starting transfers between devices, moved(): return lax.ppermute(array, ('ka', 'occ'), pairs)  13.8 us
    ppermute x3, starting transfers between devices, summed(): total = total + lax.ppermute(part, 'occ', ring)  9.68 us
    transpose x1, local copies, waits for them, and re-layouts, local(): jnp.transpose(factors, (0, 1, 3, 2, 4))  9.31 us
    ppermute x3, waiting for transfers between devices, summed(): total = total + lax.ppermute(part, 'occ', ring)  9.13 us
    ppermute x3, starting transfers between devices, with_partner(): lax.ppermute(array, 'occ', [(i, i ^ reach) for i in range(LINE * CORES)])  5.28 us
    unnamed x10, local copies, waits for them, and re-layouts  3.69 us
  transfers between devices with their start and end apart: 15, of which 10 were waited for; matrix products, arithmetic and copies ran while one was open for 14% of the time, Pallas kernels for 12%

profile of v14, /device:TPU:30, one launch (start us, length us, event | category | flops | bytes accessed | tf_op | source)
XLA Modules:
  0.0 111.1 jit_solution(12983819275282378467)
XLA Ops:
  0.0 1.9 %collective-permute-start = (s32[1,2,2,2]{3,2,1,0:T(2,128)}, s32[1,2,2,2]{3,2,1,0:T(2,128)S(1)}, u32[]{:S(2)}, u32[]{:S(2)}) collective-permute-start(s32[1,2,2,2]{3,2,1,0:T(2,128)} %bitcast.40), channel_id=1, source_target_pairs={{0,2},{1,3},{2,0},{3,1},{4,6},{5,7},{6,4},{7,5},{8,10},{9,11},{10,... | collective-permute-start | bytes 104 | tf_op jit(solution)/shard_map/ppermute | solution.py:210
  1.9 0.8 fusion.10
  2.7 2.1 %constant_dynamic-slice_fusion = (bf16[1,8,24,2,768]{4,3,2,1,0:T(2,128)(2,1)S(1)}, bf16[1,8,24,2,768]{4,3,2,1,0:T(2,128)(2,1)S(1)}) fusion(bf16[2,8,192,2,768]{4,3,2,1,0:T(2,128)(2,1)} %param.5, s32[]{:T(128)S(6)} %select_n.52), kind=kLoop, calls=%fused_computation.20 | loop fusion | bytes 2359300 | tf_op jit(solution)/shard_map/dynamic_slice | solution.py:222
  4.7 0.1 copy.29
  4.8 0.1 copy.28
  4.9 0.1 pad.23.clone
  5.0 0.1 pad_add_fusion.3.here
  5.0 1.1 %fusion.6 = (bf16[392,768]{1,0:T(8,128)(2,1)S(1)}, bf16[392,768]{1,0:T(8,128)(2,1)}) fusion(bf16[1,192]{1,0:T(2,128)(2,1)S(1)} %get-tuple-element.82, bf16[384,768]{1,0:T(8,128)(2,1)S(1)} %bitcast.38, bf16[392]{0:T(512)(128)(2,1)S(1)} %pad.23.clone, bf16[1,192]{1,0:T(2,128)(2,1)S(1)} %get-tuple-element.83, bf16[384,768]{1,0:T(8,128)(2,1)S(1)} %bitcast.39), kind=kLoop, calls=%fused_computation.8 | loop fusion | flops 4816896 | bytes 2385424 | tf_op jit(solution)/shard_map/concatenate | solution.py:228
  6.2 0.0 collective-permute-done
  6.2 3.4 %collective-permute-start.1 = (s32[2,2,2,2]{3,2,1,0:T(2,128)S(1)}, s32[2,2,2,2]{3,2,1,0:T(2,128)S(1)}, u32[]{:S(2)}, u32[]{:S(2)}) collective-permute-start(s32[2,2,2,2]{3,2,1,0:T(2,128)S(1)} %pad_add_fusion.1), channel_id=1, source_target_pairs={{0,4},{1,5},{2,6},{3,7},{4,0},{5,1},{6,2},{7,3},{8,12},{9,13},{10,... | collective-permute-start | bytes 200 | tf_op jit(solution)/shard_map/ppermute | solution.py:210
  9.5 0.1 copy.17
  9.6 0.5 collective-permute-start.3
  10.1 1.0 collective-permute-done.1
  11.1 0.0 collective-permute-start.2
  11.1 0.9 collective-permute-start.4
  12.0 0.1 copy.18
  12.1 0.1 collective-permute-done.2
  12.3 0.1 copy.19
  12.4 0.1 pad_add_fusion.2
  12.5 8.2 %collective-permute-start.5 = (bf16[392,768]{1,0:T(8,128)(2,1)}, bf16[392,768]{1,0:T(8,128)(2,1)S(1)}, u32[]{:S(2)}, u32[]{:S(2)}) collective-permute-start(bf16[392,768]{1,0:T(8,128)(2,1)} %get-tuple-element.64), channel_id=1, source_target_pairs={{24,38},{25,39},{26,36},{27,37},{28,34},{29,35},{30,32},{31,33},{5... | collective-permute-start | bytes 1806344 | tf_op jit(solution)/shard_map/ppermute | solution.py:28
  20.7 0.7 collective-permute-start.7
  21.4 3.5 %collective-permute-done.3.refs_1_ = bf16[392,768]{1,0:T(8,128)(2,1)S(1)} collective-permute-done((bf16[392,768]{1,0:T(8,128)(2,1)S(1)}, bf16[392,768]{1,0:T(8,128)(2,1)S(1)}, u32[]{:S(2)}, u32[]{:S(2)}) %collective-permute-start.3) | collective-permute-done | bytes 602144 | tf_op jit(solution)/shard_map/ppermute | solution.py:28
  25.0 3.5 %collective-permute-done.4 = bf16[392,768]{1,0:T(8,128)(2,1)} collective-permute-done((bf16[392,768]{1,0:T(8,128)(2,1)S(1)}, bf16[392,768]{1,0:T(8,128)(2,1)}, u32[]{:S(2)}, u32[]{:S(2)}) %collective-permute-start.4) | collective-permute-done | bytes 602144 | tf_op jit(solution)/shard_map/ppermute | solution.py:28
  28.5 9.3 %copy.20 = bf16[2,8,2,192,768]{4,3,2,1,0:T(8,128)(2,1)} copy(bf16[2,8,2,192,768]{4,2,3,1,0:T(2,128)(2,1)} %bitcast.37) | data formatting | bytes 18874368 | tf_op jit(solution)/shard_map/transpose | solution.py:247
  37.8 1.4 %collective-permute-start.8 = (bf16[392,768]{1,0:T(8,128)(2,1)}, bf16[392,768]{1,0:T(8,128)(2,1)}, u32[]{:S(2)}, u32[]{:S(2)}) collective-permute-start(bf16[392,768]{1,0:T(8,128)(2,1)} %get-tuple-element.64), channel_id=1, source_target_pairs={{0,8},{1,9},{2,10},{3,11},{4,12},{5,13},{6,14},{7,15},{8,16},{9,17... | collective-permute-start | bytes 1806344 | tf_op jit(solution)/shard_map/ppermute | solution.py:28
  39.2 0.7 collective-permute-start.9
  39.9 7.5 %collective-permute-done.5.refs_0_ = bf16[392,768]{1,0:T(8,128)(2,1)S(1)} collective-permute-done((bf16[392,768]{1,0:T(8,128)(2,1)}, bf16[392,768]{1,0:T(8,128)(2,1)S(1)}, u32[]{:S(2)}, u32[]{:S(2)}) %collective-permute-start.5) | collective-permute-done | bytes 602144 | tf_op jit(solution)/shard_map/ppermute | solution.py:28
  47.4 2.0 %broadcast_select_fusion = bf16[392,768]{1,0:T(8,128)(2,1)} fusion(bf16[392,768]{1,0:T(8,128)(2,1)S(1)} %collective-permute-done.5.refs_0_, bf16[392,768]{1,0:T(8,128)(2,1)} %get-tuple-element.64, pred[]{:T(512)S(6)} %eq.9), kind=kLoop, calls=%fused_computation.9 | loop fusion | flops 301056 | bytes 1806337 | tf_op jit(solution)/shard_map/jit(_where)/select_n | solution.py:249
  49.4 1.3 %collective-permute-start.10 = (bf16[392,768]{1,0:T(8,128)(2,1)}, bf16[392,768]{1,0:T(8,128)(2,1)S(1)}, u32[]{:S(2)}, u32[]{:S(2)}) collective-permute-start(bf16[392,768]{1,0:T(8,128)(2,1)} %broadcast_select_fusion), channel_id=1, source_target_pairs={{0,8},{1,9},{2,10},{3,11},{4,12},{5,13},{6,14},{7,15},{8,24},{9,25... | collective-permute-start | bytes 1806344 | tf_op jit(solution)/shard_map/ppermute | solution.py:28
  50.7 0.1 collective-permute-start.6
  50.8 0.1 copy.24.pairs
  50.9 3.7 %copy-done = bf16[2,8,2,192,768]{4,3,2,1,0:T(8,128)(2,1)S(1)} copy-done((bf16[2,8,2,192,768]{4,3,2,1,0:T(8,128)(2,1)S(1)}, bf16[2,8,2,192,768]{4,3,2,1,0:T(8,128)(2,1)}, u32[]{:S(2)}) %copy-start) | copy-done | bytes 9437208
  54.6 4.3 %shard_map.55 = (f32[4,2,24,192]{3,2,1,0:T(8,128)S(1)}, f32[4,2,24,192]{3,2,1,0:T(8,128)S(1)}) custom-call(s32[2,2]{1,0:T(2,128)S(1)} %copy-done.1, s32[8,2,2,2]{3,2,1,0:T(2,128)S(1)} %copy.24.pairs, s32[2]{0:T(128)S(1)} %pad_add_fusion.3.here, f32[8]{0:T(128)S(1)} %copy-done.2, f32[2,1,192]{2,1,0:T(1,128)S(1)} %reshape.12.own_energy, ...), custom_call_target="tpu_custom_call" | custom-call | flops 1925185536 | bytes 5308416 | tf_op jit(solution)/shard_map/pallas_call | solution.py:174
  58.9 0.9 collective-permute-done.8.refs_1_
  59.8 4.6 %shard_map.56 = (f32[4,2,24,192]{3,2,1,0:T(8,128)S(1)}, f32[4,2,24,192]{3,2,1,0:T(8,128)S(1)}) custom-call(s32[2,2]{1,0:T(2,128)S(1)} %copy-done.1, s32[8,2,2,2]{3,2,1,0:T(2,128)S(1)} %copy.24.pairs, s32[2]{0:T(128)S(1)} %pad_add_fusion.3.here, f32[8]{0:T(128)S(1)} %copy-done.2, f32[2,1,192]{2,1,0:T(1,128)S(1)} %reshape.12.own_energy, ...), custom_call_target="tpu_custom_call" | custom-call | flops 1925185536 | bytes 5308416 | tf_op jit(solution)/shard_map/pallas_call | solution.py:174
  64.4 16.0 %collective-permute-done.10.refs_1_ = bf16[392,768]{1,0:T(8,128)(2,1)S(1)} collective-permute-done((bf16[392,768]{1,0:T(8,128)(2,1)}, bf16[392,768]{1,0:T(8,128)(2,1)S(1)}, u32[]{:S(2)}, u32[]{:S(2)}) %collective-permute-start.10) | collective-permute-done | bytes 602144 | tf_op jit(solution)/shard_map/ppermute | solution.py:28
  80.4 4.5 %shard_map.57 = (f32[4,2,24,192]{3,2,1,0:T(8,128)S(1)}, f32[4,2,24,192]{3,2,1,0:T(8,128)S(1)}) custom-call(s32[2,2]{1,0:T(2,128)S(1)} %copy-done.1, s32[8,2,2,2]{3,2,1,0:T(2,128)S(1)} %copy.24.pairs, s32[2]{0:T(128)S(1)} %pad_add_fusion.3.here, f32[8]{0:T(128)S(1)} %copy-done.2, f32[2,1,192]{2,1,0:T(1,128)S(1)} %reshape.12.own_energy, ...), custom_call_target="tpu_custom_call" | custom-call | flops 1925185536 | bytes 5308416 | tf_op jit(solution)/shard_map/pallas_call | solution.py:174
  84.9 0.0 collective-permute-done.6.refs_0_
  84.9 4.7 %shard_map.58 = (f32[4,2,2,24,192]{4,3,2,1,0:T(8,128)S(1)}, f32[4,2,2,24,192]{4,3,2,1,0:T(8,128)S(1)}) custom-call(s32[2,2]{1,0:T(2,128)S(1)} %copy-done.1, s32[8,2,2,2]{3,2,1,0:T(2,128)S(1)} %copy.24.pairs, s32[2]{0:T(128)S(1)} %pad_add_fusion.3.here, f32[8]{0:T(128)S(1)} %copy-done.2, f32[2,1,192]{2,1,0:T(1,128)S(1)} %reshape.12.own_energy, ...), custom_call_target="tpu_custom_call" | custom-call | flops 1925185536 | bytes 5308416 | tf_op jit(solution)/shard_map/pallas_call | solution.py:174
  89.6 0.1 collective-permute-start.11
  89.8 1.6 %collective-permute-done.11 = f32[4,2,2,24,192]{4,3,2,1,0:T(8,128)S(1)} collective-permute-done((f32[4,2,2,24,192]{4,3,2,1,0:T(8,128)S(1)}, f32[4,2,2,24,192]{4,3,2,1,0:T(8,128)S(1)}, u32[]{:S(2)}, u32[]{:S(2)}) %collective-permute-start.11) | collective-permute-done | bytes 294944 | tf_op jit(solution)/shard_map/ppermute | solution.py:200
  91.5 0.1 add.62
  91.6 2.0 %collective-permute-start.14 = (f32[2,2,24,192]{3,2,1,0:T(8,128)S(1)}, f32[2,2,24,192]{3,2,1,0:T(8,128)S(1)}, u32[]{:S(2)}, u32[]{:S(2)}) collective-permute-start(f32[2,2,24,192]{3,2,1,0:T(8,128)S(1)} %get-tuple-element.78), channel_id=1, source_target_pairs={{0,6},{1,7},{2,0},{3,1},{4,2},{5,3},{6,4},{7,5},{8,14},{9,15},{10,... | collective-permute-start | bytes 221192 | tf_op jit(solution)/shard_map/ppermute | solution.py:205
  93.6 7.6 %collective-permute-start.13 = (f32[2,2,24,192]{3,2,1,0:T(8,128)S(1)}, f32[2,2,24,192]{3,2,1,0:T(8,128)S(1)}, u32[]{:S(2)}, u32[]{:S(2)}) collective-permute-start(f32[2,2,24,192]{3,2,1,0:T(8,128)S(1)} %get-tuple-element.79), channel_id=1, source_target_pairs={{0,4},{1,5},{2,6},{3,7},{4,0},{5,1},{6,2},{7,3},{8,12},{9,13},{10,... | collective-permute-start | bytes 221192 | tf_op jit(solution)/shard_map/ppermute | solution.py:205
  101.2 0.0 collective-permute-start.12
  101.2 1.6 %collective-permute-done.14 = f32[2,2,24,192]{3,2,1,0:T(8,128)S(1)} collective-permute-done((f32[2,2,24,192]{3,2,1,0:T(8,128)S(1)}, f32[2,2,24,192]{3,2,1,0:T(8,128)S(1)}, u32[]{:S(2)}, u32[]{:S(2)}) %collective-permute-start.14) | collective-permute-done | bytes 73760 | tf_op jit(solution)/shard_map/ppermute | solution.py:205
  102.9 7.5 %collective-permute-done.13 = f32[2,2,24,192]{3,2,1,0:T(8,128)S(1)} collective-permute-done((f32[2,2,24,192]{3,2,1,0:T(8,128)S(1)}, f32[2,2,24,192]{3,2,1,0:T(8,128)S(1)}, u32[]{:S(2)}, u32[]{:S(2)}) %collective-permute-start.13) | collective-permute-done | bytes 73760 | tf_op jit(solution)/shard_map/ppermute | solution.py:205
  110.4 0.7 copy.25
  (18 shorter events, 0.1 us)
Async XLA Ops:
  0.0 6.2 %collective-permute-start = (s32[1,2,2,2]{3,2,1,0:T(2,128)}, s32[1,2,2,2]{3,2,1,0:T(2,128)S(1)}, u32[]{:S(2)}, u32[]{:S(2)}) collective-permute-start(s32[1,2,2,2]{3,2,1,0:T(2,128)} %bitcast.40), channel_id=1, source_target_pairs={{0,2},{1,3},{2,0},{3,1},{4,6},{5,7},{6,4},{7,5},{8,10},{9,11},{10,... | collective-permute-start | bytes 104 | tf_op jit(solution)/shard_map/ppermute | solution.py:210
  5.0 1.2 %copy-start.4 = (s32[2,2,2]{2,1,0:T(2,128)S(1)}, s32[2,2,2]{2,1,0:T(2,128)}, u32[]{:S(2)}) copy-start(s32[2,2,2]{2,1,0:T(2,128)} %param.9) | copy-start | bytes 100
  5.0 16.4 %copy-start.3 = (bf16[2,192]{1,0:T(2,128)(2,1)S(1)}, bf16[2,192]{1,0:T(2,128)(2,1)}, u32[]{:S(2)}) copy-start(bf16[2,192]{1,0:T(2,128)(2,1)} %param.7) | copy-start | bytes 2308
  6.2 4.9 %collective-permute-start.1 = (s32[2,2,2,2]{3,2,1,0:T(2,128)S(1)}, s32[2,2,2,2]{3,2,1,0:T(2,128)S(1)}, u32[]{:S(2)}, u32[]{:S(2)}) collective-permute-start(s32[2,2,2,2]{3,2,1,0:T(2,128)S(1)} %pad_add_fusion.1), channel_id=1, source_target_pairs={{0,4},{1,5},{2,6},{3,7},{4,0},{5,1},{6,2},{7,3},{8,12},{9,13},{10,... | collective-permute-start | bytes 200 | tf_op jit(solution)/shard_map/ppermute | solution.py:210
  9.6 15.3 %collective-permute-start.3 = (bf16[392,768]{1,0:T(8,128)(2,1)S(1)}, bf16[392,768]{1,0:T(8,128)(2,1)S(1)}, u32[]{:S(2)}, u32[]{:S(2)}) collective-permute-start(bf16[392,768]{1,0:T(8,128)(2,1)S(1)} %get-tuple-element.44), channel_id=1, source_target_pairs={{0,8},{1,9},{2,10},{3,11},{4,12},{5,13},{6,14},{7,15},{8,16},{9,17... | collective-permute-start | bytes 1806344 | tf_op jit(solution)/shard_map/ppermute | solution.py:28
  11.1 1.2 %collective-permute-start.2 = (s32[4,2,2,2]{3,2,1,0:T(2,128)S(1)}, s32[4,2,2,2]{3,2,1,0:T(2,128)S(1)}, u32[]{:S(2)}, u32[]{:S(2)}) collective-permute-start(s32[4,2,2,2]{3,2,1,0:T(2,128)S(1)} %pad_add_fusion), channel_id=1, source_target_pairs={{0,1},{1,0},{2,3},{3,2},{4,5},{5,4},{6,7},{7,6},{8,9},{9,8},{10,11... | collective-permute-start | bytes 392 | tf_op jit(solution)/shard_map/ppermute | solution.py:210
  11.1 17.3 %collective-permute-start.4 = (bf16[392,768]{1,0:T(8,128)(2,1)S(1)}, bf16[392,768]{1,0:T(8,128)(2,1)}, u32[]{:S(2)}, u32[]{:S(2)}) collective-permute-start(bf16[392,768]{1,0:T(8,128)(2,1)S(1)} %get-tuple-element.44), channel_id=1, source_target_pairs={{0,24},{1,25},{2,26},{3,27},{4,28},{5,29},{6,30},{7,31},{8,0},{9,1... | collective-permute-start | bytes 1806344 | tf_op jit(solution)/shard_map/ppermute | solution.py:28
  12.5 34.9 %collective-permute-start.5 = (bf16[392,768]{1,0:T(8,128)(2,1)}, bf16[392,768]{1,0:T(8,128)(2,1)S(1)}, u32[]{:S(2)}, u32[]{:S(2)}) collective-permute-start(bf16[392,768]{1,0:T(8,128)(2,1)} %get-tuple-element.64), channel_id=1, source_target_pairs={{24,38},{25,39},{26,36},{27,37},{28,34},{29,35},{30,32},{31,33},{5... | collective-permute-start | bytes 1806344 | tf_op jit(solution)/shard_map/ppermute | solution.py:28
  20.7 30.2 %collective-permute-start.7 = (bf16[392,768]{1,0:T(8,128)(2,1)}, bf16[392,768]{1,0:T(8,128)(2,1)S(1)}, u32[]{:S(2)}, u32[]{:S(2)}) collective-permute-start(bf16[392,768]{1,0:T(8,128)(2,1)} %get-tuple-element.64), channel_id=1, source_target_pairs={{0,16},{1,17},{2,18},{3,19},{4,20},{5,21},{6,22},{7,23},{16,38},{1... | collective-permute-start | bytes 1806344 | tf_op jit(solution)/shard_map/ppermute | solution.py:28
  37.8 13.1 %copy-start.1 = (s32[2,2]{1,0:T(2,128)S(1)}, s32[2,2]{1,0:T(2,128)}, u32[]{:S(2)}) copy-start(s32[2,2]{1,0:T(2,128)} %conserve.7) | copy-start | bytes 52
  37.8 13.1 %copy-start.2 = (f32[8]{0:T(128)S(1)}, f32[8]{0:T(128)}, u32[]{:S(2)}) copy-start(f32[8]{0:T(128)} %occupied.7) | copy-start | bytes 100
  37.8 22.1 %collective-permute-start.8 = (bf16[392,768]{1,0:T(8,128)(2,1)}, bf16[392,768]{1,0:T(8,128)(2,1)}, u32[]{:S(2)}, u32[]{:S(2)}) collective-permute-start(bf16[392,768]{1,0:T(8,128)(2,1)} %get-tuple-element.64), channel_id=1, source_target_pairs={{0,8},{1,9},{2,10},{3,11},{4,12},{5,13},{6,14},{7,15},{8,16},{9,17... | collective-permute-start | bytes 1806344 | tf_op jit(solution)/shard_map/ppermute | solution.py:28
  39.2 25.2 %collective-permute-start.9 = (bf16[392,768]{1,0:T(8,128)(2,1)S(1)}, bf16[392,768]{1,0:T(8,128)(2,1)S(1)}, u32[]{:S(2)}, u32[]{:S(2)}) collective-permute-start(bf16[392,768]{1,0:T(8,128)(2,1)S(1)} %collective-permute-done.3.refs_1_), channel_id=1, source_target_pairs={{0,38},{1,39},{2,36},{3,37},{4,34},{5,35},{6,32},{7,33},{32,6},{33... | collective-permute-start | bytes 1806344 | tf_op jit(solution)/shard_map/ppermute | solution.py:28
  49.4 31.0 %collective-permute-start.10 = (bf16[392,768]{1,0:T(8,128)(2,1)}, bf16[392,768]{1,0:T(8,128)(2,1)S(1)}, u32[]{:S(2)}, u32[]{:S(2)}) collective-permute-start(bf16[392,768]{1,0:T(8,128)(2,1)} %broadcast_select_fusion), channel_id=1, source_target_pairs={{0,8},{1,9},{2,10},{3,11},{4,12},{5,13},{6,14},{7,15},{8,24},{9,25... | collective-permute-start | bytes 1806344 | tf_op jit(solution)/shard_map/ppermute | solution.py:28
  50.7 34.3 %collective-permute-start.6 = (bf16[392,768]{1,0:T(8,128)(2,1)}, bf16[392,768]{1,0:T(8,128)(2,1)}, u32[]{:S(2)}, u32[]{:S(2)}) collective-permute-start(bf16[392,768]{1,0:T(8,128)(2,1)} %collective-permute-done.4), channel_id=1, source_target_pairs={{0,24},{1,25},{2,26},{3,27},{4,28},{5,29},{6,30},{7,31},{8,38},{9,... | collective-permute-start | bytes 1806344 | tf_op jit(solution)/shard_map/ppermute | solution.py:28
  50.9 3.7 %copy-start = (bf16[2,8,2,192,768]{4,3,2,1,0:T(8,128)(2,1)S(1)}, bf16[2,8,2,192,768]{4,3,2,1,0:T(8,128)(2,1)}, u32[]{:S(2)}) copy-start(bf16[2,8,2,192,768]{4,3,2,1,0:T(8,128)(2,1)} %copy.20) | copy-start | bytes 28311556
  89.6 1.8 %collective-permute-start.11 = (f32[4,2,2,24,192]{4,3,2,1,0:T(8,128)S(1)}, f32[4,2,2,24,192]{4,3,2,1,0:T(8,128)S(1)}, u32[]{:S(2)}, u32[]{:S(2)}) collective-permute-start(f32[4,2,2,24,192]{4,3,2,1,0:T(8,128)S(1)} %get-tuple-element.74), channel_id=1, source_target_pairs={{0,1},{1,0},{2,3},{3,2},{4,5},{5,4},{6,7},{7,6},{8,9},{9,8},{10,11... | collective-permute-start | bytes 884744 | tf_op jit(solution)/shard_map/ppermute | solution.py:200
  91.6 11.3 %collective-permute-start.14 = (f32[2,2,24,192]{3,2,1,0:T(8,128)S(1)}, f32[2,2,24,192]{3,2,1,0:T(8,128)S(1)}, u32[]{:S(2)}, u32[]{:S(2)}) collective-permute-start(f32[2,2,24,192]{3,2,1,0:T(8,128)S(1)} %get-tuple-element.78), channel_id=1, source_target_pairs={{0,6},{1,7},{2,0},{3,1},{4,2},{5,3},{6,4},{7,5},{8,14},{9,15},{10,... | collective-permute-start | bytes 221192 | tf_op jit(solution)/shard_map/ppermute | solution.py:205
  93.6 16.8 %collective-permute-start.13 = (f32[2,2,24,192]{3,2,1,0:T(8,128)S(1)}, f32[2,2,24,192]{3,2,1,0:T(8,128)S(1)}, u32[]{:S(2)}, u32[]{:S(2)}) collective-permute-start(f32[2,2,24,192]{3,2,1,0:T(8,128)S(1)} %get-tuple-element.79), channel_id=1, source_target_pairs={{0,4},{1,5},{2,6},{3,7},{4,0},{5,1},{6,2},{7,3},{8,12},{9,13},{10,... | collective-permute-start | bytes 221192 | tf_op jit(solution)/shard_map/ppermute | solution.py:205
  101.2 9.1 %collective-permute-start.12 = (f32[2,2,24,192]{3,2,1,0:T(8,128)S(1)}, f32[2,2,24,192]{3,2,1,0:T(8,128)S(1)}, u32[]{:S(2)}, u32[]{:S(2)}) collective-permute-start(f32[2,2,24,192]{3,2,1,0:T(8,128)S(1)} %get-tuple-element.77), channel_id=1, source_target_pairs={{0,2},{1,3},{2,4},{3,5},{4,6},{5,7},{6,0},{7,1},{8,10},{9,11},{10,... | collective-permute-start | bytes 221192 | tf_op jit(solution)/shard_map/ppermute | solution.py:205

commit v15 on v14

--- a/solution.py
+++ b/solution.py
@@ -236,11 +236,11 @@
     pairs = with_partner(with_partner(pairs, 2 * CORES), 1)
     m0, pairs, factors = lax.optimization_barrier((m0, pairs, factors))
     cross_one = moved(m0, {3: (0, onto_next)})
-    two = moved(m0, {0: (2, same), 2: (0, onto_next)})
     own_energy = virtual_energy.astype(jnp.float32)[:, None, :]
     m0, plus, minus, factors, pairs, own_energy = lax.optimization_barrier(
         (m0, plus, minus, factors, pairs, own_energy)
     )
+    two = moved(m0, {0: (2, same), 2: (0, onto_next)})
     up = moved(plus, {0: (0, across)})
     back = moved(minus, {0: (3, same), 1: (0, across), 2: (1, across), 3: (2, same)})
     near_one = moved(m0, {0: (1, same), 1: (2, same), 2: (3, same)})

time: 111 us -> 116 us (1.045)
  the two profiles are of different devices: /device:TPU:30 before, /device:TPU:10 now
where the time goes in v15:
time: 116 us; the launch traced here: 114 us
  starting transfers between devices  42.7 us (37%)
  waiting for transfers between devices  32 us (28%)
  Pallas kernels  18.1 us (16%)
  local copies, waits for them, and re-layouts  17.2 us (15%)
  other arithmetic  3.34 us (3%)
    ppermute x8, starting transfers between devices, moved(): return lax.ppermute(array, ('ka', 'occ'), pairs)  24 us
    ppermute x8, waiting for transfers between devices, moved(): return lax.ppermute(array, ('ka', 'occ'), pairs)  21.8 us
    pallas_call x4, Pallas kernels, piece_density(): pl.pallas_call(functools.partial(piece_kernel, len(mates), len(before), o...  18.1 us
    ppermute x3, starting transfers between devices, summed(): total = total + lax.ppermute(part, 'occ', ring)  13.2 us
    transpose x1, local copies, waits for them, and re-layouts, local(): jnp.transpose(factors, (0, 1, 3, 2, 4))  9.31 us
    ppermute x3, waiting for transfers between devices, summed(): total = total + lax.ppermute(part, 'occ', ring)  8.11 us
    ppermute x3, starting transfers between devices, with_partner(): lax.ppermute(array, 'occ', [(i, i ^ reach) for i in range(LINE * CORES)])  5.37 us
    unnamed x10, local copies, waits for them, and re-layouts  3.69 us
  transfers between devices with their start and end apart: 15, of which 7 were waited for; matrix products, arithmetic and copies ran while one was open for 14% of the time, Pallas kernels for 12%

profile of v15, /device:TPU:10, one launch (start us, length us, event | category | flops | bytes accessed | tf_op | source)
XLA Modules:
  0.0 113.6 jit_solution(9362566699339905584)
XLA Ops:
  0.0 1.9 %collective-permute-start = (s32[1,2,2,2]{3,2,1,0:T(2,128)}, s32[1,2,2,2]{3,2,1,0:T(2,128)S(1)}, u32[]{:S(2)}, u32[]{:S(2)}) collective-permute-start(s32[1,2,2,2]{3,2,1,0:T(2,128)} %bitcast.40), channel_id=1, source_target_pairs={{0,2},{1,3},{2,0},{3,1},{4,6},{5,7},{6,4},{7,5},{8,10},{9,11},{10,... | collective-permute-start | bytes 104 | tf_op jit(solution)/shard_map/ppermute | solution.py:210
  1.9 0.8 fusion.10
  2.7 2.1 %constant_dynamic-slice_fusion = (bf16[1,8,24,2,768]{4,3,2,1,0:T(2,128)(2,1)S(1)}, bf16[1,8,24,2,768]{4,3,2,1,0:T(2,128)(2,1)S(1)}) fusion(bf16[2,8,192,2,768]{4,3,2,1,0:T(2,128)(2,1)} %param.5, s32[]{:T(128)S(6)} %select_n.52), kind=kLoop, calls=%fused_computation.20 | loop fusion | bytes 2359300 | tf_op jit(solution)/shard_map/dynamic_slice | solution.py:222
  4.7 0.1 copy.29
  4.8 0.1 copy.28
  4.9 0.1 pad.23.clone
  5.0 0.1 pad_add_fusion.3.here
  5.0 1.1 fusion.6
  6.2 0.0 collective-permute-done
  6.2 3.4 %collective-permute-start.1 = (s32[2,2,2,2]{3,2,1,0:T(2,128)S(1)}, s32[2,2,2,2]{3,2,1,0:T(2,128)S(1)}, u32[]{:S(2)}, u32[]{:S(2)}) collective-permute-start(s32[2,2,2,2]{3,2,1,0:T(2,128)S(1)} %pad_add_fusion.1), channel_id=1, source_target_pairs={{0,4},{1,5},{2,6},{3,7},{4,0},{5,1},{6,2},{7,3},{8,12},{9,13},{10,... | collective-permute-start | bytes 200 | tf_op jit(solution)/shard_map/ppermute | solution.py:210
  9.5 0.1 copy.17
  9.6 1.5 %collective-permute-start.3 = (bf16[392,768]{1,0:T(8,128)(2,1)S(1)}, bf16[392,768]{1,0:T(8,128)(2,1)S(1)}, u32[]{:S(2)}, u32[]{:S(2)}) collective-permute-start(bf16[392,768]{1,0:T(8,128)(2,1)S(1)} %get-tuple-element.44), channel_id=1, source_target_pairs={{0,8},{1,9},{2,10},{3,11},{4,12},{5,13},{6,14},{7,15},{8,16},{9,17... | collective-permute-start | bytes 1806344 | tf_op jit(solution)/shard_map/ppermute | solution.py:28
  11.1 0.0 collective-permute-done.1
  11.1 0.1 collective-permute-start.2
  11.2 0.6 collective-permute-start.4
  11.9 0.1 copy.18
  12.0 0.4 collective-permute-done.2
  12.4 0.1 copy.19
  12.5 0.1 pad_add_fusion.2
  12.6 0.7 collective-permute-start.5
  13.3 11.1 %collective-permute-done.3.refs_1_ = bf16[392,768]{1,0:T(8,128)(2,1)S(1)} collective-permute-done((bf16[392,768]{1,0:T(8,128)(2,1)S(1)}, bf16[392,768]{1,0:T(8,128)(2,1)S(1)}, u32[]{:S(2)}, u32[]{:S(2)}) %collective-permute-start.3) | collective-permute-done | bytes 602144 | tf_op jit(solution)/shard_map/ppermute | solution.py:28
  24.4 2.9 %collective-permute-done.4 = bf16[392,768]{1,0:T(8,128)(2,1)} collective-permute-done((bf16[392,768]{1,0:T(8,128)(2,1)S(1)}, bf16[392,768]{1,0:T(8,128)(2,1)}, u32[]{:S(2)}, u32[]{:S(2)}) %collective-permute-start.4) | collective-permute-done | bytes 602144 | tf_op jit(solution)/shard_map/ppermute | solution.py:28
  27.4 0.7 collective-permute-start.7
  28.1 9.2 %collective-permute-start.8 = (bf16[392,768]{1,0:T(8,128)(2,1)}, bf16[392,768]{1,0:T(8,128)(2,1)}, u32[]{:S(2)}, u32[]{:S(2)}) collective-permute-start(bf16[392,768]{1,0:T(8,128)(2,1)} %get-tuple-element.64), channel_id=1, source_target_pairs={{0,8},{1,9},{2,10},{3,11},{4,12},{5,13},{6,14},{7,15},{8,16},{9,17... | collective-permute-start | bytes 1806344 | tf_op jit(solution)/shard_map/ppermute | solution.py:28
  37.3 9.3 %copy.20 = bf16[2,8,2,192,768]{4,3,2,1,0:T(8,128)(2,1)} copy(bf16[2,8,2,192,768]{4,2,3,1,0:T(2,128)(2,1)} %bitcast.37) | data formatting | bytes 18874368 | tf_op jit(solution)/shard_map/transpose | solution.py:247
  46.6 0.8 collective-permute-start.9
  47.4 0.0 collective-permute-done.5.refs_0_
  47.4 2.0 %broadcast_select_fusion = bf16[392,768]{1,0:T(8,128)(2,1)} fusion(bf16[392,768]{1,0:T(8,128)(2,1)S(1)} %collective-permute-done.5.refs_0_, bf16[392,768]{1,0:T(8,128)(2,1)} %get-tuple-element.64, pred[]{:T(512)S(6)} %eq.9), kind=kLoop, calls=%fused_computation.9 | loop fusion | flops 301056 | bytes 1806337 | tf_op jit(solution)/shard_map/jit(_where)/select_n | solution.py:249
  49.4 6.2 %collective-permute-start.10 = (bf16[392,768]{1,0:T(8,128)(2,1)}, bf16[392,768]{1,0:T(8,128)(2,1)S(1)}, u32[]{:S(2)}, u32[]{:S(2)}) collective-permute-start(bf16[392,768]{1,0:T(8,128)(2,1)} %broadcast_select_fusion), channel_id=1, source_target_pairs={{0,8},{1,9},{2,10},{3,11},{4,12},{5,13},{6,14},{7,15},{8,24},{9,25... | collective-permute-start | bytes 1806344 | tf_op jit(solution)/shard_map/ppermute | solution.py:28
  55.7 4.2 %collective-permute-start.6 = (bf16[392,768]{1,0:T(8,128)(2,1)}, bf16[392,768]{1,0:T(8,128)(2,1)}, u32[]{:S(2)}, u32[]{:S(2)}) collective-permute-start(bf16[392,768]{1,0:T(8,128)(2,1)} %collective-permute-done.4), channel_id=1, source_target_pairs={{0,24},{1,25},{2,26},{3,27},{4,28},{5,29},{6,30},{7,31},{8,38},{9,... | collective-permute-start | bytes 1806344 | tf_op jit(solution)/shard_map/ppermute | solution.py:28
  59.9 0.1 copy.24.pairs
  60.0 3.7 %copy-done = bf16[2,8,2,192,768]{4,3,2,1,0:T(8,128)(2,1)S(1)} copy-done((bf16[2,8,2,192,768]{4,3,2,1,0:T(8,128)(2,1)S(1)}, bf16[2,8,2,192,768]{4,3,2,1,0:T(8,128)(2,1)}, u32[]{:S(2)}) %copy-start) | copy-done | bytes 9437208
  63.7 4.3 %shard_map.55 = (f32[4,2,24,192]{3,2,1,0:T(8,128)S(1)}, f32[4,2,24,192]{3,2,1,0:T(8,128)S(1)}) custom-call(s32[2,2]{1,0:T(2,128)S(1)} %copy-done.1, s32[8,2,2,2]{3,2,1,0:T(2,128)S(1)} %copy.24.pairs, s32[2]{0:T(128)S(1)} %pad_add_fusion.3.here, f32[8]{0:T(128)S(1)} %copy-done.2, f32[2,1,192]{2,1,0:T(1,128)S(1)} %reshape.12.own_energy, ...), custom_call_target="tpu_custom_call" | custom-call | flops 1925185536 | bytes 5308416 | tf_op jit(solution)/shard_map/pallas_call | solution.py:174
  68.0 0.0 collective-permute-done.8.refs_1_
  68.1 4.6 %shard_map.56 = (f32[4,2,24,192]{3,2,1,0:T(8,128)S(1)}, f32[4,2,24,192]{3,2,1,0:T(8,128)S(1)}) custom-call(s32[2,2]{1,0:T(2,128)S(1)} %copy-done.1, s32[8,2,2,2]{3,2,1,0:T(2,128)S(1)} %copy.24.pairs, s32[2]{0:T(128)S(1)} %pad_add_fusion.3.here, f32[8]{0:T(128)S(1)} %copy-done.2, f32[2,1,192]{2,1,0:T(1,128)S(1)} %reshape.12.own_energy, ...), custom_call_target="tpu_custom_call" | custom-call | flops 1925185536 | bytes 5308416 | tf_op jit(solution)/shard_map/pallas_call | solution.py:174
  72.6 7.8 %collective-permute-done.10.refs_1_ = bf16[392,768]{1,0:T(8,128)(2,1)S(1)} collective-permute-done((bf16[392,768]{1,0:T(8,128)(2,1)}, bf16[392,768]{1,0:T(8,128)(2,1)S(1)}, u32[]{:S(2)}, u32[]{:S(2)}) %collective-permute-start.10) | collective-permute-done | bytes 602144 | tf_op jit(solution)/shard_map/ppermute | solution.py:28
  80.4 4.5 %shard_map.57 = (f32[4,2,24,192]{3,2,1,0:T(8,128)S(1)}, f32[4,2,24,192]{3,2,1,0:T(8,128)S(1)}) custom-call(s32[2,2]{1,0:T(2,128)S(1)} %copy-done.1, s32[8,2,2,2]{3,2,1,0:T(2,128)S(1)} %copy.24.pairs, s32[2]{0:T(128)S(1)} %pad_add_fusion.3.here, f32[8]{0:T(128)S(1)} %copy-done.2, f32[2,1,192]{2,1,0:T(1,128)S(1)} %reshape.12.own_energy, ...), custom_call_target="tpu_custom_call" | custom-call | flops 1925185536 | bytes 5308416 | tf_op jit(solution)/shard_map/pallas_call | solution.py:174
  84.9 0.0 collective-permute-done.6.refs_0_
  84.9 4.7 %shard_map.58 = (f32[4,2,2,24,192]{4,3,2,1,0:T(8,128)S(1)}, f32[4,2,2,24,192]{4,3,2,1,0:T(8,128)S(1)}) custom-call(s32[2,2]{1,0:T(2,128)S(1)} %copy-done.1, s32[8,2,2,2]{3,2,1,0:T(2,128)S(1)} %copy.24.pairs, s32[2]{0:T(128)S(1)} %pad_add_fusion.3.here, f32[8]{0:T(128)S(1)} %copy-done.2, f32[2,1,192]{2,1,0:T(1,128)S(1)} %reshape.12.own_energy, ...), custom_call_target="tpu_custom_call" | custom-call | flops 1925185536 | bytes 5308416 | tf_op jit(solution)/shard_map/pallas_call | solution.py:174
  89.6 0.1 collective-permute-start.11
  89.8 1.6 %collective-permute-done.11 = f32[4,2,2,24,192]{4,3,2,1,0:T(8,128)S(1)} collective-permute-done((f32[4,2,2,24,192]{4,3,2,1,0:T(8,128)S(1)}, f32[4,2,2,24,192]{4,3,2,1,0:T(8,128)S(1)}, u32[]{:S(2)}, u32[]{:S(2)}) %collective-permute-start.11) | collective-permute-done | bytes 294944 | tf_op jit(solution)/shard_map/ppermute | solution.py:200
  91.4 0.1 add.62
  91.5 2.0 %collective-permute-start.14 = (f32[2,2,24,192]{3,2,1,0:T(8,128)S(1)}, f32[2,2,24,192]{3,2,1,0:T(8,128)S(1)}, u32[]{:S(2)}, u32[]{:S(2)}) collective-permute-start(f32[2,2,24,192]{3,2,1,0:T(8,128)S(1)} %get-tuple-element.78), channel_id=1, source_target_pairs={{0,6},{1,7},{2,0},{3,1},{4,2},{5,3},{6,4},{7,5},{8,14},{9,15},{10,... | collective-permute-start | bytes 221192 | tf_op jit(solution)/shard_map/ppermute | solution.py:205
  93.6 10.1 %collective-permute-start.13 = (f32[2,2,24,192]{3,2,1,0:T(8,128)S(1)}, f32[2,2,24,192]{3,2,1,0:T(8,128)S(1)}, u32[]{:S(2)}, u32[]{:S(2)}) collective-permute-start(f32[2,2,24,192]{3,2,1,0:T(8,128)S(1)} %get-tuple-element.79), channel_id=1, source_target_pairs={{0,4},{1,5},{2,6},{3,7},{4,0},{5,1},{6,2},{7,3},{8,12},{9,13},{10,... | collective-permute-start | bytes 221192 | tf_op jit(solution)/shard_map/ppermute | solution.py:205
  103.7 1.0 collective-permute-start.12
  104.7 0.6 collective-permute-done.14
  105.4 7.5 %collective-permute-done.13 = f32[2,2,24,192]{3,2,1,0:T(8,128)S(1)} collective-permute-done((f32[2,2,24,192]{3,2,1,0:T(8,128)S(1)}, f32[2,2,24,192]{3,2,1,0:T(8,128)S(1)}, u32[]{:S(2)}, u32[]{:S(2)}) %collective-permute-start.13) | collective-permute-done | bytes 73760 | tf_op jit(solution)/shard_map/ppermute | solution.py:205
  112.9 0.7 copy.25
  (18 shorter events, 0.1 us)
Async XLA Ops:
  0.0 6.2 %collective-permute-start = (s32[1,2,2,2]{3,2,1,0:T(2,128)}, s32[1,2,2,2]{3,2,1,0:T(2,128)S(1)}, u32[]{:S(2)}, u32[]{:S(2)}) collective-permute-start(s32[1,2,2,2]{3,2,1,0:T(2,128)} %bitcast.40), channel_id=1, source_target_pairs={{0,2},{1,3},{2,0},{3,1},{4,6},{5,7},{6,4},{7,5},{8,10},{9,11},{10,... | collective-permute-start | bytes 104 | tf_op jit(solution)/shard_map/ppermute | solution.py:210
  5.0 1.2 %copy-start.4 = (s32[2,2,2]{2,1,0:T(2,128)S(1)}, s32[2,2,2]{2,1,0:T(2,128)}, u32[]{:S(2)}) copy-start(s32[2,2,2]{2,1,0:T(2,128)} %param.9) | copy-start | bytes 100
  5.0 8.3 %copy-start.3 = (bf16[2,192]{1,0:T(2,128)(2,1)S(1)}, bf16[2,192]{1,0:T(2,128)(2,1)}, u32[]{:S(2)}) copy-start(bf16[2,192]{1,0:T(2,128)(2,1)} %param.7) | copy-start | bytes 2308
  6.2 5.0 %collective-permute-start.1 = (s32[2,2,2,2]{3,2,1,0:T(2,128)S(1)}, s32[2,2,2,2]{3,2,1,0:T(2,128)S(1)}, u32[]{:S(2)}, u32[]{:S(2)}) collective-permute-start(s32[2,2,2,2]{3,2,1,0:T(2,128)S(1)} %pad_add_fusion.1), channel_id=1, source_target_pairs={{0,4},{1,5},{2,6},{3,7},{4,0},{5,1},{6,2},{7,3},{8,12},{9,13},{10,... | collective-permute-start | bytes 200 | tf_op jit(solution)/shard_map/ppermute | solution.py:210
  9.6 14.8 %collective-permute-start.3 = (bf16[392,768]{1,0:T(8,128)(2,1)S(1)}, bf16[392,768]{1,0:T(8,128)(2,1)S(1)}, u32[]{:S(2)}, u32[]{:S(2)}) collective-permute-start(bf16[392,768]{1,0:T(8,128)(2,1)S(1)} %get-tuple-element.44), channel_id=1, source_target_pairs={{0,8},{1,9},{2,10},{3,11},{4,12},{5,13},{6,14},{7,15},{8,16},{9,17... | collective-permute-start | bytes 1806344 | tf_op jit(solution)/shard_map/ppermute | solution.py:28
  11.1 1.3 %collective-permute-start.2 = (s32[4,2,2,2]{3,2,1,0:T(2,128)S(1)}, s32[4,2,2,2]{3,2,1,0:T(2,128)S(1)}, u32[]{:S(2)}, u32[]{:S(2)}) collective-permute-start(s32[4,2,2,2]{3,2,1,0:T(2,128)S(1)} %pad_add_fusion), channel_id=1, source_target_pairs={{0,1},{1,0},{2,3},{3,2},{4,5},{5,4},{6,7},{7,6},{8,9},{9,8},{10,11... | collective-permute-start | bytes 392 | tf_op jit(solution)/shard_map/ppermute | solution.py:210
  11.2 16.1 %collective-permute-start.4 = (bf16[392,768]{1,0:T(8,128)(2,1)S(1)}, bf16[392,768]{1,0:T(8,128)(2,1)}, u32[]{:S(2)}, u32[]{:S(2)}) collective-permute-start(bf16[392,768]{1,0:T(8,128)(2,1)S(1)} %get-tuple-element.44), channel_id=1, source_target_pairs={{0,24},{1,25},{2,26},{3,27},{4,28},{5,29},{6,30},{7,31},{8,0},{9,1... | collective-permute-start | bytes 1806344 | tf_op jit(solution)/shard_map/ppermute | solution.py:28
  12.6 34.8 %collective-permute-start.5 = (bf16[392,768]{1,0:T(8,128)(2,1)}, bf16[392,768]{1,0:T(8,128)(2,1)S(1)}, u32[]{:S(2)}, u32[]{:S(2)}) collective-permute-start(bf16[392,768]{1,0:T(8,128)(2,1)} %get-tuple-element.64), channel_id=1, source_target_pairs={{24,38},{25,39},{26,36},{27,37},{28,34},{29,35},{30,32},{31,33},{5... | collective-permute-start | bytes 1806344 | tf_op jit(solution)/shard_map/ppermute | solution.py:28
  27.4 32.7 %collective-permute-start.7 = (bf16[392,768]{1,0:T(8,128)(2,1)}, bf16[392,768]{1,0:T(8,128)(2,1)S(1)}, u32[]{:S(2)}, u32[]{:S(2)}) collective-permute-start(bf16[392,768]{1,0:T(8,128)(2,1)} %get-tuple-element.64), channel_id=1, source_target_pairs={{0,16},{1,17},{2,18},{3,19},{4,20},{5,21},{6,22},{7,23},{16,38},{1... | collective-permute-start | bytes 1806344 | tf_op jit(solution)/shard_map/ppermute | solution.py:28
  28.1 40.0 %collective-permute-start.8 = (bf16[392,768]{1,0:T(8,128)(2,1)}, bf16[392,768]{1,0:T(8,128)(2,1)}, u32[]{:S(2)}, u32[]{:S(2)}) collective-permute-start(bf16[392,768]{1,0:T(8,128)(2,1)} %get-tuple-element.64), channel_id=1, source_target_pairs={{0,8},{1,9},{2,10},{3,11},{4,12},{5,13},{6,14},{7,15},{8,16},{9,17... | collective-permute-start | bytes 1806344 | tf_op jit(solution)/shard_map/ppermute | solution.py:28
  46.6 13.4 %copy-start.1 = (s32[2,2]{1,0:T(2,128)S(1)}, s32[2,2]{1,0:T(2,128)}, u32[]{:S(2)}) copy-start(s32[2,2]{1,0:T(2,128)} %conserve.7) | copy-start | bytes 52
  46.6 13.4 %copy-start.2 = (f32[8]{0:T(128)S(1)}, f32[8]{0:T(128)}, u32[]{:S(2)}) copy-start(f32[8]{0:T(128)} %occupied.7) | copy-start | bytes 100
  46.6 26.0 %collective-permute-start.9 = (bf16[392,768]{1,0:T(8,128)(2,1)S(1)}, bf16[392,768]{1,0:T(8,128)(2,1)S(1)}, u32[]{:S(2)}, u32[]{:S(2)}) collective-permute-start(bf16[392,768]{1,0:T(8,128)(2,1)S(1)} %collective-permute-done.3.refs_1_), channel_id=1, source_target_pairs={{0,38},{1,39},{2,36},{3,37},{4,34},{5,35},{6,32},{7,33},{32,6},{33... | collective-permute-start | bytes 1806344 | tf_op jit(solution)/shard_map/ppermute | solution.py:28
  49.4 31.0 %collective-permute-start.10 = (bf16[392,768]{1,0:T(8,128)(2,1)}, bf16[392,768]{1,0:T(8,128)(2,1)S(1)}, u32[]{:S(2)}, u32[]{:S(2)}) collective-permute-start(bf16[392,768]{1,0:T(8,128)(2,1)} %broadcast_select_fusion), channel_id=1, source_target_pairs={{0,8},{1,9},{2,10},{3,11},{4,12},{5,13},{6,14},{7,15},{8,24},{9,25... | collective-permute-start | bytes 1806344 | tf_op jit(solution)/shard_map/ppermute | solution.py:28
  55.7 29.3 %collective-permute-start.6 = (bf16[392,768]{1,0:T(8,128)(2,1)}, bf16[392,768]{1,0:T(8,128)(2,1)}, u32[]{:S(2)}, u32[]{:S(2)}) collective-permute-start(bf16[392,768]{1,0:T(8,128)(2,1)} %collective-permute-done.4), channel_id=1, source_target_pairs={{0,24},{1,25},{2,26},{3,27},{4,28},{5,29},{6,30},{7,31},{8,38},{9,... | collective-permute-start | bytes 1806344 | tf_op jit(solution)/shard_map/ppermute | solution.py:28
  60.0 3.7 %copy-start = (bf16[2,8,2,192,768]{4,3,2,1,0:T(8,128)(2,1)S(1)}, bf16[2,8,2,192,768]{4,3,2,1,0:T(8,128)(2,1)}, u32[]{:S(2)}) copy-start(bf16[2,8,2,192,768]{4,3,2,1,0:T(8,128)(2,1)} %copy.20) | copy-start | bytes 28311556
  89.6 1.8 %collective-permute-start.11 = (f32[4,2,2,24,192]{4,3,2,1,0:T(8,128)S(1)}, f32[4,2,2,24,192]{4,3,2,1,0:T(8,128)S(1)}, u32[]{:S(2)}, u32[]{:S(2)}) collective-permute-start(f32[4,2,2,24,192]{4,3,2,1,0:T(8,128)S(1)} %get-tuple-element.74), channel_id=1, source_target_pairs={{0,1},{1,0},{2,3},{3,2},{4,5},{5,4},{6,7},{7,6},{8,9},{9,8},{10,11... | collective-permute-start | bytes 884744 | tf_op jit(solution)/shard_map/ppermute | solution.py:200
  91.5 13.8 %collective-permute-start.14 = (f32[2,2,24,192]{3,2,1,0:T(8,128)S(1)}, f32[2,2,24,192]{3,2,1,0:T(8,128)S(1)}, u32[]{:S(2)}, u32[]{:S(2)}) collective-permute-start(f32[2,2,24,192]{3,2,1,0:T(8,128)S(1)} %get-tuple-element.78), channel_id=1, source_target_pairs={{0,6},{1,7},{2,0},{3,1},{4,2},{5,3},{6,4},{7,5},{8,14},{9,15},{10,... | collective-permute-start | bytes 221192 | tf_op jit(solution)/shard_map/ppermute | solution.py:205
  93.6 19.3 %collective-permute-start.13 = (f32[2,2,24,192]{3,2,1,0:T(8,128)S(1)}, f32[2,2,24,192]{3,2,1,0:T(8,128)S(1)}, u32[]{:S(2)}, u32[]{:S(2)}) collective-permute-start(f32[2,2,24,192]{3,2,1,0:T(8,128)S(1)} %get-tuple-element.79), channel_id=1, source_target_pairs={{0,4},{1,5},{2,6},{3,7},{4,0},{5,1},{6,2},{7,3},{8,12},{9,13},{10,... | collective-permute-start | bytes 221192 | tf_op jit(solution)/shard_map/ppermute | solution.py:205
  103.7 9.1 %collective-permute-start.12 = (f32[2,2,24,192]{3,2,1,0:T(8,128)S(1)}, f32[2,2,24,192]{3,2,1,0:T(8,128)S(1)}, u32[]{:S(2)}, u32[]{:S(2)}) collective-permute-start(f32[2,2,24,192]{3,2,1,0:T(8,128)S(1)} %get-tuple-element.77), channel_id=1, source_target_pairs={{0,2},{1,3},{2,4},{3,5},{4,6},{5,7},{6,0},{7,1},{8,10},{9,11},{10,... | collective-permute-start | bytes 221192 | tf_op jit(solution)/shard_map/ppermute | solution.py:205
